TPU v7x, 32 devices: a whole 2x2x4 slice. The times are simulated.
32 devices in a mesh: dp: 4 (over z), ctx: 8 (over y, x, core).
Axes of the slice: x: 2, y: 2, z: 4, core: 2. Of those that a mesh axis runs over, the one named last changes fastest.
Arguments:
- tokens: bfloat16 [2, 4, 1024, 2048], P(None, 'dp', 'ctx'), may hold values from -6 to 6
- cotangent: bfloat16 [2, 4, 1024, 2048], P(None, 'dp', 'ctx'), may hold values from -6 to 6
- routes: int32 [2, 4, 1024, 8], P(None, 'dp', 'ctx'), may hold values from 0 to 15, all different within a row; in each aligned block of 128 rows (0 to 127, 128 to 255, ..., all dimensions but the last counted through in order) at most 67 rows name the same one
- lengths: int32 [2, 4], P(None, 'dp'), may hold values from 256 to 1024, as said below
- block_order: int32 [16], replicated, may hold values from 0 to 15, each once
- w_query: bfloat16 [2048, 2048], P(('dp', 'ctx')), may hold values from -0.125 to 0.125
- w_key: bfloat16 [2048, 2048], P(('dp', 'ctx')), may hold values from -0.125 to 0.125
- w_value: bfloat16 [2048, 2048], P(('dp', 'ctx')), may hold values from -0.125 to 0.125
- w_out: bfloat16 [2048, 2048], P(('dp', 'ctx')), may hold values from -2 to 2
- w_router: bfloat16 [2048, 16], P(('dp', 'ctx')), may hold values from -0.0625 to 0.0625
- w_gate: bfloat16 [16, 2048, 1024], P('ctx', 'dp'), may hold values from -0.125 to 0.125
- w_up: bfloat16 [16, 2048, 1024], P('ctx', 'dp'), may hold values from -0.125 to 0.125
- w_down: bfloat16 [16, 1024, 2048], P('ctx', 'dp'), may hold values from -3 to 3
- attn_gain: bfloat16 [2048], P(('dp', 'ctx')), may hold values from 0.099609375 to 1.8984375
- mlp_gain: bfloat16 [2048], P(('dp', 'ctx')), may hold values from 0.099609375 to 1.8984375
- query_gain: bfloat16 [2048], P(('dp', 'ctx')), may hold values from 0.099609375 to 1.8984375
- key_gain: bfloat16 [2048], P(('dp', 'ctx')), may hold values from 0.099609375 to 1.8984375
Outputs:
- mixed: bfloat16 [2, 4, 1024, 2048], P(None, 'dp', 'ctx')
- d_tokens: float32 [2, 4, 1024, 2048], P(None, 'dp', 'ctx')
- d_w_query: float32 [2048, 2048], P(('dp', 'ctx'))
- d_w_key: float32 [2048, 2048], P(('dp', 'ctx'))
- d_w_value: float32 [2048, 2048], P(('dp', 'ctx'))
- d_w_out: float32 [2048, 2048], P(('dp', 'ctx'))
- d_w_router: float32 [2048, 16], P(('dp', 'ctx'))
- d_w_gate: float32 [16, 2048, 1024], P('ctx', 'dp')
- d_w_up: float32 [16, 2048, 1024], P('ctx', 'dp')
- d_w_down: float32 [16, 1024, 2048], P('ctx', 'dp')
- d_attn_gain: float32 [2048], P(('dp', 'ctx'))
- d_mlp_gain: float32 [2048], P(('dp', 'ctx'))
- d_query_gain: float32 [2048], P(('dp', 'ctx'))
- d_key_gain: float32 [2048], P(('dp', 'ctx'))
Inputs may be any that keep to these rules, and one draw needn't show every extreme that they name: `routes`: within the rows of one device (aligned blocks of 128 rows) no expert is named more than 67 times, a bound that some block reaches. `lengths`: in every micro-batch some slot is full. `block_order`: each block number appears once.
All inputs are finite; a program needn't handle non-finite values.
Results may differ from a plain program's by a relative error of at most 0.02.
Values may be sent and summed in bfloat16 or wider, within the bound.
A program may use at most 448 MiB of HBM per device.

v0:
```python
import math

import jax
import jax.numpy as jnp
from jax import lax
from jax.sharding import PartitionSpec as P

HEAD = 128


EPSILON = 1e-05
ROPE_BASE = 10000.0
MASKED = -1e30


def norm_rows(values, gain_vec):
    inv_root = lax.rsqrt(jnp.mean(values * values, axis=-1, keepdims=True) + EPSILON)
    return (values * inv_root * gain_vec, inv_root)


def norm_back(values, inv_root, gain_vec, grad_in):
    weighted = grad_in * gain_vec
    inner = jnp.mean(weighted * values, axis=-1, keepdims=True)
    grad_values = inv_root * weighted - values * (inv_root * inv_root * inv_root) * inner
    return (grad_values, jnp.sum(grad_in * values * inv_root, axis=0))


def positions(stored, block_order, half_size):
    block_ids = stored // half_size
    numbers = jnp.arange(block_order.shape[0], dtype=jnp.int32)
    match_marks = block_ids[:, None] == numbers[None, :]
    first_place = jnp.sum(jnp.where(match_marks, block_order[None, :], 0), axis=1)
    return first_place * half_size + stored % half_size


def angles(places, head_width):
    index = jnp.arange(head_width // 2, dtype=jnp.float32)
    freqs = jnp.power(ROPE_BASE, -2.0 * index / head_width)
    turning = places.astype(jnp.float32)[:, None] * freqs[None, :]
    turning = jnp.concatenate([turning, turning], axis=1)
    return (jnp.cos(turning)[:, None, :], jnp.sin(turning)[:, None, :])


def rotate(values, cosine, sine):
    half_size = values.shape[-1] // 2
    turned = jnp.concatenate([-values[..., half_size:], values[..., :half_size]], axis=-1)
    return values * cosine + turned * sine


def rotate_back(grad_in, cosine, sine):
    half_size = grad_in.shape[-1] // 2
    moved = grad_in * sine
    return grad_in * cosine + jnp.concatenate(
        [moved[..., half_size:], -moved[..., :half_size]], axis=-1
    )


def on_device(
    tokens,
    cotangent,
    routes,
    lengths,
    block_order,
    w_query,
    w_key,
    w_value,
    w_out,
    w_router,
    w_gate,
    w_up,
    w_down,
    attn_gain,
    mlp_gain,
    query_gain,
    key_gain,
):
    batches = tokens.shape[0]
    tok_rows = tokens.shape[2]
    model_width = tokens.shape[3]
    ctx_size = lax.axis_size("ctx")
    slot_len = tok_rows * ctx_size
    half_size = tok_rows // 2
    head_dim = HEAD
    head_count = model_width // head_dim
    expert_count = w_router.shape[1]
    local_experts = w_gate.shape[0]
    top_count = routes.shape[-1]
    assigned = tok_rows * top_count
    capacity = assigned // expert_count + assigned // (32 * expert_count) + 1
    factor = 1.0 / math.sqrt(head_dim)
    bf_zero = jnp.zeros((), jnp.bfloat16)
    here = lax.axis_index("ctx")
    my_pos = positions(
        here * tok_rows + jnp.arange(tok_rows, dtype=jnp.int32), block_order, half_size
    )
    all_pos = positions(jnp.arange(slot_len, dtype=jnp.int32), block_order, half_size)
    cosine, sine = angles(my_pos, head_dim)
    expert_range = jnp.arange(expert_count, dtype=jnp.int32)
    acc_attn_gain = jnp.zeros((model_width,), jnp.float32)
    acc_mlp_gain = jnp.zeros((model_width,), jnp.float32)
    acc_query_gain = jnp.zeros((model_width,), jnp.float32)
    acc_key_gain = jnp.zeros((model_width,), jnp.float32)
    act_list = []
    dq_list = []
    dk_list = []
    dv_list = []
    attended_list = []
    datt_list = []
    mixed_list = []
    dlogit_list = []
    recv_list = []
    hidden_list = []
    dexp_list = []
    dgate_list = []
    dup_list = []
    outputs = []
    input_grads = []
    for batch_index in range(batches):
        dense_full = (
            lax.all_gather(w_query, ("dp", "ctx"), axis=0, tiled=True),
            lax.all_gather(w_key, ("dp", "ctx"), axis=0, tiled=True),
            lax.all_gather(w_value, ("dp", "ctx"), axis=0, tiled=True),
            lax.all_gather(w_out, ("dp", "ctx"), axis=0, tiled=True),
            lax.all_gather(w_router, ("dp", "ctx"), axis=0, tiled=True),
            lax.all_gather(attn_gain, ("dp", "ctx"), axis=0, tiled=True),
            lax.all_gather(mlp_gain, ("dp", "ctx"), axis=0, tiled=True),
            lax.all_gather(query_gain, ("dp", "ctx"), axis=0, tiled=True),
            lax.all_gather(key_gain, ("dp", "ctx"), axis=0, tiled=True),
        )
        expert_full = (
            lax.all_gather(w_gate, "dp", axis=1, tiled=True),
            lax.all_gather(w_up, "dp", axis=1, tiled=True),
            lax.all_gather(w_down, "dp", axis=1, tiled=True),
        )
        query_w, key_w, value_w, out_w, router_w, gain_attn, gain_mlp, gain_query, gain_key = (
            dense_full
        )
        gate_full, up_full, down_full = expert_full
        gain_attn = gain_attn.astype(jnp.float32)
        gain_mlp = gain_mlp.astype(jnp.float32)
        gain_query = gain_query.astype(jnp.float32)
        gain_key = gain_key.astype(jnp.float32)
        inputs = tokens[batch_index, 0].astype(jnp.float32)
        act_f, attn_root = norm_rows(inputs, gain_attn)
        act = act_f.astype(jnp.bfloat16)
        query_pre = jnp.dot(act, query_w, preferred_element_type=jnp.float32)
        key_pre = jnp.dot(act, key_w, preferred_element_type=jnp.float32)
        value_pre = jnp.dot(act, value_w, preferred_element_type=jnp.float32)
        query_n, query_root = norm_rows(query_pre, gain_query)
        key_n, key_root = norm_rows(key_pre, gain_key)
        query = rotate(query_n.reshape(tok_rows, head_count, head_dim), cosine, sine).astype(
            jnp.bfloat16
        )
        key_rot = (
            rotate(key_n.reshape(tok_rows, head_count, head_dim), cosine, sine)
            .astype(jnp.bfloat16)
            .reshape(tok_rows, model_width)
        )
        values = value_pre.astype(jnp.bfloat16)
        keys_all, values_all = (
            lax.all_gather(key_rot, "ctx", axis=0, tiled=True),
            lax.all_gather(values, "ctx", axis=0, tiled=True),
        )
        keys_all = keys_all.reshape(slot_len, head_count, head_dim)
        values_all = values_all.reshape(slot_len, head_count, head_dim)
        length = lengths[batch_index, 0]
        allowed = (all_pos[None, :] <= my_pos[:, None]) & (all_pos[None, :] < length)
        scores = (
            jnp.einsum("qhd,khd->hqk", query, keys_all, preferred_element_type=jnp.float32) * factor
        )
        scores = jnp.where(allowed[None], scores, MASKED)
        peak = jnp.max(scores, axis=-1, keepdims=True)
        expo = jnp.exp(scores - peak)
        totals = jnp.sum(expo, axis=-1, keepdims=True)
        probs_low = (expo / totals).astype(jnp.bfloat16)
        attended = jnp.einsum(
            "hqk,khd->qhd", probs_low, values_all, preferred_element_type=jnp.float32
        )
        attended = attended.reshape(tok_rows, model_width).astype(jnp.bfloat16)
        x_mid = inputs + jnp.dot(attended, out_w, preferred_element_type=jnp.float32)
        mixed_f, mlp_root = norm_rows(x_mid, gain_mlp)
        mixed_in = mixed_f.astype(jnp.bfloat16)
        logits = jnp.dot(mixed_in, router_w, preferred_element_type=jnp.float32)
        router = jax.nn.softmax(logits, axis=-1)
        route_ids = routes[batch_index, 0]
        chosen = (route_ids[:, :, None] == expert_range[None, None, :]).astype(jnp.float32)
        gates = jnp.sum(chosen * router[:, None, :], axis=-1)
        flat_ids = route_ids.reshape(assigned)
        match_marks = (flat_ids[:, None] == expert_range[None, :]).astype(jnp.int32)
        slot_rank = jnp.sum((jnp.cumsum(match_marks, axis=0) - 1) * match_marks, axis=1)
        slot_index = flat_ids * capacity + slot_rank
        slot_table = (
            jnp.zeros((expert_count * capacity,), jnp.int32)
            .at[slot_index]
            .set(jnp.arange(1, assigned + 1, dtype=jnp.int32))
        )
        filled = (slot_table > 0)[:, None]
        source = jnp.maximum(slot_table - 1, 0)
        send_rows = jnp.where(filled, mixed_in[source // top_count], bf_zero)
        received = lax.all_to_all(
            send_rows.reshape(ctx_size, local_experts * capacity, model_width),
            "ctx",
            split_axis=0,
            concat_axis=0,
            tiled=True,
        )
        received = received.reshape(ctx_size, local_experts, capacity, model_width)
        gate_pre = jnp.einsum(
            "secd,edf->secf", received, gate_full, preferred_element_type=jnp.float32
        )
        up_pre = jnp.einsum("secd,edf->secf", received, up_full, preferred_element_type=jnp.float32)
        hidden = (jax.nn.silu(gate_pre) * up_pre).astype(jnp.bfloat16)
        expert_rows = jnp.einsum(
            "secf,efd->secd", hidden, down_full, preferred_element_type=jnp.float32
        ).astype(jnp.bfloat16)
        returned_all = lax.all_to_all(
            expert_rows.reshape(ctx_size, local_experts * capacity, model_width),
            "ctx",
            split_axis=0,
            concat_axis=0,
            tiled=True,
        )
        returned = returned_all.reshape(expert_count * capacity, model_width)[slot_index].reshape(
            tok_rows, top_count, model_width
        )
        moe_sum = jnp.sum(gates[:, :, None] * returned.astype(jnp.float32), axis=1)
        outputs.append((x_mid + moe_sum).astype(jnp.bfloat16))
        grad_out = cotangent[batch_index, 0].astype(jnp.float32)
        d_gates = jnp.sum(returned.astype(jnp.float32) * grad_out[:, None, :], axis=-1)
        d_returned = (
            (gates[:, :, None] * grad_out[:, None, :])
            .astype(jnp.bfloat16)
            .reshape(assigned, model_width)
        )
        d_send = jnp.where(filled, d_returned[source], bf_zero)
        d_expert = lax.all_to_all(
            d_send.reshape(ctx_size, local_experts * capacity, model_width),
            "ctx",
            split_axis=0,
            concat_axis=0,
            tiled=True,
        )
        d_expert = d_expert.reshape(ctx_size, local_experts, capacity, model_width)
        d_hidden = jnp.einsum(
            "secd,efd->secf", d_expert, down_full, preferred_element_type=jnp.float32
        )
        sigma = jax.nn.sigmoid(gate_pre)
        d_gate_pre = (d_hidden * up_pre * sigma * (1.0 + gate_pre * (1.0 - sigma))).astype(
            jnp.bfloat16
        )
        d_up_pre = (d_hidden * gate_pre * sigma).astype(jnp.bfloat16)
        recv_list.append(received)
        hidden_list.append(hidden)
        dexp_list.append(d_expert)
        dgate_list.append(d_gate_pre)
        dup_list.append(d_up_pre)
        d_received = jnp.einsum(
            "secf,edf->secd", d_gate_pre, gate_full, preferred_element_type=jnp.float32
        )
        d_received = d_received + jnp.einsum(
            "secf,edf->secd", d_up_pre, up_full, preferred_element_type=jnp.float32
        )
        d_back = lax.all_to_all(
            d_received.astype(jnp.bfloat16).reshape(
                ctx_size, local_experts * capacity, model_width
            ),
            "ctx",
            split_axis=0,
            concat_axis=0,
            tiled=True,
        )
        d_routed = d_back.reshape(expert_count * capacity, model_width)[slot_index].reshape(
            tok_rows, top_count, model_width
        )
        d_mixed = jnp.sum(d_routed.astype(jnp.float32), axis=1)
        d_router = jnp.sum(chosen * d_gates[:, :, None], axis=1)
        d_logits = (
            router * (d_router - jnp.sum(router * d_router, axis=-1, keepdims=True))
        ).astype(jnp.bfloat16)
        mixed_list.append(mixed_in)
        dlogit_list.append(d_logits)
        d_mixed = d_mixed + jnp.einsum(
            "te,de->td", d_logits, router_w, preferred_element_type=jnp.float32
        )
        d_mid, gain_part = norm_back(x_mid, mlp_root, gain_mlp, d_mixed)
        acc_mlp_gain = acc_mlp_gain + gain_part
        d_mid = d_mid + grad_out
        d_att_out = d_mid.astype(jnp.bfloat16)
        attended_list.append(attended)
        datt_list.append(d_att_out)
        d_attended = jnp.einsum("te,de->td", d_att_out, out_w, preferred_element_type=jnp.float32)
        d_attended = d_attended.astype(jnp.bfloat16).reshape(tok_rows, head_count, head_dim)
        keys_again, values_again = (
            lax.all_gather(key_rot, "ctx", axis=0, tiled=True),
            lax.all_gather(values, "ctx", axis=0, tiled=True),
        )
        keys_again = keys_again.reshape(slot_len, head_count, head_dim)
        values_again = values_again.reshape(slot_len, head_count, head_dim)
        scores = (
            jnp.einsum("qhd,khd->hqk", query, keys_again, preferred_element_type=jnp.float32)
            * factor
        )
        scores = jnp.where(allowed[None], scores, MASKED)
        probs = jnp.exp(scores - peak) / totals
        d_probs = jnp.einsum(
            "qhd,khd->hqk", d_attended, values_again, preferred_element_type=jnp.float32
        )
        inner = jnp.sum(probs * d_probs, axis=-1, keepdims=True)
        d_scores = (probs * (d_probs - inner)).astype(jnp.bfloat16)
        d_query = (
            jnp.einsum("hqk,khd->qhd", d_scores, keys_again, preferred_element_type=jnp.float32)
            * factor
        )
        d_keys = (
            jnp.einsum("hqk,qhd->khd", d_scores, query, preferred_element_type=jnp.float32) * factor
        )
        d_values = jnp.einsum(
            "hqk,qhd->khd", probs_low, d_attended, preferred_element_type=jnp.float32
        )
        d_key_own, d_value_own = (
            lax.psum_scatter(
                d_keys.reshape(slot_len, model_width).astype(jnp.bfloat16),
                "ctx",
                scatter_dimension=0,
                tiled=True,
            ).astype(jnp.float32),
            lax.psum_scatter(
                d_values.reshape(slot_len, model_width).astype(jnp.bfloat16),
                "ctx",
                scatter_dimension=0,
                tiled=True,
            ).astype(jnp.float32),
        )
        d_query_n = rotate_back(d_query, cosine, sine).reshape(tok_rows, model_width)
        d_key_n = rotate_back(
            d_key_own.reshape(tok_rows, head_count, head_dim), cosine, sine
        ).reshape(tok_rows, model_width)
        d_query_pre, query_gain_part = norm_back(query_pre, query_root, gain_query, d_query_n)
        d_key_pre, key_gain_part = norm_back(key_pre, key_root, gain_key, d_key_n)
        acc_query_gain = acc_query_gain + query_gain_part
        acc_key_gain = acc_key_gain + key_gain_part
        d_query_low = d_query_pre.astype(jnp.bfloat16)
        d_key_low = d_key_pre.astype(jnp.bfloat16)
        d_value_low = d_value_own.astype(jnp.bfloat16)
        act_list.append(act)
        dq_list.append(d_query_low)
        dk_list.append(d_key_low)
        dv_list.append(d_value_low)
        d_act = jnp.einsum("te,de->td", d_query_low, query_w, preferred_element_type=jnp.float32)
        d_act = d_act + jnp.einsum(
            "te,de->td", d_key_low, key_w, preferred_element_type=jnp.float32
        )
        d_act = d_act + jnp.einsum(
            "te,de->td", d_value_low, value_w, preferred_element_type=jnp.float32
        )
        d_inputs, attn_gain_part = norm_back(inputs, attn_root, gain_attn, d_act)
        acc_attn_gain = acc_attn_gain + attn_gain_part
        input_grads.append(d_inputs + d_mid)
    acts_both = jnp.concatenate(act_list, axis=0)
    acc_query = jnp.einsum(
        "td,te->de", acts_both, jnp.concatenate(dq_list, axis=0), preferred_element_type=jnp.float32
    )
    acc_key = jnp.einsum(
        "td,te->de", acts_both, jnp.concatenate(dk_list, axis=0), preferred_element_type=jnp.float32
    )
    acc_value = jnp.einsum(
        "td,te->de", acts_both, jnp.concatenate(dv_list, axis=0), preferred_element_type=jnp.float32
    )
    acc_out = jnp.einsum(
        "td,te->de",
        jnp.concatenate(attended_list, axis=0),
        jnp.concatenate(datt_list, axis=0),
        preferred_element_type=jnp.float32,
    )
    acc_router = jnp.einsum(
        "td,te->de",
        jnp.concatenate(mixed_list, axis=0),
        jnp.concatenate(dlogit_list, axis=0),
        preferred_element_type=jnp.float32,
    )
    recv_both = jnp.concatenate(recv_list, axis=2)
    acc_down = jnp.einsum(
        "secf,secd->efd",
        jnp.concatenate(hidden_list, axis=2),
        jnp.concatenate(dexp_list, axis=2),
        preferred_element_type=jnp.float32,
    )
    acc_gate = jnp.einsum(
        "secd,secf->edf",
        recv_both,
        jnp.concatenate(dgate_list, axis=2),
        preferred_element_type=jnp.float32,
    )
    acc_up = jnp.einsum(
        "secd,secf->edf",
        recv_both,
        jnp.concatenate(dup_list, axis=2),
        preferred_element_type=jnp.float32,
    )
    dense_grads = (
        lax.psum_scatter(acc_query, ("dp", "ctx"), scatter_dimension=0, tiled=True),
        lax.psum_scatter(acc_key, ("dp", "ctx"), scatter_dimension=0, tiled=True),
        lax.psum_scatter(acc_value, ("dp", "ctx"), scatter_dimension=0, tiled=True),
        lax.psum_scatter(acc_out, ("dp", "ctx"), scatter_dimension=0, tiled=True),
        lax.psum_scatter(acc_router, ("dp", "ctx"), scatter_dimension=0, tiled=True),
        lax.psum_scatter(acc_attn_gain, ("dp", "ctx"), scatter_dimension=0, tiled=True),
        lax.psum_scatter(acc_mlp_gain, ("dp", "ctx"), scatter_dimension=0, tiled=True),
        lax.psum_scatter(acc_query_gain, ("dp", "ctx"), scatter_dimension=0, tiled=True),
        lax.psum_scatter(acc_key_gain, ("dp", "ctx"), scatter_dimension=0, tiled=True),
    )
    expert_grads = (
        lax.psum_scatter(
            acc_gate.astype(jnp.bfloat16), "dp", scatter_dimension=1, tiled=True
        ).astype(jnp.float32),
        lax.psum_scatter(acc_up.astype(jnp.bfloat16), "dp", scatter_dimension=1, tiled=True).astype(
            jnp.float32
        ),
        lax.psum_scatter(
            acc_down.astype(jnp.bfloat16), "dp", scatter_dimension=1, tiled=True
        ).astype(jnp.float32),
    )
    mixed = jnp.stack(outputs).reshape(batches, 1, tok_rows, model_width)
    d_tokens = jnp.stack(input_grads).reshape(batches, 1, tok_rows, model_width)
    return (
        mixed,
        d_tokens,
        dense_grads[0],
        dense_grads[1],
        dense_grads[2],
        dense_grads[3],
        dense_grads[4],
        expert_grads[0],
        expert_grads[1],
        expert_grads[2],
        dense_grads[5],
        dense_grads[6],
        dense_grads[7],
        dense_grads[8],
    )


def solution(mesh):
    placed = (
        P(None, "dp", "ctx", None),
        P(None, "dp", "ctx", None),
        P(None, "dp", "ctx", None),
        P(None, "dp"),
        P(),
        P(("dp", "ctx"), None),
        P(("dp", "ctx"), None),
        P(("dp", "ctx"), None),
        P(("dp", "ctx"), None),
        P(("dp", "ctx"), None),
        P("ctx", "dp", None),
        P("ctx", "dp", None),
        P("ctx", "dp", None),
        P(("dp", "ctx")),
        P(("dp", "ctx")),
        P(("dp", "ctx")),
        P(("dp", "ctx")),
    )
    return jax.shard_map(
        on_device,
        mesh=mesh,
        in_specs=placed,
        out_specs=(
            P(None, "dp", "ctx", None),
            P(None, "dp", "ctx", None),
            P(("dp", "ctx"), None),
            P(("dp", "ctx"), None),
            P(("dp", "ctx"), None),
            P(("dp", "ctx"), None),
            P(("dp", "ctx"), None),
            P("ctx", "dp", None),
            P("ctx", "dp", None),
            P("ctx", "dp", None),
            P(("dp", "ctx")),
            P(("dp", "ctx")),
            P(("dp", "ctx")),
            P(("dp", "ctx")),
        ),
        check_vma=False,
    )
```

profile of v0, /device:TPU:0, one launch (start us, length us, event | category | flops | bytes accessed | tf_op | source)
XLA Modules:
  0.0 2968.4 jit_solution(3004354757128956071)
XLA Ops:
  12.9 42.6 %all-reduce.9 = (bf16[2048]{0:T(1024)(128)(2,1)S(1)}, bf16[2048]{0:T(1024)(128)(2,1)S(1)}, bf16[2048]{0:T(1024)(128)(2,1)S(1)}, bf16[2048]{0:T(1024)(128)(2,1)S(1)}) all-reduce(bf16[2048]{0:T(1024)(128)(2,1)S(1)} %dynamic-update-slice, bf16[2048]{0:T(1024)(128)(2,1)S(1)} %dynamic-update-slice.1, ...), channel_id=1, replica_groups=mesh['dp'=4,'ctx'=8] {'dp','ctx'}, use_global_device_ids=true, to_apply=%add | all-reduce | flops 8192 | bytes 32768
  59.9 31.5 %all-gather.19.cloned.1.call-done = bf16[2048,2048]{1,0:T(8,128)(2,1)} async-done(((bf16[64,2048]{1,0:T(8,128)(2,1)}), bf16[2048,2048]{1,0:T(8,128)(2,1)}) %all-gather.19.cloned.1.call-update) | async-done | bytes 8388624 | tf_op jit(solution)/shard_map/all_gather | solution.py:121
  104.2 66.2 %all-gather.17.cloned.1.call-done = bf16[2048,2048]{1,0:T(8,128)(2,1)} async-done(((bf16[64,2048]{1,0:T(8,128)(2,1)}), bf16[2048,2048]{1,0:T(8,128)(2,1)}) %all-gather.17.cloned.1.call-update) | async-done | bytes 8388624 | tf_op jit(solution)/shard_map/all_gather | solution.py:120
  197.6 51.6 %all-gather.13.cloned.1.call-done = bf16[2048,2048]{1,0:T(8,128)(2,1)} async-done(((bf16[64,2048]{1,0:T(8,128)(2,1)}), bf16[2048,2048]{1,0:T(8,128)(2,1)}) %all-gather.13.cloned.1.call-update) | async-done | bytes 8388624 | tf_op jit(solution)/shard_map/all_gather | solution.py:122
  258.5 39.8 %all-gather = bf16[32,64,16]{1,2,0:T(8,128)(2,1)S(1)} all-gather(bf16[1,64,16]{1,2,0:T(8,128)(2,1)S(1)} %bitcast.472), channel_id=1, replica_groups=mesh['dp'=4,'ctx'=8] {'dp','ctx'}, dimensions={0}, use_global_device_ids=true | all-gather | bytes 67584 | tf_op jit(solution)/shard_map/all_gather | solution.py:124
  336.2 70.6 %all-gather.23.cloned.1.call-done = bf16[2048,2048]{1,0:T(8,128)(2,1)} async-done(((bf16[64,2048]{1,0:T(8,128)(2,1)}), bf16[2048,2048]{1,0:T(8,128)(2,1)}) %all-gather.23.cloned.1.call-update) | async-done | bytes 8388624 | tf_op jit(solution)/shard_map/all_gather | solution.py:123
  460.6 55.1 %all_to_all.40 = bf16[8,134,2048]{2,1,0:T(8,128)(2,1)} all-to-all(bf16[8,134,2048]{2,1,0:T(8,128)(2,1)S(1)} %get-tuple-element.203), channel_id=1, replica_groups=mesh['dp'=4,'ctx'=8] {'ctx'}, dimensions={0} | all-to-all | bytes 8781824 | tf_op jit(solution)/shard_map/all_to_all | solution.py:200
  532.5 24.1 all-gather.27.cloned.1.call-done
  570.3 135.7 %all-gather.25.cloned.1.call-done = bf16[2,2048,1024]{2,1,0:T(8,128)(2,1)} async-done(((bf16[2,512,1024]{2,1,0:T(8,128)(2,1)}), bf16[2,2048,1024]{2,1,0:T(8,128)(2,1)}) %all-gather.25.cloned.1.call-update) | async-done | bytes 8388624 | tf_op jit(solution)/shard_map/all_gather | solution.py:131
  726.5 128.9 %all-gather.29.cloned.1.call-done = bf16[2,1024,2048]{2,1,0:T(8,128)(2,1)} async-done(((bf16[2,256,2048]{2,1,0:T(8,128)(2,1)}), bf16[2,1024,2048]{2,1,0:T(8,128)(2,1)}) %all-gather.29.cloned.1.call-update) | async-done | bytes 8388624 | tf_op jit(solution)/shard_map/all_gather | solution.py:133
  932.8 38.2 %all-to-all-done.5 = bf16[8,134,2048]{2,1,0:T(8,128)(2,1)} async-done(((bf16[8,134,2048]{2,1,0:T(8,128)(2,1)}), bf16[8,134,2048]{2,1,0:T(8,128)(2,1)}, u32[]{:S(2)}, u32[]{:S(2)}) %all-to-all-start.5) | async-done | bytes 4390944 | tf_op jit(solution)/shard_map/all_to_all | solution.py:263
  1091.4 55.1 %all_to_all.41 = bf16[8,134,2048]{2,1,0:T(8,128)(2,1)} all-to-all(bf16[8,134,2048]{2,1,0:T(8,128)(2,1)S(1)} %get-tuple-element.205), channel_id=1, replica_groups=mesh['dp'=4,'ctx'=8] {'ctx'}, dimensions={0} | all-to-all | bytes 8781824 | tf_op jit(solution)/shard_map/all_to_all | solution.py:200
  1178.8 24.2 all-to-all-done.6
  1270.9 36.4 %all-to-all-done.7 = bf16[8,134,2048]{2,1,0:T(8,128)(2,1)} async-done(((bf16[8,134,2048]{2,1,0:T(8,128)(2,1)}), bf16[8,134,2048]{2,1,0:T(8,128)(2,1)}, u32[]{:S(2)}, u32[]{:S(2)}) %all-to-all-start.7) | async-done | bytes 4390944 | tf_op jit(solution)/shard_map/all_to_all | solution.py:263
  1334.1 29.6 all-to-all-done.3
  1660.8 112.8 %reduce-scatter.41.cloned.1.call-done = f32[64,16]{1,0:T(8,128)} async-done(((f32[2048,16]{1,0:T(8,128)}), f32[64,16]{1,0:T(8,128)}) %reduce-scatter.41.cloned.1.call-update) | async-done | bytes 4112
  1799.5 42.3 %all-reduce.8 = (f32[2048]{0:T(1024)S(1)}, f32[2048]{0:T(1024)S(1)}, f32[2048]{0:T(1024)S(1)}, f32[2048]{0:T(1024)S(1)}) all-reduce(f32[2048]{0:T(1024)S(1)} %add.420, f32[2048]{0:T(1024)S(1)} %add.421, f32[2048]{0:T(1024)S(1)} %add.422, f32[2048]{0:T(1024)S(1)} %add.423), channel_id=14, replica_groups=mesh['dp'=4,'ctx'=8] {'dp','ctx'}, use_global_device_ids=true, to_apply=%region_62.63.clone | all-reduce | flops 8192 | bytes 65536
  1847.8 69.5 %reduce-scatter.31.cloned.1.call-done = bf16[2,512,1024]{2,1,0:T(8,128)(2,1)} async-done(((bf16[2,2048,1024]{2,1,0:T(8,128)(2,1)}), bf16[2,512,1024]{2,1,0:T(8,128)(2,1)}) %reduce-scatter.31.cloned.1.call-update) | async-done | bytes 2097168 | tf_op jit(solution)/shard_map/reduce_scatter | solution.py:412
  1921.4 143.4 %reduce-scatter.33.cloned.1.call-done = bf16[2,512,1024]{2,1,0:T(8,128)(2,1)} async-done(((bf16[2,2048,1024]{2,1,0:T(8,128)(2,1)}), bf16[2,512,1024]{2,1,0:T(8,128)(2,1)}) %reduce-scatter.33.cloned.1.call-update) | async-done | bytes 2097168 | tf_op jit(solution)/shard_map/reduce_scatter | solution.py:415
  2069.0 143.6 %reduce-scatter.35.cloned.1.call-done = bf16[2,256,2048]{2,1,0:T(8,128)(2,1)} async-done(((bf16[2,1024,2048]{2,1,0:T(8,128)(2,1)}), bf16[2,256,2048]{2,1,0:T(8,128)(2,1)}) %reduce-scatter.35.cloned.1.call-update) | async-done | bytes 2097168 | tf_op jit(solution)/shard_map/reduce_scatter | solution.py:418
  2216.7 182.1 %reduce-scatter.23.cloned.1.call-done = f32[64,2048]{1,0:T(8,128)} async-done(((f32[2048,2048]{1,0:T(8,128)}), f32[64,2048]{1,0:T(8,128)}) %reduce-scatter.23.cloned.1.call-update) | async-done | bytes 524304 | tf_op jit(solution)/shard_map/reduce_scatter | solution.py:401
  2398.9 187.6 %reduce-scatter.29.cloned.1.call-done = f32[64,2048]{1,0:T(8,128)} async-done(((f32[2048,2048]{1,0:T(8,128)}), f32[64,2048]{1,0:T(8,128)}) %reduce-scatter.29.cloned.1.call-update) | async-done | bytes 524304 | tf_op jit(solution)/shard_map/reduce_scatter | solution.py:404
  2586.5 187.5 %reduce-scatter.25.cloned.1.call-done = f32[64,2048]{1,0:T(8,128)} async-done(((f32[2048,2048]{1,0:T(8,128)}), f32[64,2048]{1,0:T(8,128)}) %reduce-scatter.25.cloned.1.call-update) | async-done | bytes 524304 | tf_op jit(solution)/shard_map/reduce_scatter | solution.py:402
  2773.9 187.5 %reduce-scatter.27.cloned.1.call-done = f32[64,2048]{1,0:T(8,128)} async-done(((f32[2048,2048]{1,0:T(8,128)}), f32[64,2048]{1,0:T(8,128)}) %reduce-scatter.27.cloned.1.call-update) | async-done | bytes 524304 | tf_op jit(solution)/shard_map/reduce_scatter | solution.py:403
  (639 shorter events, 865.8 us)
Async XLA Ops:
  7.2 84.2 %all-gather.19.cloned.1.call-start = ((), (), s32[]{:S(2)}) async-start(), calls=%async_computation.23 | async-start | bytes 8650752 | tf_op jit(solution)/shard_map/all_gather | solution.py:121
  7.9 162.4 %all-gather.17.cloned.1.call-start = ((), (), s32[]{:S(2)}) async-start(), calls=%async_computation.22 | async-start | bytes 8650752 | tf_op jit(solution)/shard_map/all_gather | solution.py:120
  8.7 240.6 %all-gather.13.cloned.1.call-start = ((), (), s32[]{:S(2)}) async-start(), calls=%async_computation.20 | async-start | bytes 8650752 | tf_op jit(solution)/shard_map/all_gather | solution.py:122
  9.4 304.4 %all-gather.21.cloned.1.call-start = ((), (), s32[]{:S(2)}) async-start(), calls=%async_computation.24 | async-start | bytes 4718592 | tf_op jit(solution)/shard_map/all_gather | solution.py:161
  197.3 132.3 %all-gather.15.cloned.1.call-start = ((), (), s32[]{:S(2)}) async-start(), calls=%async_computation.21 | async-start | bytes 4718592 | tf_op jit(solution)/shard_map/all_gather | solution.py:162
  254.7 152.0 %all-gather.23.cloned.1.call-start = ((), (), s32[]{:S(2)}) async-start(), calls=%async_computation.25 | async-start | bytes 8650752 | tf_op jit(solution)/shard_map/all_gather | solution.py:123
  255.3 301.3 %all-gather.27.cloned.1.call-start = ((), (), s32[]{:S(2)}) async-start(), calls=%async_computation.27 | async-start | bytes 10485760 | tf_op jit(solution)/shard_map/all_gather | solution.py:132
  256.1 449.9 %all-gather.25.cloned.1.call-start = ((), (), s32[]{:S(2)}) async-start(), calls=%async_computation.26 | async-start | bytes 10485760 | tf_op jit(solution)/shard_map/all_gather | solution.py:131
  256.8 598.6 %all-gather.29.cloned.1.call-start = ((), (), s32[]{:S(2)}) async-start(), calls=%async_computation.28 | async-start | bytes 10485760 | tf_op jit(solution)/shard_map/all_gather | solution.py:133
  257.5 718.5 %all-gather.33.cloned.1.call-start = ((), (), s32[]{:S(2)}) async-start(), calls=%async_computation.30 | async-start | bytes 4718592 | tf_op jit(solution)/shard_map/all_gather | solution.py:161
  515.7 204.1 %all-to-all-start.4 = ((bf16[8,134,2048]{2,1,0:T(8,128)(2,1)}), bf16[8,134,2048]{2,1,0:T(8,128)(2,1)}, u32[]{:S(2)}, u32[]{:S(2)}) async-start(bf16[8,134,2048]{2,1,0:T(8,128)(2,1)} %get-tuple-element.202), calls=%async_computation.4 | async-start | bytes 8912896 | tf_op jit(solution)/shard_map/all_to_all | solution.py:236
  520.3 471.2 %all-gather.31.cloned.1.call-start = ((), (), s32[]{:S(2)}) async-start(), calls=%async_computation.29 | async-start | bytes 4718592 | tf_op jit(solution)/shard_map/all_gather | solution.py:162
  1311.8 284.4 %reduce-scatter.19.cloned.1.call-start = ((), (), s32[]{:S(2)}) async-start(), calls=%async_computation.31 | async-start | bytes 4718592 | tf_op jit(solution)/shard_map/reduce_scatter | solution.py:321
  1421.1 176.4 %reduce-scatter.21.cloned.1.call-start = ((), (), s32[]{:S(2)}) async-start(), calls=%async_computation.32 | async-start | bytes 4718592 | tf_op jit(solution)/shard_map/reduce_scatter | solution.py:321
  1450.1 171.7 %reduce-scatter.39.cloned.1.call-start = ((), (), s32[]{:S(2)}) async-start(), calls=%async_computation.41 | async-start | bytes 4718592
  1463.7 172.7 %reduce-scatter.37.cloned.1.call-start = ((), (), s32[]{:S(2)}) async-start(), calls=%async_computation.40 | async-start | bytes 4718592
  1477.1 296.5 %reduce-scatter.41.cloned.1.call-start = ((), (), s32[]{:S(2)}) async-start(), calls=%async_computation.42 | async-start | bytes 1081344
  1493.1 424.2 %reduce-scatter.31.cloned.1.call-start = ((), (), s32[]{:S(2)}) async-start(), calls=%async_computation.37 | async-start | bytes 10485760 | tf_op jit(solution)/shard_map/reduce_scatter | solution.py:412
  1510.3 554.6 %reduce-scatter.33.cloned.1.call-start = ((), (), s32[]{:S(2)}) async-start(), calls=%async_computation.38 | async-start | bytes 10485760 | tf_op jit(solution)/shard_map/reduce_scatter | solution.py:415
  1528.9 683.7 %reduce-scatter.35.cloned.1.call-start = ((), (), s32[]{:S(2)}) async-start(), calls=%async_computation.39 | async-start | bytes 10485760 | tf_op jit(solution)/shard_map/reduce_scatter | solution.py:418
  1559.9 838.9 %reduce-scatter.23.cloned.1.call-start = ((), (), s32[]{:S(2)}) async-start(), calls=%async_computation.33 | async-start | bytes 17301504 | tf_op jit(solution)/shard_map/reduce_scatter | solution.py:401
  1585.1 1001.3 %reduce-scatter.29.cloned.1.call-start = ((), (), s32[]{:S(2)}) async-start(), calls=%async_computation.36 | async-start | bytes 17301504 | tf_op jit(solution)/shard_map/reduce_scatter | solution.py:404
  1596.1 1177.8 %reduce-scatter.25.cloned.1.call-start = ((), (), s32[]{:S(2)}) async-start(), calls=%async_computation.34 | async-start | bytes 17301504 | tf_op jit(solution)/shard_map/reduce_scatter | solution.py:402
  1621.5 1339.9 %reduce-scatter.27.cloned.1.call-start = ((), (), s32[]{:S(2)}) async-start(), calls=%async_computation.35 | async-start | bytes 17301504 | tf_op jit(solution)/shard_map/reduce_scatter | solution.py:403
  (161 other events, 3488.9 us)
Sparse Core Ops, SparseCore 0:
  10.9 80.4 all-gather.18
  94.2 76.0 all-gather.16
  173.2 76.0 all-gather.12
  251.6 35.8 all-gather.20
  289.8 36.7 all-gather.14
  329.3 77.4 all-gather.22
  408.3 148.2 all-gather.26
  558.1 147.8 all-gather.24
  707.6 147.8 all-gather.28
  857.7 34.8 all-gather.32
  895.2 64.8 all-gather.30
  1421.3 50.4 reduce-scatter.18
  1475.4 51.3 reduce-scatter.20
  1530.0 51.2 reduce-scatter.38
  1584.9 51.3 reduce-scatter.36
  1638.4 135.1 reduce-scatter.40
  1775.9 141.4 reduce-scatter.30
  1919.7 145.1 reduce-scatter.32
  2067.4 145.1 reduce-scatter.34
  2215.4 183.4 reduce-scatter.22
  2401.8 184.5 reduce-scatter.28
  2589.4 184.4 reduce-scatter.24
  2776.9 184.4 reduce-scatter.26
where the time goes:
time: 2980 us; the launch traced here: 2970 us
  waiting for transfers between devices  1870 us (63%)
  matrix products  391 us (13%)
  local copies, waits for them, and re-layouts  313 us (11%)
  blocking collectives  235 us (8%)
  other arithmetic  111 us (4%)
  starting transfers between devices  30.2 us (1%)
    reduce_scatter x1, waiting for transfers between devices, on_device(): lax.psum_scatter(acc_out, ('dp', 'ctx'), scatter_dimension=0, tiled=True)  188 us
    reduce_scatter x1, waiting for transfers between devices, on_device(): lax.psum_scatter(acc_key, ('dp', 'ctx'), scatter_dimension=0, tiled=True)  187 us
    reduce_scatter x1, waiting for transfers between devices, on_device(): lax.psum_scatter(acc_value, ('dp', 'ctx'), scatter_dimension=0, tiled=True)  187 us
    reduce_scatter x1, waiting for transfers between devices, on_device(): lax.psum_scatter(acc_query, ('dp', 'ctx'), scatter_dimension=0, tiled=True)  182 us
    reduce_scatter x1, waiting for transfers between devices, on_device(): lax.psum_scatter(acc_down.astype(jnp.bfloat16), 'dp', scatter_dimension=1...  144 us
    reduce_scatter x1, waiting for transfers between devices, on_device(): lax.psum_scatter(acc_up.astype(jnp.bfloat16), 'dp', scatter_dimension=1,...  143 us
    all_gather x1, waiting for transfers between devices, on_device(): lax.all_gather(w_gate, 'dp', axis=1, tiled=True)  136 us
    unnamed x26, waiting for transfers between devices  131 us
  transfers between devices with their start and end apart: 29, of which 21 were waited for; matrix products, arithmetic and copies ran while one was open for 21% of the time, Pallas kernels for 0%

commit v1 on v0

v1 whole, which is shorter than its diff:
```python
import math

import jax
import jax.numpy as jnp
from jax import lax
from jax.sharding import Mesh
from jax.sharding import PartitionSpec as P

HEAD = 128
EPSILON = 1e-05
ROPE_BASE = 10000.0
MASKED = -1e30
BF = jnp.bfloat16
F32 = jnp.float32
DP = ("half", "lane")
CTX = ("quad", "pair")
ALL = DP + CTX


def dot(spec, left, right):
    return jnp.einsum(spec, left, right, preferred_element_type=F32)


def inv_rms(values):
    return lax.rsqrt(jnp.mean(values * values, axis=-1, keepdims=True) + EPSILON)


def norm_back(values, inv_root, gain_vec, grad_in):
    weighted = grad_in * gain_vec
    inner = jnp.mean(weighted * values, axis=-1, keepdims=True)
    grad_values = inv_root * weighted - values * (inv_root * inv_root * inv_root) * inner
    return (grad_values, jnp.sum(grad_in * values * inv_root, axis=0))


def angles(places, head_width):
    index = jnp.arange(head_width // 2, dtype=F32)
    freqs = jnp.power(ROPE_BASE, -2.0 * index / head_width)
    turning = places.astype(F32)[:, None] * freqs[None, :]
    turning = jnp.concatenate([turning, turning], axis=1)
    return (jnp.cos(turning)[:, None, :], jnp.sin(turning)[:, None, :])


def rotate(values, cosine, sine):
    half_size = values.shape[-1] // 2
    turned = jnp.concatenate([-values[..., half_size:], values[..., :half_size]], axis=-1)
    return values * cosine + turned * sine


def rotate_back(grad_in, cosine, sine):
    half_size = grad_in.shape[-1] // 2
    moved = grad_in * sine
    return grad_in * cosine + jnp.concatenate(
        [moved[..., half_size:], -moved[..., :half_size]], axis=-1
    )


def swap(values, axis):
    return lax.ppermute(values, axis, [(0, 1), (1, 0)])


def exchange(blocks, axes):
    return lax.all_to_all(blocks, axes, split_axis=0, concat_axis=0, tiled=True)


def spread(values, axes):
    count = lax.axis_size(axes)
    return exchange(jnp.broadcast_to(values[None], (count,) + values.shape), axes)


def gather_ctx(rows):
    own = spread(rows, "quad")
    return jnp.stack([own, swap(own, "pair")])


def scatter_ctx(own_part, other_part):
    merged = own_part.astype(F32) + swap(other_part.astype(BF), "pair").astype(F32)
    received = exchange(merged.astype(BF), "quad")
    return jnp.sum(received.astype(F32), axis=0)


def relative(blocks):
    split = blocks.reshape((-1, 2) + blocks.shape[1:]).swapaxes(0, 1)
    return jnp.where(lax.axis_index("pair") == 0, split, split[::-1])


def absolute(blocks):
    split = jnp.where(lax.axis_index("pair") == 0, blocks, blocks[::-1])
    return split.swapaxes(0, 1).reshape((-1,) + blocks.shape[2:])


def sum_ctx(values):
    values = values + swap(values, "pair")[:, ::-1]
    count = lax.axis_size("quad")
    step = 1
    while step < count:
        values = values + lax.ppermute(values, "quad", [(i, i ^ step) for i in range(count)])
        step *= 2
    return values


def gather_lane(values):
    if lax.axis_size("lane") == 2:
        other = swap(values, "lane")
        first = lax.axis_index("lane") == 0
        return jnp.stack([jnp.where(first, values, other), jnp.where(first, other, values)])
    return lax.all_gather(values, "lane", axis=0, tiled=False)


def scatter_lane(values):
    count = lax.axis_size("lane")
    here = lax.axis_index("lane")
    own = lax.dynamic_index_in_dim(values, here, 0, keepdims=False)
    if count == 2:
        other = lax.dynamic_index_in_dim(values, 1 - here, 0, keepdims=False)
        return own + swap(other.astype(BF), "lane").astype(F32)
    return lax.psum_scatter(values.astype(BF), "lane", scatter_dimension=0, tiled=False).astype(F32)


def reduce_small(values):
    over_ctx = jnp.sum(exchange(values.swapaxes(0, 1), CTX), axis=0)
    return jnp.sum(exchange(over_ctx, DP), axis=0)


def on_device(
    tokens,
    cotangent,
    routes,
    lengths,
    block_order,
    w_query,
    w_key,
    w_value,
    w_out,
    w_router,
    w_gate,
    w_up,
    w_down,
    attn_gain,
    mlp_gain,
    query_gain,
    key_gain,
):
    batches, _, rows, width = tokens.shape
    dp_size = lax.axis_size(DP)
    ctx_size = lax.axis_size(CTX)
    quads = lax.axis_size("quad")
    lanes = lax.axis_size("lane")
    slot_len = rows * ctx_size
    block_rows = rows // 2
    head_width = width // ctx_size
    heads = head_width // HEAD
    shard = w_query.shape[0]
    expert_count = w_router.shape[1]
    local_experts = w_gate.shape[0]
    hidden_units = w_gate.shape[2]
    hidden_half = hidden_units // 2
    depth_part = w_gate.shape[1]
    factor = 1.0 / math.sqrt(HEAD)
    half = lax.axis_index("half")
    pair = lax.axis_index("pair")

    small = jnp.concatenate(
        [attn_gain, mlp_gain, query_gain, key_gain, w_router.reshape(shard * expert_count)]
    )
    small = spread(spread(small, CTX), DP).reshape(dp_size * ctx_size, -1)
    gain_attn = small[:, :shard].reshape(width).astype(F32)
    gain_mlp = small[:, shard : 2 * shard].reshape(width).astype(F32)
    gain_query = small[:, 2 * shard : 3 * shard].reshape(ctx_size, head_width)
    gain_key = small[:, 3 * shard : 4 * shard].reshape(ctx_size, head_width)
    router_w = small[:, 4 * shard :].reshape(width, expert_count)
    here = lax.axis_index(CTX)
    gain_query = lax.dynamic_index_in_dim(gain_query, here, 0, keepdims=False).astype(F32)
    gain_key = lax.dynamic_index_in_dim(gain_key, here, 0, keepdims=False).astype(F32)

    qkv = jnp.stack([w_query, w_key, w_value], axis=1).reshape(shard, 3, ctx_size, head_width)
    qkv = exchange(
        qkv.transpose(2, 0, 1, 3).reshape(ctx_size, shard, 3 * head_width), CTX
    ).reshape(ctx_size * shard, 3 * head_width)
    qkv_w = lax.all_gather(qkv, DP, axis=0, tiled=True)
    out_w = lax.all_gather(w_out, ALL, axis=0, tiled=True)

    def gather_depth(weights):
        split = weights.reshape(local_experts, depth_part, 2, hidden_half)
        own = lax.dynamic_index_in_dim(split, half, 2, keepdims=False)
        other = swap(lax.dynamic_index_in_dim(split, 1 - half, 2, keepdims=False), "half")
        first = half == 0
        both = jnp.stack([jnp.where(first, own, other), jnp.where(first, other, own)])
        gathered = gather_lane(both)
        return gathered.transpose(2, 1, 0, 3, 4).reshape(local_experts, width, hidden_half)

    down_w = gather_lane(w_down).transpose(1, 0, 2, 3).reshape(local_experts, hidden_half, width)
    gate_w = gather_depth(w_gate)
    up_w = gather_depth(w_up)

    def places_of(device):
        stored = device * rows + jnp.arange(rows, dtype=jnp.int32)
        match_marks = (stored // block_rows)[:, None] == jnp.arange(
            block_order.shape[0], dtype=jnp.int32
        )[None, :]
        first_place = jnp.sum(jnp.where(match_marks, block_order[None, :], 0), axis=1)
        return first_place * block_rows + stored % block_rows

    places = jnp.concatenate(
        [places_of(quad * 2 + (pair ^ other)) for other in range(2) for quad in range(quads)]
    )
    cosine, sine = angles(places, HEAD)
    expert_range = jnp.arange(expert_count, dtype=jnp.int32)

    saved = []
    for m in range(batches):
        inputs = tokens[m, 0].astype(F32)
        attn_root = inv_rms(inputs)
        act_own = (inputs * attn_root * gain_attn).astype(BF)
        act = gather_ctx(act_own).reshape(slot_len, width)
        pre = dot("td,de->te", act, qkv_w)
        query_pre = pre[:, :head_width]
        key_pre = pre[:, head_width : 2 * head_width]
        value = pre[:, 2 * head_width :].astype(BF).reshape(slot_len, heads, HEAD)
        squares = jnp.stack(
            [jnp.sum(query_pre * query_pre, axis=1), jnp.sum(key_pre * key_pre, axis=1)]
        ).reshape(2, 2, slot_len // 2)
        squares = sum_ctx(squares).reshape(2, slot_len, 1)
        query_root = lax.rsqrt(squares[0] / width + EPSILON)
        key_root = lax.rsqrt(squares[1] / width + EPSILON)
        query = rotate(
            (query_pre * query_root * gain_query).reshape(slot_len, heads, HEAD), cosine, sine
        ).astype(BF)
        key = rotate(
            (key_pre * key_root * gain_key).reshape(slot_len, heads, HEAD), cosine, sine
        ).astype(BF)
        allowed = (places[None, :] <= places[:, None]) & (places[None, :] < lengths[m, 0])
        scores = dot("qhd,khd->hqk", query, key) * factor
        scores = jnp.where(allowed[None], scores, MASKED)
        expo = jnp.exp(scores - jnp.max(scores, axis=-1, keepdims=True))
        probs = expo / jnp.sum(expo, axis=-1, keepdims=True)
        probs_low = probs.astype(BF)
        attended = dot("hqk,khd->qhd", probs_low, value).astype(BF)
        attended = exchange(absolute(attended.reshape(2, quads, rows, head_width)), CTX)
        attended = attended.transpose(1, 0, 2).reshape(rows, width)
        x_mid = inputs + dot("td,de->te", attended, out_w)
        mlp_root = inv_rms(x_mid)
        mixed_in = (x_mid * mlp_root * gain_mlp).astype(BF)
        router = jax.nn.softmax(dot("td,de->te", mixed_in, router_w), axis=-1)
        routed = jnp.any(routes[m, 0][:, :, None] == expert_range[None, None, :], axis=1)
        routed = routed.astype(F32)
        gates = (router * routed).T.reshape(ctx_size, local_experts, rows)
        gates = relative(exchange(gates, CTX))
        gates = gates.transpose(0, 1, 3, 2).reshape(2, slot_len // 2, local_experts)
        grad_low = cotangent[m, 0]
        chunks = []
        for rows_in, grad_in, gate_in in (
            (swap(mixed_in, "half"), swap(grad_low, "half"), swap(gates, "half")),
            (mixed_in, grad_low, gates),
        ):
            chunks.append(
                (
                    gather_ctx(rows_in).reshape(slot_len, width),
                    gather_ctx(grad_in).reshape(slot_len, width),
                    gate_in.reshape(slot_len, local_experts),
                )
            )
        saved.append(
            dict(
                inputs=inputs, attn_root=attn_root, act=act, query_pre=query_pre,
                key_pre=key_pre, query_root=query_root, key_root=key_root, query=query, key=key,
                value=value, probs=probs, probs_low=probs_low, attended=attended, x_mid=x_mid,
                mlp_root=mlp_root, mixed_in=mixed_in, router=router, routed=routed,
                grad_low=grad_low, chunks=chunks,
            )
        )

    outputs = []
    input_grads = []
    x_list, g_list, hid_list, dgate_list, dup_list = [], [], [], [], []
    part_mlp_gain = part_attn_gain = part_query_gain = part_key_gain = 0.0
    for m in range(batches):
        s = saved[m]
        sums = []
        for x_rows, g_rows, gate in s["chunks"]:
            gate = gate[:, :, None]
            gate_pre = dot("td,edf->tef", x_rows, gate_w)
            up_pre = dot("td,edf->tef", x_rows, up_w)
            d_hidden = dot("td,efd->tef", g_rows, down_w)
            sigma = jax.nn.sigmoid(gate_pre)
            hidden = gate_pre * sigma * up_pre
            d_gates = jnp.sum(hidden * d_hidden, axis=2)
            scaled = (hidden * gate).astype(BF)
            d_hidden = d_hidden * gate
            d_gate_pre = (d_hidden * up_pre * sigma * (1.0 + gate_pre * (1.0 - sigma))).astype(BF)
            d_up_pre = (d_hidden * gate_pre * sigma).astype(BF)
            moe = dot("tef,efd->td", scaled, down_w).astype(BF)
            d_rows = dot("tef,edf->td", d_gate_pre, gate_w)
            d_rows = (d_rows + dot("tef,edf->td", d_up_pre, up_w)).astype(BF)
            moe = moe.reshape(2, quads, rows, width)
            d_rows = d_rows.reshape(2, quads, rows, width)
            sums.append((scatter_ctx(moe[0], moe[1]), scatter_ctx(d_rows[0], d_rows[1]), d_gates))
            x_list.append(x_rows)
            g_list.append(g_rows)
            hid_list.append(scaled)
            dgate_list.append(d_gate_pre)
            dup_list.append(d_up_pre)
        partner, own = sums
        moe_sum = own[0] + swap(partner[0].astype(BF), "half").astype(F32)
        d_mixed = own[1] + swap(partner[1].astype(BF), "half").astype(F32)
        d_gates = own[2] + swap(partner[2], "half")
        d_gates = d_gates.reshape(2, quads, rows, local_experts).swapaxes(2, 3)
        d_router = exchange(absolute(d_gates), CTX).reshape(expert_count, rows).T * s["routed"]
        outputs.append((s["x_mid"] + moe_sum).astype(BF))
        router = s["router"]
        d_logits = (
            router * (d_router - jnp.sum(router * d_router, axis=-1, keepdims=True))
        ).astype(BF)
        s["d_logits"] = d_logits
        d_mixed = d_mixed + dot("te,de->td", d_logits, router_w)
        d_mid, gain_part = norm_back(s["x_mid"], s["mlp_root"], gain_mlp, d_mixed)
        part_mlp_gain = part_mlp_gain + gain_part
        d_mid = d_mid + s["grad_low"].astype(F32)
        d_att_out = d_mid.astype(BF)
        s["d_att_out"] = d_att_out
        d_attended = dot("te,de->td", d_att_out, out_w).astype(BF)
        d_attended = exchange(
            d_attended.reshape(rows, ctx_size, head_width).swapaxes(0, 1), CTX
        )
        d_attended = relative(d_attended).reshape(slot_len, heads, HEAD)
        probs, query, key = s["probs"], s["query"], s["key"]
        d_probs = dot("qhd,khd->hqk", d_attended, s["value"])
        inner = jnp.sum(probs * d_probs, axis=-1, keepdims=True)
        d_scores = (probs * (d_probs - inner)).astype(BF)
        d_query = dot("hqk,khd->qhd", d_scores, key) * factor
        d_key = dot("hqk,qhd->khd", d_scores, query) * factor
        d_value = dot("hqk,qhd->khd", s["probs_low"], d_attended)
        d_query = rotate_back(d_query, cosine, sine).reshape(slot_len, head_width)
        d_key = rotate_back(d_key, cosine, sine).reshape(slot_len, head_width)
        query_pre, key_pre = s["query_pre"], s["key_pre"]
        query_root, key_root = s["query_root"], s["key_root"]
        inners = jnp.stack(
            [
                jnp.sum(d_query * gain_query * query_pre, axis=1),
                jnp.sum(d_key * gain_key * key_pre, axis=1),
            ]
        ).reshape(2, 2, slot_len // 2)
        inners = sum_ctx(inners).reshape(2, slot_len, 1) / width
        d_query_pre = query_root * (d_query * gain_query) - query_pre * query_root**3 * inners[0]
        d_key_pre = key_root * (d_key * gain_key) - key_pre * key_root**3 * inners[1]
        part_query_gain = part_query_gain + jnp.sum(d_query * query_pre * query_root, axis=0)
        part_key_gain = part_key_gain + jnp.sum(d_key * key_pre * key_root, axis=0)
        d_pre = jnp.concatenate(
            [
                d_query_pre.astype(BF),
                d_key_pre.astype(BF),
                d_value.reshape(slot_len, head_width).astype(BF),
            ],
            axis=1,
        )
        s["d_pre"] = d_pre
        d_act = dot("te,de->td", d_pre, qkv_w).astype(BF).reshape(2, quads, rows, width)
        d_act = scatter_ctx(d_act[0], d_act[1])
        d_inputs, gain_part = norm_back(s["inputs"], s["attn_root"], gain_attn, d_act)
        part_attn_gain = part_attn_gain + gain_part
        input_grads.append(d_inputs + d_mid)

    def both(name):
        return jnp.concatenate([s[name] for s in saved], axis=0)

    x_all = jnp.concatenate(x_list, axis=0)
    g_all = jnp.concatenate(g_list, axis=0)
    grad_down = dot("tef,td->efd", jnp.concatenate(hid_list, axis=0), g_all)
    grad_down = grad_down.reshape(local_experts, lanes, -1, width).swapaxes(0, 1)
    grad_down = scatter_lane(grad_down)

    def scatter_depth(parts):
        grad = dot("td,tef->edf", x_all, jnp.concatenate(parts, axis=0))
        grad = grad.reshape(local_experts, 2, lanes, depth_part, hidden_half)
        grad = scatter_lane(grad.transpose(2, 1, 0, 3, 4)).astype(BF)
        own = lax.dynamic_index_in_dim(grad, half, 0, keepdims=False)
        other = swap(lax.dynamic_index_in_dim(grad, 1 - half, 0, keepdims=False), "half")
        first = half == 0
        return jnp.concatenate(
            [jnp.where(first, own, other), jnp.where(first, other, own)], axis=2
        ).astype(F32)

    grad_gate = scatter_depth(dgate_list)
    grad_up = scatter_depth(dup_list)

    grad_out = dot("td,te->de", both("attended"), both("d_att_out")).astype(BF)
    grad_out = lax.psum_scatter(grad_out, ALL, scatter_dimension=0, tiled=True).astype(F32)
    grad_qkv = dot("td,te->de", both("act"), both("d_pre")).astype(BF)
    grad_qkv = lax.psum_scatter(grad_qkv, DP, scatter_dimension=0, tiled=True)
    grad_qkv = exchange(grad_qkv.reshape(ctx_size, shard, 3 * head_width), CTX).astype(F32)
    grad_qkv = grad_qkv.reshape(ctx_size, shard, 3, head_width).transpose(2, 1, 0, 3)
    grad_qkv = grad_qkv.reshape(3, shard, width)

    grad_router = dot("td,te->de", both("mixed_in"), both("d_logits"))
    columns = jnp.arange(ctx_size, dtype=jnp.int32)[:, None] == here

    def placed(part):
        return jnp.where(columns, part[None, :], 0.0).reshape(width)

    gains = jnp.stack(
        [part_attn_gain, part_mlp_gain, placed(part_query_gain), placed(part_key_gain)]
    )
    gains = gains.reshape(4, dp_size, ctx_size, shard).transpose(1, 2, 0, 3)
    packed = jnp.concatenate(
        [
            gains.reshape(dp_size, ctx_size, 4 * shard),
            grad_router.reshape(dp_size, ctx_size, shard * expert_count),
        ],
        axis=2,
    )
    packed = reduce_small(packed)
    return (
        jnp.stack(outputs).reshape(batches, 1, rows, width),
        jnp.stack(input_grads).reshape(batches, 1, rows, width),
        grad_qkv[0],
        grad_qkv[1],
        grad_qkv[2],
        grad_out,
        packed[4 * shard :].reshape(shard, expert_count),
        grad_gate,
        grad_up,
        grad_down,
        packed[:shard],
        packed[shard : 2 * shard],
        packed[2 * shard : 3 * shard],
        packed[3 * shard : 4 * shard],
    )


def solution(mesh):
    dp_size, ctx_size = mesh.shape["dp"], mesh.shape["ctx"]
    grid = Mesh(mesh.devices.reshape(2, dp_size // 2, ctx_size // 2, 2), ALL)
    rows = P(None, DP, CTX, None)
    dense = P(ALL, None)
    expert = P(CTX, DP, None)
    vector = P(ALL)
    return jax.shard_map(
        on_device,
        mesh=grid,
        in_specs=(rows, rows, rows, P(None, DP), P())
        + (dense,) * 5
        + (expert,) * 3
        + (vector,) * 4,
        out_specs=(rows, rows) + (dense,) * 5 + (expert,) * 3 + (vector,) * 4,
        check_vma=False,
    )
```

time: 2980 us -> 1610 us (0.54)
  waiting for transfers between devices: 1870 us -> 525 us
  blocking collectives: 235 us -> 24.8 us
  starting transfers between devices: 30.2 us -> 166 us
  other arithmetic: 111 us -> 190 us
  local copies, waits for them, and re-layouts: 313 us -> 238 us
  matrix products: 391 us -> 431 us
    reduce_scatter x9 -> x2, waiting for transfers between devices: 1100 us -> 0.01 us  [the longest x1 0.01 us: on_device(): lax.psum_scatter(grad_out, ALL, scatter_dimension=0, tiled=True).astype(F32)]
    all_gather x11 -> x2, waiting for transfers between devices: 508 us -> 0.02 us  [the longest x1 0.02 us: on_device(): out_w = lax.all_gather(w_out, ALL, axis=0, tiled=True)]
    ppermute x0 -> x54, waiting for transfers between devices: none -> 308 us  [the longest x46 301 us: swap(): return lax.ppermute(values, axis, [(0, 1), (1, 0)])]
    unnamed x26 -> x4, waiting for transfers between devices: 131 us -> 0.07 us
    gather x12 -> x0, local copies, waits for them, and re-layouts: 114 us -> none  [the longest x4 35.5 us: on_device(): d_send = jnp.where(filled, d_returned[source], bf_zero)]
    all_to_all x6 -> x32, starting transfers between devices: 28.2 us -> 132 us  [exchange(): return lax.all_to_all(blocks, axes, split_axis=0, concat_axis=0, tiled=True)]
    all_to_all x6 -> x32, waiting for transfers between devices: 130 us -> 217 us  [exchange(): return lax.all_to_all(blocks, axes, split_axis=0, concat_axis=0, tiled=True)]
    all_to_all x2, blocking collectives: 110 us -> 24.8 us  [exchange(): return lax.all_to_all(blocks, axes, split_axis=0, concat_axis=0, tiled=True)]
  transfers between devices with their start and end apart: 29 -> 90, of which waited for: 21 -> 43; matrix products, arithmetic and copies ran while one was open for 21% -> 49% of each run, Pallas kernels for 0% -> 0%
where the time goes in v1:
time: 1610 us; the launch traced here: 1590 us
  waiting for transfers between devices  525 us (33%)
  matrix products  431 us (27%)
  local copies, waits for them, and re-layouts  238 us (15%)
  other arithmetic  190 us (12%)
  starting transfers between devices  166 us (10%)
  blocking collectives  24.8 us (2%)
  between operations  17.1 us (1%)
    dot_general x52, matrix products, dot(): return jnp.einsum(spec, left, right, preferred_element_type=F32)  417 us
    ppermute x46, waiting for transfers between devices, swap(): return lax.ppermute(values, axis, [(0, 1), (1, 0)])  301 us
    all_to_all x32, waiting for transfers between devices, exchange(): return lax.all_to_all(blocks, axes, split_axis=0, concat_axis=0, tiled=True)  217 us
    all_to_all x32, starting transfers between devices, exchange(): return lax.all_to_all(blocks, axes, split_axis=0, concat_axis=0, tiled=True)  132 us
    unnamed x367, local copies, waits for them, and re-layouts  72 us
    convert_element_type x10, other arithmetic, scatter_ctx(): received = exchange(merged.astype(BF), 'quad')  38.7 us
    another operation x10, other arithmetic, gather_ctx(): return jnp.stack([own, swap(own, 'pair')])  35.6 us
  transfers between devices with their start and end apart: 90, of which 43 were waited for; matrix products, arithmetic and copies ran while one was open for 49% of the time, Pallas kernels for 0%

profile of v1, /device:TPU:0, one launch (start us, length us, event | category | flops | bytes accessed | tf_op | source)
XLA Modules:
  0.0 1591.0 jit_solution(517677586306169494)
XLA Ops:
  14.3 17.6 %all_to_all.175 = bf16[8,64,768]{2,1,0:T(8,128)(2,1)} all-to-all(bf16[8,64,768]{2,1,0:T(8,128)(2,1)S(1)} %reshape.1247), channel_id=1, replica_groups=mesh['half'=2,'lane'=2,'quad'=4,'pair'=2] {'quad','pair'}, dimensions={0} | all-to-all | bytes 1572864 | tf_op jit(solution)/shard_map/all_to_all | solution.py:62
  71.0 14.5 all-to-all-done.17
  122.6 24.0 %all-to-all-done.2 = bf16[4,128,2048]{2,1,0:T(8,128)(2,1)S(1)} async-done(((bf16[4,128,2048]{2,1,0:T(8,128)(2,1)}), bf16[4,128,2048]{2,1,0:T(8,128)(2,1)S(1)}, u32[]{:S(2)}, u32[]{:S(2)}) %all-to-all-start.2) | async-done | bytes 2097184 | tf_op jit(solution)/shard_map/all_to_all | solution.py:62
  186.1 28.1 %collective-permute-done.7 = bf16[2,512,512]{2,1,0:T(8,128)(2,1)} collective-permute-done((bf16[2,512,512]{2,1,0:T(8,128)(2,1)}, bf16[2,512,512]{2,1,0:T(8,128)(2,1)}, u32[]{:S(2)}, u32[]{:S(2)}) %collective-permute-start.7) | collective-permute-done | bytes 1048608 | tf_op jit(solution)/shard_map/ppermute | solution.py:58
  219.3 17.3 %collective-permute-done.5 = bf16[2,512,512]{2,1,0:T(8,128)(2,1)} collective-permute-done((bf16[2,512,512]{2,1,0:T(8,128)(2,1)}, bf16[2,512,512]{2,1,0:T(8,128)(2,1)}, u32[]{:S(2)}, u32[]{:S(2)}) %collective-permute-start.5) | collective-permute-done | bytes 1048608 | tf_op jit(solution)/shard_map/ppermute | solution.py:58
  257.5 57.9 %collective-permute-done.8 = bf16[2,2,512,512]{3,2,1,0:T(8,128)(2,1)} collective-permute-done((bf16[2,2,512,512]{3,2,1,0:T(8,128)(2,1)}, bf16[2,2,512,512]{3,2,1,0:T(8,128)(2,1)}, u32[]{:S(2)}, u32[]{:S(2)}) %collective-permute-start.8) | collective-permute-done | bytes 2097184 | tf_op jit(solution)/shard_map/ppermute | solution.py:58
  320.2 40.1 %collective-permute-done.6 = bf16[2,2,512,512]{3,2,1,0:T(8,128)(2,1)} collective-permute-done((bf16[2,2,512,512]{3,2,1,0:T(8,128)(2,1)}, bf16[2,2,512,512]{3,2,1,0:T(8,128)(2,1)}, u32[]{:S(2)}, u32[]{:S(2)}) %collective-permute-start.6) | collective-permute-done | bytes 2097184 | tf_op jit(solution)/shard_map/ppermute | solution.py:58
  471.2 12.2 all-to-all-done.5
  509.8 15.5 all-to-all-done.8
  667.4 11.6 collective-permute-done.32
  699.1 15.4 all-to-all-done.12
  845.6 12.9 all-to-all-done.9
  884.3 12.4 all-to-all-done.14
  909.8 16.1 %all-to-all-done.25 = bf16[4,128,2048]{2,1,0:T(8,128)(2,1)} async-done(((bf16[4,128,2048]{2,1,0:T(8,128)(2,1)}), bf16[4,128,2048]{2,1,0:T(8,128)(2,1)}, u32[]{:S(2)}, u32[]{:S(2)}) %all-to-all-start.25) | async-done | bytes 2097184 | tf_op jit(solution)/shard_map/all_to_all | solution.py:62
  934.9 19.8 %all-to-all-done.27 = bf16[4,128,2048]{2,1,0:T(8,128)(2,1)} async-done(((bf16[4,128,2048]{2,1,0:T(8,128)(2,1)}), bf16[4,128,2048]{2,1,0:T(8,128)(2,1)}, u32[]{:S(2)}, u32[]{:S(2)}) %all-to-all-start.27) | async-done | bytes 2097184 | tf_op jit(solution)/shard_map/all_to_all | solution.py:62
  987.9 34.8 %collective-permute-done.43 = bf16[128,2048]{1,0:T(8,128)(2,1)} collective-permute-done((bf16[128,2048]{1,0:T(8,128)(2,1)}, bf16[128,2048]{1,0:T(8,128)(2,1)}, u32[]{:S(2)}, u32[]{:S(2)}) %collective-permute-start.43) | collective-permute-done | bytes 524320 | tf_op jit(solution)/shard_map/ppermute | solution.py:58
  1137.5 44.2 %fusion.42 = f32[2,2048,512]{1,2,0:T(8,128)} fusion(bf16[1024,2048]{1,0:T(8,128)(2,1)} %bitcast.653, bf16[1024,2048]{1,0:T(8,128)(2,1)} %bitcast.657, bf16[1024,2048]{1,0:T(8,128)(2,1)} %bitcast.619, bf16[1024,2048]{1,0:T(8,128)(2,1)} %bitcast.623, bf16[1024,2,512]{2,0,1:T(8,128)(2,1)} %get-tuple-element.140, bf16[1024,2,512]{2,0,1:T(8,128)(2,1)} %get-tuple-element.138, ...), kind=kOutput, calls=%fused_computation.63 | convolution fusion | flops 17280532480 | bytes 33554432 | tf_op jit(solution)/shard_map/td,tef->edf/dot_general | solution.py:21
  1189.1 41.1 %fusion.45 = f32[2,2048,512]{1,2,0:T(8,128)} fusion(bf16[1024,2048]{1,0:T(8,128)(2,1)} %bitcast.654, bf16[1024,2048]{1,0:T(8,128)(2,1)} %bitcast.658, bf16[1024,2048]{1,0:T(8,128)(2,1)} %bitcast.620, bf16[1024,2048]{1,0:T(8,128)(2,1)} %bitcast.624, bf16[1024,2,512]{2,0,1:T(8,128)(2,1)} %copy-done.161, bf16[1024,2,512]{2,0,1:T(8,128)(2,1)} %copy-done.162, ...), kind=kOutput, calls=%fused_computation.64 | convolution fusion | flops 17280532480 | bytes 33554432 | tf_op jit(solution)/shard_map/td,tef->edf/dot_general | solution.py:21
  1230.2 11.7 reshape.1308
  1261.6 11.9 reshape.1307
  1302.4 43.9 %fusion.2 = f32[2,512,2048]{2,1,0:T(8,128)} fusion(bf16[1024,2048]{1,0:T(8,128)(2,1)} %bitcast.614, bf16[1024,2048]{1,0:T(8,128)(2,1)} %bitcast.642, bf16[1024,2048]{1,0:T(8,128)(2,1)} %bitcast.608, bf16[1024,2048]{1,0:T(8,128)(2,1)} %bitcast.616, bf16[1024,2,512]{2,0,1:T(8,128)(2,1)} %copy-done.164, bf16[1024,2,512]{2,0,1:T(8,128)(2,1)} %get-tuple-element.139, ...), kind=kOutput, calls=%fused_computation.4 | convolution fusion | flops 17280532480 | bytes 33554432 | tf_op jit(solution)/shard_map/tef,td->efd/dot_general | solution.py:21
  1381.2 11.3 copy.334
  1420.0 53.8 %collective-permute-done.49 = bf16[2,2,512,512]{3,2,1,0:T(8,128)(2,1)} collective-permute-done((bf16[2,2,512,512]{3,2,1,0:T(8,128)(2,1)}, bf16[2,2,512,512]{3,2,1,0:T(8,128)(2,1)}, u32[]{:S(2)}, u32[]{:S(2)}) %collective-permute-start.49) | collective-permute-done | bytes 2097184 | tf_op jit(solution)/shard_map/ppermute | solution.py:58
  1498.0 29.6 %collective-permute-done.50 = bf16[2,512,512]{2,1,0:T(8,128)(2,1)} collective-permute-done((bf16[2,512,512]{2,1,0:T(8,128)(2,1)}, bf16[2,512,512]{2,1,0:T(8,128)(2,1)}, u32[]{:S(2)}, u32[]{:S(2)}) %collective-permute-start.50) | collective-permute-done | bytes 1048608 | tf_op jit(solution)/shard_map/ppermute | solution.py:58
  (852 shorter events, 975.9 us)
Async XLA Ops:
  7.2 367.7 %all-gather.3.cloned.1.call-start = ((), (), s32[]{:S(2)}) async-start(), calls=%async_computation.36 | async-start | bytes 3932160 | tf_op jit(solution)/shard_map/all_gather | solution.py:179
  60.2 109.1 %collective-permute-start.29 = (bf16[128,2048]{1,0:T(8,128)(2,1)}, bf16[128,2048]{1,0:T(8,128)(2,1)}, u32[]{:S(2)}, u32[]{:S(2)}) collective-permute-start(bf16[128,2048]{1,0:T(8,128)(2,1)} %get-tuple-element.203), channel_id=1, source_target_pairs={{0,16},{16,0},{1,17},{17,1},{2,18},{18,2},{3,19},{19,3},{4,20},{20... | collective-permute-start | bytes 1572872 | tf_op jit(solution)/shard_map/ppermute | solution.py:58
  61.0 183.5 %collective-permute-start.40 = (bf16[128,2048]{1,0:T(8,128)(2,1)}, bf16[128,2048]{1,0:T(8,128)(2,1)}, u32[]{:S(2)}, u32[]{:S(2)}) collective-permute-start(bf16[128,2048]{1,0:T(8,128)(2,1)} %get-tuple-element.204), channel_id=1, source_target_pairs={{0,16},{16,0},{1,17},{17,1},{2,18},{18,2},{3,19},{19,3},{4,20},{20... | collective-permute-start | bytes 1572872 | tf_op jit(solution)/shard_map/ppermute | solution.py:58
  92.6 353.1 %all-gather.5.cloned.1.call-start = ((), (), s32[]{:S(2)}) async-start(), calls=%async_computation.37 | async-start | bytes 8650752 | tf_op jit(solution)/shard_map/all_gather | solution.py:180
  105.1 109.0 %collective-permute-start.7 = (bf16[2,512,512]{2,1,0:T(8,128)(2,1)}, bf16[2,512,512]{2,1,0:T(8,128)(2,1)}, u32[]{:S(2)}, u32[]{:S(2)}) collective-permute-start(bf16[2,512,512]{2,1,0:T(8,128)(2,1)} %bitcast.569), channel_id=1, source_target_pairs={{0,16},{16,0},{1,17},{17,1},{2,18},{18,2},{3,19},{19,3},{4,20},{20... | collective-permute-start | bytes 3145736 | tf_op jit(solution)/shard_map/ppermute | solution.py:58
  106.4 130.3 %collective-permute-start.5 = (bf16[2,512,512]{2,1,0:T(8,128)(2,1)}, bf16[2,512,512]{2,1,0:T(8,128)(2,1)}, u32[]{:S(2)}, u32[]{:S(2)}) collective-permute-start(bf16[2,512,512]{2,1,0:T(8,128)(2,1)} %bitcast.570), channel_id=1, source_target_pairs={{0,16},{16,0},{1,17},{17,1},{2,18},{18,2},{3,19},{19,3},{4,20},{20... | collective-permute-start | bytes 3145736 | tf_op jit(solution)/shard_map/ppermute | solution.py:58
  109.3 142.7 %collective-permute-start.9 = (bf16[2,256,2048]{2,1,0:T(8,128)(2,1)}, bf16[2,256,2048]{2,1,0:T(8,128)(2,1)}, u32[]{:S(2)}, u32[]{:S(2)}) collective-permute-start(bf16[2,256,2048]{2,1,0:T(8,128)(2,1)} %param.29), channel_id=1, source_target_pairs={{0,8},{8,0},{1,9},{9,1},{2,10},{10,2},{3,11},{11,3},{4,12},{12,4},... | collective-permute-start | bytes 6291464 | tf_op jit(solution)/shard_map/ppermute | solution.py:58
  218.7 96.7 %collective-permute-start.8 = (bf16[2,2,512,512]{3,2,1,0:T(8,128)(2,1)}, bf16[2,2,512,512]{3,2,1,0:T(8,128)(2,1)}, u32[]{:S(2)}, u32[]{:S(2)}) collective-permute-start(bf16[2,2,512,512]{3,2,1,0:T(8,128)(2,1)} %pad_maximum_fusion.11), channel_id=1, source_target_pairs={{0,8},{8,0},{1,9},{9,1},{2,10},{10,2},{3,11},{11,3},{4,12},{12,4},... | collective-permute-start | bytes 6291464 | tf_op jit(solution)/shard_map/ppermute | solution.py:58
  241.3 119.1 %collective-permute-start.6 = (bf16[2,2,512,512]{3,2,1,0:T(8,128)(2,1)}, bf16[2,2,512,512]{3,2,1,0:T(8,128)(2,1)}, u32[]{:S(2)}, u32[]{:S(2)}) collective-permute-start(bf16[2,2,512,512]{3,2,1,0:T(8,128)(2,1)} %pad_maximum_fusion.10), channel_id=1, source_target_pairs={{0,8},{8,0},{1,9},{9,1},{2,10},{10,2},{3,11},{11,3},{4,12},{12,4},... | collective-permute-start | bytes 6291464 | tf_op jit(solution)/shard_map/ppermute | solution.py:58
  244.4 147.5 %collective-permute-start.27 = (bf16[4,128,2048]{2,1,0:T(8,128)(2,1)}, bf16[4,128,2048]{2,1,0:T(8,128)(2,1)}, u32[]{:S(2)}, u32[]{:S(2)}) collective-permute-start(bf16[4,128,2048]{2,1,0:T(8,128)(2,1)} %all-to-all-done.17), channel_id=1, source_target_pairs={{0,1},{1,0},{2,3},{3,2},{4,5},{5,4},{6,7},{7,6},{8,9},{9,8},{10,11... | collective-permute-start | bytes 6291464 | tf_op jit(solution)/shard_map/ppermute | solution.py:58
  244.5 120.7 %collective-permute-start = (bf16[4,128,2048]{2,1,0:T(8,128)(2,1)}, bf16[4,128,2048]{2,1,0:T(8,128)(2,1)}, u32[]{:S(2)}, u32[]{:S(2)}) collective-permute-start(bf16[4,128,2048]{2,1,0:T(8,128)(2,1)} %copy-done.39), channel_id=1, source_target_pairs={{0,1},{1,0},{2,3},{3,2},{4,5},{5,4},{6,7},{7,6},{8,9},{9,8},{10,11... | collective-permute-start | bytes 6291464 | tf_op jit(solution)/shard_map/ppermute | solution.py:58
  247.6 117.6 %all-to-all-start.26 = ((bf16[4,128,2048]{2,1,0:T(8,128)(2,1)}), bf16[4,128,2048]{2,1,0:T(8,128)(2,1)}, u32[]{:S(2)}, u32[]{:S(2)}) async-start(bf16[4,128,2048]{2,1,0:T(8,128)(2,1)} %broadcast_in_dim.141), calls=%async_computation.26 | async-start | bytes 4194304 | tf_op jit(solution)/shard_map/all_to_all | solution.py:62
  252.0 118.2 %collective-permute-start.16 = (bf16[4,128,2048]{2,1,0:T(8,128)(2,1)}, bf16[4,128,2048]{2,1,0:T(8,128)(2,1)}, u32[]{:S(2)}, u32[]{:S(2)}) collective-permute-start(bf16[4,128,2048]{2,1,0:T(8,128)(2,1)} %all-to-all-done.10), channel_id=1, source_target_pairs={{0,1},{1,0},{2,3},{3,2},{4,5},{5,4},{6,7},{7,6},{8,9},{9,8},{10,11... | collective-permute-start | bytes 6291464 | tf_op jit(solution)/shard_map/ppermute | solution.py:58
  315.4 120.3 %collective-permute-start.38 = (bf16[4,128,2048]{2,1,0:T(8,128)(2,1)}, bf16[4,128,2048]{2,1,0:T(8,128)(2,1)}, u32[]{:S(2)}, u32[]{:S(2)}) collective-permute-start(bf16[4,128,2048]{2,1,0:T(8,128)(2,1)} %all-to-all-done.24), channel_id=1, source_target_pairs={{0,1},{1,0},{2,3},{3,2},{4,5},{5,4},{6,7},{7,6},{8,9},{9,8},{10,11... | collective-permute-start | bytes 6291464 | tf_op jit(solution)/shard_map/ppermute | solution.py:58
  360.3 80.0 %collective-permute-start.30 = (bf16[4,128,2048]{2,1,0:T(8,128)(2,1)}, bf16[4,128,2048]{2,1,0:T(8,128)(2,1)}, u32[]{:S(2)}, u32[]{:S(2)}) collective-permute-start(bf16[4,128,2048]{2,1,0:T(8,128)(2,1)} %all-to-all-done.19), channel_id=1, source_target_pairs={{0,1},{1,0},{2,3},{3,2},{4,5},{5,4},{6,7},{7,6},{8,9},{9,8},{10,11... | collective-permute-start | bytes 6291464 | tf_op jit(solution)/shard_map/ppermute | solution.py:58
  365.2 352.6 %collective-permute-start.41 = (bf16[4,128,2048]{2,1,0:T(8,128)(2,1)}, bf16[4,128,2048]{2,1,0:T(8,128)(2,1)}, u32[]{:S(2)}, u32[]{:S(2)}) collective-permute-start(bf16[4,128,2048]{2,1,0:T(8,128)(2,1)} %all-to-all-done.26), channel_id=1, source_target_pairs={{0,1},{1,0},{2,3},{3,2},{4,5},{5,4},{6,7},{7,6},{8,9},{9,8},{10,11... | collective-permute-start | bytes 6291464 | tf_op jit(solution)/shard_map/ppermute | solution.py:58
  650.7 90.0 %collective-permute-start.10 = (bf16[4,128,2048]{2,1,0:T(8,128)(2,1)}, bf16[4,128,2048]{2,1,0:T(8,128)(2,1)}, u32[]{:S(2)}, u32[]{:S(2)}) collective-permute-start(bf16[4,128,2048]{2,1,0:T(8,128)(2,1)} %bitcast.52), channel_id=1, source_target_pairs={{0,1},{1,0},{2,3},{3,2},{4,5},{5,4},{6,7},{7,6},{8,9},{9,8},{10,11... | collective-permute-start | bytes 6291464 | tf_op jit(solution)/shard_map/ppermute | solution.py:58
  1063.0 494.8 %reduce-scatter.3.cloned.1.call-start = ((), (), s32[]{:S(2)}) async-start(), calls=%async_computation.38 | async-start | bytes 3932160 | tf_op jit(solution)/shard_map/reduce_scatter | solution.py:388
  1136.8 445.7 %reduce-scatter.5.cloned.1.call-start = ((), (), s32[]{:S(2)}) async-start(), calls=%async_computation.39 | async-start | bytes 8650752 | tf_op jit(solution)/shard_map/reduce_scatter | solution.py:386
  1261.6 143.1 %collective-permute-start.51 = (bf16[2,2,512,512]{3,2,1,0:T(8,128)(2,1)}, bf16[2,2,512,512]{3,2,1,0:T(8,128)(2,1)}, u32[]{:S(2)}, u32[]{:S(2)}) collective-permute-start(bf16[2,2,512,512]{3,2,1,0:T(8,128)(2,1)} %bitcast.471), channel_id=1, source_target_pairs={{0,8},{8,0},{1,9},{9,1},{2,10},{10,2},{3,11},{11,3},{4,12},{12,4},... | collective-permute-start | bytes 6291464 | tf_op jit(solution)/shard_map/ppermute | solution.py:58
  1357.7 122.1 %collective-permute-start.53 = (bf16[2,256,2048]{2,1,0:T(8,128)(2,1)}, bf16[2,256,2048]{2,1,0:T(8,128)(2,1)}, u32[]{:S(2)}, u32[]{:S(2)}) collective-permute-start(bf16[2,256,2048]{2,1,0:T(8,128)(2,1)} %fusion.80), channel_id=1, source_target_pairs={{0,8},{8,0},{1,9},{9,1},{2,10},{10,2},{3,11},{11,3},{4,12},{12,4},... | collective-permute-start | bytes 6291464 | tf_op jit(solution)/shard_map/ppermute | solution.py:58
  1381.1 92.7 %collective-permute-start.49 = (bf16[2,2,512,512]{3,2,1,0:T(8,128)(2,1)}, bf16[2,2,512,512]{3,2,1,0:T(8,128)(2,1)}, u32[]{:S(2)}, u32[]{:S(2)}) collective-permute-start(bf16[2,2,512,512]{3,2,1,0:T(8,128)(2,1)} %bitcast.660), channel_id=1, source_target_pairs={{0,8},{8,0},{1,9},{9,1},{2,10},{10,2},{3,11},{11,3},{4,12},{12,4},... | collective-permute-start | bytes 6291464 | tf_op jit(solution)/shard_map/ppermute | solution.py:58
  1404.5 81.2 %collective-permute-start.37 = (bf16[4,128,2048]{2,1,0:T(8,128)(2,1)}, bf16[4,128,2048]{2,1,0:T(8,128)(2,1)}, u32[]{:S(2)}, u32[]{:S(2)}) collective-permute-start(bf16[4,128,2048]{2,1,0:T(8,128)(2,1)} %bitcast.134), channel_id=1, source_target_pairs={{0,1},{1,0},{2,3},{3,2},{4,5},{5,4},{6,7},{7,6},{8,9},{9,8},{10,11... | collective-permute-start | bytes 6291464 | tf_op jit(solution)/shard_map/ppermute | solution.py:58
  1410.4 83.6 %collective-permute-start.52 = (bf16[2,512,512]{2,1,0:T(8,128)(2,1)}, bf16[2,512,512]{2,1,0:T(8,128)(2,1)S(1)}, u32[]{:S(2)}, u32[]{:S(2)}) collective-permute-start(bf16[2,512,512]{2,1,0:T(8,128)(2,1)} %dynamic-slice_bitcast_fusion), channel_id=1, source_target_pairs={{0,16},{16,0},{1,17},{17,1},{2,18},{18,2},{3,19},{19,3},{4,20},{20... | collective-permute-start | bytes 3145736 | tf_op jit(solution)/shard_map/ppermute | solution.py:58
  (233 other events, 5183.8 us)
Sparse Core Ops, SparseCore 0:
  32.1 148.6 all-gather.2
  183.6 131.2 all-gather.4
  1136.9 57.6 reduce-scatter.2
  1196.8 158.9 reduce-scatter.4

commit v2 on v1

v2 whole, which is shorter than its diff:
```python
import functools
import math

import jax
import jax.numpy as jnp
from jax import lax
from jax.experimental import pallas as pl
from jax.experimental.pallas import tpu as pltpu
from jax.sharding import Mesh
from jax.sharding import PartitionSpec as P

HEAD = 128
EPSILON = 1e-05
ROPE_BASE = 10000.0
MASKED = -1e30
BF = jnp.bfloat16
F32 = jnp.float32
DP = ("half", "lane")
CTX = ("quad", "pair")
ALL = DP + CTX
MESH = pl.DeviceIdType.MESH


def dot(spec, left, right):
    return jnp.einsum(spec, left, right, preferred_element_type=F32)


def inv_rms(values):
    return lax.rsqrt(jnp.mean(values * values, axis=-1, keepdims=True) + EPSILON)


def norm_back(values, inv_root, gain_vec, grad_in):
    weighted = grad_in * gain_vec
    inner = jnp.mean(weighted * values, axis=-1, keepdims=True)
    grad_values = inv_root * weighted - values * (inv_root * inv_root * inv_root) * inner
    return (grad_values, jnp.sum(grad_in * values * inv_root, axis=0))


def angles(places, head_width):
    index = jnp.arange(head_width // 2, dtype=F32)
    freqs = jnp.power(ROPE_BASE, -2.0 * index / head_width)
    turning = places.astype(F32)[:, None] * freqs[None, :]
    turning = jnp.concatenate([turning, turning], axis=1)
    return (jnp.cos(turning)[:, None, :], jnp.sin(turning)[:, None, :])


def rotate(values, cosine, sine):
    half_size = values.shape[-1] // 2
    turned = jnp.concatenate([-values[..., half_size:], values[..., :half_size]], axis=-1)
    return values * cosine + turned * sine


def rotate_back(grad_in, cosine, sine):
    half_size = grad_in.shape[-1] // 2
    moved = grad_in * sine
    return grad_in * cosine + jnp.concatenate(
        [moved[..., half_size:], -moved[..., :half_size]], axis=-1
    )


def swap(values, axis):
    return lax.ppermute(values, axis, [(0, 1), (1, 0)])


def exchange(blocks, axes):
    return lax.all_to_all(blocks, axes, split_axis=0, concat_axis=0, tiled=True)


def spread(values, axes):
    count = lax.axis_size(axes)
    return exchange(jnp.broadcast_to(values[None], (count,) + values.shape), axes)


def from_relative(blocks):
    quads = blocks.shape[1]
    pair, quad = lax.axis_index("pair"), lax.axis_index("quad")
    cores = jnp.where(pair == 0, blocks, blocks[::-1])
    step = 1
    while step < quads:
        split = cores.reshape((2, quads // (2 * step), 2, step) + blocks.shape[2:])
        flipped = split[:, :, ::-1].reshape(blocks.shape)
        cores = jnp.where((quad & step) == 0, cores, flipped)
        step *= 2
    return cores.swapaxes(0, 1).reshape((2 * quads,) + blocks.shape[2:])


def to_relative(blocks):
    split = blocks.reshape((-1, 2) + blocks.shape[1:]).swapaxes(0, 1)
    again = from_relative(split)
    return again.reshape((-1, 2) + blocks.shape[1:]).swapaxes(0, 1)


def sum_ctx(values):
    values = values + swap(values, "pair")[:, ::-1]
    kinds, _, quads = values.shape[:3]
    step = 1
    while step < quads:
        moved = lax.ppermute(values, "quad", [(i, i ^ step) for i in range(quads)])
        split = moved.reshape((kinds, 2, quads // (2 * step), 2, step, -1))
        values = values + split[:, :, :, ::-1].reshape(values.shape)
        step *= 2
    return values


def gather_lane(values):
    if lax.axis_size("lane") == 2:
        other = swap(values, "lane")
        first = lax.axis_index("lane") == 0
        return jnp.stack([jnp.where(first, values, other), jnp.where(first, other, values)])
    return lax.all_gather(values, "lane", axis=0, tiled=False)


def scatter_lane(values):
    count = lax.axis_size("lane")
    here = lax.axis_index("lane")
    if count == 2:
        own = jnp.where(here == 0, values[0], values[1])
        other = jnp.where(here == 0, values[1], values[0]).astype(BF)
        return own + swap(other, "lane").astype(F32)
    return lax.psum_scatter(values.astype(BF), "lane", scatter_dimension=0, tiled=False).astype(F32)


def reduce_small(values):
    over_ctx = jnp.sum(exchange(values.swapaxes(0, 1), CTX), axis=0)
    return jnp.sum(exchange(over_ctx, DP), axis=0)


def toggled(index, bits):
    step = 1
    while step <= bits:
        if bits & step:
            index = index + step - 2 * step * ((index // step) % 2)
        step *= 2
    return index


def greet(peers):
    barrier = pltpu.get_barrier_semaphore()
    for peer in peers:
        pl.semaphore_signal(barrier, inc=1, device_id=peer, device_id_type=MESH)
    pl.semaphore_wait(barrier, len(peers))


def gather_sems(quads, count, partner):
    return count * (2 if partner else 1) * (13 if quads == 4 else 2 * quads - 1) + (count if partner else 0)


def gather_body(quads, count, partner, x_ref, own_ref, other_ref, *rest):
    if partner:
        keep_ref, local, send, recv = rest
    else:
        keep_ref = None
        local, send, recv = rest
    rows = x_ref.shape[1]
    half = rows // 2
    first, second = pl.ds(0, half), pl.ds(half, half)
    quad = lax.axis_index("quad")
    to_quad = [{"quad": toggled(quad, k)} for k in range(quads)]
    sibling = {"pair": 1 - lax.axis_index("pair")}
    peers = to_quad[1:] + [sibling]
    if partner:
        across = {"half": 1 - lax.axis_index("half")}
        peers = peers + [across]
    greet(peers)
    number = iter(range(send.shape[0]))

    def copy(src, dst, device):
        i = next(number)
        return pltpu.make_async_remote_copy(
            src_ref=src, dst_ref=dst, send_sem=send.at[i], recv_sem=recv.at[i],
            device_id=device, device_id_type=MESH)

    finish = []

    def go(*copies):
        for c in copies:
            c.start()
            finish.append(c)

    def at(ref, k, s, part=None):
        view = ref.at[k, s]
        return view if part is None else view.at[part]

    def plan(src, s):
        p = {}
        p["o0"] = copy(src, at(other_ref, 0, s), sibling)
        if quads == 4:
            for k in (1, 2):
                for name, part in (("a", first), ("b", second)):
                    p[f"s{k}{name}"] = copy(src.at[part], at(own_ref, k, s, part), to_quad[k])
            p["f3a"] = copy(at(own_ref, 1, s, first), at(own_ref, 3, s, first), to_quad[2])
            p["f3b"] = copy(at(own_ref, 2, s, second), at(own_ref, 3, s, second), to_quad[1])
            for k in (1, 2, 3):
                for name, part in (("a", first), ("b", second)):
                    p[f"o{k}{name}"] = copy(
                        at(own_ref, k, s, part), at(other_ref, k, s, part), sibling)
        else:
            for k in range(1, quads):
                p[f"s{k}"] = copy(src, at(own_ref, k, s), to_quad[k])
                p[f"o{k}"] = copy(at(own_ref, k, s), at(other_ref, k, s), sibling)
        return p

    def begin(p):
        if quads == 4:
            go(p["s1a"], p["s2b"], p["s1b"], p["s2a"], p["o0"])
        else:
            go(*[p[f"s{k}"] for k in range(1, quads)], p["o0"])

    def forward(p):
        if quads == 4:
            p["s1a"].wait_recv(); go(p["f3a"], p["o1a"])
            p["s2b"].wait_recv(); go(p["f3b"], p["o2b"])
            p["s1b"].wait_recv(); go(p["o1b"])
            p["s2a"].wait_recv(); go(p["o2a"])
        else:
            for k in range(1, quads):
                p[f"s{k}"].wait_recv(); go(p[f"o{k}"])

    def last(p):
        if quads == 4:
            p["f3a"].wait_recv(); go(p["o3a"])
            p["f3b"].wait_recv(); go(p["o3b"])

    def done(p):
        for name, c in p.items():
            if name[0] == "o":
                c.wait_recv()

    locals_ = []
    plans = []
    zs = []
    if partner:
        for s in range(count):
            z = copy(x_ref.at[s], keep_ref.at[s], across)
            go(z)
            zs.append(z)
    for s in range(count):
        p = plan(x_ref.at[s], s)
        begin(p)
        plans.append(p)
        c = pltpu.make_async_copy(x_ref.at[s], own_ref.at[0, s], local.at[s])
        c.start()
        locals_.append(c)
    for p in plans:
        forward(p)
    for p in plans:
        last(p)
    if partner:
        later = []
        for s in range(count):
            zs[s].wait_recv()
            p = plan(keep_ref.at[s], count + s)
            begin(p)
            later.append(p)
            c = pltpu.make_async_copy(keep_ref.at[s], own_ref.at[0, count + s], local.at[count + s])
            c.start()
            locals_.append(c)
        for p in later:
            forward(p)
        for p in later:
            last(p)
        plans += later
    for p in plans:
        done(p)
    for c in finish:
        c.wait_send()
    for c in locals_:
        c.wait()


def gather_rows(x, partner, name, cid):
    count, rows, width = x.shape
    quads = lax.axis_size("quad")
    total = count * (2 if partner else 1)
    sems = gather_sems(quads, count, partner)
    shape = jax.ShapeDtypeStruct((quads, total, rows, width), x.dtype)
    scratch = [pltpu.VMEM((count, rows, width), x.dtype)] if partner else []
    return pl.pallas_call(
        functools.partial(gather_body, quads, count, partner),
        out_shape=(shape, shape),
        in_specs=[pl.BlockSpec(memory_space=pltpu.VMEM)],
        out_specs=(pl.BlockSpec(memory_space=pl.ANY),) * 2,
        scratch_shapes=scratch + [
            pltpu.SemaphoreType.DMA((total,)),
            pltpu.SemaphoreType.DMA((sems,)),
            pltpu.SemaphoreType.DMA((sems,)),
        ],
        compiler_params=pltpu.CompilerParams(collective_id=cid, has_side_effects=True),
        name=name,
    )(x)


def scatter_sems(quads, total, partner):
    per = quads + (6 if quads == 4 else quads - 1)
    return total * per + (total // 2 if partner else 0)


def add_rows(out_ref, *refs):
    rows = out_ref.shape[0]
    step = 16

    @pl.loop(0, rows // step)
    def _(i):
        part = pl.ds(pl.multiple_of(i * step, step), step)
        total = refs[0][part].astype(F32)
        for ref in refs[1:]:
            total = total + ref[part].astype(F32)
        out_ref[part] = total.astype(out_ref.dtype)


def scatter_body(quads, count, partner, own_ref, other_ref, out_ref, *rest):
    if partner:
        mine, theirs, merged, relay, arrived, summed, back, local, send, recv = rest
    else:
        mine, theirs, merged, relay, arrived, local, send, recv = rest
        summed = back = None
    total, rows = own_ref.shape[1:3]
    half = rows // 2
    first, second = pl.ds(0, half), pl.ds(half, half)
    quad = lax.axis_index("quad")
    to_quad = [{"quad": toggled(quad, k)} for k in range(quads)]
    sibling = {"pair": 1 - lax.axis_index("pair")}
    peers = to_quad[1:] + [sibling]
    if partner:
        across = {"half": 1 - lax.axis_index("half")}
        peers = peers + [across]
    greet(peers)
    number = iter(range(send.shape[0]))

    def copy(src, dst, device):
        i = next(number)
        return pltpu.make_async_remote_copy(
            src_ref=src, dst_ref=dst, send_sem=send.at[i], recv_sem=recv.at[i],
            device_id=device, device_id_type=MESH)

    finish = []

    def go(c):
        c.start()
        finish.append(c)
        return c

    order = list(range(count, total)) + list(range(count))
    ks = [3, 1, 2, 0] if quads == 4 else list(range(quads - 1, -1, -1))
    sib, loc = {}, {}
    for s in order:
        for k in ks:
            sib[s, k] = go(copy(other_ref.at[k, s], theirs.at[s, k], sibling))
            loc[s, k] = pltpu.make_async_copy(own_ref.at[k, s], mine.at[s, k], local.at[s * quads + k])
            loc[s, k].start()
    sends = {}
    for s in order:
        for k in ks:
            sib[s, k].wait_recv()
            loc[s, k].wait()
            add_rows(merged.at[s, k], mine.at[s, k], theirs.at[s, k])
            if quads == 4:
                if k == 3:
                    sends[s, "3a"] = go(copy(merged.at[s, 3, first], relay.at[s, 0], to_quad[2]))
                    sends[s, "3b"] = go(copy(merged.at[s, 3, second], relay.at[s, 1], to_quad[1]))
                elif k == 1:
                    sends[s, "1b"] = go(copy(merged.at[s, 1, second], arrived.at[s, 0, second], to_quad[1]))
                elif k == 2:
                    sends[s, "2a"] = go(copy(merged.at[s, 2, first], arrived.at[s, 1, first], to_quad[2]))
            elif k:
                sends[s, k] = go(copy(merged.at[s, k], arrived.at[s, k - 1], to_quad[k]))
        if quads == 4:
            sends[s, "3a"].wait_recv()
            add_rows(mine.at[s, 1, first], merged.at[s, 1, first], relay.at[s, 0])
            sends[s, "1a"] = go(copy(mine.at[s, 1, first], arrived.at[s, 0, first], to_quad[1]))
            sends[s, "3b"].wait_recv()
            add_rows(mine.at[s, 2, second], merged.at[s, 2, second], relay.at[s, 1])
            sends[s, "2b"] = go(copy(mine.at[s, 2, second], arrived.at[s, 1, second], to_quad[2]))
    backs = {}
    for s in order:
        if quads == 4:
            for name in ("1b", "2a", "1a", "2b"):
                sends[s, name].wait_recv()
        else:
            for k in range(1, quads):
                sends[s, k].wait_recv()
        parts = [merged.at[s, 0]] + [arrived.at[s, i] for i in range(arrived.shape[1])]
        if s >= count:
            add_rows(summed.at[s - count], *parts)
            backs[s] = go(copy(summed.at[s - count], back.at[s - count], across))
        else:
            if partner:
                backs[s + count].wait_recv()
                parts.append(back.at[s])
            add_rows(out_ref.at[s], *parts)
    for c in finish:
        c.wait_send()


def scatter_rows(own, other, partner, name, cid):
    quads, total, rows, width = own.shape
    count = total // 2 if partner else total
    sems = scatter_sems(quads, total, partner)
    incoming = 2 if quads == 4 else quads - 1
    def buf(*lead):
        return pltpu.VMEM(lead + (rows, width), BF)
    scratch = [buf(total, quads), buf(total, quads), buf(total, quads),
               pltpu.VMEM((total, 2, rows // 2, width), BF), buf(total, incoming)]
    if partner:
        scratch += [buf(count), buf(count)]
    return pl.pallas_call(
        functools.partial(scatter_body, quads, count, partner),
        out_shape=jax.ShapeDtypeStruct((count, rows, width), F32),
        in_specs=[pl.BlockSpec(memory_space=pl.ANY)] * 2,
        out_specs=pl.BlockSpec(memory_space=pltpu.VMEM),
        scratch_shapes=scratch + [
            pltpu.SemaphoreType.DMA((total * quads,)),
            pltpu.SemaphoreType.DMA((sems,)),
            pltpu.SemaphoreType.DMA((sems,)),
        ],
        compiler_params=pltpu.CompilerParams(collective_id=cid, has_side_effects=True, vmem_limit_bytes=60 << 20),
        name=name,
    )(own, other)


def scatter_all(own, other, partner, name, number):
    if own.shape[0] == 4:
        return scatter_rows(own, other, partner, name, number)
    count = own.shape[1] // 2 if partner else own.shape[1]
    return jnp.concatenate(
        [
            scatter_rows(own[:, m::count], other[:, m::count], partner, name, number)
            for m in range(count)
        ]
    )


def on_device(
    tokens,
    cotangent,
    routes,
    lengths,
    block_order,
    w_query,
    w_key,
    w_value,
    w_out,
    w_router,
    w_gate,
    w_up,
    w_down,
    attn_gain,
    mlp_gain,
    query_gain,
    key_gain,
):
    batches, _, rows, width = tokens.shape
    dp_size = lax.axis_size(DP)
    ctx_size = lax.axis_size(CTX)
    quads = lax.axis_size("quad")
    lanes = lax.axis_size("lane")
    slot_len = rows * ctx_size
    block_rows = rows // 2
    head_width = width // ctx_size
    heads = head_width // HEAD
    shard = w_query.shape[0]
    expert_count = w_router.shape[1]
    local_experts = w_gate.shape[0]
    hidden_units = w_gate.shape[2]
    hidden_half = hidden_units // 2
    depth_part = w_gate.shape[1]
    factor = 1.0 / math.sqrt(HEAD)
    pair = lax.axis_index("pair")

    small = jnp.concatenate(
        [attn_gain, mlp_gain, query_gain, key_gain, w_router.reshape(shard * expert_count)]
    )
    small = spread(spread(small, CTX), DP).reshape(dp_size * ctx_size, -1)
    gain_attn = small[:, :shard].reshape(width).astype(F32)
    gain_mlp = small[:, shard : 2 * shard].reshape(width).astype(F32)
    gain_query = small[:, 2 * shard : 3 * shard].reshape(ctx_size, head_width)
    gain_key = small[:, 3 * shard : 4 * shard].reshape(ctx_size, head_width)
    router_w = small[:, 4 * shard :].reshape(width, expert_count)
    here = lax.axis_index(CTX)
    gain_query = lax.dynamic_index_in_dim(gain_query, here, 0, keepdims=False).astype(F32)
    gain_key = lax.dynamic_index_in_dim(gain_key, here, 0, keepdims=False).astype(F32)

    qkv = jnp.stack([w_query, w_key, w_value], axis=1).reshape(shard, 3, ctx_size, head_width)
    qkv = exchange(
        qkv.transpose(2, 0, 1, 3).reshape(ctx_size, shard, 3 * head_width), CTX
    ).reshape(ctx_size * shard, 3 * head_width)
    qkv_w = lax.all_gather(qkv, DP, axis=0, tiled=True)
    out_w = lax.all_gather(w_out, ALL, axis=0, tiled=True)

    def gather_depth(weights):
        halves = jnp.stack([weights[:, :, :hidden_half], weights[:, :, hidden_half:]])
        blocks = exchange(jnp.repeat(halves, lanes, axis=0), DP)
        return blocks.swapaxes(0, 1).reshape(local_experts, width, hidden_half)

    gate_w = gather_depth(w_gate)
    up_w = gather_depth(w_up)
    down_w = gather_lane(w_down).swapaxes(0, 1).reshape(local_experts, hidden_half, width)

    def places_of(device):
        stored = device * rows + jnp.arange(rows, dtype=jnp.int32)
        match_marks = (stored // block_rows)[:, None] == jnp.arange(
            block_order.shape[0], dtype=jnp.int32
        )[None, :]
        first_place = jnp.sum(jnp.where(match_marks, block_order[None, :], 0), axis=1)
        return first_place * block_rows + stored % block_rows

    places = jnp.concatenate(
        [
            places_of((lax.axis_index("quad") ^ k) * 2 + (pair ^ other))
            for other in range(2)
            for k in range(quads)
        ]
    )
    cosine, sine = angles(places, HEAD)
    expert_range = jnp.arange(expert_count, dtype=jnp.int32)

    inputs = tokens[:, 0].astype(F32)
    attn_root = inv_rms(inputs)
    act = gather_rows((inputs * attn_root * gain_attn).astype(BF), False, "gather_act", 0)
    grad_low = cotangent[:, 0]
    g_rows = gather_rows(grad_low, True, "gather_cotangent", 1)
    pre = [
        dot("td,de->te", part.reshape(-1, width), qkv_w).reshape(quads, batches, rows, -1)
        for part in act
    ]
    pre = jnp.stack(pre)

    saved = []
    attended_all = []
    for m in range(batches):
        pre_m = pre[:, :, m].reshape(slot_len, 3 * head_width)
        query_pre = pre_m[:, :head_width]
        key_pre = pre_m[:, head_width : 2 * head_width]
        value = pre_m[:, 2 * head_width :].astype(BF).reshape(slot_len, heads, HEAD)
        squares = jnp.stack(
            [jnp.sum(query_pre * query_pre, axis=1), jnp.sum(key_pre * key_pre, axis=1)]
        ).reshape(2, 2, quads, rows)
        squares = sum_ctx(squares).reshape(2, slot_len, 1)
        query_root = lax.rsqrt(squares[0] / width + EPSILON)
        key_root = lax.rsqrt(squares[1] / width + EPSILON)
        query = rotate(
            (query_pre * query_root * gain_query).reshape(slot_len, heads, HEAD), cosine, sine
        ).astype(BF)
        key = rotate(
            (key_pre * key_root * gain_key).reshape(slot_len, heads, HEAD), cosine, sine
        ).astype(BF)
        allowed = (places[None, :] <= places[:, None]) & (places[None, :] < lengths[m, 0])
        scores = dot("qhd,khd->hqk", query, key) * factor
        scores = jnp.where(allowed[None], scores, MASKED)
        expo = jnp.exp(scores - jnp.max(scores, axis=-1, keepdims=True))
        probs = expo / jnp.sum(expo, axis=-1, keepdims=True)
        probs_low = probs.astype(BF)
        attended = dot("hqk,khd->qhd", probs_low, value).astype(BF)
        attended_all.append(attended.reshape(2, quads, rows, head_width))
        saved.append(
            dict(
                query_pre=query_pre, key_pre=key_pre, query_root=query_root, key_root=key_root,
                query=query, key=key, value=value, probs=probs, probs_low=probs_low,
            )
        )
    attended = exchange(from_relative(jnp.stack(attended_all, axis=2)), CTX)
    attended = attended.transpose(1, 2, 0, 3).reshape(batches, rows, width)
    x_mid = inputs + dot("mtd,de->mte", attended, out_w)
    mlp_root = inv_rms(x_mid)
    mixed_in = (x_mid * mlp_root * gain_mlp).astype(BF)
    router = jax.nn.softmax(dot("mtd,de->mte", mixed_in, router_w), axis=-1)
    routed = jnp.any(routes[:, 0, :, :, None] == expert_range, axis=2).astype(F32)
    gates = (router * routed).transpose(2, 0, 1).reshape(ctx_size, local_experts, batches, rows)
    gates = to_relative(exchange(gates, CTX))
    gates = jnp.concatenate([gates, swap(gates, "half")], axis=3)
    gates = gates.transpose(0, 1, 3, 4, 2).reshape(2, -1, local_experts, 1)
    x_rows = gather_rows(mixed_in, True, "gather_mixed", 2)
    x_rows = [part.reshape(-1, width) for part in x_rows]
    g_rows = [part.reshape(-1, width) for part in g_rows]

    moe_list, d_list, d_gates_list, hid_list, dgate_list, dup_list = [], [], [], [], [], []
    shards = (quads, 2 * batches, rows)
    for x_part, g_part, gate in zip(x_rows, g_rows, (gates[0], gates[1])):
        gate_pre = dot("td,edf->tef", x_part, gate_w)
        up_pre = dot("td,edf->tef", x_part, up_w)
        d_hidden = dot("td,efd->tef", g_part, down_w)
        sigma = jax.nn.sigmoid(gate_pre)
        hidden = gate_pre * sigma * up_pre
        d_gates_list.append(jnp.sum(hidden * d_hidden, axis=2).reshape(shards + (local_experts,)))
        scaled = (hidden * gate).astype(BF)
        d_hidden = d_hidden * gate
        d_gate_pre = (d_hidden * up_pre * sigma * (1.0 + gate_pre * (1.0 - sigma))).astype(BF)
        d_up_pre = (d_hidden * gate_pre * sigma).astype(BF)
        moe_list.append(dot("tef,efd->td", scaled, down_w).astype(BF).reshape(shards + (width,)))
        d_part = dot("tef,edf->td", d_gate_pre, gate_w)
        d_part = (d_part + dot("tef,edf->td", d_up_pre, up_w)).astype(BF)
        d_list.append(d_part.reshape(shards + (width,)))
        hid_list.append(scaled)
        dgate_list.append(d_gate_pre)
        dup_list.append(d_up_pre)
    d_mixed = scatter_all(d_list[0], d_list[1], True, "scatter_mixed", 3)
    d_gates = jnp.stack(d_gates_list).transpose(0, 1, 4, 2, 3)
    d_gates = d_gates[:, :, :, :batches] + swap(d_gates[:, :, :, batches:], "half")
    d_router = exchange(from_relative(d_gates), CTX).reshape(expert_count, batches, rows)
    d_router = d_router.transpose(1, 2, 0) * routed
    d_logits = (
        router * (d_router - jnp.sum(router * d_router, axis=-1, keepdims=True))
    ).astype(BF)
    d_mixed = d_mixed + dot("mte,de->mtd", d_logits, router_w)

    def norm_back_all(values, root, gain, grad):
        d_values, d_gain = norm_back(values, root, gain, grad)
        return d_values, jnp.sum(d_gain, axis=0)

    d_mid, part_mlp_gain = norm_back_all(x_mid, mlp_root, gain_mlp, d_mixed)
    d_mid = d_mid + grad_low.astype(F32)
    d_att_out = d_mid.astype(BF)
    d_attended = dot("mte,de->mtd", d_att_out, out_w).astype(BF)
    d_attended = d_attended.reshape(batches, rows, ctx_size, head_width).transpose(2, 0, 1, 3)
    d_attended = to_relative(exchange(d_attended, CTX))
    part_query_gain = part_key_gain = 0.0
    d_pre_all = []
    for m in range(batches):
        s = saved[m]
        d_att = d_attended[:, :, m].reshape(slot_len, heads, HEAD)
        probs, query, key = s["probs"], s["query"], s["key"]
        d_probs = dot("qhd,khd->hqk", d_att, s["value"])
        inner = jnp.sum(probs * d_probs, axis=-1, keepdims=True)
        d_scores = (probs * (d_probs - inner)).astype(BF)
        d_query = dot("hqk,khd->qhd", d_scores, key) * factor
        d_key = dot("hqk,qhd->khd", d_scores, query) * factor
        d_value = dot("hqk,qhd->khd", s["probs_low"], d_att)
        d_query = rotate_back(d_query, cosine, sine).reshape(slot_len, head_width)
        d_key = rotate_back(d_key, cosine, sine).reshape(slot_len, head_width)
        query_pre, key_pre = s["query_pre"], s["key_pre"]
        query_root, key_root = s["query_root"], s["key_root"]
        inners = jnp.stack(
            [
                jnp.sum(d_query * gain_query * query_pre, axis=1),
                jnp.sum(d_key * gain_key * key_pre, axis=1),
            ]
        ).reshape(2, 2, quads, rows)
        inners = sum_ctx(inners).reshape(2, slot_len, 1) / width
        d_query_pre = query_root * (d_query * gain_query) - query_pre * query_root**3 * inners[0]
        d_key_pre = key_root * (d_key * gain_key) - key_pre * key_root**3 * inners[1]
        part_query_gain = part_query_gain + jnp.sum(d_query * query_pre * query_root, axis=0)
        part_key_gain = part_key_gain + jnp.sum(d_key * key_pre * key_root, axis=0)
        d_pre = jnp.concatenate(
            [
                d_query_pre.astype(BF),
                d_key_pre.astype(BF),
                d_value.reshape(slot_len, head_width).astype(BF),
            ],
            axis=1,
        )
        d_pre_all.append(d_pre.reshape(2, quads, rows, 3 * head_width))
    d_pre = jnp.stack(d_pre_all, axis=2).reshape(2, -1, 3 * head_width)
    d_act = [
        dot("te,de->td", d_pre[i], qkv_w).astype(BF).reshape(quads, batches, rows, width)
        for i in range(2)
    ]
    d_act = scatter_all(d_act[0], d_act[1], False, "scatter_act", 4)
    d_inputs, part_attn_gain = norm_back_all(inputs, attn_root, gain_attn, d_act)
    moe_sum = scatter_all(moe_list[0], moe_list[1], True, "scatter_moe", 5)
    mixed = (x_mid + moe_sum).astype(BF)

    def total(spec, left, right):
        return sum(dot(spec, x, y) for x, y in zip(left, right))

    grad_down = total("tef,td->efd", hid_list, g_rows)
    grad_down = grad_down.reshape(local_experts, lanes, -1, width).swapaxes(0, 1)
    grad_down = scatter_lane(grad_down)

    def scatter_depth(parts):
        grad = total("td,tef->edf", x_rows, parts).astype(BF)
        grad = grad.reshape(local_experts, dp_size, depth_part, hidden_half).swapaxes(0, 1)
        grad = exchange(grad, DP).astype(F32)
        grad = grad.reshape(2, lanes, local_experts, depth_part, hidden_half).sum(axis=1)
        return grad.transpose(1, 2, 0, 3).reshape(local_experts, depth_part, hidden_units)

    grad_gate = scatter_depth(dgate_list)
    grad_up = scatter_depth(dup_list)

    grad_out = dot("mtd,mte->de", attended, d_att_out).astype(BF)
    grad_out = lax.psum_scatter(grad_out, ALL, scatter_dimension=0, tiled=True).astype(F32)
    acts = [part.reshape(-1, width) for part in act]
    grad_qkv = total("td,te->de", acts, d_pre).astype(BF)
    grad_qkv = lax.psum_scatter(grad_qkv, DP, scatter_dimension=0, tiled=True)
    grad_qkv = exchange(grad_qkv.reshape(ctx_size, shard, 3 * head_width), CTX).astype(F32)
    grad_qkv = grad_qkv.reshape(ctx_size, shard, 3, head_width).transpose(2, 1, 0, 3)
    grad_qkv = grad_qkv.reshape(3, shard, width)

    grad_router = dot("mtd,mte->de", mixed_in, d_logits)
    columns = jnp.arange(ctx_size, dtype=jnp.int32)[:, None] == here

    def placed(part):
        return jnp.where(columns, part[None, :], 0.0).reshape(width)

    gains = jnp.stack(
        [part_attn_gain, part_mlp_gain, placed(part_query_gain), placed(part_key_gain)]
    )
    gains = gains.reshape(4, dp_size, ctx_size, shard).transpose(1, 2, 0, 3)
    packed = jnp.concatenate(
        [
            gains.reshape(dp_size, ctx_size, 4 * shard),
            grad_router.reshape(dp_size, ctx_size, shard * expert_count),
        ],
        axis=2,
    )
    packed = reduce_small(packed)
    return (
        mixed[:, None],
        (d_inputs + d_mid)[:, None],
        grad_qkv[0],
        grad_qkv[1],
        grad_qkv[2],
        grad_out,
        packed[4 * shard :].reshape(shard, expert_count),
        grad_gate,
        grad_up,
        grad_down,
        packed[:shard],
        packed[shard : 2 * shard],
        packed[2 * shard : 3 * shard],
        packed[3 * shard : 4 * shard],
    )


def solution(mesh):
    dp_size, ctx_size = mesh.shape["dp"], mesh.shape["ctx"]
    grid = Mesh(mesh.devices.reshape(2, dp_size // 2, ctx_size // 2, 2), ALL)
    rows = P(None, DP, CTX, None)
    dense = P(ALL, None)
    expert = P(CTX, DP, None)
    vector = P(ALL)
    return jax.shard_map(
        on_device,
        mesh=grid,
        in_specs=(rows, rows, rows, P(None, DP), P())
        + (dense,) * 5
        + (expert,) * 3
        + (vector,) * 4,
        out_specs=(rows, rows) + (dense,) * 5 + (expert,) * 3 + (vector,) * 4,
        check_vma=False,
    )
```

time: 1610 us -> 1610 us (level)
  Pallas kernels: 0 us -> 586 us
  waiting for transfers between devices: 525 us -> 311 us
  local copies, waits for them, and re-layouts: 238 us -> 122 us
  other arithmetic: 190 us -> 80.9 us
  starting transfers between devices: 166 us -> 84 us
  matrix products: 431 us -> 380 us
    pallas_call x0 -> x6, Pallas kernels: none -> 586 us  [the longest x3 320 us: gather_rows(): pl.pallas_call(functools.partial(gather_body, quads, count, partner), out...]
    ppermute x46 -> x8, waiting for transfers between devices: 301 us -> 22.6 us  [swap(): return lax.ppermute(values, axis, [(0, 1), (1, 0)])]
    all_to_all x32 -> x13, waiting for transfers between devices: 217 us -> 281 us  [exchange(): return lax.all_to_all(blocks, axes, split_axis=0, concat_axis=0, tiled=True)]
    all_to_all x32 -> x13, starting transfers between devices: 132 us -> 68.9 us  [exchange(): return lax.all_to_all(blocks, axes, split_axis=0, concat_axis=0, tiled=True)]
    convert_element_type x16 -> x2, other arithmetic: 55.7 us -> 2.96 us  [the longest x1 1.68 us: scatter_lane(): other = jnp.where(here == 0, values[1], values[0]).astype(BF)]
    dot_general x52 -> x39, matrix products: 417 us -> 364 us  [dot(): return jnp.einsum(spec, left, right, preferred_element_type=F32)]
    another operation x15 -> x9, other arithmetic: 45 us -> 3.96 us  [the longest x2 2.93 us: gather_depth(): jnp.stack([weights[:, :, :hidden_half], weights[:, :, hidden_half:]])]
    unnamed x367 -> x217, local copies, waits for them, and re-layouts: 72 us -> 33.6 us
  transfers between devices with their start and end apart: 90 -> 33, of which waited for: 43 -> 14; matrix products, arithmetic and copies ran while one was open for 49% -> 26% of each run, Pallas kernels for 0% -> 32%
where the time goes in v2:
time: 1610 us; the launch traced here: 1600 us
  Pallas kernels  586 us (36%)
  matrix products  380 us (24%)
  waiting for transfers between devices  311 us (19%)
  local copies, waits for them, and re-layouts  122 us (8%)
  starting transfers between devices  84 us (5%)
  other arithmetic  80.9 us (5%)
  blocking collectives  17.6 us (1%)
  between operations  16.4 us (1%)
    dot_general x39, matrix products, dot(): return jnp.einsum(spec, left, right, preferred_element_type=F32)  364 us
    pallas_call x3, Pallas kernels, gather_rows(): pl.pallas_call(functools.partial(gather_body, quads, count, partner), out...  320 us
    all_to_all x13, waiting for transfers between devices, exchange(): return lax.all_to_all(blocks, axes, split_axis=0, concat_axis=0, tiled=True)  281 us
    pallas_call x3, Pallas kernels, scatter_rows(): pl.pallas_call(functools.partial(scatter_body, quads, count, partner), ou...  266 us
    all_to_all x13, starting transfers between devices, exchange(): return lax.all_to_all(blocks, axes, split_axis=0, concat_axis=0, tiled=True)  68.9 us
    unnamed x217, local copies, waits for them, and re-layouts  33.6 us
  transfers between devices with their start and end apart: 33, of which 14 were waited for; matrix products, arithmetic and copies ran while one was open for 26% of the time, Pallas kernels for 32%

profile of v2, /device:TPU:0, one launch (start us, length us, event | category | flops | bytes accessed | tf_op | source)
XLA Modules:
  0.0 1597.3 jit_solution(16109639326347341811)
XLA Ops:
  14.3 17.6 %all_to_all.75 = bf16[8,64,768]{2,1,0:T(8,128)(2,1)} all-to-all(bf16[8,64,768]{2,1,0:T(8,128)(2,1)S(1)} %reshape.1104), channel_id=1, replica_groups=mesh['half'=2,'lane'=2,'quad'=4,'pair'=2] {'quad','pair'}, dimensions={0} | all-to-all | bytes 1572864 | tf_op jit(solution)/shard_map/all_to_all | solution.py:66
  52.3 85.3 %all-to-all-done.1 = bf16[4,8,1280]{2,1,0:T(8,128)(2,1)S(1)} async-done(((bf16[4,8,1280]{2,1,0:T(8,128)(2,1)}), bf16[4,8,1280]{2,1,0:T(8,128)(2,1)S(1)}, u32[]{:S(2)}, u32[]{:S(2)}) %all-to-all-start.1) | async-done | bytes 81952 | tf_op jit(solution)/shard_map/all_to_all | solution.py:66
  149.1 200.9 %gather_cotangent.1 = (bf16[4,4,128,2048]{3,2,1,0:T(8,128)(2,1)}, bf16[4,4,128,2048]{3,2,1,0:T(8,128)(2,1)}) custom-call(bf16[2,128,2048]{2,1,0:T(8,128)(2,1)} %bitcast.506), custom_call_target="tpu_custom_call" | custom-call | tf_op jit(solution)/shard_map/gather_cotangent/pallas_call | solution.py:278
  359.8 41.4 %gather_act.1 = (bf16[4,2,128,2048]{3,2,1,0:T(8,128)(2,1)}, bf16[4,2,128,2048]{3,2,1,0:T(8,128)(2,1)}) custom-call(bf16[2,128,2048]{2,1,0:T(8,128)(2,1)} %fusion.32.x_ref), custom_call_target="tpu_custom_call" | custom-call | tf_op jit(solution)/shard_map/gather_act/pallas_call | solution.py:278
  479.6 51.4 %all-to-all-done.5 = bf16[4,2,512,512]{2,3,1,0:T(8,128)(2,1)} async-done(((bf16[4,2,512,512]{2,3,1,0:T(8,128)(2,1)}), bf16[4,2,512,512]{2,3,1,0:T(8,128)(2,1)}, u32[]{:S(2)}, u32[]{:S(2)}) %all-to-all-start.5) | async-done | bytes 4194336 | tf_op jit(solution)/shard_map/all_to_all | solution.py:66
  559.0 77.8 %gather_mixed.1 = (bf16[4,4,128,2048]{3,2,1,0:T(8,128)(2,1)}, bf16[4,4,128,2048]{3,2,1,0:T(8,128)(2,1)}) custom-call(bf16[2,128,2048]{2,1,0:T(8,128)(2,1)} %multiply_convert_fusion.8.x_ref), custom_call_target="tpu_custom_call" | custom-call | tf_op jit(solution)/shard_map/gather_mixed/pallas_call | solution.py:278
  680.6 14.8 fusion.133
  695.6 16.3 %bitcast_convert_fusion.2 = bf16[2048,2048]{1,0:T(8,128)(2,1)} fusion(bf16[2,512,2048]{2,1,0:T(8,128)(2,1)} %bitcast.497, f32[2048,2]{0,1:T(2,128)S(1)} %mul.845, f32[2048,2,512]{0,2,1:T(8,128)} %fusion.134, f32[2048,2,512]{0,2,1:T(8,128)} %fusion.133), kind=kOutput, calls=%fused_computation.9 | convolution fusion | flops 8608808960 | bytes 29376512 | tf_op jit(solution)/shard_map/tef,efd->td/dot_general | solution.py:25
  711.9 21.4 %fusion.6 = (f32[2048,2]{0,1:T(2,128)S(1)}, bf16[2048,2,512]{0,2,1:T(8,128)(2,1)}, bf16[2048,2,512]{0,2,1:T(8,128)(2,1)}) fusion(f32[2048,2,512]{0,2,1:T(8,128)} %fusion.134, f32[2048,2,512]{0,2,1:T(8,128)} %fusion.133, f32[2048,2]{0,1:T(2,128)S(1)} %mul.845, bf16[2,512,2048]{2,1,0:T(8,128)(2,1)S(1)} %bitcast.499, bf16[2048,2048,1]{1,0,2:T(8,128)(2,1)} %bitcast.627), kind=kOutput, calls=%fused_computation.17 | convolution fusion | flops 8627679232 | bytes 37781504 | tf_op jit(solution)/shard_map/td,efd->tef/dot_general | solution.py:25
  733.4 16.3 %bitcast_convert_fusion.1 = bf16[2048,2048]{1,0:T(8,128)(2,1)} fusion(bf16[2,512,2048]{2,1,0:T(8,128)(2,1)} %bitcast.498, f32[2048,2]{0,1:T(2,128)S(1)} %mul.850, f32[2048,2,512]{0,2,1:T(8,128)} %fusion.136, f32[2048,2,512]{0,2,1:T(8,128)} %fusion.135), kind=kOutput, calls=%fused_computation.8 | convolution fusion | flops 8608808960 | bytes 29376512 | tf_op jit(solution)/shard_map/tef,efd->td/dot_general | solution.py:25
  749.7 21.1 %fusion.5 = (f32[2048,2]{0,1:T(2,128)S(1)}, bf16[2048,2,512]{0,2,1:T(8,128)(2,1)}, bf16[2048,2,512]{0,2,1:T(8,128)(2,1)}) fusion(f32[2048,2,512]{0,2,1:T(8,128)} %fusion.136, f32[2048,2,512]{0,2,1:T(8,128)} %fusion.135, f32[2048,2]{0,1:T(2,128)S(1)} %mul.850, bf16[2,512,2048]{2,1,0:T(8,128)(2,1)S(1)} %bitcast.500, bf16[2048,2048,1]{1,0,2:T(8,128)(2,1)} %bitcast.625), kind=kOutput, calls=%fused_computation.14 | convolution fusion | flops 8627679232 | bytes 37781504 | tf_op jit(solution)/shard_map/td,efd->tef/dot_general | solution.py:25
  773.0 15.5 fusion.138
  788.5 15.0 fusion.3
  822.9 16.6 %fusion.4 = bf16[2048,2048]{1,0:T(8,128)(2,1)} fusion(f32[2048,2048,1]{1,0,2:T(8,128)} %fusion.137, bf16[2048,2,512]{0,2,1:T(8,128)(2,1)} %get-tuple-element.171, bf16[2,2048,512]{1,2,0:T(8,128)(2,1)} %bitcast.490), kind=kOutput, calls=%fused_computation.7 | convolution fusion | flops 8598323200 | bytes 33554432 | tf_op jit(solution)/shard_map/tef,edf->td/dot_general | solution.py:25
  839.5 112.5 %scatter_moe.1 = f32[2,128,2048]{2,1,0:T(8,128)} custom-call(bf16[4,4,128,2048]{3,2,1,0:T(8,128)(2,1)} %bitcast.473, bf16[4,4,128,2048]{3,2,1,0:T(8,128)(2,1)} %bitcast.474), custom_call_target="tpu_custom_call" | custom-call | tf_op jit(solution)/shard_map/scatter_moe/pallas_call | solution.py:406
  952.0 112.5 %scatter_mixed.1 = f32[2,128,2048]{2,1,0:T(8,128)} custom-call(bf16[4,4,128,2048]{3,2,1,0:T(8,128)(2,1)} %bitcast.476, bf16[4,4,128,2048]{3,2,1,0:T(8,128)(2,1)} %bitcast.475), custom_call_target="tpu_custom_call" | custom-call | tf_op jit(solution)/shard_map/scatter_mixed/pallas_call | solution.py:406
  1080.6 15.0 all-to-all-done.8
  1199.4 40.7 %scatter_act.1 = f32[2,128,2048]{2,1,0:T(8,128)} custom-call(bf16[4,2,128,2048]{3,2,1,0:T(8,128)(2,1)} %bitcast.502, bf16[4,2,128,2048]{3,2,1,0:T(8,128)(2,1)} %bitcast.501), custom_call_target="tpu_custom_call" | custom-call | tf_op jit(solution)/shard_map/scatter_act/pallas_call | solution.py:406
  1320.2 72.9 %all-to-all-done.13 = bf16[4,2,512,512]{2,3,1,0:T(8,128)(2,1)} async-done(((bf16[4,2,512,512]{2,3,1,0:T(8,128)(2,1)}), bf16[4,2,512,512]{2,3,1,0:T(8,128)(2,1)}, u32[]{:S(2)}, u32[]{:S(2)}) %all-to-all-start.13) | async-done | bytes 4194336 | tf_op jit(solution)/shard_map/all_to_all | solution.py:66
  1393.1 19.5 %all-to-all-start.12 = ((bf16[4,2,512,512]{2,3,1,0:T(8,128)(2,1)}), bf16[4,2,512,512]{2,3,1,0:T(8,128)(2,1)}, u32[]{:S(2)}, u32[]{:S(2)}) async-start(bf16[4,2,512,512]{2,3,1,0:T(8,128)(2,1)} %bitcast.455), calls=%async_computation.14 | async-start | bytes 8388608 | tf_op jit(solution)/shard_map/all_to_all | solution.py:66
  1412.6 17.3 %fusion.54 = f32[2,512,2048]{2,1,0:T(8,128)} fusion(bf16[2048,2048,1]{1,0,2:T(8,128)(2,1)} %bitcast.628, f32[2048,2]{0,1:T(2,128)S(1)} %copy-done.72, f32[2048,2,512]{0,2,1:T(8,128)} %fusion.134, f32[2048,2,512]{0,2,1:T(8,128)} %fusion.133), kind=kOutput, calls=%fused_computation.116 | convolution fusion | flops 8604614656 | bytes 33570816 | tf_op jit(solution)/shard_map/tef,td->efd/dot_general | solution.py:25
  1429.9 18.5 %convolution_add_fusion = f32[2,512,2048]{2,1,0:T(8,128)} fusion(f32[2,512,2048]{2,1,0:T(8,128)} %fusion.54, bf16[2048,2048,1]{1,0,2:T(8,128)(2,1)} %bitcast.626, f32[2048,2]{0,1:T(2,128)S(1)} %copy-done.70, f32[2048,2,512]{0,2,1:T(8,128)} %fusion.136, f32[2048,2,512]{0,2,1:T(8,128)} %fusion.135), kind=kOutput, calls=%fused_computation.71 | convolution fusion | flops 8606711808 | bytes 41959424 | tf_op jit(solution)/shard_map/tef,td->efd/dot_general | solution.py:25
  1463.0 56.4 %all-to-all-done.12 = bf16[4,2,512,512]{2,3,1,0:T(8,128)(2,1)} async-done(((bf16[4,2,512,512]{2,3,1,0:T(8,128)(2,1)}), bf16[4,2,512,512]{2,3,1,0:T(8,128)(2,1)}, u32[]{:S(2)}, u32[]{:S(2)}) %all-to-all-start.12) | async-done | bytes 4194336 | tf_op jit(solution)/shard_map/all_to_all | solution.py:66
  1523.8 21.0 %collective-permute-done.15 = bf16[2,256,2048]{2,1,0:T(8,128)(2,1)} collective-permute-done((bf16[2,256,2048]{2,1,0:T(8,128)(2,1)}, bf16[2,256,2048]{2,1,0:T(8,128)(2,1)}, u32[]{:S(2)}, u32[]{:S(2)}) %collective-permute-start.15) | collective-permute-done | bytes 2097184 | tf_op jit(solution)/shard_map/ppermute | solution.py:62
  (535 shorter events, 483.4 us)
Async XLA Ops:
  7.2 394.0 %all-gather.3.cloned.1.call-start = ((), (), s32[]{:S(2)}) async-start(), calls=%async_computation.16 | async-start | bytes 3932160 | tf_op jit(solution)/shard_map/all_gather | solution.py:487
  37.6 512.6 %all-gather.5.cloned.1.call-start = ((), (), s32[]{:S(2)}) async-start(), calls=%async_computation.17 | async-start | bytes 8650752 | tf_op jit(solution)/shard_map/all_gather | solution.py:488
  37.6 497.0 %collective-permute-start.7 = (bf16[2,256,2048]{2,1,0:T(8,128)(2,1)}, bf16[2,256,2048]{2,1,0:T(8,128)(2,1)}, u32[]{:S(2)}, u32[]{:S(2)}) collective-permute-start(bf16[2,256,2048]{2,1,0:T(8,128)(2,1)} %param.29), channel_id=1, source_target_pairs={{0,8},{8,0},{1,9},{9,1},{2,10},{10,2},{3,11},{11,3},{4,12},{12,4},... | collective-permute-start | bytes 6291464 | tf_op jit(solution)/shard_map/ppermute | solution.py:62
  44.1 93.5 %all-to-all-start.1 = ((bf16[4,8,1280]{2,1,0:T(8,128)(2,1)}), bf16[4,8,1280]{2,1,0:T(8,128)(2,1)S(1)}, u32[]{:S(2)}, u32[]{:S(2)}) async-start(bf16[4,8,1280]{2,1,0:T(8,128)(2,1)} %broadcast_in_dim.196), calls=%async_computation.1 | async-start | bytes 163840 | tf_op jit(solution)/shard_map/all_to_all | solution.py:66
  140.0 289.4 %all-to-all-start.4 = ((bf16[4,2,512,512]{2,3,1,0:T(8,128)(2,1)}), bf16[4,2,512,512]{2,3,1,0:T(8,128)(2,1)}, u32[]{:S(2)}, u32[]{:S(2)}) async-start(bf16[4,2,512,512]{2,3,1,0:T(8,128)(2,1)} %bitcast.453), calls=%async_computation.4 | async-start | bytes 8388608 | tf_op jit(solution)/shard_map/all_to_all | solution.py:66
  418.7 10.6 collective-permute-start.2
  419.5 9.9 collective-permute-start.5
  433.4 97.6 %all-to-all-start.5 = ((bf16[4,2,512,512]{2,3,1,0:T(8,128)(2,1)}), bf16[4,2,512,512]{2,3,1,0:T(8,128)(2,1)}, u32[]{:S(2)}, u32[]{:S(2)}) async-start(bf16[4,2,512,512]{2,3,1,0:T(8,128)(2,1)} %bitcast.454), calls=%async_computation.5 | async-start | bytes 8388608 | tf_op jit(solution)/shard_map/all_to_all | solution.py:66
  530.9 19.1 %all-to-all-start.3 = ((bf16[8,2,128,256]{3,2,1,0:T(8,128)(2,1)}), bf16[8,2,128,256]{3,2,1,0:T(8,128)(2,1)S(1)}, u32[]{:S(2)}, u32[]{:S(2)}) async-start(bf16[8,2,128,256]{3,2,1,0:T(8,128)(2,1)} %bitcast.47), calls=%async_computation.3 | async-start | bytes 2097152 | tf_op jit(solution)/shard_map/all_to_all | solution.py:66
  639.1 40.5 %all-to-all-start.6 = ((f32[8,2,2,128]{3,1,2,0:T(2,128)}), f32[8,2,2,128]{3,1,2,0:T(2,128)S(1)}, u32[]{:S(2)}, u32[]{:S(2)}) async-start(f32[8,2,2,128]{3,1,2,0:T(2,128)} %copy.597), calls=%async_computation.6 | async-start | bytes 32768 | tf_op jit(solution)/shard_map/all_to_all | solution.py:66
  679.7 15.7 collective-permute-start.6
  770.9 46.7 %collective-permute-start.8 = (f32[2,4,2,2,128]{4,0,1,3,2:T(2,128)S(1)}, f32[2,4,2,2,128]{4,0,1,3,2:T(2,128)S(1)}, u32[]{:S(2)}, u32[]{:S(2)}) collective-permute-start(f32[2,4,2,2,128]{4,0,1,3,2:T(2,128)S(1)} %slice.299), channel_id=1, source_target_pairs={{0,16},{16,0},{1,17},{17,1},{2,18},{18,2},{3,19},{19,3},{4,20},{20... | collective-permute-start | bytes 49160 | tf_op jit(solution)/shard_map/ppermute | solution.py:62
  818.3 246.2 %all-to-all-start.7 = ((f32[8,2,2,128]{3,1,2,0:T(2,128)}), f32[8,2,2,128]{3,1,2,0:T(2,128)S(1)}, u32[]{:S(2)}, u32[]{:S(2)}) async-start(f32[8,2,2,128]{3,1,2,0:T(2,128)} %copy.614), calls=%async_computation.7 | async-start | bytes 32768 | tf_op jit(solution)/shard_map/all_to_all | solution.py:66
  1076.7 18.9 %all-to-all-start.8 = ((bf16[8,2,128,256]{3,2,1,0:T(8,128)(2,1)}), bf16[8,2,128,256]{3,2,1,0:T(8,128)(2,1)S(1)}, u32[]{:S(2)}, u32[]{:S(2)}) async-start(bf16[8,2,128,256]{3,2,1,0:T(8,128)(2,1)} %bitcast.421), calls=%async_computation.8 | async-start | bytes 2097152 | tf_op jit(solution)/shard_map/all_to_all | solution.py:66
  1080.3 439.1 %reduce-scatter.3.cloned.1.call-start = ((), (), s32[]{:S(2)}) async-start(), calls=%async_computation.18 | async-start | bytes 3932160 | tf_op jit(solution)/shard_map/reduce_scatter | solution.py:683
  1139.1 11.7 collective-permute-start.11
  1155.3 10.1 collective-permute-start.12
  1243.3 18.1 %all-to-all-start.10 = ((f32[8,4,1280]{2,1,0:T(4,128)}), f32[8,4,1280]{2,1,0:T(4,128)S(1)}, u32[]{:S(2)}, u32[]{:S(2)}) async-start(f32[8,4,1280]{2,1,0:T(4,128)} %copy.648), calls=%async_computation.12 | async-start | bytes 327680 | tf_op jit(solution)/shard_map/all_to_all | solution.py:66
  1262.0 19.5 %all-to-all-start.11 = ((f32[4,1,1280]{2,1,0:T(1,128)}), f32[4,1,1280]{2,1,0:T(1,128)S(1)}, u32[]{:S(2)}, u32[]{:S(2)}) async-start(f32[4,1,1280]{2,1,0:T(1,128)} %all_to_all.57), calls=%async_computation.13 | async-start | bytes 40960 | tf_op jit(solution)/shard_map/all_to_all | solution.py:66
  1281.5 111.5 %all-to-all-start.13 = ((bf16[4,2,512,512]{2,3,1,0:T(8,128)(2,1)}), bf16[4,2,512,512]{2,3,1,0:T(8,128)(2,1)}, u32[]{:S(2)}, u32[]{:S(2)}) async-start(bf16[4,2,512,512]{2,3,1,0:T(8,128)(2,1)} %bitcast.456), calls=%async_computation.15 | async-start | bytes 8388608 | tf_op jit(solution)/shard_map/all_to_all | solution.py:66
  1286.7 302.1 %reduce-scatter.5.cloned.1.call-start = ((), (), s32[]{:S(2)}) async-start(), calls=%async_computation.19 | async-start | bytes 8650752 | tf_op jit(solution)/shard_map/reduce_scatter | solution.py:680
  1393.1 126.3 %all-to-all-start.12 = ((bf16[4,2,512,512]{2,3,1,0:T(8,128)(2,1)}), bf16[4,2,512,512]{2,3,1,0:T(8,128)(2,1)}, u32[]{:S(2)}, u32[]{:S(2)}) async-start(bf16[4,2,512,512]{2,3,1,0:T(8,128)(2,1)} %bitcast.455), calls=%async_computation.14 | async-start | bytes 8388608 | tf_op jit(solution)/shard_map/all_to_all | solution.py:66
  1457.6 87.2 %collective-permute-start.15 = (bf16[2,256,2048]{2,1,0:T(8,128)(2,1)}, bf16[2,256,2048]{2,1,0:T(8,128)(2,1)}, u32[]{:S(2)}, u32[]{:S(2)}) collective-permute-start(bf16[2,256,2048]{2,1,0:T(8,128)(2,1)} %fusion.29), channel_id=1, source_target_pairs={{0,8},{8,0},{1,9},{9,1},{2,10},{10,2},{3,11},{11,3},{4,12},{12,4},... | collective-permute-start | bytes 6291464 | tf_op jit(solution)/shard_map/ppermute | solution.py:62
  1519.4 63.3 %all-to-all-start.9 = ((bf16[8,64,768]{2,1,0:T(8,128)(2,1)}), bf16[8,64,768]{2,1,0:T(8,128)(2,1)S(1)}, u32[]{:S(2)}, u32[]{:S(2)}) async-start(bf16[8,64,768]{2,1,0:T(8,128)(2,1)} %bitcast.519), calls=%async_computation.10 | async-start | bytes 1572864 | tf_op jit(solution)/shard_map/all_to_all | solution.py:66
  (110 other events, 3026.2 us)
Sparse Core Ops, SparseCore 0:
  32.1 104.6 all-gather.2
  139.7 189.1 all-gather.4
  1187.5 57.9 reduce-scatter.2
  1293.8 185.9 reduce-scatter.4

commit v3 on v1

v3 whole, which is shorter than its diff:
```python
import functools
import math

import jax
import jax.numpy as jnp
from jax import lax
from jax.experimental import pallas as pl
from jax.experimental.pallas import tpu as pltpu
from jax.sharding import Mesh
from jax.sharding import PartitionSpec as P

HEAD = 128
EPSILON = 1e-05
ROPE_BASE = 10000.0
MASKED = -1e30
BF = jnp.bfloat16
F32 = jnp.float32
DP = ("half", "lane")
CTX = ("quad", "pair")
ALL = DP + CTX
MESH = pl.DeviceIdType.MESH


def dot(spec, left, right):
    return jnp.einsum(spec, left, right, preferred_element_type=F32)


def inv_rms(values):
    return lax.rsqrt(jnp.mean(values * values, axis=-1, keepdims=True) + EPSILON)


def norm_back(values, inv_root, gain_vec, grad_in):
    weighted = grad_in * gain_vec
    inner = jnp.mean(weighted * values, axis=-1, keepdims=True)
    grad_values = inv_root * weighted - values * (inv_root * inv_root * inv_root) * inner
    return (grad_values, jnp.sum(grad_in * values * inv_root, axis=0))


def angles(places, head_width):
    index = jnp.arange(head_width // 2, dtype=F32)
    freqs = jnp.power(ROPE_BASE, -2.0 * index / head_width)
    turning = places.astype(F32)[:, None] * freqs[None, :]
    turning = jnp.concatenate([turning, turning], axis=1)
    return (jnp.cos(turning)[:, None, :], jnp.sin(turning)[:, None, :])


def rotate(values, cosine, sine):
    half_size = values.shape[-1] // 2
    turned = jnp.concatenate([-values[..., half_size:], values[..., :half_size]], axis=-1)
    return values * cosine + turned * sine


def rotate_back(grad_in, cosine, sine):
    half_size = grad_in.shape[-1] // 2
    moved = grad_in * sine
    return grad_in * cosine + jnp.concatenate(
        [moved[..., half_size:], -moved[..., :half_size]], axis=-1
    )


def swap(values, axis):
    return lax.ppermute(values, axis, [(0, 1), (1, 0)])


def exchange(blocks, axes):
    return lax.all_to_all(blocks, axes, split_axis=0, concat_axis=0, tiled=True)


def lane_parts(values):
    if lax.axis_size("lane") == 2:
        return swap(values, "lane")
    return lax.all_gather(values, "lane", axis=0, tiled=False)


def gather_lane(values, parts):
    if lax.axis_size("lane") == 2:
        first = lax.axis_index("lane") == 0
        return jnp.stack([jnp.where(first, values, parts), jnp.where(first, parts, values)])
    return parts


def reduce_small(values):
    return jnp.sum(exchange_rows(values, "all", "small_gradients", 15), axis=(0, 1))


def toggled(index, bits):
    step = 1
    while step <= bits:
        if bits & step:
            index = index + step - 2 * step * ((index // step) % 2)
        step *= 2
    return index


def greet(peers):
    barrier = pltpu.get_barrier_semaphore()
    for peer in peers:
        pl.semaphore_signal(barrier, inc=1, device_id=peer, device_id_type=MESH)
    pl.semaphore_wait(barrier, len(peers))


class Mover:
    def __init__(self, send, recv, local):
        self.send, self.recv, self.local = send, recv, local
        self.number, self.local_number = 0, 0
        self.sent, self.kept = [], []

    def copy(self, src, dst, device):
        i = self.number
        self.number += 1
        return pltpu.make_async_remote_copy(
            src_ref=src, dst_ref=dst, send_sem=self.send.at[i], recv_sem=self.recv.at[i],
            device_id=device, device_id_type=MESH,
        )

    def go(self, *copies):
        for c in copies:
            c.start()
            self.sent.append(c)

    def keep(self, src, dst):
        c = pltpu.make_async_copy(src, dst, self.local.at[self.local_number])
        self.local_number += 1
        c.start()
        self.kept.append(c)
        return c

    def finish(self):
        for c in self.sent:
            c.wait_send()
        for c in self.kept:
            c.wait()


class Spread:
    def __init__(self, mover, quads, src, slot):
        self.mover, self.quads = mover, quads
        quad = lax.axis_index("quad")
        to_quad = [{"quad": toggled(quad, k)} for k in range(quads)]
        sibling = {"pair": 1 - lax.axis_index("pair")}
        rows = src.shape[0]
        halves = (("a", pl.ds(0, rows // 2)), ("b", pl.ds(rows // 2, rows // 2)))
        p = {"o0": mover.copy(src, slot(1, 0, 0), sibling)}
        if quads == 4:
            for k in (1, 2):
                for name, part in halves:
                    p[f"s{k}{name}"] = mover.copy(
                        src.at[part], slot(0, k, 0).at[part], to_quad[k]
                    )
            for k, (name, part) in zip((1, 2), halves):
                p[f"f3{name}"] = mover.copy(
                    slot(0, k, k).at[part], slot(0, 3, k).at[part], to_quad[3 - k]
                )
            for k in (1, 2, 3):
                for name, part in halves:
                    p[f"o{k}{name}"] = mover.copy(
                        slot(0, k, k).at[part], slot(1, k, k).at[part], sibling
                    )
        else:
            for k in range(1, quads):
                p[f"s{k}"] = mover.copy(src, slot(0, k, 0), to_quad[k])
                p[f"o{k}"] = mover.copy(slot(0, k, k), slot(1, k, k), sibling)
        self.copies = p

    @staticmethod
    def count(quads):
        return 13 if quads == 4 else 2 * quads - 1

    def begin(self):
        names = [f"s{k}" for k in range(1, self.quads)]
        if self.quads == 4:
            names = ["s1a", "s2b", "s1b", "s2a"]
        self.mover.go(*[self.copies[name] for name in names + ["o0"]])

    def forward(self):
        p = self.copies
        steps = [(f"s{k}", (f"o{k}",)) for k in range(1, self.quads)]
        if self.quads == 4:
            steps = [
                ("s1a", ("f3a", "o1a")), ("s2b", ("f3b", "o2b")), ("s1b", ("o1b",)),
                ("s2a", ("o2a",)), ("f3a", ("o3a",)), ("f3b", ("o3b",)),
            ]
        for name, then in steps:
            p[name].wait_recv()
            self.mover.go(*[p[t] for t in then])

    def arrive(self):
        for name, c in self.copies.items():
            if name[0] == "o":
                c.wait_recv()


def relative_slots(own_ref, other_ref, s):
    return lambda core, kr, km: (other_ref if core else own_ref).at[kr, s]


def ctx_peers(quads):
    return [ctx_at(quads, n)[0] for n in range(1, 2 * quads)]


def planes_of(lanes):
    half, lane = lax.axis_index("half"), lax.axis_index("lane")
    result = []
    for n in range(1, 2 * lanes):
        h, l = toggled(half, n // lanes), toggled(lane, n % lanes)
        result.append(({"half": h, "lane": l}, h * lanes + l))
    return half * lanes + lane, result


def gather_body(quads, lanes, partners, *refs):
    inputs = refs[: len(partners)]
    blocks_ref = refs[len(partners)]
    refs = refs[len(partners) + 1 :]
    outputs = [(refs[2 * i], refs[2 * i + 1]) for i in range(len(partners))]
    blocks_out, held = refs[2 * len(partners) : 2 * len(partners) + 2]
    refs = refs[2 * len(partners) + 2 :]
    keeps = {}
    for i, partner in enumerate(partners):
        if partner:
            keeps[i], refs = refs[0], refs[1:]
    local, send, recv = refs
    mover = Mover(send, recv, local)
    across = {"half": 1 - lax.axis_index("half")}
    quad = lax.axis_index("quad")
    peers = [{"quad": toggled(quad, k)} for k in range(1, quads)]
    peers.append({"pair": 1 - lax.axis_index("pair")})
    me, planes = planes_of(lanes)
    greet(peers + [device for device, _ in planes])

    def add(sources, i, offset):
        plans = []
        for s, src in enumerate(sources):
            p = Spread(mover, quads, src, relative_slots(*outputs[i], offset + s))
            p.begin()
            plans.append(p)
            mover.keep(src, outputs[i][0].at[0, offset + s])
        return plans

    crossing = {}
    for i, keep in keeps.items():
        crossing[i] = [
            mover.copy(inputs[i].at[s], keep.at[s], across) for s in range(inputs[i].shape[0])
        ]
        mover.go(*crossing[i])
    plans = []
    for i, ref in enumerate(inputs):
        plans += add([ref.at[s] for s in range(ref.shape[0])], i, 0)
    blocks = [
        mover.copy(blocks_ref.at[place // lanes], blocks_out.at[me], device)
        for device, place in planes
    ]
    mover.go(*blocks)
    into = mover.keep(blocks_ref.at[me // lanes], held)
    plans[0].forward()
    into.wait()
    mover.kept = [c for c in mover.kept if c is not into]
    mover.keep(held, blocks_out.at[me])
    for p in plans[1:]:
        p.forward()
    late = []
    for i, keep in keeps.items():
        for c in crossing[i]:
            c.wait_recv()
        late += add([keep.at[s] for s in range(keep.shape[0])], i, keep.shape[0])
    for p in late:
        p.forward()
    for p in plans + late:
        p.arrive()
    for c in blocks:
        c.wait_recv()
    mover.finish()


def gather_rows(sources, partners, blocks, name, number):
    quads, lanes = lax.axis_size("quad"), lax.axis_size("lane")
    shapes, keeps = [], []
    sems = total = 0
    for x, partner in zip(sources, partners):
        count = x.shape[0] * (2 if partner else 1)
        total += count
        sems += count * Spread.count(quads) + (x.shape[0] if partner else 0)
        shapes += [jax.ShapeDtypeStruct((quads, count) + x.shape[1:], x.dtype)] * 2
        if partner:
            keeps.append(pltpu.VMEM(x.shape, x.dtype))
    shapes.append(jax.ShapeDtypeStruct((2 * lanes,) + blocks.shape[1:], blocks.dtype))
    sems += 2 * lanes - 1
    out = pl.pallas_call(
        functools.partial(gather_body, quads, lanes, partners),
        out_shape=shapes,
        in_specs=[pl.BlockSpec(memory_space=pltpu.VMEM)] * len(sources)
        + [pl.BlockSpec(memory_space=pl.ANY)],
        out_specs=[pl.BlockSpec(memory_space=pl.ANY)] * len(shapes),
        scratch_shapes=[pltpu.VMEM(blocks.shape[1:], blocks.dtype)]
        + keeps
        + [
            pltpu.SemaphoreType.DMA((total + 2,)),
            pltpu.SemaphoreType.DMA((sems,)),
            pltpu.SemaphoreType.DMA((sems,)),
        ],
        compiler_params=pltpu.CompilerParams(collective_id=number, has_side_effects=True),
        name=name,
    )(*sources, blocks)
    return [(out[2 * i], out[2 * i + 1]) for i in range(len(sources))], out[-1]


def start_body(
    quads, lanes, tok_ref, qkv_ref, small_ref, wout_ref,
    tok_own, tok_other, qkv_out, small_out, wout_out, local, send, recv,
):
    mover = Mover(send, recv, local)
    half, lane = lax.axis_index("half"), lax.axis_index("lane")
    plane, here = half * lanes + lane, ctx_place()
    partner = (1 - half) * lanes + lane
    across = {"half": 1 - half}
    devices = 4 * lanes * quads
    others = [all_at(lanes, quads, n)[0] for n in range(1, devices)]
    greet(others)
    mine = mover.keep(small_ref, small_out.at[plane * 2 * quads + here])
    shared = [mover.copy(small_ref, small_out.at[plane * 2 * quads + here], d) for d in others]
    mover.go(*shared)

    def planes(src, view):
        first = mover.copy(src, view(plane), across)
        rest = [
            mover.copy(src, view(plane), {"lane": toggled(lane, d)}) for d in range(1, lanes)
        ]
        then = [
            mover.copy(view(partner), view(partner), {"lane": toggled(lane, d)})
            for d in range(1, lanes)
        ]
        mover.go(first, *rest)
        return first, rest, then

    mover.keep(wout_ref, wout_out.at[plane, here])
    w_first, w_rest, w_then = planes(wout_ref, lambda p: wout_out.at[p, here])
    kept = mover.keep(qkv_ref.at[here], qkv_out.at[plane, here])
    columns = []
    for n in range(1, 2 * quads):
        device, place = ctx_at(quads, n)
        columns.append(mover.copy(qkv_ref.at[place], qkv_out.at[plane, here], device))
    mover.go(*columns)
    tokens = []
    for s in range(tok_ref.shape[0]):
        p = Spread(mover, quads, tok_ref.at[s], relative_slots(tok_own, tok_other, s))
        p.begin()
        tokens.append(p)
        mover.keep(tok_ref.at[s], tok_own.at[0, s])
    for c in columns:
        c.wait_recv()
    kept.wait()
    mover.kept = [c for c in mover.kept if c is not kept]
    q_first, q_rest, q_then = planes(qkv_out.at[plane], lambda p: qkv_out.at[p])
    w_first.wait_recv()
    mover.go(*w_then)

    def wout_slots(p):
        pair = lax.axis_index("pair")
        quad = lax.axis_index("quad")
        return lambda core, kr, km: wout_out.at[p, toggled(quad, km) * 2 + pair]

    weights = [Spread(mover, quads, wout_ref, wout_slots(plane))]
    weights[0].begin()
    tokens[0].forward()
    for c in w_rest:
        c.wait_recv()
    for c in w_then:
        c.wait_recv()
    for n in range(1, 2 * lanes):
        p = toggled(half, n // lanes) * lanes + toggled(lane, n % lanes)
        weights.append(Spread(mover, quads, wout_out.at[p, here], wout_slots(p)))
        weights[-1].begin()
    q_first.wait_recv()
    mover.go(*q_then)
    for p in tokens[1:] + weights:
        p.forward()
    for p in tokens + weights:
        p.arrive()
    for c in shared + q_rest + q_then:
        c.wait_recv()
    mover.finish()


def start_gather(tokens, qkv, small, w_out):
    quads, lanes = lax.axis_size("quad"), lax.axis_size("lane")
    count = tokens.shape[0]
    planes, devices = 2 * lanes, 4 * lanes * quads

    def like(lead, x, dtype=BF):
        return jax.ShapeDtypeStruct(lead + x.shape, dtype)

    sems = (devices - 1) + 2 * (2 * lanes - 1) + (2 * quads - 1)
    sems += Spread.count(quads) * (count + planes)
    return pl.pallas_call(
        functools.partial(start_body, quads, lanes),
        out_shape=[like((quads,), tokens)] * 2
        + [like((planes,), qkv), like((devices,), small)]
        + [like((planes, 2 * quads), w_out)],
        in_specs=[pl.BlockSpec(memory_space=pltpu.VMEM)] * 4,
        out_specs=[pl.BlockSpec(memory_space=pl.ANY)] * 5,
        scratch_shapes=[
            pltpu.SemaphoreType.DMA((3 + count,)),
            pltpu.SemaphoreType.DMA((sems,)),
            pltpu.SemaphoreType.DMA((sems,)),
        ],
        compiler_params=pltpu.CompilerParams(collective_id=0, has_side_effects=True),
        name="start_gather",
    )(tokens, qkv, small, w_out)


def add_rows(out_ref, *refs):
    rows = out_ref.shape[0]
    step = 16

    @pl.loop(0, rows // step)
    def _(i):
        part = pl.ds(pl.multiple_of(i * step, step), step)
        total = refs[0][part].astype(F32)
        for ref in refs[1:]:
            total = total + ref[part].astype(F32)
        out_ref[part] = total.astype(out_ref.dtype)


def scatter_body(quads, lanes, kinds, count, partner, extra, *refs):
    inputs = [(refs[2 * i], refs[2 * i + 1]) for i in range(kinds)]
    refs = refs[2 * kinds :]
    if extra:
        blocks_ref, down_ref, *refs = refs
    outputs, refs = refs[:kinds], refs[kinds:]
    if extra:
        blocks_out, down_out, held, *refs = refs
    mine, theirs, relay, arrived, *rest = refs
    if partner:
        summed, back, *rest = rest
    local, send, recv = rest
    mover = Mover(send, recv, local)
    mover.local_number = local.shape[0] - 2
    total, rows = inputs[0][0].shape[1:3]
    first, second = pl.ds(0, rows // 2), pl.ds(rows // 2, rows // 2)
    quad = lax.axis_index("quad")
    to_quad = [{"quad": toggled(quad, k)} for k in range(quads)]
    sibling = {"pair": 1 - lax.axis_index("pair")}
    across = {"half": 1 - lax.axis_index("half")}
    peers = to_quad[1:] + [sibling]
    if extra:
        me, planes = planes_of(lanes)
        peers += [device for device, _ in planes]
    elif partner:
        peers.append(across)
    greet(peers)

    def go(src, dst, device):
        c = mover.copy(src, dst, device)
        mover.go(c)
        return c

    order = [(i, s) for i in range(kinds) for s in range(count, total)]
    order += [(i, s) for i in range(kinds) for s in range(count)]
    ks = [3, 1, 2, 0] if quads == 4 else list(range(quads - 1, -1, -1))
    sib, loc = {}, {}
    for n, (i, s) in enumerate(order):
        for k in ks:
            sib[n, k] = go(inputs[i][1].at[k, s], theirs.at[n, k], sibling)
            loc[n, k] = pltpu.make_async_copy(
                inputs[i][0].at[k, s], mine.at[n, k], local.at[n * quads + k]
            )
            loc[n, k].start()
    sends = {}

    def merge(n):
        for k in ks:
            sib[n, k].wait_recv()
            loc[n, k].wait()
            add_rows(mine.at[n, k], mine.at[n, k], theirs.at[n, k])
            if quads == 4:
                if k == 3:
                    sends[n, "3a"] = go(mine.at[n, 3, first], relay.at[n, 0], to_quad[2])
                    sends[n, "3b"] = go(mine.at[n, 3, second], relay.at[n, 1], to_quad[1])
                elif k == 1:
                    sends[n, "1b"] = go(mine.at[n, 1, second], arrived.at[n, 0, second], to_quad[1])
                elif k == 2:
                    sends[n, "2a"] = go(mine.at[n, 2, first], arrived.at[n, 1, first], to_quad[2])
            elif k:
                sends[n, k] = go(mine.at[n, k], arrived.at[n, k - 1], to_quad[k])

    def pass_on(n):
        if quads == 4:
            sends[n, "3a"].wait_recv()
            add_rows(mine.at[n, 1, first], mine.at[n, 1, first], relay.at[n, 0])
            sends[n, "1a"] = go(mine.at[n, 1, first], arrived.at[n, 0, first], to_quad[1])
            sends[n, "3b"].wait_recv()
            add_rows(mine.at[n, 2, second], mine.at[n, 2, second], relay.at[n, 1])
            sends[n, "2b"] = go(mine.at[n, 2, second], arrived.at[n, 1, second], to_quad[2])

    backs = {}

    def total_of(n):
        i, s = order[n]
        for name in ("1b", "2a", "1a", "2b") if quads == 4 else range(1, quads):
            sends[n, name].wait_recv()
        parts = [mine.at[n, 0]] + [arrived.at[n, j] for j in range(arrived.shape[1])]
        if s >= count:
            slot = i * count + s - count
            add_rows(summed.at[slot], *parts)
            backs[slot] = go(summed.at[slot], back.at[slot], across)
        else:
            if partner:
                backs[i * count + s].wait_recv()
                parts.append(back.at[i * count + s])
            add_rows(outputs[i].at[s], *parts)

    ahead = 2
    exchanged = []

    def exchange_grads():
        lane = lax.axis_index("lane")
        part = down_ref.shape[1] // lanes
        for e in range(down_ref.shape[0]):
            for d in range(1, lanes):
                to = toggled(lane, d)
                src = down_ref.at[e, pl.ds(pl.multiple_of(to * part, part), part)]
                exchanged.append(go(src, down_out.at[d - 1, e], {"lane": to}))
        for device, place in planes:
            exchanged.append(go(blocks_ref.at[place], blocks_out.at[me], device))

    if extra:
        into = mover.keep(blocks_ref.at[me], held)
    for n in range(len(order) + 2 * ahead):
        if extra and n == kinds * count + 2 * ahead:
            exchange_grads()
            into.wait()
            mover.kept = [c for c in mover.kept if c is not into]
            mover.keep(held, blocks_out.at[me])
        if n < len(order):
            merge(n)
        if 0 <= n - 1 < len(order):
            pass_on(n - 1)
        if 0 <= n - 2 * ahead < len(order):
            total_of(n - 2 * ahead)
    for c in exchanged:
        c.wait_recv()
    mover.finish()


def scatter_rows(pairs, partner, name, number, extra=()):
    lanes = lax.axis_size("lane")
    quads, total, rows, width = pairs[0][0].shape
    count = total // 2 if partner else total
    kinds = len(pairs)
    shards = kinds * total
    incoming = 2 if quads == 4 else quads - 1
    sems = shards * (quads + (6 if quads == 4 else quads - 1)) + (kinds * count if partner else 0)

    def buf(*lead):
        return pltpu.VMEM(lead + (rows, width), BF)

    scratch = [buf(shards, quads), buf(shards, quads)]
    scratch += [pltpu.VMEM((shards, 2, rows // 2, width), BF), buf(shards, incoming)]
    if partner:
        scratch += [buf(kinds * count), buf(kinds * count)]
    shapes = [jax.ShapeDtypeStruct((count, rows, width), F32)] * kinds
    specs = [pl.BlockSpec(memory_space=pltpu.VMEM)] * kinds
    anywhere = pl.BlockSpec(memory_space=pl.ANY)
    if extra:
        blocks, down = extra
        n_exp, hidden = down.shape[:2]
        shapes = shapes + [
            jax.ShapeDtypeStruct(blocks.shape, BF),
            jax.ShapeDtypeStruct((lanes - 1, n_exp, hidden // lanes, width), BF),
        ]
        specs = specs + [anywhere] * 2
        scratch = [pltpu.VMEM(blocks.shape[1:], BF)] + scratch
        sems += 2 * lanes - 1 + n_exp * (lanes - 1)
    return pl.pallas_call(
        functools.partial(scatter_body, quads, lanes, kinds, count, partner, bool(extra)),
        out_shape=shapes,
        in_specs=[anywhere] * (2 * kinds + len(extra)),
        out_specs=specs,
        scratch_shapes=scratch
        + [
            pltpu.SemaphoreType.DMA((shards * quads + 2,)),
            pltpu.SemaphoreType.DMA((sems,)),
            pltpu.SemaphoreType.DMA((sems,)),
        ],
        compiler_params=pltpu.CompilerParams(
            collective_id=number, has_side_effects=True, vmem_limit_bytes=60 << 20
        ),
        name=name,
    )(*[ref for pair in pairs for ref in pair], *extra)


def ctx_place():
    return lax.axis_index("quad") * 2 + lax.axis_index("pair")


def ctx_at(quads, number):
    core, distance = number // quads, number % quads
    quad = toggled(lax.axis_index("quad"), distance)
    pair = toggled(lax.axis_index("pair"), core)
    return {"quad": quad, "pair": pair}, quad * 2 + pair


def all_at(lanes, quads, number):
    half = toggled(lax.axis_index("half"), number // (lanes * 2 * quads))
    lane = toggled(lax.axis_index("lane"), number // (2 * quads) % lanes)
    device, place = ctx_at(quads, number % (2 * quads))
    return {"half": half, "lane": lane, **device}, (half * lanes + lane) * 2 * quads + place


def exchange_body(mode, lanes, quads, halves, x_ref, out_ref, local, send, recv):
    copies = []
    peers = []
    if mode in ("shared", "all"):
        me = (lax.axis_index("half") * lanes + lax.axis_index("lane")) * 2 * quads + ctx_place()
        for n in range(2 * lanes * 2 * quads):
            device, place = all_at(lanes, quads, n)
            copies.append((x_ref if mode == "shared" else x_ref.at[place], out_ref.at[me], device))
    else:
        for h in range(halves):
            for n in range(2 * quads):
                device, place = ctx_at(quads, n)
                if halves == 2:
                    device = {"half": toggled(lax.axis_index("half"), h), **device}
                if mode == "inward":
                    pair = (x_ref.at[h, n], out_ref.at[h, ctx_place()])
                elif mode == "outward":
                    pair = (x_ref.at[place], out_ref.at[h, n])
                else:
                    pair = (x_ref.at[place], out_ref.at[ctx_place()])
                copies.append(pair + (device,))
    own = pltpu.make_async_copy(copies[0][0], copies[0][1], local)
    own.start()
    greet([device for _, _, device in copies[1:]])
    started = []
    for i, (src, dst, device) in enumerate(copies[1:]):
        c = pltpu.make_async_remote_copy(
            src_ref=src, dst_ref=dst, send_sem=send.at[i], recv_sem=recv.at[i],
            device_id=device, device_id_type=MESH,
        )
        c.start()
        started.append(c)
    own.wait()
    for c in started:
        c.wait_recv()
    for c in started:
        c.wait_send()


def exchange_rows(x, mode, name, number, halves=1):
    quads, lanes = lax.axis_size("quad"), lax.axis_size("lane")
    count = halves * 2 * quads - 1
    shape = x.shape
    if mode == "outward":
        shape = (halves, 2 * quads) + x.shape[1:]
    elif mode in ("shared", "all"):
        count = 4 * lanes * quads - 1
        if mode == "shared":
            shape = (count + 1,) + x.shape
    return pl.pallas_call(
        functools.partial(exchange_body, mode, lanes, quads, halves),
        out_shape=jax.ShapeDtypeStruct(shape, x.dtype),
        in_specs=[pl.BlockSpec(memory_space=pltpu.VMEM)],
        out_specs=pl.BlockSpec(memory_space=pltpu.VMEM),
        scratch_shapes=[
            pltpu.SemaphoreType.DMA,
            pltpu.SemaphoreType.DMA((count,)),
            pltpu.SemaphoreType.DMA((count,)),
        ],
        compiler_params=pltpu.CompilerParams(collective_id=number, has_side_effects=True),
        name=name,
    )(x)


def sum_body(quads, x_ref, out_ref, landed, send, recv):
    count = 2 * quads
    greet([ctx_at(quads, n)[0] for n in range(1, count)])
    started = []
    for n in range(1, count):
        c = pltpu.make_async_remote_copy(
            src_ref=x_ref, dst_ref=landed.at[n - 1], send_sem=send.at[n - 1],
            recv_sem=recv.at[n - 1], device_id=ctx_at(quads, n)[0], device_id_type=MESH,
        )
        c.start()
        started.append(c)
    for c in started:
        c.wait_recv()
    for j in range(count):
        total = x_ref[j]
        for n in range(1, count):
            total = total + landed[n - 1, j ^ n]
        out_ref[j] = total
    for c in started:
        c.wait_send()


def sum_ctx(x, name, number):
    quads = lax.axis_size("quad")
    count = 2 * quads - 1
    return pl.pallas_call(
        functools.partial(sum_body, quads),
        out_shape=jax.ShapeDtypeStruct(x.shape, x.dtype),
        in_specs=[pl.BlockSpec(memory_space=pltpu.VMEM)],
        out_specs=pl.BlockSpec(memory_space=pltpu.VMEM),
        scratch_shapes=[
            pltpu.VMEM((count,) + x.shape, x.dtype),
            pltpu.SemaphoreType.DMA((count,)),
            pltpu.SemaphoreType.DMA((count,)),
        ],
        compiler_params=pltpu.CompilerParams(collective_id=number, has_side_effects=True),
        name=name,
    )(x)


def nn(left, right):
    return lax.dot_general(left, right, (((1,), (0,)), ((), ())), preferred_element_type=F32)


def nt(left, right):
    return lax.dot_general(left, right, (((1,), (1,)), ((), ())), preferred_element_type=F32)


def tn(left, right):
    return lax.dot_general(left, right, (((0,), (0,)), ((), ())), preferred_element_type=F32)


def expert_body(quads, before, gate_ref, xo_ref, xt_ref, goo_ref, got_ref, gpo_ref, gpt_ref, both_ref,
                down_ref, *refs):
    sums = refs[:4] if before else None
    mo_ref, mt_ref, do_ref, dt_ref, dgate_ref, hid_ref, dg_ref, du_ref = refs[-8:]
    t = pl.program_id(0)
    core_other = t >= 2 * quads
    partner = t % 2 == 1
    hidden, width = down_ref.shape
    x = jnp.where(core_other, xt_ref[0], xo_ref[0]).reshape(-1, width)
    g_own = jnp.where(partner, gpo_ref[0], goo_ref[0])
    g_other = jnp.where(partner, gpt_ref[0], got_ref[0])
    g = jnp.where(core_other, g_other, g_own).reshape(-1, width)
    gate = gate_ref[0]
    wg = both_ref[:, 0].reshape(width, hidden)
    wu = both_ref[:, 1].reshape(width, hidden)
    wd = down_ref[...]
    gate_pre = nn(x, wg)
    up_pre = nn(x, wu)
    d_hidden = nt(g, wd)
    sigma = 1.0 / (1.0 + jnp.exp(-gate_pre))
    silu = gate_pre * sigma
    hid = silu * up_pre
    dgate_ref[0] = jnp.sum(hid * d_hidden, axis=1, keepdims=True)
    d_hidden = d_hidden * gate
    scaled = (hid * gate).astype(BF)
    d_gate_pre = (d_hidden * up_pre * (sigma + silu * (1.0 - sigma))).astype(BF)
    d_up_pre = (d_hidden * silu).astype(BF)
    hid_ref[0] = scaled
    dg_ref[0] = d_gate_pre
    du_ref[0] = d_up_pre
    moe = nn(scaled, wd).reshape(mo_ref.shape[1:])
    d_rows = (nt(d_gate_pre, wg) + nt(d_up_pre, wu)).reshape(mo_ref.shape[1:])
    if before:
        moe = moe + jnp.where(core_other, sums[1][0], sums[0][0]).astype(F32)
        d_rows = d_rows + jnp.where(core_other, sums[3][0], sums[2][0]).astype(F32)
    moe, d_rows = moe.astype(BF), d_rows.astype(BF)

    @pl.when(jnp.logical_not(core_other))
    def _():
        mo_ref[0] = moe
        do_ref[0] = d_rows

    @pl.when(core_other)
    def _():
        mt_ref[0] = moe
        dt_ref[0] = d_rows


def expert(gates, x_rows, g_rows, both, down, before, name):
    quads, shards, rows, width = x_rows[0].shape
    batches = shards // 2
    hidden = down.shape[0]
    tiles = 4 * quads
    tile = batches * rows

    def own(t):
        return (jnp.minimum(t, 2 * quads - 1) // 2, jnp.minimum(t, 2 * quads - 1) % 2, 0, 0)

    def other(t):
        u = jnp.maximum(t - 2 * quads, 0)
        return (u // 2, u % 2, 0, 0)

    def own_g(t):
        return (jnp.minimum(t // 2, quads - 1), 0, 0, 0)

    def other_g(t):
        return (jnp.maximum(t // 2 - quads, 0), 0, 0, 0)

    shard_block = (1, batches, rows, width)
    saved_spec = pl.BlockSpec((1, tile, hidden), lambda t: (t, 0, 0))
    saved = jax.ShapeDtypeStruct((tiles, tile, hidden), BF)
    rows_shape = jax.ShapeDtypeStruct(x_rows[0].shape, BF)
    fixed = dict(pipeline_mode=pl.Buffered(1))
    sums_specs = [
        pl.BlockSpec(shard_block, own), pl.BlockSpec(shard_block, other),
        pl.BlockSpec(shard_block, own), pl.BlockSpec(shard_block, other),
    ]
    return pl.pallas_call(
        functools.partial(expert_body, quads, bool(before)),
        out_shape=(rows_shape,) * 4
        + (jax.ShapeDtypeStruct((tiles, tile, 1), F32), saved, saved, saved),
        grid_spec=pl.GridSpec(
            grid=(tiles,),
            in_specs=[
                pl.BlockSpec((1, tile, 1), lambda t: (t, 0, 0)),
                pl.BlockSpec(shard_block, own),
                pl.BlockSpec(shard_block, other),
                pl.BlockSpec(shard_block, own_g), pl.BlockSpec(shard_block, other_g),
                pl.BlockSpec(shard_block, own_g), pl.BlockSpec(shard_block, other_g),
                pl.BlockSpec(both.shape, lambda t: (0, 0, 0, 0), **fixed),
                pl.BlockSpec(down.shape, lambda t: (0, 0), **fixed),
            ]
            + (sums_specs if before else []),
            out_specs=sums_specs
            + [pl.BlockSpec((1, tile, 1), lambda t: (t, 0, 0)), saved_spec, saved_spec, saved_spec],
        ),
        input_output_aliases={9 + i: i for i in range(4)} if before else {},
        compiler_params=pltpu.CompilerParams(
            dimension_semantics=("arbitrary",), vmem_limit_bytes=60 << 20
        ),
        name=name,
    )(gates, *x_rows, *g_rows, both, down, *before)


def grads_body(quads, xo_ref, xt_ref, goo_ref, got_ref, gpo_ref, gpt_ref, hid_ref, dg_ref, du_ref, both_ref, down_ref,
               gate_acc, up_acc, down_acc):
    t = pl.program_id(0)
    width = down_acc.shape[1]
    hidden = down_acc.shape[0]

    @pl.when(t == 0)
    def _():
        gate_acc[...] = jnp.zeros_like(gate_acc)
        up_acc[...] = jnp.zeros_like(up_acc)
        down_acc[...] = jnp.zeros_like(down_acc)

    x = jnp.where(t >= quads, xt_ref[0], xo_ref[0]).reshape(-1, width)
    g_own = jnp.where(t >= quads, got_ref[0], goo_ref[0]).reshape(-1, width)
    g_partner = jnp.where(t >= quads, gpt_ref[0], gpo_ref[0]).reshape(-1, width)
    g = jnp.concatenate([g_own, g_partner], axis=0)
    gate_acc[...] += tn(x, dg_ref[...].reshape(-1, hidden))
    up_acc[...] += tn(x, du_ref[...].reshape(-1, hidden))
    down_acc[...] += tn(hid_ref[...].reshape(-1, hidden), g)

    @pl.when(t == pl.num_programs(0) - 1)
    def _():
        part = both_ref.shape[0]
        both_ref[:, 0] = gate_acc[...].astype(BF).reshape(part, -1, hidden)
        both_ref[:, 1] = up_acc[...].astype(BF).reshape(part, -1, hidden)
        down_ref[...] = down_acc[...].astype(BF)


def expert_grads(x_rows, g_rows, hid, dg, du, dp, name):
    quads, shards, rows, width = x_rows[0].shape
    batches = shards // 2
    tiles, tile, hidden = hid.shape

    saved = pl.BlockSpec((2, tile, hidden), lambda t: (t, 0, 0))

    def own(t):
        return (jnp.minimum(t, quads - 1), 0, 0, 0)

    def other(t):
        return (jnp.maximum(t - quads, 0), 0, 0, 0)

    g_block = (1, batches, rows, width)
    return pl.pallas_call(
        functools.partial(grads_body, quads),
        out_shape=(
            jax.ShapeDtypeStruct((dp, 2, width // dp, hidden), BF),
            jax.ShapeDtypeStruct((hidden, width), BF),
        ),
        grid_spec=pl.GridSpec(
            grid=(tiles // 2,),
            in_specs=[
                pl.BlockSpec((1, shards, rows, width), own),
                pl.BlockSpec((1, shards, rows, width), other),
                pl.BlockSpec(g_block, own), pl.BlockSpec(g_block, other),
                pl.BlockSpec(g_block, own), pl.BlockSpec(g_block, other),
                saved, saved, saved,
            ],
            out_specs=[
                pl.BlockSpec((dp, 2, width // dp, hidden), lambda t: (0, 0, 0, 0)),
                pl.BlockSpec((hidden, width), lambda t: (0, 0)),
            ],
            scratch_shapes=[pltpu.VMEM((width, hidden), F32), pltpu.VMEM((width, hidden), F32),
                            pltpu.VMEM((hidden, width), F32)],
        ),
        compiler_params=pltpu.CompilerParams(
            dimension_semantics=("arbitrary",), vmem_limit_bytes=60 << 20
        ),
        name=name,
    )(*x_rows, *g_rows, hid, dg, du)


def scatter_all(pairs, partner, name, number, extra=()):
    if pairs[0][0].shape[0] == 4:
        return scatter_rows(pairs, partner, name, number, extra)
    total = pairs[0][0].shape[1]
    count = total // 2 if partner else total
    sums = [
        jnp.concatenate(
            [
                scatter_rows([(own[:, m::count], other[:, m::count])], partner, name, number)[0]
                for m in range(count)
            ]
        )
        for own, other in pairs
    ]
    if not extra:
        return sums
    blocks, down = extra
    lanes, lane = lax.axis_size("lane"), lax.axis_index("lane")
    down = down.reshape(down.shape[0], lanes, -1, down.shape[2]).swapaxes(0, 1)
    moved = [
        lax.ppermute(
            lax.dynamic_index_in_dim(down, lane ^ d, 0, keepdims=False),
            "lane", [(i, i ^ d) for i in range(lanes)],
        )
        for d in range(1, lanes)
    ]
    return sums + [exchange(blocks, DP), jnp.stack(moved)]


def on_device(
    tokens,
    cotangent,
    routes,
    lengths,
    block_order,
    w_query,
    w_key,
    w_value,
    w_out,
    w_router,
    w_gate,
    w_up,
    w_down,
    attn_gain,
    mlp_gain,
    query_gain,
    key_gain,
):
    batches, _, rows, width = tokens.shape
    dp_size = lax.axis_size(DP)
    ctx_size = lax.axis_size(CTX)
    quads = lax.axis_size("quad")
    lanes = lax.axis_size("lane")
    slot_len = rows * ctx_size
    block_rows = rows // 2
    head_width = width // ctx_size
    heads = head_width // HEAD
    shard = w_query.shape[0]
    expert_count = w_router.shape[1]
    local_experts = w_gate.shape[0]
    hidden_units = w_gate.shape[2]
    hidden_half = hidden_units // 2
    depth_part = w_gate.shape[1]
    factor = 1.0 / math.sqrt(HEAD)
    pair = lax.axis_index("pair")

    qkv = jnp.stack([w_query, w_key, w_value], axis=1).reshape(shard, 3, ctx_size, head_width)
    qkv = qkv.transpose(2, 0, 1, 3).reshape(ctx_size, shard, 3 * head_width)
    small = jnp.concatenate(
        [attn_gain, mlp_gain, query_gain, key_gain, w_router.reshape(shard * expert_count)]
    )
    grad_low = cotangent[:, 0]
    tok_own, tok_other, qkv_w, small, out_w = start_gather(
        tokens[:, 0], qkv, small.reshape(1, -1), w_out
    )
    token_rows = (tok_own, tok_other)
    qkv_w = qkv_w.reshape(width, 3 * head_width)
    out_w = out_w.reshape(width, width)
    small = small.reshape(dp_size * ctx_size, -1)
    gain_attn = small[:, :shard].reshape(width).astype(F32)
    gain_mlp = small[:, shard : 2 * shard].reshape(width).astype(F32)
    gain_query = small[:, 2 * shard : 3 * shard].reshape(ctx_size, head_width)
    gain_key = small[:, 3 * shard : 4 * shard].reshape(ctx_size, head_width)
    router_w = small[:, 4 * shard :].reshape(width, expert_count)
    here = lax.axis_index(CTX)
    gain_query = lax.dynamic_index_in_dim(gain_query, here, 0, keepdims=False).astype(F32)
    gain_key = lax.dynamic_index_in_dim(gain_key, here, 0, keepdims=False).astype(F32)

    w_gate, w_up, w_down, crossing, qkv_w = lax.optimization_barrier(
        (w_gate, w_up, w_down, grad_low, qkv_w)
    )
    halves = [
        jnp.stack(
            [
                jnp.stack([w_gate[e, :, part], w_up[e, :, part]])
                for part in (slice(0, hidden_half), slice(hidden_half, hidden_units))
            ]
        )
        for e in range(local_experts)
    ]
    both_w = [exchange(jnp.repeat(part, lanes, axis=0), DP) for part in halves[:-1]]
    down_parts = lane_parts(w_down)
    cot_cross = swap(crossing, "half")

    def places_of(device):
        stored = device * rows + jnp.arange(rows, dtype=jnp.int32)
        match_marks = (stored // block_rows)[:, None] == jnp.arange(
            block_order.shape[0], dtype=jnp.int32
        )[None, :]
        first_place = jnp.sum(jnp.where(match_marks, block_order[None, :], 0), axis=1)
        return first_place * block_rows + stored % block_rows

    places = jnp.concatenate(
        [
            places_of((lax.axis_index("quad") ^ k) * 2 + (pair ^ other))
            for other in range(2)
            for k in range(quads)
        ]
    )
    cosine, sine = angles(places, HEAD)
    expert_range = jnp.arange(expert_count, dtype=jnp.int32)

    inputs = tokens[:, 0].astype(F32)
    attn_root = inv_rms(inputs)
    act = []
    for part in token_rows:
        values = part.astype(F32)
        act.append((values * inv_rms(values) * gain_attn).astype(BF))
    pre = [
        dot("td,de->te", part.reshape(-1, width), qkv_w).reshape(quads, batches, rows, -1)
        for part in act
    ]
    pre = jnp.stack(pre)

    squares = jnp.stack(
        [
            jnp.sum(part * part, axis=-1)
            for part in (pre[..., :head_width], pre[..., head_width : 2 * head_width])
        ],
        axis=2,
    )
    squares = sum_ctx(squares.reshape(2 * quads, 2 * batches, rows), "sum_squares", 6)
    roots = lax.rsqrt(squares.reshape(2 * quads, 2, batches, rows) / width + EPSILON)

    saved = []
    attended_all = []
    for m in range(batches):
        pre_m = pre[:, :, m].reshape(slot_len, 3 * head_width)
        query_pre = pre_m[:, :head_width]
        key_pre = pre_m[:, head_width : 2 * head_width]
        value = pre_m[:, 2 * head_width :].astype(BF).reshape(slot_len, heads, HEAD)
        query_root = roots[:, 0, m].reshape(slot_len, 1)
        key_root = roots[:, 1, m].reshape(slot_len, 1)
        query = rotate(
            (query_pre * query_root * gain_query).reshape(slot_len, heads, HEAD), cosine, sine
        ).astype(BF)
        key = rotate(
            (key_pre * key_root * gain_key).reshape(slot_len, heads, HEAD), cosine, sine
        ).astype(BF)
        allowed = (places[None, :] <= places[:, None]) & (places[None, :] < lengths[m, 0])
        scores = dot("qhd,khd->hqk", query, key) * factor
        scores = jnp.where(allowed[None], scores, MASKED)
        expo = jnp.exp(scores - jnp.max(scores, axis=-1, keepdims=True))
        probs = expo / jnp.sum(expo, axis=-1, keepdims=True)
        probs_low = probs.astype(BF)
        attended = dot("hqk,khd->qhd", probs_low, value).astype(BF)
        attended_all.append(attended.reshape(2 * quads, rows, head_width))
        saved.append(
            dict(
                query_pre=query_pre, key_pre=key_pre, query_root=query_root, key_root=key_root,
                query=query, key=key, value=value, probs=probs, probs_low=probs_low,
            )
        )
    attended = jnp.stack(attended_all, axis=1)[None]
    attended = exchange_rows(attended, "inward", "attended_to_rows", 7)[0]
    attended = attended.transpose(1, 2, 0, 3).reshape(batches, rows, width)
    x_mid = inputs + dot("mtd,de->mte", attended, out_w)
    mlp_root = inv_rms(x_mid)
    mixed_in = (x_mid * mlp_root * gain_mlp).astype(BF)
    router = jax.nn.softmax(dot("mtd,de->mte", mixed_in, router_w), axis=-1)
    routed = jnp.any(routes[:, 0, :, :, None] == expert_range, axis=2).astype(F32)
    gates = (router * routed).transpose(2, 0, 1).reshape(ctx_size, local_experts, batches, rows)
    gates = exchange_rows(gates, "outward", "gates_to_experts", 8, 2)
    gates = gates.transpose(1, 0, 3, 4, 2).reshape(4 * quads, batches * rows, local_experts)
    (x_rows, cot_rows, cross_rows), last_w = gather_rows(
        [mixed_in, grad_low, cot_cross], (True, False, False), halves[-1], "gather_mixed", 2
    )
    both_w = both_w + [last_w]
    g_rows = cot_rows + cross_rows
    x_rows, both_w, down_parts = lax.optimization_barrier((x_rows, both_w, down_parts))
    down_w = gather_lane(w_down, down_parts).swapaxes(0, 1)
    down_w = down_w.reshape(local_experts, hidden_half, width)

    sums = ()
    d_gates, grads_both, grads_down = [], [], []
    for e in range(local_experts):
        *sums, d_gate, hid, d_gate_pre, d_up_pre = expert(
            gates[..., e : e + 1], x_rows, g_rows, both_w[e], down_w[e], tuple(sums), f"expert_{e}"
        )
        d_gates.append(d_gate)
        grad_both, grad_down = expert_grads(
            x_rows, g_rows, hid, d_gate_pre, d_up_pre, dp_size, f"expert_grads_{e}"
        )
        sums[0], grad_both = lax.optimization_barrier((sums[0], grad_both))
        grads_both.append(exchange(grad_both, DP) if e < local_experts - 1 else grad_both)
        grads_down.append(grad_down)
    moe_own, moe_other, d_own, d_other = sums
    d_own, grads_both, grads_down = lax.optimization_barrier((d_own, grads_both, grads_down))
    grads_down = jnp.stack(grads_down)
    d_mixed, moe_sum, last_both, down_others = scatter_all(
        [(d_own, d_other), (moe_own, moe_other)], True, "scatter_experts", 3,
        (grads_both[-1], grads_down),
    )
    grads_both[-1] = last_both
    d_gates = jnp.concatenate(d_gates, axis=-1)
    d_gates = d_gates.reshape(2 * quads, 2, batches, rows, local_experts)
    d_gates = d_gates.transpose(1, 0, 4, 2, 3)
    d_gates, d_mixed = lax.optimization_barrier((d_gates, d_mixed))
    d_router = exchange_rows(d_gates, "inward", "gate_gradients", 9, 2)
    d_router = jnp.sum(d_router, axis=0).reshape(expert_count, batches, rows)
    d_router = d_router.transpose(1, 2, 0) * routed
    d_logits = (
        router * (d_router - jnp.sum(router * d_router, axis=-1, keepdims=True))
    ).astype(BF)
    d_mixed = d_mixed + dot("mte,de->mtd", d_logits, router_w)

    def norm_back_all(values, root, gain, grad):
        d_values, d_gain = norm_back(values, root, gain, grad)
        return d_values, jnp.sum(d_gain, axis=0)

    d_mid, part_mlp_gain = norm_back_all(x_mid, mlp_root, gain_mlp, d_mixed)
    d_mid = d_mid + grad_low.astype(F32)
    d_att_out = d_mid.astype(BF)
    d_attended = dot("mte,de->mtd", d_att_out, out_w).astype(BF)
    d_attended = d_attended.reshape(batches, rows, ctx_size, head_width).transpose(2, 0, 1, 3)
    d_attended = exchange_rows(d_attended, "outward", "attended_gradients", 10)[0]
    part_query_gain = part_key_gain = 0.0
    parts = []
    inners = []
    for m in range(batches):
        s = saved[m]
        d_att = d_attended[:, m].reshape(slot_len, heads, HEAD)
        probs, query, key = s["probs"], s["query"], s["key"]
        d_probs = dot("qhd,khd->hqk", d_att, s["value"])
        inner = jnp.sum(probs * d_probs, axis=-1, keepdims=True)
        d_scores = (probs * (d_probs - inner)).astype(BF)
        d_query = dot("hqk,khd->qhd", d_scores, key) * factor
        d_key = dot("hqk,qhd->khd", d_scores, query) * factor
        d_value = dot("hqk,qhd->khd", s["probs_low"], d_att)
        d_query = rotate_back(d_query, cosine, sine).reshape(slot_len, head_width)
        d_key = rotate_back(d_key, cosine, sine).reshape(slot_len, head_width)
        parts.append((d_query, d_key, d_value))
        inners += [
            jnp.sum(d_query * gain_query * s["query_pre"], axis=1).reshape(-1, rows),
            jnp.sum(d_key * gain_key * s["key_pre"], axis=1).reshape(-1, rows),
        ]
    inners = sum_ctx(jnp.stack(inners, axis=1), "sum_inner", 11) / width
    d_pre_all = []
    for m in range(batches):
        s = saved[m]
        d_query, d_key, d_value = parts[m]
        query_pre, key_pre = s["query_pre"], s["key_pre"]
        query_root, key_root = s["query_root"], s["key_root"]
        query_inner = inners[:, 2 * m].reshape(slot_len, 1)
        key_inner = inners[:, 2 * m + 1].reshape(slot_len, 1)
        d_query_pre = query_root * (d_query * gain_query) - query_pre * query_root**3 * query_inner
        d_key_pre = key_root * (d_key * gain_key) - key_pre * key_root**3 * key_inner
        part_query_gain = part_query_gain + jnp.sum(d_query * query_pre * query_root, axis=0)
        part_key_gain = part_key_gain + jnp.sum(d_key * key_pre * key_root, axis=0)
        d_pre = jnp.concatenate(
            [
                d_query_pre.astype(BF),
                d_key_pre.astype(BF),
                d_value.reshape(slot_len, head_width).astype(BF),
            ],
            axis=1,
        )
        d_pre_all.append(d_pre.reshape(2, quads, rows, 3 * head_width))
    d_pre = jnp.stack(d_pre_all, axis=2).reshape(2, -1, 3 * head_width)
    d_act = [
        dot("te,de->td", d_pre[i], qkv_w).astype(BF).reshape(quads, batches, rows, width)
        for i in range(2)
    ]
    d_act = scatter_all([(d_act[0], d_act[1])], False, "scatter_act", 4)[0]
    d_inputs, part_attn_gain = norm_back_all(inputs, attn_root, gain_attn, d_act)
    mixed = (x_mid + moe_sum).astype(BF)

    grads_both = jnp.stack(grads_both, axis=2).astype(F32)
    grads_both = grads_both.reshape(2, lanes, 2, local_experts, depth_part, hidden_half).sum(axis=1)
    grads_both = grads_both.transpose(1, 2, 3, 0, 4)
    grad_gate, grad_up = grads_both.reshape(2, local_experts, depth_part, hidden_units)
    grads_down = grads_down.reshape(local_experts, lanes, -1, width)
    grad_down = lax.dynamic_index_in_dim(grads_down, lax.axis_index("lane"), 1, keepdims=False)
    grad_down = grad_down.astype(F32) + jnp.sum(down_others.astype(F32), axis=0)

    grad_out = dot("mtd,mte->de", attended, d_att_out).astype(BF)
    grad_out = lax.psum_scatter(grad_out, ALL, scatter_dimension=0, tiled=True).astype(F32)
    acts = [part.reshape(-1, width) for part in act]
    grad_qkv = sum(dot("td,te->de", x, y) for x, y in zip(acts, d_pre)).astype(BF)
    grad_qkv = lax.psum_scatter(grad_qkv, DP, scatter_dimension=0, tiled=True)
    grad_qkv = grad_qkv.reshape(ctx_size, shard, 3 * head_width)
    grad_qkv = exchange_rows(grad_qkv, "ctx", "qkv_gradients", 14).astype(F32)
    grad_qkv = grad_qkv.reshape(ctx_size, shard, 3, head_width).transpose(2, 1, 0, 3)
    grad_qkv = grad_qkv.reshape(3, shard, width)

    grad_router = dot("mtd,mte->de", mixed_in, d_logits)
    columns = jnp.arange(ctx_size, dtype=jnp.int32)[:, None] == here

    def placed(part):
        return jnp.where(columns, part[None, :], 0.0).reshape(width)

    gains = jnp.stack(
        [part_attn_gain, part_mlp_gain, placed(part_query_gain), placed(part_key_gain)]
    )
    gains = gains.reshape(4, dp_size, ctx_size, shard).transpose(1, 2, 0, 3)
    packed = jnp.concatenate(
        [
            gains.reshape(dp_size * ctx_size, 1, 4 * shard),
            grad_router.reshape(dp_size * ctx_size, 1, shard * expert_count),
        ],
        axis=2,
    )
    packed = reduce_small(packed)
    return (
        mixed[:, None],
        (d_inputs + d_mid)[:, None],
        grad_qkv[0],
        grad_qkv[1],
        grad_qkv[2],
        grad_out,
        packed[4 * shard :].reshape(shard, expert_count),
        grad_gate,
        grad_up,
        grad_down,
        packed[:shard],
        packed[shard : 2 * shard],
        packed[2 * shard : 3 * shard],
        packed[3 * shard : 4 * shard],
    )


def solution(mesh):
    dp_size, ctx_size = mesh.shape["dp"], mesh.shape["ctx"]
    grid = Mesh(mesh.devices.reshape(2, dp_size // 2, ctx_size // 2, 2), ALL)
    rows = P(None, DP, CTX, None)
    dense = P(ALL, None)
    expert = P(CTX, DP, None)
    vector = P(ALL)
    return jax.shard_map(
        on_device,
        mesh=grid,
        in_specs=(rows, rows, rows, P(None, DP), P())
        + (dense,) * 5
        + (expert,) * 3
        + (vector,) * 4,
        out_specs=(rows, rows) + (dense,) * 5 + (expert,) * 3 + (vector,) * 4,
        check_vma=False,
    )
```

time: 1610 us -> 1280 us (0.80)
  Pallas kernels: 0 us -> 919 us
  waiting for transfers between devices: 525 us -> 25 us
  matrix products: 431 us -> 95.7 us
  starting transfers between devices: 166 us -> 13 us
  local copies, waits for them, and re-layouts: 238 us -> 114 us
  other arithmetic: 190 us -> 94.5 us
  blocking collectives: 24.8 us -> 0 us
    pallas_call x0 -> x16, Pallas kernels: none -> 919 us  [the longest x2 330 us: scatter_rows(): pl.pallas_call(functools.partial(scatter_body, quads, lanes, kinds, count...]
    dot_general x52 -> x21, matrix products: 417 us -> 83.4 us  [dot(): return jnp.einsum(spec, left, right, preferred_element_type=F32)]
    ppermute x46 -> x2, waiting for transfers between devices: 301 us -> 0.01 us  [swap(): return lax.ppermute(values, axis, [(0, 1), (1, 0)])]
    all_to_all x32 -> x2, waiting for transfers between devices: 217 us -> 0.01 us  [exchange(): return lax.all_to_all(blocks, axes, split_axis=0, concat_axis=0, tiled=True)]
    all_to_all x32 -> x2, starting transfers between devices: 132 us -> 9.99 us  [exchange(): return lax.all_to_all(blocks, axes, split_axis=0, concat_axis=0, tiled=True)]
    convert_element_type x16 -> x1, other arithmetic: 55.7 us -> 4.64 us  [on_device(): act.append((values * inv_rms(values) * gain_attn).astype(BF))]
    unnamed x367 -> x137, local copies, waits for them, and re-layouts: 72 us -> 26.6 us
    another operation x18 -> x12, other arithmetic: 51.2 us -> 15.5 us  [the longest x6 4.64 us: on_device(): jnp.stack([jnp.stack([w_gate[e, :, part], w_up[e, :, part]]) for part in...]
  transfers between devices with their start and end apart: 90 -> 6, of which waited for: 43 -> 1; matrix products, arithmetic and copies ran while one was open for 49% -> 15% of each run, Pallas kernels for 0% -> 32%
where the time goes in v3:
time: 1280 us
  Pallas kernels  919 us (72%)
  local copies, waits for them, and re-layouts  114 us (9%)
  matrix products  95.7 us (7%)
  other arithmetic  94.5 us (7%)
  waiting for transfers between devices  25 us (2%)
  between operations  15.8 us (1%)
  starting transfers between devices  13 us (1%)
    pallas_call x2, Pallas kernels, scatter_rows(): pl.pallas_call(functools.partial(scatter_body, quads, lanes, kinds, count...  330 us
    pallas_call x1, Pallas kernels, gather_rows(): pl.pallas_call(functools.partial(gather_body, quads, lanes, partners), ou...  151 us
    pallas_call x2, Pallas kernels, expert(): pl.pallas_call(functools.partial(expert_body, quads, bool(before)), out_s...  143 us
    pallas_call x1, Pallas kernels, start_gather(): pl.pallas_call(functools.partial(start_body, quads, lanes), out_shape=[li...  110 us
    pallas_call x6, Pallas kernels, exchange_rows(): pl.pallas_call(functools.partial(exchange_body, mode, lanes, quads, halve...  95.4 us
    dot_general x21, matrix products, dot(): return jnp.einsum(spec, left, right, preferred_element_type=F32)  83.4 us
    pallas_call x2, Pallas kernels, expert_grads(): pl.pallas_call(functools.partial(grads_body, quads), out_shape=(jax.Shape...  74.6 us
    unnamed x137, local copies, waits for them, and re-layouts  26.6 us
  transfers between devices with their start and end apart: 6, of which 1 were waited for; matrix products, arithmetic and copies ran while one was open for 15% of the time, Pallas kernels for 32%

profile of v3, /device:TPU:0, one launch (start us, length us, event | category | flops | bytes accessed | tf_op | source)
XLA Modules:
  0.0 1276.7 jit_solution(700692335722548620)
XLA Ops:
  19.2 109.7 %start_gather.1 = (bf16[4,2,128,2048]{3,2,1,0:T(8,128)(2,1)}, bf16[4,2,128,2048]{3,2,1,0:T(8,128)(2,1)}, bf16[4,8,64,768]{3,2,1,0:T(8,128)(2,1)}, bf16[32,1,1280]{2,1,0:T(2,128)(2,1)}, bf16[4,8,64,2048]{3,2,1,0:T(8,128)(2,1)}) custom-call(bf16[2,128,2048]{2,1,0:T(8,128)(2,1)} %bitcast.262, bf16[8,64,768]{2,1,0:T(8,128)(2,1)} %reshape.873.qkv_ref, ...), custom_call_target="tpu_custom_call" | custom-call | tf_op jit(solution)/shard_map/start_gather/pallas_call | solution.py:393
  167.6 7.8 sum_squares.1
  226.0 17.3 %attended_to_rows.1 = bf16[1,8,2,128,256]{4,3,2,1,0:T(8,128)(2,1)} custom-call(bf16[1,8,2,128,256]{4,3,2,1,0:T(8,128)(2,1)} %maximum_bitcast_fusion.2.x_ref), custom_call_target="tpu_custom_call" | custom-call | tf_op jit(solution)/shard_map/attended_to_rows/pallas_call | solution.py:658
  245.8 6.2 multiply_reduce_fusion.4
  256.0 15.8 %gates_to_experts.1 = f32[2,8,2,2,128]{4,3,2,1,0:T(2,128)} custom-call(f32[8,2,2,128]{3,2,1,0:T(2,128)} %bitcast.354), custom_call_target="tpu_custom_call" | custom-call | tf_op jit(solution)/shard_map/gates_to_experts/pallas_call | solution.py:658
  281.6 151.2 %gather_mixed.1 = (bf16[4,4,128,2048]{3,2,1,0:T(8,128)(2,1)}, bf16[4,4,128,2048]{3,2,1,0:T(8,128)(2,1)}, bf16[4,2,128,2048]{3,2,1,0:T(8,128)(2,1)}, bf16[4,2,128...) custom-call(bf16[2,128,2048]{2,1,0:T(8,128)(2,1)} %copy-done.8, ...), custom_call_target="tpu_custom_call" | custom-call | tf_op jit(solution)/shard_map/gather_mixed/pallas_call | solution.py:287
  437.9 70.8 %expert_0.1 = (bf16[4,4,128,2048]{3,2,1,0:T(8,128)(2,1)}, bf16[4,4,128,2048]{3,2,1,0:T(8,128)(2,1)}, bf16[4,4,128,2048]{3,2,1,0:T(8,128)(2,1)}, bf16[4,4,128,204...) custom-call(f32[16,256,1]{2,1,0:T(8,128)} %get-tuple-element.261.gat, ...), custom_call_target="tpu_custom_call" | custom-call | tf_op jit(solution)/shard_map/expert_0/pallas_call | solution.py:802
  508.7 37.2 %expert_grads_0.1 = (bf16[4,2,512,512]{3,2,1,0:T(8,128)(2,1)}, bf16[512,2048]{1,0:T(8,128)(2,1)}) custom-call(bf16[4,4,128,2048]{3,2,1,0:T(8,128)(2,1)} %get-tuple-element.84.xo_ref, bf16[4,4,128,2048]{3,2,1,0:T(8,128)(2,1)} %get-tuple-element.85.xt_ref, bf16[4,2,128,2048]{3,2,1,0:T(8,128)(2,1)} %get-tuple-element.86.goo_ref, ...), custom_call_target="tpu_custom_call" | custom-call | tf_op jit(solution)/shard_map/expert_grads_0/pallas_call | solution.py:871
  553.1 72.4 %expert_1.1 = (bf16[4,4,128,2048]{3,2,1,0:T(8,128)(2,1)}, bf16[4,4,128,2048]{3,2,1,0:T(8,128)(2,1)}, bf16[4,4,128,2048]{3,2,1,0:T(8,128)(2,1)}, bf16[4,4,128,204...) custom-call(f32[16,256,1]{2,1,0:T(8,128)} %get-tuple-element.262.gat, ...), custom_call_target="tpu_custom_call", output_to_operand_aliasing={{0}: (9, {}), {1}: (10, {}), {2}: (11, {}), {3}: (12, {})} | custom-call | tf_op jit(solution)/shard_map/expert_1/pallas_call | solution.py:802
  625.4 37.4 %expert_grads_1.1 = (bf16[4,2,512,512]{3,2,1,0:T(8,128)(2,1)}, bf16[512,2048]{1,0:T(8,128)(2,1)}) custom-call(bf16[4,4,128,2048]{3,2,1,0:T(8,128)(2,1)} %get-tuple-element.84.xo_ref, bf16[4,4,128,2048]{3,2,1,0:T(8,128)(2,1)} %get-tuple-element.85.xt_ref, bf16[4,2,128,2048]{3,2,1,0:T(8,128)(2,1)} %get-tuple-element.86.goo_ref, ...), custom_call_target="tpu_custom_call" | custom-call | tf_op jit(solution)/shard_map/expert_grads_1/pallas_call | solution.py:871
  670.3 254.9 %scatter_experts.1 = (f32[2,128,2048]{2,1,0:T(8,128)}, f32[2,128,2048]{2,1,0:T(8,128)}, bf16[4,2,512,512]{3,2,1,0:T(8,128)(2,1)}, bf16[1,2,256,2048]{3,2,1,0:T(8,128)(2,1)}) custom-call(bf16[4,4,128,2048]{3,2,1,0:T(8,128)(2,1)} %get-tuple-element.112.refs_0_, bf16[4,4,128,2048]{3,2,1,0:T(8,128)(2,1)} %get-tuple-element.113.refs_1_, ...), custom_call_target="tpu_custom_call" | custom-call | tf_op jit(solution)/shard_map/scatter_experts/pallas_call | solution.py:573
  925.2 8.2 gate_gradients.1
  945.7 17.2 %attended_gradients.1 = bf16[1,8,2,128,256]{4,3,2,1,0:T(8,128)(2,1)} custom-call(bf16[8,2,128,256]{3,2,1,0:T(8,128)(2,1)} %bitcast.303), custom_call_target="tpu_custom_call" | custom-call | tf_op jit(solution)/shard_map/attended_gradients/pallas_call | solution.py:658
  969.8 7.9 multiply_reduce_fusion.1
  995.5 7.0 multiply_convert_fusion.1
  1022.0 6.5 sum_inner.1
  1058.5 9.2 convert_reduce_fusion
  1067.7 7.8 fusion.100
  1091.4 5.4 copy.395
  1097.0 7.9 convolution_convert_fusion
  1109.9 75.4 %scatter_act.1 = f32[2,128,2048]{2,1,0:T(8,128)} custom-call(bf16[4,2,128,2048]{3,2,1,0:T(8,128)(2,1)} %bitcast.299, bf16[4,2,128,2048]{3,2,1,0:T(8,128)(2,1)} %bitcast.298), custom_call_target="tpu_custom_call" | custom-call | tf_op jit(solution)/shard_map/scatter_act/pallas_call | solution.py:573
  1188.7 13.1 %small_gradients.1 = f32[32,1,1280]{2,1,0:T(1,128)} custom-call(f32[32,1,1280]{2,1,0:T(1,128)} %pad_maximum_fusion.8.x_ref), custom_call_target="tpu_custom_call" | custom-call | tf_op jit(solution)/shard_map/small_gradients/pallas_call | solution.py:658
  1211.3 23.8 %qkv_gradients.1 = bf16[8,64,768]{2,1,0:T(8,128)(2,1)} custom-call(bf16[8,64,768]{2,1,0:T(8,128)(2,1)} %bitcast.317), custom_call_target="tpu_custom_call" | custom-call | tf_op jit(solution)/shard_map/qkv_gradients/pallas_call | solution.py:658
  1242.9 24.9 %reduce-scatter.5.cloned.1.call-done = bf16[64,2048]{1,0:T(8,128)(2,1)} async-done(((bf16[2048,2048]{1,0:T(8,128)(2,1)}), bf16[64,2048]{1,0:T(8,128)(2,1)}) %reduce-scatter.5.cloned.1.call-update) | async-done | bytes 262160 | tf_op jit(solution)/shard_map/reduce_scatter | solution.py:1196
  (332 shorter events, 265.9 us)
Async XLA Ops:
  15.7 116.1 %copy-start.31 = (bf16[2,512,1024]{2,1,0:T(8,128)(2,1)S(1)}, bf16[2,512,1024]{2,1,0:T(8,128)(2,1)}, u32[]{:S(2)}) copy-start(bf16[2,512,1024]{2,1,0:T(8,128)(2,1)} %param.27) | copy-start | bytes 6291460
  128.9 152.7 %collective-permute-start = (bf16[2,128,2048]{2,1,0:T(8,128)(2,1)}, bf16[2,128,2048]{2,1,0:T(8,128)(2,1)}, u32[]{:S(2)}, u32[]{:S(2)}) collective-permute-start(bf16[2,128,2048]{2,1,0:T(8,128)(2,1)} %bitcast.2.refs_1_), channel_id=1, source_target_pairs={{0,16},{16,0},{1,17},{17,1},{2,18},{18,2},{3,19},{19,3},{4,20},{20... | collective-permute-start | bytes 3145736 | tf_op jit(solution)/shard_map/ppermute | solution.py:62
  129.1 303.7 %collective-permute-start.1 = (bf16[2,256,2048]{2,1,0:T(8,128)(2,1)}, bf16[2,256,2048]{2,1,0:T(8,128)(2,1)}, u32[]{:S(2)}, u32[]{:S(2)}) collective-permute-start(bf16[2,256,2048]{2,1,0:T(8,128)(2,1)} %param.29), channel_id=1, source_target_pairs={{0,8},{8,0},{1,9},{9,1},{2,10},{10,2},{3,11},{11,3},{4,12},{12,4},... | collective-permute-start | bytes 6291464 | tf_op jit(solution)/shard_map/ppermute | solution.py:62
  137.7 295.1 %all-to-all-start = ((bf16[4,2,512,512]{3,2,1,0:T(8,128)(2,1)}), bf16[4,2,512,512]{3,2,1,0:T(8,128)(2,1)}, u32[]{:S(2)}, u32[]{:S(2)}) async-start(bf16[4,2,512,512]{3,2,1,0:T(8,128)(2,1)} %bitcast.264), calls=%async_computation | async-start | bytes 8388608 | tf_op jit(solution)/shard_map/all_to_all | solution.py:66
  162.8 37.0 %copy-start = (f32[2,4,1,128,768]{4,3,2,1,0:T(8,128)}, f32[2,4,1,128,768]{4,3,2,1,0:T(8,128)S(1)}, u32[]{:S(2)}) copy-start(f32[2,4,1,128,768]{4,3,2,1,0:T(8,128)S(1)} %get-tuple-element.241) | copy-start | bytes 9437188
  215.1 5.3 copy-start.42
  225.0 20.8 %copy-start.2 = (bf16[2,1,128,2048]{3,2,1,0:T(8,128)(2,1)S(1)}, bf16[2,1,128,2048]{3,2,1,0:T(8,128)(2,1)}, u32[]{:S(2)}) copy-start(bf16[2,1,128,2048]{3,2,1,0:T(8,128)(2,1)} %param.17) | copy-start | bytes 3145732
  245.8 6.2 copy-start.53
  253.5 23.8 %copy-start.8 = (bf16[2,128,2048]{2,1,0:T(8,128)(2,1)}, bf16[2,128,2048]{2,1,0:T(8,128)(2,1)S(1)}, u32[]{:S(2)}) copy-start(bf16[2,128,2048]{2,1,0:T(8,128)(2,1)S(1)} %multiply_convert_fusion.2.refs_0_) | copy-start | bytes 3145732
  545.9 119.8 %all-to-all-start.1 = ((bf16[4,2,512,512]{3,2,1,0:T(8,128)(2,1)}), bf16[4,2,512,512]{3,2,1,0:T(8,128)(2,1)}, u32[]{:S(2)}, u32[]{:S(2)}) async-start(bf16[4,2,512,512]{3,2,1,0:T(8,128)(2,1)} %get-tuple-element.103), calls=%async_computation.1 | async-start | bytes 8388608 | tf_op jit(solution)/shard_map/all_to_all | solution.py:66
  550.8 660.5 %reduce-scatter.3.cloned.1.call-start = ((), (), s32[]{:S(2)}) async-start(), calls=%async_computation.4 | async-start | bytes 3932160 | tf_op jit(solution)/shard_map/reduce_scatter | solution.py:1199
  670.3 263.9 %copy-start.19 = (bf16[2048,16]{1,0:T(8,128)(2,1)S(1)}, bf16[2048,16]{1,0:T(8,128)(2,1)}, u32[]{:S(2)}) copy-start(bf16[2048,16]{1,0:T(8,128)(2,1)} %reshape.889) | copy-start | bytes 196612
  934.3 7.1 slice-start
  978.3 10.0 slice-start.2
  995.5 7.0 copy-start.34
  1010.0 7.8 copy-start.1
  1010.0 7.8 copy-start.50
  1010.0 7.8 copy-start.52
  1033.8 6.8 copy-start.37
  1033.9 6.8 copy-start.39
  1045.9 222.0 %reduce-scatter.5.cloned.1.call-start = ((), (), s32[]{:S(2)}) async-start(), calls=%async_computation.5 | async-start | bytes 8650752 | tf_op jit(solution)/shard_map/reduce_scatter | solution.py:1196
  1097.0 7.9 copy-start.38
  1097.0 7.9 copy-start.57
  1109.9 75.4 %copy-start.48 = (f32[2048]{0:T(1024)S(1)}, f32[2048]{0:T(1024)}, u32[]{:S(2)}) copy-start(f32[2048]{0:T(1024)} %copy-done.47) | copy-start | bytes 24580
  (44 other events, 152.8 us)
Sparse Core Ops, SparseCore 0:
  1046.0 59.0 reduce-scatter.2
  1107.4 160.3 reduce-scatter.4

commit v4 on v3

--- a/solution.py
+++ b/solution.py
@@ -207,13 +207,11 @@
     return half * lanes + lane, result
 
 
-def gather_body(quads, lanes, partners, *refs):
+def gather_body(quads, partners, *refs):
     inputs = refs[: len(partners)]
-    blocks_ref = refs[len(partners)]
-    refs = refs[len(partners) + 1 :]
+    refs = refs[len(partners) :]
     outputs = [(refs[2 * i], refs[2 * i + 1]) for i in range(len(partners))]
-    blocks_out, held = refs[2 * len(partners) : 2 * len(partners) + 2]
-    refs = refs[2 * len(partners) + 2 :]
+    refs = refs[2 * len(partners) :]
     keeps = {}
     for i, partner in enumerate(partners):
         if partner:
@@ -224,8 +222,7 @@
     quad = lax.axis_index("quad")
     peers = [{"quad": toggled(quad, k)} for k in range(1, quads)]
     peers.append({"pair": 1 - lax.axis_index("pair")})
-    me, planes = planes_of(lanes)
-    greet(peers + [device for device, _ in planes])
+    greet(peers + ([across] if keeps else []))
 
     def add(sources, i, offset):
         plans = []
@@ -245,17 +242,7 @@
     plans = []
     for i, ref in enumerate(inputs):
         plans += add([ref.at[s] for s in range(ref.shape[0])], i, 0)
-    blocks = [
-        mover.copy(blocks_ref.at[place // lanes], blocks_out.at[me], device)
-        for device, place in planes
-    ]
-    mover.go(*blocks)
-    into = mover.keep(blocks_ref.at[me // lanes], held)
-    plans[0].forward()
-    into.wait()
-    mover.kept = [c for c in mover.kept if c is not into]
-    mover.keep(held, blocks_out.at[me])
-    for p in plans[1:]:
+    for p in plans:
         p.forward()
     late = []
     for i, keep in keeps.items():
@@ -266,13 +253,11 @@
         p.forward()
     for p in plans + late:
         p.arrive()
-    for c in blocks:
-        c.wait_recv()
     mover.finish()
 
 
-def gather_rows(sources, partners, blocks, name, number):
-    quads, lanes = lax.axis_size("quad"), lax.axis_size("lane")
+def gather_rows(sources, partners, name, number):
+    quads = lax.axis_size("quad")
     shapes, keeps = [], []
     sems = total = 0
     for x, partner in zip(sources, partners):
@@ -282,25 +267,21 @@
         shapes += [jax.ShapeDtypeStruct((quads, count) + x.shape[1:], x.dtype)] * 2
         if partner:
             keeps.append(pltpu.VMEM(x.shape, x.dtype))
-    shapes.append(jax.ShapeDtypeStruct((2 * lanes,) + blocks.shape[1:], blocks.dtype))
-    sems += 2 * lanes - 1
     out = pl.pallas_call(
-        functools.partial(gather_body, quads, lanes, partners),
+        functools.partial(gather_body, quads, partners),
         out_shape=shapes,
-        in_specs=[pl.BlockSpec(memory_space=pltpu.VMEM)] * len(sources)
-        + [pl.BlockSpec(memory_space=pl.ANY)],
+        in_specs=[pl.BlockSpec(memory_space=pltpu.VMEM)] * len(sources),
         out_specs=[pl.BlockSpec(memory_space=pl.ANY)] * len(shapes),
-        scratch_shapes=[pltpu.VMEM(blocks.shape[1:], blocks.dtype)]
-        + keeps
+        scratch_shapes=keeps
         + [
-            pltpu.SemaphoreType.DMA((total + 2,)),
+            pltpu.SemaphoreType.DMA((total,)),
             pltpu.SemaphoreType.DMA((sems,)),
             pltpu.SemaphoreType.DMA((sems,)),
         ],
         compiler_params=pltpu.CompilerParams(collective_id=number, has_side_effects=True),
         name=name,
-    )(*sources, blocks)
-    return [(out[2 * i], out[2 * i + 1]) for i in range(len(sources))], out[-1]
+    )(*sources)
+    return [(out[2 * i], out[2 * i + 1]) for i in range(len(sources))]
 
 
 def start_body(
@@ -511,7 +492,7 @@
     ahead = 2
     exchanged = []
 
-    def exchange_grads():
+    def exchange_gate():
         lane = lax.axis_index("lane")
         part = down_ref.shape[1] // lanes
         for e in range(down_ref.shape[0]):
@@ -520,13 +501,18 @@
                 src = down_ref.at[e, pl.ds(pl.multiple_of(to * part, part), part)]
                 exchanged.append(go(src, down_out.at[d - 1, e], {"lane": to}))
         for device, place in planes:
-            exchanged.append(go(blocks_ref.at[place], blocks_out.at[me], device))
+            exchanged.append(go(blocks_ref.at[place, 0], blocks_out.at[me, 0], device))
+
+    def exchange_up():
+        for device, place in planes:
+            exchanged.append(go(blocks_ref.at[place, 1], blocks_out.at[me, 1], device))
 
     if extra:
         into = mover.keep(blocks_ref.at[me], held)
+        exchange_gate()
     for n in range(len(order) + 2 * ahead):
         if extra and n == kinds * count + 2 * ahead:
-            exchange_grads()
+            exchange_up()
             into.wait()
             mover.kept = [c for c in mover.kept if c is not into]
             mover.keep(held, blocks_out.at[me])
@@ -569,7 +555,7 @@
         ]
         specs = specs + [anywhere] * 2
         scratch = [pltpu.VMEM(blocks.shape[1:], BF)] + scratch
-        sems += 2 * lanes - 1 + n_exp * (lanes - 1)
+        sems += 2 * (2 * lanes - 1) + n_exp * (lanes - 1)
     return pl.pallas_call(
         functools.partial(scatter_body, quads, lanes, kinds, count, partner, bool(extra)),
         out_shape=shapes,
@@ -722,8 +708,7 @@
     return lax.dot_general(left, right, (((0,), (0,)), ((), ())), preferred_element_type=F32)
 
 
-def expert_body(quads, before, gate_ref, xo_ref, xt_ref, goo_ref, got_ref, gpo_ref, gpt_ref, both_ref,
-                down_ref, *refs):
+def expert_body(quads, before, _, gate_ref, xo_ref, xt_ref, go_ref, gp_ref, both_ref, down_ref, *refs):
     sums = refs[:4] if before else None
     mo_ref, mt_ref, do_ref, dt_ref, dgate_ref, hid_ref, dg_ref, du_ref = refs[-8:]
     t = pl.program_id(0)
@@ -731,9 +716,7 @@
     partner = t % 2 == 1
     hidden, width = down_ref.shape
     x = jnp.where(core_other, xt_ref[0], xo_ref[0]).reshape(-1, width)
-    g_own = jnp.where(partner, gpo_ref[0], goo_ref[0])
-    g_other = jnp.where(partner, gpt_ref[0], got_ref[0])
-    g = jnp.where(core_other, g_other, g_own).reshape(-1, width)
+    g = jnp.where(partner, gp_ref[0], go_ref[0]).reshape(-1, width)
     gate = gate_ref[0]
     wg = both_ref[:, 0].reshape(width, hidden)
     wu = both_ref[:, 1].reshape(width, hidden)
@@ -770,28 +753,25 @@
         dt_ref[0] = d_rows
 
 
-def expert(gates, x_rows, g_rows, both, down, before, name):
+def expert(place, gates, x_rows, g_rows, both, down, before, name):
     quads, shards, rows, width = x_rows[0].shape
     batches = shards // 2
     hidden = down.shape[0]
     tiles = 4 * quads
     tile = batches * rows
 
-    def own(t):
+    def own(t, p):
         return (jnp.minimum(t, 2 * quads - 1) // 2, jnp.minimum(t, 2 * quads - 1) % 2, 0, 0)
 
-    def other(t):
+    def other(t, p):
         u = jnp.maximum(t - 2 * quads, 0)
         return (u // 2, u % 2, 0, 0)
 
-    def own_g(t):
-        return (jnp.minimum(t // 2, quads - 1), 0, 0, 0)
-
-    def other_g(t):
-        return (jnp.maximum(t // 2 - quads, 0), 0, 0, 0)
+    def cot(t, p):
+        return (p[t // 2], 0, 0, 0)
 
     shard_block = (1, batches, rows, width)
-    saved_spec = pl.BlockSpec((1, tile, hidden), lambda t: (t, 0, 0))
+    saved_spec = pl.BlockSpec((1, tile, hidden), lambda t, p: (t, 0, 0))
     saved = jax.ShapeDtypeStruct((tiles, tile, hidden), BF)
     rows_shape = jax.ShapeDtypeStruct(x_rows[0].shape, BF)
     fixed = dict(pipeline_mode=pl.Buffered(1))
@@ -803,30 +783,30 @@
         functools.partial(expert_body, quads, bool(before)),
         out_shape=(rows_shape,) * 4
         + (jax.ShapeDtypeStruct((tiles, tile, 1), F32), saved, saved, saved),
-        grid_spec=pl.GridSpec(
+        grid_spec=pltpu.PrefetchScalarGridSpec(
+            num_scalar_prefetch=1,
             grid=(tiles,),
             in_specs=[
-                pl.BlockSpec((1, tile, 1), lambda t: (t, 0, 0)),
+                pl.BlockSpec((1, tile, 1), lambda t, p: (t, 0, 0)),
                 pl.BlockSpec(shard_block, own),
                 pl.BlockSpec(shard_block, other),
-                pl.BlockSpec(shard_block, own_g), pl.BlockSpec(shard_block, other_g),
-                pl.BlockSpec(shard_block, own_g), pl.BlockSpec(shard_block, other_g),
-                pl.BlockSpec(both.shape, lambda t: (0, 0, 0, 0), **fixed),
-                pl.BlockSpec(down.shape, lambda t: (0, 0), **fixed),
+                pl.BlockSpec(shard_block, cot), pl.BlockSpec(shard_block, cot),
+                pl.BlockSpec(both.shape, lambda t, p: (0, 0, 0, 0), **fixed),
+                pl.BlockSpec(down.shape, lambda t, p: (0, 0), **fixed),
             ]
             + (sums_specs if before else []),
             out_specs=sums_specs
-            + [pl.BlockSpec((1, tile, 1), lambda t: (t, 0, 0)), saved_spec, saved_spec, saved_spec],
+            + [pl.BlockSpec((1, tile, 1), lambda t, p: (t, 0, 0)), saved_spec, saved_spec, saved_spec],
         ),
-        input_output_aliases={9 + i: i for i in range(4)} if before else {},
+        input_output_aliases={8 + i: i for i in range(4)} if before else {},
         compiler_params=pltpu.CompilerParams(
             dimension_semantics=("arbitrary",), vmem_limit_bytes=60 << 20
         ),
         name=name,
-    )(gates, *x_rows, *g_rows, both, down, *before)
-
-
-def grads_body(quads, xo_ref, xt_ref, goo_ref, got_ref, gpo_ref, gpt_ref, hid_ref, dg_ref, du_ref, both_ref, down_ref,
+    )(place, gates, *x_rows, *g_rows, both, down, *before)
+
+
+def grads_body(quads, _, xo_ref, xt_ref, go_ref, gp_ref, hid_ref, dg_ref, du_ref, both_ref, down_ref,
                gate_acc, up_acc, down_acc):
     t = pl.program_id(0)
     width = down_acc.shape[1]
@@ -839,9 +819,7 @@
         down_acc[...] = jnp.zeros_like(down_acc)
 
     x = jnp.where(t >= quads, xt_ref[0], xo_ref[0]).reshape(-1, width)
-    g_own = jnp.where(t >= quads, got_ref[0], goo_ref[0]).reshape(-1, width)
-    g_partner = jnp.where(t >= quads, gpt_ref[0], gpo_ref[0]).reshape(-1, width)
-    g = jnp.concatenate([g_own, g_partner], axis=0)
+    g = jnp.concatenate([go_ref[0].reshape(-1, width), gp_ref[0].reshape(-1, width)], axis=0)
     gate_acc[...] += tn(x, dg_ref[...].reshape(-1, hidden))
     up_acc[...] += tn(x, du_ref[...].reshape(-1, hidden))
     down_acc[...] += tn(hid_ref[...].reshape(-1, hidden), g)
@@ -854,18 +832,21 @@
         down_ref[...] = down_acc[...].astype(BF)
 
 
-def expert_grads(x_rows, g_rows, hid, dg, du, dp, name):
+def expert_grads(place, x_rows, g_rows, hid, dg, du, dp, name):
     quads, shards, rows, width = x_rows[0].shape
     batches = shards // 2
     tiles, tile, hidden = hid.shape
 
-    saved = pl.BlockSpec((2, tile, hidden), lambda t: (t, 0, 0))
-
-    def own(t):
+    saved = pl.BlockSpec((2, tile, hidden), lambda t, p: (t, 0, 0))
+
+    def own(t, p):
         return (jnp.minimum(t, quads - 1), 0, 0, 0)
 
-    def other(t):
+    def other(t, p):
         return (jnp.maximum(t - quads, 0), 0, 0, 0)
+
+    def cot(t, p):
+        return (p[t], 0, 0, 0)
 
     g_block = (1, batches, rows, width)
     return pl.pallas_call(
@@ -874,18 +855,18 @@
             jax.ShapeDtypeStruct((dp, 2, width // dp, hidden), BF),
             jax.ShapeDtypeStruct((hidden, width), BF),
         ),
-        grid_spec=pl.GridSpec(
+        grid_spec=pltpu.PrefetchScalarGridSpec(
+            num_scalar_prefetch=1,
             grid=(tiles // 2,),
             in_specs=[
                 pl.BlockSpec((1, shards, rows, width), own),
                 pl.BlockSpec((1, shards, rows, width), other),
-                pl.BlockSpec(g_block, own), pl.BlockSpec(g_block, other),
-                pl.BlockSpec(g_block, own), pl.BlockSpec(g_block, other),
+                pl.BlockSpec(g_block, cot), pl.BlockSpec(g_block, cot),
                 saved, saved, saved,
             ],
             out_specs=[
-                pl.BlockSpec((dp, 2, width // dp, hidden), lambda t: (0, 0, 0, 0)),
-                pl.BlockSpec((hidden, width), lambda t: (0, 0)),
+                pl.BlockSpec((dp, 2, width // dp, hidden), lambda t, p: (0, 0, 0, 0)),
+                pl.BlockSpec((hidden, width), lambda t, p: (0, 0)),
             ],
             scratch_shapes=[pltpu.VMEM((width, hidden), F32), pltpu.VMEM((width, hidden), F32),
                             pltpu.VMEM((hidden, width), F32)],
@@ -894,7 +875,34 @@
             dimension_semantics=("arbitrary",), vmem_limit_bytes=60 << 20
         ),
         name=name,
-    )(*x_rows, *g_rows, hid, dg, du)
+    )(place, *x_rows, *g_rows, hid, dg, du)
+
+
+def finish_body(lanes, *refs):
+    gate_ref, up_ref = refs[-2:]
+    for e, ref in enumerate(refs[:-2]):
+        for kind, out_ref in enumerate((gate_ref, up_ref)):
+            hidden = ref.shape[3]
+            for h in range(2):
+                total = ref[h * lanes, kind].astype(F32)
+                for l in range(1, lanes):
+                    total = total + ref[h * lanes + l, kind].astype(F32)
+                out_ref[e, :, h * hidden : (h + 1) * hidden] = total
+
+
+def finish_grads(parts):
+    planes, _, depth, hidden = parts[0].shape
+    step = 128
+    shape = jax.ShapeDtypeStruct((len(parts), depth, 2 * hidden), F32)
+    out_spec = pl.BlockSpec((len(parts), step, 2 * hidden), lambda i: (0, i, 0))
+    return pl.pallas_call(
+        functools.partial(finish_body, planes // 2),
+        out_shape=(shape, shape),
+        grid=(depth // step,),
+        in_specs=[pl.BlockSpec((planes, 2, step, hidden), lambda i: (0, 0, i, 0))] * len(parts),
+        out_specs=(out_spec, out_spec),
+        name="finish_gradients",
+    )(*parts)
 
 
 def scatter_all(pairs, partner, name, number, extra=()):
@@ -997,9 +1005,13 @@
         )
         for e in range(local_experts)
     ]
-    both_w = [exchange(jnp.repeat(part, lanes, axis=0), DP) for part in halves[:-1]]
+    halves = [jnp.repeat(part, lanes, axis=0) for part in halves]
+    next_w = exchange(halves[0], DP)
     down_parts = lane_parts(w_down)
-    cot_cross = swap(crossing, "half")
+    g_rows = [
+        lax.all_gather(part, CTX, axis=0, tiled=False)
+        for part in (crossing, swap(crossing, "half"))
+    ]
 
     def places_of(device):
         stored = device * rows + jnp.arange(rows, dtype=jnp.int32)
@@ -1081,26 +1093,31 @@
     gates = (router * routed).transpose(2, 0, 1).reshape(ctx_size, local_experts, batches, rows)
     gates = exchange_rows(gates, "outward", "gates_to_experts", 8, 2)
     gates = gates.transpose(1, 0, 3, 4, 2).reshape(4 * quads, batches * rows, local_experts)
-    (x_rows, cot_rows, cross_rows), last_w = gather_rows(
-        [mixed_in, grad_low, cot_cross], (True, False, False), halves[-1], "gather_mixed", 2
+    gates, mixed_rows = lax.optimization_barrier((gates, mixed_in))
+    x_rows = gather_rows([mixed_rows], (True,), "gather_mixed", 2)[0]
+    number = jnp.arange(2 * quads, dtype=jnp.int32)
+    place = (lax.axis_index("quad") ^ (number % quads)) * 2 + (pair ^ (number // quads))
+    x_rows, next_w, down_parts, halves, gates = lax.optimization_barrier(
+        (x_rows, next_w, down_parts, halves, gates)
     )
-    both_w = both_w + [last_w]
-    g_rows = cot_rows + cross_rows
-    x_rows, both_w, down_parts = lax.optimization_barrier((x_rows, both_w, down_parts))
     down_w = gather_lane(w_down, down_parts).swapaxes(0, 1)
     down_w = down_w.reshape(local_experts, hidden_half, width)
 
     sums = ()
     d_gates, grads_both, grads_down = [], [], []
     for e in range(local_experts):
+        both_w = next_w
+        if e < local_experts - 1:
+            next_w = exchange(halves[e + 1], DP)
         *sums, d_gate, hid, d_gate_pre, d_up_pre = expert(
-            gates[..., e : e + 1], x_rows, g_rows, both_w[e], down_w[e], tuple(sums), f"expert_{e}"
+            place, gates[..., e : e + 1], x_rows, g_rows, both_w, down_w[e], tuple(sums),
+            f"expert_{e}",
         )
         d_gates.append(d_gate)
         grad_both, grad_down = expert_grads(
-            x_rows, g_rows, hid, d_gate_pre, d_up_pre, dp_size, f"expert_grads_{e}"
+            place, x_rows, g_rows, hid, d_gate_pre, d_up_pre, dp_size, f"expert_grads_{e}"
         )
-        sums[0], grad_both = lax.optimization_barrier((sums[0], grad_both))
+        sums[0], grad_both, next_w = lax.optimization_barrier((sums[0], grad_both, next_w))
         grads_both.append(exchange(grad_both, DP) if e < local_experts - 1 else grad_both)
         grads_down.append(grad_down)
     moe_own, moe_other, d_own, d_other = sums
@@ -1130,7 +1147,10 @@
     d_mid, part_mlp_gain = norm_back_all(x_mid, mlp_root, gain_mlp, d_mixed)
     d_mid = d_mid + grad_low.astype(F32)
     d_att_out = d_mid.astype(BF)
+    grad_out = dot("mtd,mte->de", attended, d_att_out).astype(BF)
     d_attended = dot("mte,de->mtd", d_att_out, out_w).astype(BF)
+    d_attended, grad_out = lax.optimization_barrier((d_attended, grad_out))
+    grad_out = lax.psum_scatter(grad_out, ALL, scatter_dimension=0, tiled=True).astype(F32)
     d_attended = d_attended.reshape(batches, rows, ctx_size, head_width).transpose(2, 0, 1, 3)
     d_attended = exchange_rows(d_attended, "outward", "attended_gradients", 10)[0]
     part_query_gain = part_key_gain = 0.0
@@ -1184,18 +1204,14 @@
     d_inputs, part_attn_gain = norm_back_all(inputs, attn_root, gain_attn, d_act)
     mixed = (x_mid + moe_sum).astype(BF)
 
-    grads_both = jnp.stack(grads_both, axis=2).astype(F32)
-    grads_both = grads_both.reshape(2, lanes, 2, local_experts, depth_part, hidden_half).sum(axis=1)
-    grads_both = grads_both.transpose(1, 2, 3, 0, 4)
-    grad_gate, grad_up = grads_both.reshape(2, local_experts, depth_part, hidden_units)
+    grad_gate, grad_up = finish_grads(grads_both)
     grads_down = grads_down.reshape(local_experts, lanes, -1, width)
     grad_down = lax.dynamic_index_in_dim(grads_down, lax.axis_index("lane"), 1, keepdims=False)
     grad_down = grad_down.astype(F32) + jnp.sum(down_others.astype(F32), axis=0)
 
-    grad_out = dot("mtd,mte->de", attended, d_att_out).astype(BF)
-    grad_out = lax.psum_scatter(grad_out, ALL, scatter_dimension=0, tiled=True).astype(F32)
     acts = [part.reshape(-1, width) for part in act]
     grad_qkv = sum(dot("td,te->de", x, y) for x, y in zip(acts, d_pre)).astype(BF)
+    grad_qkv, grad_out = lax.optimization_barrier((grad_qkv, grad_out))
     grad_qkv = lax.psum_scatter(grad_qkv, DP, scatter_dimension=0, tiled=True)
     grad_qkv = grad_qkv.reshape(ctx_size, shard, 3 * head_width)
     grad_qkv = exchange_rows(grad_qkv, "ctx", "qkv_gradients", 14).astype(F32)

time: 1280 us -> 1140 us (0.89)
  Pallas kernels: 919 us -> 792 us
  local copies, waits for them, and re-layouts: 114 us -> 88 us
  waiting for transfers between devices: 25 us -> 42 us
    pallas_call x2, Pallas kernels: 330 us -> 252 us  [scatter_rows(): pl.pallas_call(functools.partial(scatter_body, quads, lanes, kinds, count...]
    pallas_call x1 -> x2, Pallas kernels: 151 us -> 96.6 us  [the longest x1 89.3 us: gather_rows(): pl.pallas_call(functools.partial(gather_body, quads, partners), out_shape...]
    another operation x3 -> x0, local copies, waits for them, and re-layouts: 18.3 us -> none  [on_device(): grad_gate, grad_up = grads_both.reshape(2, local_experts, depth_part, hid...]
    reduce_scatter x1, waiting for transfers between devices: 24.9 us -> 41.9 us  [on_device(): lax.psum_scatter(grad_out, ALL, scatter_dimension=0, tiled=True).astype(F32)]
    unnamed x137 -> x159, local copies, waits for them, and re-layouts: 26.6 us -> 15.5 us
  transfers between devices with their start and end apart: 6 -> 9, of which waited for: 1 -> 1; matrix products, arithmetic and copies ran while one was open for 15% -> 19% of each run, Pallas kernels for 32% -> 39%
where the time goes in v4:
time: 1140 us; the launch traced here: 1130 us
  Pallas kernels  792 us (69%)
  matrix products  89.3 us (8%)
  local copies, waits for them, and re-layouts  88 us (8%)
  other arithmetic  87.5 us (8%)
  waiting for transfers between devices  42 us (4%)
  starting transfers between devices  18.4 us (2%)
  between operations  15.6 us (1%)
    pallas_call x2, Pallas kernels, scatter_rows(): pl.pallas_call(functools.partial(scatter_body, quads, lanes, kinds, count...  252 us
    pallas_call x2, Pallas kernels, expert(): pl.pallas_call(functools.partial(expert_body, quads, bool(before)), out_s...  143 us
    pallas_call x1, Pallas kernels, start_gather(): pl.pallas_call(functools.partial(start_body, quads, lanes), out_shape=[li...  110 us
    pallas_call x6, Pallas kernels, exchange_rows(): pl.pallas_call(functools.partial(exchange_body, mode, lanes, quads, halve...  98.4 us
    pallas_call x1, Pallas kernels, gather_rows(): pl.pallas_call(functools.partial(gather_body, quads, partners), out_shape...  89.3 us
    dot_general x21, matrix products, dot(): return jnp.einsum(spec, left, right, preferred_element_type=F32)  74.8 us
    pallas_call x2, Pallas kernels, expert_grads(): pl.pallas_call(functools.partial(grads_body, quads), out_shape=(jax.Shape...  74.7 us
    reduce_scatter x1, waiting for transfers between devices, on_device(): lax.psum_scatter(grad_out, ALL, scatter_dimension=0, tiled=True).astype(F32)  41.9 us
  transfers between devices with their start and end apart: 9, of which 1 were waited for; matrix products, arithmetic and copies ran while one was open for 19% of the time, Pallas kernels for 39%

profile of v4, /device:TPU:0, one launch (start us, length us, event | category | flops | bytes accessed | tf_op | source)
XLA Modules:
  0.0 1132.4 jit_solution(9691200007578750185)
XLA Ops:
  19.2 109.7 %start_gather.1 = (bf16[4,2,128,2048]{3,2,1,0:T(8,128)(2,1)}, bf16[4,2,128,2048]{3,2,1,0:T(8,128)(2,1)}, bf16[4,8,64,768]{3,2,1,0:T(8,128)(2,1)}, bf16[32,1,1280]{2,1,0:T(2,128)(2,1)}, bf16[4,8,64,2048]{3,2,1,0:T(8,128)(2,1)}) custom-call(bf16[2,128,2048]{2,1,0:T(8,128)(2,1)} %bitcast.267, bf16[8,64,768]{2,1,0:T(8,128)(2,1)} %reshape.866.qkv_ref, ...), custom_call_target="tpu_custom_call" | custom-call | tf_op jit(solution)/shard_map/start_gather/pallas_call | solution.py:374
  143.0 5.3 fusion.3
  160.8 9.3 sum_squares.1
  214.6 7.3 fusion.119
  226.7 5.3 fusion.118
  237.8 17.8 %attended_to_rows.1 = bf16[1,8,2,128,256]{4,3,2,1,0:T(8,128)(2,1)} custom-call(bf16[1,8,2,128,256]{4,3,2,1,0:T(8,128)(2,1)} %maximum_bitcast_fusion.2.x_ref), custom_call_target="tpu_custom_call" | custom-call | tf_op jit(solution)/shard_map/attended_to_rows/pallas_call | solution.py:644
  257.9 6.2 multiply_reduce_fusion.4
  266.8 8.2 gates_to_experts.1
  277.8 89.3 %gather_mixed.1 = (bf16[4,4,128,2048]{3,2,1,0:T(8,128)(2,1)}, bf16[4,4,128,2048]{3,2,1,0:T(8,128)(2,1)}) custom-call(bf16[2,128,2048]{2,1,0:T(8,128)(2,1)} %copy-done.11), custom_call_target="tpu_custom_call" | custom-call | tf_op jit(solution)/shard_map/gather_mixed/pallas_call | solution.py:270
  390.1 70.4 %expert_0.1 = (bf16[4,4,128,2048]{3,2,1,0:T(8,128)(2,1)}, bf16[4,4,128,2048]{3,2,1,0:T(8,128)(2,1)}, bf16[4,4,128,2048]{3,2,1,0:T(8,128)(2,1)}, bf16[4,4,128,204...) custom-call(s32[8]{0:T(128)} %fusion.98._, ...), custom_call_target="tpu_custom_call" | custom-call | tf_op jit(solution)/shard_map/expert_0/pallas_call | solution.py:782
  460.5 37.3 %expert_grads_0.1 = (bf16[4,2,512,512]{3,2,1,0:T(8,128)(2,1)}, bf16[512,2048]{1,0:T(8,128)(2,1)}) custom-call(s32[8]{0:T(128)} %fusion.98._, bf16[4,4,128,2048]{3,2,1,0:T(8,128)(2,1)} %get-tuple-element.90.xo_ref, bf16[4,4,128,2048]{3,2,1,0:T(8,128)(2,1)} %get-tuple-element.91.xt_ref, bf16[8,2,128,2048]{3,2,1,0:T(8,128)(2,1)} %bitcast.252, ...), custom_call_target="tpu_custom_call" | custom-call | tf_op jit(solution)/shard_map/expert_grads_0/pallas_call | solution.py:852
  505.1 72.9 %expert_1.1 = (bf16[4,4,128,2048]{3,2,1,0:T(8,128)(2,1)}, bf16[4,4,128,2048]{3,2,1,0:T(8,128)(2,1)}, bf16[4,4,128,2048]{3,2,1,0:T(8,128)(2,1)}, bf16[4,4,128,204...) custom-call(s32[8]{0:T(128)} %fusion.98._, ...), custom_call_target="tpu_custom_call", output_to_operand_aliasing={{0}: (8, {}), {1}: (9, {}), {2}: (10, {}), {3}: (11, {})} | custom-call | tf_op jit(solution)/shard_map/expert_1/pallas_call | solution.py:782
  578.0 37.4 %expert_grads_1.1 = (bf16[4,2,512,512]{3,2,1,0:T(8,128)(2,1)}, bf16[512,2048]{1,0:T(8,128)(2,1)}) custom-call(s32[8]{0:T(128)} %fusion.98._, bf16[4,4,128,2048]{3,2,1,0:T(8,128)(2,1)} %get-tuple-element.90.xo_ref, bf16[4,4,128,2048]{3,2,1,0:T(8,128)(2,1)} %get-tuple-element.91.xt_ref, bf16[8,2,128,2048]{3,2,1,0:T(8,128)(2,1)} %bitcast.254, ...), custom_call_target="tpu_custom_call" | custom-call | tf_op jit(solution)/shard_map/expert_grads_1/pallas_call | solution.py:852
  622.9 211.5 %scatter_experts.1 = (f32[2,128,2048]{2,1,0:T(8,128)}, f32[2,128,2048]{2,1,0:T(8,128)}, bf16[4,2,512,512]{3,2,1,0:T(8,128)(2,1)}, bf16[1,2,256,2048]{3,2,1,0:T(8,128)(2,1)}) custom-call(bf16[4,4,128,2048]{3,2,1,0:T(8,128)(2,1)} %get-tuple-element.116.refs_0_, bf16[4,4,128,2048]{3,2,1,0:T(8,128)(2,1)} %get-tuple-element.117.refs_1_, ...), custom_call_target="tpu_custom_call" | custom-call | tf_op jit(solution)/shard_map/scatter_experts/pallas_call | solution.py:559
  834.4 18.0 %gate_gradients.1 = f32[2,8,2,2,128]{4,3,2,1,0:T(2,128)} custom-call(f32[2,8,2,2,128]{4,3,2,1,0:T(2,128)} %bitcast.340), custom_call_target="tpu_custom_call" | custom-call | tf_op jit(solution)/shard_map/gate_gradients/pallas_call | solution.py:644
  868.7 28.8 %attended_gradients.1 = bf16[1,8,2,128,256]{4,3,2,1,0:T(8,128)(2,1)} custom-call(bf16[8,2,128,256]{3,2,1,0:T(8,128)(2,1)} %bitcast.307), custom_call_target="tpu_custom_call" | custom-call | tf_op jit(solution)/shard_map/attended_gradients/pallas_call | solution.py:644
  948.3 7.9 sum_inner.1
  968.4 5.4 add_convert_fusion
  973.8 41.9 %reduce-scatter.3.cloned.1.call-done = bf16[64,2048]{1,0:T(8,128)(2,1)} async-done(((bf16[2048,2048]{1,0:T(8,128)(2,1)}), bf16[64,2048]{1,0:T(8,128)(2,1)}) %reduce-scatter.3.cloned.1.call-update) | async-done | bytes 262160 | tf_op jit(solution)/shard_map/reduce_scatter | solution.py:1153
  1019.0 8.0 convolution_convert_fusion
  1032.0 40.2 %scatter_act.1 = f32[2,128,2048]{2,1,0:T(8,128)} custom-call(bf16[4,2,128,2048]{3,2,1,0:T(8,128)(2,1)} %bitcast.303, bf16[4,2,128,2048]{3,2,1,0:T(8,128)(2,1)} %bitcast.302), custom_call_target="tpu_custom_call" | custom-call | tf_op jit(solution)/shard_map/scatter_act/pallas_call | solution.py:559
  1075.6 11.4 %small_gradients.1 = f32[32,1,1280]{2,1,0:T(1,128)} custom-call(f32[32,1,1280]{2,1,0:T(1,128)} %pad_maximum_fusion.8.x_ref), custom_call_target="tpu_custom_call" | custom-call | tf_op jit(solution)/shard_map/small_gradients/pallas_call | solution.py:644
  1088.8 7.3 finish_gradients.1
  1103.4 14.2 %qkv_gradients.1 = bf16[8,64,768]{2,1,0:T(8,128)(2,1)} custom-call(bf16[8,64,768]{2,1,0:T(8,128)(2,1)} %bitcast.320), custom_call_target="tpu_custom_call" | custom-call | tf_op jit(solution)/shard_map/qkv_gradients/pallas_call | solution.py:644
  (361 shorter events, 245.8 us)
Async XLA Ops:
  7.2 382.9 %all-gather.5.cloned.1.call-start = ((), (), s32[]{:S(2)}) async-start(), calls=%async_computation.7 | async-start | bytes 9437184 | tf_op jit(solution)/shard_map/all_gather | solution.py:1012
  17.5 114.4 %copy-start.36 = (bf16[2,512,1024]{2,1,0:T(8,128)(2,1)S(1)}, bf16[2,512,1024]{2,1,0:T(8,128)(2,1)}, u32[]{:S(2)}) copy-start(bf16[2,512,1024]{2,1,0:T(8,128)(2,1)} %param.27) | copy-start | bytes 6291460
  129.0 60.5 %collective-permute-start.1 = (bf16[2,128,2048]{2,1,0:T(8,128)(2,1)}, bf16[2,128,2048]{2,1,0:T(8,128)(2,1)}, u32[]{:S(2)}, u32[]{:S(2)}) collective-permute-start(bf16[2,128,2048]{2,1,0:T(8,128)(2,1)} %bitcast.2), channel_id=1, source_target_pairs={{0,16},{16,0},{1,17},{17,1},{2,18},{18,2},{3,19},{19,3},{4,20},{20... | collective-permute-start | bytes 3145736 | tf_op jit(solution)/shard_map/ppermute | solution.py:62
  129.2 242.0 %collective-permute-start = (bf16[2,256,2048]{2,1,0:T(8,128)(2,1)}, bf16[2,256,2048]{2,1,0:T(8,128)(2,1)}, u32[]{:S(2)}, u32[]{:S(2)}) collective-permute-start(bf16[2,256,2048]{2,1,0:T(8,128)(2,1)} %param.29), channel_id=1, source_target_pairs={{0,8},{8,0},{1,9},{9,1},{2,10},{10,2},{3,11},{11,3},{4,12},{12,4},... | collective-permute-start | bytes 6291464 | tf_op jit(solution)/shard_map/ppermute | solution.py:62
  137.8 233.5 %all-to-all-start = ((bf16[4,2,512,512]{3,2,1,0:T(8,128)(2,1)}), bf16[4,2,512,512]{3,2,1,0:T(8,128)(2,1)}, u32[]{:S(2)}, u32[]{:S(2)}) async-start(bf16[4,2,512,512]{3,2,1,0:T(8,128)(2,1)} %bitcast.269), calls=%async_computation | async-start | bytes 8388608 | tf_op jit(solution)/shard_map/all_to_all | solution.py:66
  142.8 247.3 %all-gather.7.cloned.1.call-start = ((), (), s32[]{:S(2)}) async-start(), calls=%async_computation.8 | async-start | bytes 9437184 | tf_op jit(solution)/shard_map/all_gather | solution.py:1012
  158.5 11.7 %copy-start.67 = (s32[16]{0:T(128)S(1)}, s32[16]{0:T(128)}, u32[]{:S(2)}) copy-start(s32[16]{0:T(128)} %param.21) | copy-start | bytes 196
  175.1 28.3 %copy-start = (f32[2,4,1,128,768]{4,3,2,1,0:T(8,128)}, f32[2,4,1,128,768]{4,3,2,1,0:T(8,128)S(1)}, u32[]{:S(2)}) copy-start(f32[2,4,1,128,768]{4,3,2,1,0:T(8,128)S(1)} %get-tuple-element.235) | copy-start | bytes 9437188
  214.6 12.1 %copy-start.21 = (bf16[1024,2,128]{0,2,1:T(8,128)(2,1)}, bf16[1024,2,128]{0,2,1:T(8,128)(2,1)S(1)}, u32[]{:S(2)}) copy-start(bf16[1024,2,128]{0,2,1:T(8,128)(2,1)S(1)} %get-tuple-element.277) | copy-start | bytes 1572868
  214.6 12.1 %copy-start.40 = (bf16[1024,2,128]{0,2,1:T(8,128)(2,1)}, bf16[1024,2,128]{0,2,1:T(8,128)(2,1)S(1)}, u32[]{:S(2)}) copy-start(bf16[1024,2,128]{0,2,1:T(8,128)(2,1)S(1)} %get-tuple-element.276) | copy-start | bytes 1572868
  236.7 21.2 %copy-start.65 = (s32[2,1,128,8]{2,3,1,0:T(8,128)S(1)}, s32[2,1,128,8]{2,3,1,0:T(8,128)}, u32[]{:S(2)}) copy-start(s32[2,1,128,8]{2,3,1,0:T(8,128)} %param.19) | copy-start | bytes 24580
  236.7 21.2 %copy-start.3 = (bf16[2,1,128,2048]{3,2,1,0:T(8,128)(2,1)S(1)}, bf16[2,1,128,2048]{3,2,1,0:T(8,128)(2,1)}, u32[]{:S(2)}) copy-start(bf16[2,1,128,2048]{3,2,1,0:T(8,128)(2,1)} %param.17) | copy-start | bytes 3145732
  264.4 13.5 %copy-start.11 = (bf16[2,128,2048]{2,1,0:T(8,128)(2,1)}, bf16[2,128,2048]{2,1,0:T(8,128)(2,1)S(1)}, u32[]{:S(2)}) copy-start(bf16[2,128,2048]{2,1,0:T(8,128)(2,1)S(1)} %multiply_convert_fusion.2.refs_0_) | copy-start | bytes 3145732
  375.2 122.6 %all-to-all-start.1 = ((bf16[4,2,512,512]{3,2,1,0:T(8,128)(2,1)}), bf16[4,2,512,512]{3,2,1,0:T(8,128)(2,1)}, u32[]{:S(2)}, u32[]{:S(2)}) async-start(bf16[4,2,512,512]{3,2,1,0:T(8,128)(2,1)} %bitcast.270), calls=%async_computation.1 | async-start | bytes 8388608 | tf_op jit(solution)/shard_map/all_to_all | solution.py:66
  497.8 120.5 %all-to-all-start.2 = ((bf16[4,2,512,512]{3,2,1,0:T(8,128)(2,1)}), bf16[4,2,512,512]{3,2,1,0:T(8,128)(2,1)}, u32[]{:S(2)}, u32[]{:S(2)}) async-start(bf16[4,2,512,512]{3,2,1,0:T(8,128)(2,1)} %get-tuple-element.107), calls=%async_computation.2 | async-start | bytes 8388608 | tf_op jit(solution)/shard_map/all_to_all | solution.py:66
  502.9 512.8 %reduce-scatter.3.cloned.1.call-start = ((), (), s32[]{:S(2)}) async-start(), calls=%async_computation.5 | async-start | bytes 8650752 | tf_op jit(solution)/shard_map/reduce_scatter | solution.py:1153
  622.9 230.4 %copy-start.24 = (bf16[2048,16]{1,0:T(8,128)(2,1)S(1)}, bf16[2048,16]{1,0:T(8,128)(2,1)}, u32[]{:S(2)}) copy-start(bf16[2048,16]{1,0:T(8,128)(2,1)} %reshape.882) | copy-start | bytes 196612
  866.1 237.3 %reduce-scatter.5.cloned.1.call-start = ((), (), s32[]{:S(2)}) async-start(), calls=%async_computation.6 | async-start | bytes 3932160 | tf_op jit(solution)/shard_map/reduce_scatter | solution.py:1215
  912.0 12.1 %slice-start.2 = ((s8[8388608]{0:T(1024)(128)(4,1)}), s8[4194304]{0:T(1024)(128)(4,1)S(1)}, s32[]{:S(2)}) async-start(s8[8388608]{0:T(1024)(128)(4,1)} %bitcast.285), calls=%async_computation.11 | async-start | bytes 8388608
  973.8 43.8 %copy-start.4 = (bf16[2,1,128,2048]{3,2,1,0:T(8,128)(2,1)S(1)}, bf16[2,1,128,2048]{3,2,1,0:T(8,128)(2,1)}, u32[]{:S(2)}) copy-start(bf16[2,1,128,2048]{3,2,1,0:T(8,128)(2,1)} %param.17) | copy-start | bytes 3145732
  973.8 44.1 %copy-start.12 = (bf16[2,128,2048]{2,1,0:T(8,128)(2,1)S(1)}, bf16[2,128,2048]{2,1,0:T(8,128)(2,1)}, u32[]{:S(2)}) copy-start(bf16[2,128,2048]{2,1,0:T(8,128)(2,1)} %copy-done.11) | copy-start | bytes 3145732
  1019.0 8.0 copy-start.43
  1019.0 8.0 copy-start.69
  1032.0 40.2 %copy-start.52 = (f32[2048]{0:T(1024)S(1)}, f32[2048]{0:T(1024)}, u32[]{:S(2)}) copy-start(f32[2048]{0:T(1024)} %copy-done.51) | copy-start | bytes 24580
  (59 other events, 246.6 us)
Sparse Core Ops, SparseCore 0:
  129.1 56.2 all-gather.4
  189.6 54.9 all-gather.6
  866.2 149.4 reduce-scatter.2
  1017.8 58.0 reduce-scatter.4

commit v5 on v4

--- a/solution.py
+++ b/solution.py
@@ -42,20 +42,6 @@
     turning = places.astype(F32)[:, None] * freqs[None, :]
     turning = jnp.concatenate([turning, turning], axis=1)
     return (jnp.cos(turning)[:, None, :], jnp.sin(turning)[:, None, :])
-
-
-def rotate(values, cosine, sine):
-    half_size = values.shape[-1] // 2
-    turned = jnp.concatenate([-values[..., half_size:], values[..., :half_size]], axis=-1)
-    return values * cosine + turned * sine
-
-
-def rotate_back(grad_in, cosine, sine):
-    half_size = grad_in.shape[-1] // 2
-    moved = grad_in * sine
-    return grad_in * cosine + jnp.concatenate(
-        [moved[..., half_size:], -moved[..., :half_size]], axis=-1
-    )
 
 
 def swap(values, axis):
@@ -214,7 +200,7 @@
     refs = refs[2 * len(partners) :]
     keeps = {}
     for i, partner in enumerate(partners):
-        if partner:
+        if partner != "own":
             keeps[i], refs = refs[0], refs[1:]
     local, send, recv = refs
     mover = Mover(send, recv, local)
@@ -241,6 +227,8 @@
         mover.go(*crossing[i])
     plans = []
     for i, ref in enumerate(inputs):
+        if partners[i] == "partner":
+            continue
         plans += add([ref.at[s] for s in range(ref.shape[0])], i, 0)
     for p in plans:
         p.forward()
@@ -248,7 +236,8 @@
     for i, keep in keeps.items():
         for c in crossing[i]:
             c.wait_recv()
-        late += add([keep.at[s] for s in range(keep.shape[0])], i, keep.shape[0])
+        offset = keep.shape[0] if partners[i] == "both" else 0
+        late += add([keep.at[s] for s in range(keep.shape[0])], i, offset)
     for p in late:
         p.forward()
     for p in plans + late:
@@ -261,11 +250,11 @@
     shapes, keeps = [], []
     sems = total = 0
     for x, partner in zip(sources, partners):
-        count = x.shape[0] * (2 if partner else 1)
+        count = x.shape[0] * (2 if partner == "both" else 1)
         total += count
-        sems += count * Spread.count(quads) + (x.shape[0] if partner else 0)
+        sems += count * Spread.count(quads) + (x.shape[0] if partner != "own" else 0)
         shapes += [jax.ShapeDtypeStruct((quads, count) + x.shape[1:], x.dtype)] * 2
-        if partner:
+        if partner != "own":
             keeps.append(pltpu.VMEM(x.shape, x.dtype))
     out = pl.pallas_call(
         functools.partial(gather_body, quads, partners),
@@ -312,8 +301,8 @@
         mover.go(first, *rest)
         return first, rest, then
 
-    mover.keep(wout_ref, wout_out.at[plane, here])
-    w_first, w_rest, w_then = planes(wout_ref, lambda p: wout_out.at[p, here])
+    mover.keep(wout_ref, wout_out.at[plane])
+    w_first, w_rest, w_then = planes(wout_ref, lambda p: wout_out.at[p])
     kept = mover.keep(qkv_ref.at[here], qkv_out.at[plane, here])
     columns = []
     for n in range(1, 2 * quads):
@@ -333,30 +322,14 @@
     q_first, q_rest, q_then = planes(qkv_out.at[plane], lambda p: qkv_out.at[p])
     w_first.wait_recv()
     mover.go(*w_then)
-
-    def wout_slots(p):
-        pair = lax.axis_index("pair")
-        quad = lax.axis_index("quad")
-        return lambda core, kr, km: wout_out.at[p, toggled(quad, km) * 2 + pair]
-
-    weights = [Spread(mover, quads, wout_ref, wout_slots(plane))]
-    weights[0].begin()
     tokens[0].forward()
-    for c in w_rest:
-        c.wait_recv()
-    for c in w_then:
-        c.wait_recv()
-    for n in range(1, 2 * lanes):
-        p = toggled(half, n // lanes) * lanes + toggled(lane, n % lanes)
-        weights.append(Spread(mover, quads, wout_out.at[p, here], wout_slots(p)))
-        weights[-1].begin()
     q_first.wait_recv()
     mover.go(*q_then)
-    for p in tokens[1:] + weights:
+    for p in tokens[1:]:
         p.forward()
-    for p in tokens + weights:
+    for p in tokens:
         p.arrive()
-    for c in shared + q_rest + q_then:
+    for c in shared + q_rest + q_then + w_rest + w_then:
         c.wait_recv()
     mover.finish()
 
@@ -370,12 +343,11 @@
         return jax.ShapeDtypeStruct(lead + x.shape, dtype)
 
     sems = (devices - 1) + 2 * (2 * lanes - 1) + (2 * quads - 1)
-    sems += Spread.count(quads) * (count + planes)
+    sems += Spread.count(quads) * count
     return pl.pallas_call(
         functools.partial(start_body, quads, lanes),
         out_shape=[like((quads,), tokens)] * 2
-        + [like((planes,), qkv), like((devices,), small)]
-        + [like((planes, 2 * quads), w_out)],
+        + [like((planes,), qkv), like((devices,), small), like((planes,), w_out)],
         in_specs=[pl.BlockSpec(memory_space=pltpu.VMEM)] * 4,
         out_specs=[pl.BlockSpec(memory_space=pl.ANY)] * 5,
         scratch_shapes=[
@@ -401,21 +373,22 @@
         out_ref[part] = total.astype(out_ref.dtype)
 
 
-def scatter_body(quads, lanes, kinds, count, partner, extra, *refs):
+def scatter_body(quads, lanes, partners, count, extra, *refs):
+    kinds = len(partners)
     inputs = [(refs[2 * i], refs[2 * i + 1]) for i in range(kinds)]
     refs = refs[2 * kinds :]
     if extra:
-        blocks_ref, down_ref, *refs = refs
+        blocks_ref, *refs = refs
     outputs, refs = refs[:kinds], refs[kinds:]
     if extra:
-        blocks_out, down_out, held, *refs = refs
+        blocks_out, held, *refs = refs
     mine, theirs, relay, arrived, *rest = refs
-    if partner:
+    if any(partners):
         summed, back, *rest = rest
     local, send, recv = rest
     mover = Mover(send, recv, local)
     mover.local_number = local.shape[0] - 2
-    total, rows = inputs[0][0].shape[1:3]
+    rows = inputs[0][0].shape[2]
     first, second = pl.ds(0, rows // 2), pl.ds(rows // 2, rows // 2)
     quad = lax.axis_index("quad")
     to_quad = [{"quad": toggled(quad, k)} for k in range(quads)]
@@ -425,7 +398,7 @@
     if extra:
         me, planes = planes_of(lanes)
         peers += [device for device, _ in planes]
-    elif partner:
+    elif any(partners):
         peers.append(across)
     greet(peers)
 
@@ -434,7 +407,7 @@
         mover.go(c)
         return c
 
-    order = [(i, s) for i in range(kinds) for s in range(count, total)]
+    order = [(i, s) for i in range(kinds) if partners[i] for s in range(count, 2 * count)]
     order += [(i, s) for i in range(kinds) for s in range(count)]
     ks = [3, 1, 2, 0] if quads == 4 else list(range(quads - 1, -1, -1))
     sib, loc = {}, {}
@@ -484,7 +457,7 @@
             add_rows(summed.at[slot], *parts)
             backs[slot] = go(summed.at[slot], back.at[slot], across)
         else:
-            if partner:
+            if partners[i]:
                 backs[i * count + s].wait_recv()
                 parts.append(back.at[i * count + s])
             add_rows(outputs[i].at[s], *parts)
@@ -492,27 +465,12 @@
     ahead = 2
     exchanged = []
 
-    def exchange_gate():
-        lane = lax.axis_index("lane")
-        part = down_ref.shape[1] // lanes
-        for e in range(down_ref.shape[0]):
-            for d in range(1, lanes):
-                to = toggled(lane, d)
-                src = down_ref.at[e, pl.ds(pl.multiple_of(to * part, part), part)]
-                exchanged.append(go(src, down_out.at[d - 1, e], {"lane": to}))
-        for device, place in planes:
-            exchanged.append(go(blocks_ref.at[place, 0], blocks_out.at[me, 0], device))
-
-    def exchange_up():
-        for device, place in planes:
-            exchanged.append(go(blocks_ref.at[place, 1], blocks_out.at[me, 1], device))
-
     if extra:
         into = mover.keep(blocks_ref.at[me], held)
-        exchange_gate()
+        for device, place in planes:
+            exchanged.append(go(blocks_ref.at[place], blocks_out.at[me], device))
     for n in range(len(order) + 2 * ahead):
-        if extra and n == kinds * count + 2 * ahead:
-            exchange_up()
+        if extra and n == 1:
             into.wait()
             mover.kept = [c for c in mover.kept if c is not into]
             mover.keep(held, blocks_out.at[me])
@@ -527,37 +485,33 @@
     mover.finish()
 
 
-def scatter_rows(pairs, partner, name, number, extra=()):
+def scatter_rows(pairs, partners, name, number, extra=()):
     lanes = lax.axis_size("lane")
-    quads, total, rows, width = pairs[0][0].shape
-    count = total // 2 if partner else total
+    quads, _, rows, width = pairs[0][0].shape
+    shards = sum(own.shape[1] for own, _ in pairs)
     kinds = len(pairs)
-    shards = kinds * total
+    count = shards // sum(2 if partner else 1 for partner in partners)
     incoming = 2 if quads == 4 else quads - 1
-    sems = shards * (quads + (6 if quads == 4 else quads - 1)) + (kinds * count if partner else 0)
+    sems = shards * (quads + (6 if quads == 4 else quads - 1)) + count * sum(partners)
 
     def buf(*lead):
         return pltpu.VMEM(lead + (rows, width), BF)
 
     scratch = [buf(shards, quads), buf(shards, quads)]
     scratch += [pltpu.VMEM((shards, 2, rows // 2, width), BF), buf(shards, incoming)]
-    if partner:
+    if any(partners):
         scratch += [buf(kinds * count), buf(kinds * count)]
     shapes = [jax.ShapeDtypeStruct((count, rows, width), F32)] * kinds
     specs = [pl.BlockSpec(memory_space=pltpu.VMEM)] * kinds
     anywhere = pl.BlockSpec(memory_space=pl.ANY)
     if extra:
-        blocks, down = extra
-        n_exp, hidden = down.shape[:2]
-        shapes = shapes + [
-            jax.ShapeDtypeStruct(blocks.shape, BF),
-            jax.ShapeDtypeStruct((lanes - 1, n_exp, hidden // lanes, width), BF),
-        ]
-        specs = specs + [anywhere] * 2
+        blocks = extra[0]
+        shapes = shapes + [jax.ShapeDtypeStruct(blocks.shape, BF)]
+        specs = specs + [anywhere]
         scratch = [pltpu.VMEM(blocks.shape[1:], BF)] + scratch
-        sems += 2 * (2 * lanes - 1) + n_exp * (lanes - 1)
+        sems += 2 * lanes - 1
     return pl.pallas_call(
-        functools.partial(scatter_body, quads, lanes, kinds, count, partner, bool(extra)),
+        functools.partial(scatter_body, quads, lanes, partners, count, bool(extra)),
         out_shape=shapes,
         in_specs=[anywhere] * (2 * kinds + len(extra)),
         out_specs=specs,
@@ -708,7 +662,8 @@
     return lax.dot_general(left, right, (((0,), (0,)), ((), ())), preferred_element_type=F32)
 
 
-def expert_body(quads, before, _, gate_ref, xo_ref, xt_ref, go_ref, gp_ref, both_ref, down_ref, *refs):
+def expert_body(quads, before, _, gate_ref, xo_ref, xt_ref, go_ref, gpo_ref, gpt_ref, both_ref,
+                down_ref, *refs):
     sums = refs[:4] if before else None
     mo_ref, mt_ref, do_ref, dt_ref, dgate_ref, hid_ref, dg_ref, du_ref = refs[-8:]
     t = pl.program_id(0)
@@ -716,7 +671,8 @@
     partner = t % 2 == 1
     hidden, width = down_ref.shape
     x = jnp.where(core_other, xt_ref[0], xo_ref[0]).reshape(-1, width)
-    g = jnp.where(partner, gp_ref[0], go_ref[0]).reshape(-1, width)
+    g_partner = jnp.where(core_other, gpt_ref[0], gpo_ref[0])
+    g = jnp.where(partner, g_partner, go_ref[0]).reshape(-1, width)
     gate = gate_ref[0]
     wg = both_ref[:, 0].reshape(width, hidden)
     wu = both_ref[:, 1].reshape(width, hidden)
@@ -770,6 +726,12 @@
     def cot(t, p):
         return (p[t // 2], 0, 0, 0)
 
+    def own_g(t, p):
+        return (jnp.minimum(t // 2, quads - 1), 0, 0, 0)
+
+    def other_g(t, p):
+        return (jnp.maximum(t // 2 - quads, 0), 0, 0, 0)
+
     shard_block = (1, batches, rows, width)
     saved_spec = pl.BlockSpec((1, tile, hidden), lambda t, p: (t, 0, 0))
     saved = jax.ShapeDtypeStruct((tiles, tile, hidden), BF)
@@ -790,7 +752,8 @@
                 pl.BlockSpec((1, tile, 1), lambda t, p: (t, 0, 0)),
                 pl.BlockSpec(shard_block, own),
                 pl.BlockSpec(shard_block, other),
-                pl.BlockSpec(shard_block, cot), pl.BlockSpec(shard_block, cot),
+                pl.BlockSpec(shard_block, cot),
+                pl.BlockSpec(shard_block, own_g), pl.BlockSpec(shard_block, other_g),
                 pl.BlockSpec(both.shape, lambda t, p: (0, 0, 0, 0), **fixed),
                 pl.BlockSpec(down.shape, lambda t, p: (0, 0), **fixed),
             ]
@@ -798,7 +761,7 @@
             out_specs=sums_specs
             + [pl.BlockSpec((1, tile, 1), lambda t, p: (t, 0, 0)), saved_spec, saved_spec, saved_spec],
         ),
-        input_output_aliases={8 + i: i for i in range(4)} if before else {},
+        input_output_aliases={9 + i: i for i in range(4)} if before else {},
         compiler_params=pltpu.CompilerParams(
             dimension_semantics=("arbitrary",), vmem_limit_bytes=60 << 20
         ),
@@ -806,7 +769,7 @@
     )(place, gates, *x_rows, *g_rows, both, down, *before)
 
 
-def grads_body(quads, _, xo_ref, xt_ref, go_ref, gp_ref, hid_ref, dg_ref, du_ref, both_ref, down_ref,
+def grads_body(quads, _, xo_ref, xt_ref, go_ref, gpo_ref, gpt_ref, hid_ref, dg_ref, du_ref, both_ref, down_ref,
                gate_acc, up_acc, down_acc):
     t = pl.program_id(0)
     width = down_acc.shape[1]
@@ -819,7 +782,8 @@
         down_acc[...] = jnp.zeros_like(down_acc)
 
     x = jnp.where(t >= quads, xt_ref[0], xo_ref[0]).reshape(-1, width)
-    g = jnp.concatenate([go_ref[0].reshape(-1, width), gp_ref[0].reshape(-1, width)], axis=0)
+    g_partner = jnp.where(t >= quads, gpt_ref[0], gpo_ref[0]).reshape(-1, width)
+    g = jnp.concatenate([go_ref[0].reshape(-1, width), g_partner], axis=0)
     gate_acc[...] += tn(x, dg_ref[...].reshape(-1, hidden))
     up_acc[...] += tn(x, du_ref[...].reshape(-1, hidden))
     down_acc[...] += tn(hid_ref[...].reshape(-1, hidden), g)
@@ -861,7 +825,7 @@
             in_specs=[
                 pl.BlockSpec((1, shards, rows, width), own),
                 pl.BlockSpec((1, shards, rows, width), other),
-                pl.BlockSpec(g_block, cot), pl.BlockSpec(g_block, cot),
+                pl.BlockSpec(g_block, cot), pl.BlockSpec(g_block, own), pl.BlockSpec(g_block, other),
                 saved, saved, saved,
             ],
             out_specs=[
@@ -905,33 +869,337 @@
     )(*parts)
 
 
-def scatter_all(pairs, partner, name, number, extra=()):
+def row_sums(values):
+    ones = jnp.ones((8, values.shape[1]), F32)
+    sums = lax.dot_general(
+        ones, values, (((1,), (1,)), ((), ())), preferred_element_type=F32,
+        precision=lax.Precision.HIGHEST,
+    )
+    return sums[:1]
+
+
+def columns(values):
+    turned = jnp.transpose(values)
+    return jnp.concatenate([turned[:, i : i + 1] for i in range(values.shape[0])], axis=0)
+
+
+def qkv_body(quads, xo_ref, xt_ref, gain_ref, w_ref, ao_ref, at_ref, pre_ref, square_ref):
+    n = pl.program_id(0)
+    other = n >= quads
+    batches, rows, width = xo_ref.shape[1:]
+    head_width = w_ref.shape[1] // 3
+    x = jnp.where(other, xt_ref[0], xo_ref[0]).astype(F32).reshape(-1, width)
+    root = lax.rsqrt(jnp.mean(x * x, axis=1, keepdims=True) + EPSILON)
+    act = (x * root * gain_ref[...]).astype(BF)
+    pre = nn(act, w_ref[...])
+    pre_ref[:, 0] = pre.reshape(batches, rows, -1)
+    for kind in range(2):
+        part = pre[:, kind * head_width : (kind + 1) * head_width]
+        sums = row_sums(part * part)
+        for m in range(batches):
+            i = kind * batches + m
+            square_ref[0, i : i + 1] = sums[:, m * rows : (m + 1) * rows]
+    act = act.reshape(batches, rows, width)
+
+    @pl.when(jnp.logical_not(other))
+    def _():
+        ao_ref[0] = act
+
+    @pl.when(other)
+    def _():
+        at_ref[0] = act
+
+
+def own_block(quads):
+    return lambda n: (jnp.minimum(n, quads - 1), 0, 0, 0)
+
+
+def other_block(quads):
+    return lambda n: (jnp.maximum(n - quads, 0), 0, 0, 0)
+
+
+def project(token_rows, gain, weights):
+    quads, batches, rows, width = token_rows[0].shape
+    total = weights.shape[1]
+    block = (1, batches, rows, width)
+    fixed = dict(pipeline_mode=pl.Buffered(1))
+    own, other = pl.BlockSpec(block, own_block(quads)), pl.BlockSpec(block, other_block(quads))
+    return pl.pallas_call(
+        functools.partial(qkv_body, quads),
+        out_shape=(
+            jax.ShapeDtypeStruct(token_rows[0].shape, BF),
+            jax.ShapeDtypeStruct(token_rows[0].shape, BF),
+            jax.ShapeDtypeStruct((batches, 2 * quads, rows, total), F32),
+            jax.ShapeDtypeStruct((2 * quads, 2 * batches, rows), F32),
+        ),
+        grid=(2 * quads,),
+        in_specs=[
+            own, other,
+            pl.BlockSpec((1, width), lambda n: (0, 0)),
+            pl.BlockSpec((width, total), lambda n: (0, 0), **fixed),
+        ],
+        out_specs=(
+            own, other,
+            pl.BlockSpec((batches, 1, rows, total), lambda n: (0, n, 0, 0)),
+            pl.BlockSpec((1, 2 * batches, rows), lambda n: (n, 0, 0)),
+        ),
+        compiler_params=pltpu.CompilerParams(vmem_limit_bytes=40 << 20),
+        name="project",
+    )(*token_rows, gain.reshape(1, width), weights)
+
+
+def turned(values, cosine, sine):
+    return values * cosine + pltpu.roll(values, HEAD // 2, 1) * sine
+
+
+def turned_back(grad, cosine, sine):
+    return grad * cosine - pltpu.roll(grad, HEAD // 2, 1) * sine
+
+
+def head_probs(query, key, column, row, length):
+    scores = nt(query, key) * (1.0 / math.sqrt(HEAD))
+    scores = jnp.where((row <= column) & (row < length), scores, MASKED)
+    expo = jnp.exp(scores - jnp.max(scores, axis=1, keepdims=True))
+    return expo / jnp.sum(expo, axis=1, keepdims=True)
+
+
+def attend_body(
+    step, pre_ref, sum_ref, gain_ref, cos_ref, sin_ref, column_ref, row_ref, length_ref,
+    query_ref, key_ref, value_ref, out_ref, att,
+):
+    m = pl.program_id(0)
+    places, rows = pre_ref.shape[1:3]
+    slot = places * rows
+    head_width = query_ref.shape[2]
+    cosine, sine = cos_ref[...], sin_ref[...]
+    pre = pre_ref[0].reshape(slot, 3 * head_width)
+    for kind, ref in enumerate((query_ref, key_ref)):
+        root = lax.rsqrt(columns(sum_ref[0, kind]) / (head_width * places) + EPSILON)
+        part = pre[:, kind * head_width : (kind + 1) * head_width] * root * gain_ref[kind]
+        for h in range(head_width // HEAD):
+            here = slice(h * HEAD, (h + 1) * HEAD)
+            ref[0, :, here] = turned(part[:, here], cosine, sine).astype(BF)
+    value_ref[0] = pre[:, 2 * head_width :].astype(BF)
+    length = length_ref[m]
+    row = row_ref[...]
+    for h in range(head_width // HEAD):
+        here = slice(h * HEAD, (h + 1) * HEAD)
+
+        @pl.loop(0, slot // step)
+        def _(i):
+            part = pl.ds(pl.multiple_of(i * step, step), step)
+            probs = head_probs(query_ref[0, part, here], key_ref[0, :, here], column_ref[part], row, length)
+            att[part, here] = nn(probs.astype(BF), value_ref[0, :, here]).astype(BF)
+
+    out_ref[:, 0] = att[...].reshape(places, rows, head_width)
+
+
+def attend(pre, sums, gains, cosine, sine, column, row, lengths):
+    batches, places, rows, total = pre.shape
+    head_width, slot = total // 3, places * rows
+    saved = jax.ShapeDtypeStruct((batches, slot, head_width), BF)
+    saved_spec = pl.BlockSpec((1, slot, head_width), lambda m: (m, 0, 0))
+    return pl.pallas_call(
+        functools.partial(attend_body, 256),
+        out_shape=(saved,) * 3
+        + (jax.ShapeDtypeStruct((places, batches, rows, head_width), BF),),
+        grid=(batches,),
+        in_specs=[
+            pl.BlockSpec((1,) + pre.shape[1:], lambda m: (m, 0, 0, 0)),
+            pl.BlockSpec((1,) + sums.shape[1:], lambda m: (m, 0, 0, 0)),
+            pl.BlockSpec(gains.shape, lambda m: (0, 0, 0)),
+            pl.BlockSpec(cosine.shape, lambda m: (0, 0)),
+            pl.BlockSpec(sine.shape, lambda m: (0, 0)),
+            pl.BlockSpec(column.shape, lambda m: (0, 0)),
+            pl.BlockSpec(row.shape, lambda m: (0, 0)),
+            pl.BlockSpec(memory_space=pltpu.SMEM),
+        ],
+        out_specs=(saved_spec,) * 3
+        + (pl.BlockSpec((places, 1, rows, head_width), lambda m: (0, m, 0, 0)),),
+        scratch_shapes=[pltpu.VMEM((slot, head_width), BF)],
+        compiler_params=pltpu.CompilerParams(vmem_limit_bytes=60 << 20),
+        name="attend",
+    )(pre, sums, gains, cosine, sine, column, row, lengths)
+
+
+def attend_back_body(
+    step, query_ref, key_ref, value_ref, datt_ref, pre_ref, sum_ref, gain_ref, cos_ref, sin_ref,
+    column_ref, row_ref, length_ref, dn_ref, dv_ref, inner_ref, dgain_ref, att, dq, dk, dv,
+):
+    m = pl.program_id(0)
+    places, rows = pre_ref.shape[1:3]
+    slot = places * rows
+    head_width = query_ref.shape[2]
+    factor = 1.0 / math.sqrt(HEAD)
+    att[...] = datt_ref[:, 0].reshape(slot, head_width)
+    length = length_ref[m]
+    row = row_ref[...]
+    dk[...] = jnp.zeros_like(dk)
+    dv[...] = jnp.zeros_like(dv)
+    for h in range(head_width // HEAD):
+        here = slice(h * HEAD, (h + 1) * HEAD)
+
+        @pl.loop(0, slot // step)
+        def _(i):
+            part = pl.ds(pl.multiple_of(i * step, step), step)
+            query, grad = query_ref[0, part, here], att[part, here]
+            probs = head_probs(query, key_ref[0, :, here], column_ref[part], row, length)
+            d_probs = nt(grad, value_ref[0, :, here])
+            inner = jnp.sum(probs * d_probs, axis=1, keepdims=True)
+            d_scores = (probs * (d_probs - inner)).astype(BF)
+            dq[part, here] = nn(d_scores, key_ref[0, :, here]) * factor
+            dk[:, here] += tn(d_scores, query) * factor
+            dv[:, here] += tn(probs.astype(BF), grad)
+
+    dv_ref[0] = dv[...].astype(BF)
+    cosine, sine = cos_ref[...], sin_ref[...]
+    for kind, ref in enumerate((dq, dk)):
+        root = lax.rsqrt(columns(sum_ref[0, kind]) / (head_width * places) + EPSILON)
+        for h in range(head_width // HEAD):
+            here = slice(h * HEAD, (h + 1) * HEAD)
+            ref[:, here] = turned_back(ref[:, here], cosine, sine)
+        grad = ref[...]
+        pre = pre_ref[0, :, :, kind * head_width : (kind + 1) * head_width].reshape(slot, head_width)
+        product = grad * pre
+        gain_part = jnp.sum(product * root, axis=0, keepdims=True)
+        before = jnp.where(m == 0, jnp.zeros_like(gain_part), dgain_ref[kind])
+        dgain_ref[kind] = before + gain_part
+        weighted = grad * gain_ref[kind]
+        dn_ref[0, kind] = weighted
+        sums = row_sums(product * gain_ref[kind])
+        for n in range(places):
+            inner_ref[0, kind, n : n + 1] = sums[:, n * rows : (n + 1) * rows]
+
+
+def attend_back(saved, d_att, pre, sums, gains, cosine, sine, column, row, lengths):
+    batches, places, rows, total = pre.shape
+    head_width, slot = total // 3, places * rows
+    saved_spec = pl.BlockSpec((1, slot, head_width), lambda m: (m, 0, 0))
+    return pl.pallas_call(
+        functools.partial(attend_back_body, 256),
+        out_shape=(
+            jax.ShapeDtypeStruct((batches, 2, slot, head_width), F32),
+            jax.ShapeDtypeStruct((batches, slot, head_width), BF),
+            jax.ShapeDtypeStruct(sums.shape, F32),
+            jax.ShapeDtypeStruct(gains.shape, F32),
+        ),
+        grid=(batches,),
+        in_specs=[saved_spec] * 3
+        + [
+            pl.BlockSpec((places, 1, rows, head_width), lambda m: (0, m, 0, 0)),
+            pl.BlockSpec((1,) + pre.shape[1:], lambda m: (m, 0, 0, 0)),
+            pl.BlockSpec((1,) + sums.shape[1:], lambda m: (m, 0, 0, 0)),
+            pl.BlockSpec(gains.shape, lambda m: (0, 0, 0)),
+            pl.BlockSpec(cosine.shape, lambda m: (0, 0)),
+            pl.BlockSpec(sine.shape, lambda m: (0, 0)),
+            pl.BlockSpec(column.shape, lambda m: (0, 0)),
+            pl.BlockSpec(row.shape, lambda m: (0, 0)),
+            pl.BlockSpec(memory_space=pltpu.SMEM),
+        ],
+        out_specs=(
+            pl.BlockSpec((1, 2, slot, head_width), lambda m: (m, 0, 0, 0)),
+            saved_spec,
+            pl.BlockSpec((1,) + sums.shape[1:], lambda m: (m, 0, 0, 0)),
+            pl.BlockSpec(gains.shape, lambda m: (0, 0, 0)),
+        ),
+        scratch_shapes=[pltpu.VMEM((slot, head_width), BF)]
+        + [pltpu.VMEM((slot, head_width), F32)] * 3,
+        compiler_params=pltpu.CompilerParams(vmem_limit_bytes=60 << 20),
+        name="attend_back",
+    )(*saved, d_att, pre, sums, gains, cosine, sine, column, row, lengths)
+
+
+def back_body(
+    quads, dn_ref, dv_ref, pre_ref, sum_ref, inner_ref, ao_ref, at_ref, w_ref,
+    do_ref, dt_ref, dw_ref, dw, cols,
+):
+    n = pl.program_id(0)
+    other = n >= quads
+    batches, _, rows, head_width = dn_ref.shape
+    width = w_ref.shape[0]
+    total = head_width * 2 * quads
+    for m in range(batches):
+        here = pl.ds(m * rows, rows)
+        for kind in range(2):
+            root = lax.rsqrt(columns(sum_ref[0, m, kind]) / total + EPSILON)
+            inner = columns(inner_ref[0, m, kind]) / total
+            part = slice(kind * head_width, (kind + 1) * head_width)
+            pre = pre_ref[m, 0, :, part]
+            grad = root * dn_ref[m, kind] - pre * (root * root * root) * inner
+            cols[here, part] = grad.astype(BF)
+        cols[here, 2 * head_width :] = dv_ref[m]
+    d_pre = cols[...]
+    act = jnp.where(other, at_ref[0], ao_ref[0]).reshape(-1, width)
+    d_act = nt(d_pre, w_ref[...]).astype(BF).reshape(batches, rows, width)
+    part = tn(act, d_pre)
+
+    @pl.when(n == 0)
+    def _():
+        dw[...] = part
+
+    @pl.when(n > 0)
+    def _():
+        dw[...] += part
+
+    @pl.when(n == pl.num_programs(0) - 1)
+    def _():
+        dw_ref[...] = dw[...].astype(BF)
+
+    @pl.when(jnp.logical_not(other))
+    def _():
+        do_ref[0] = d_act
+
+    @pl.when(other)
+    def _():
+        dt_ref[0] = d_act
+
+
+def project_back(d_norm, d_value, pre, sums, inners, act, weights):
+    batches, places, rows, total = pre.shape
+    quads, width, head_width = places // 2, weights.shape[0], total // 3
+    block = (1, batches, rows, width)
+    fixed = dict(pipeline_mode=pl.Buffered(1))
+    own, other = pl.BlockSpec(block, own_block(quads)), pl.BlockSpec(block, other_block(quads))
+    sums = sums.transpose(2, 0, 1, 3)[:, :, :, None]
+    inners = inners[:, :, :, None]
+    small = pl.BlockSpec((1, batches, 2, 1, rows), lambda n: (n, 0, 0, 0, 0))
+    return pl.pallas_call(
+        functools.partial(back_body, quads),
+        out_shape=(
+            jax.ShapeDtypeStruct(act[0].shape, BF), jax.ShapeDtypeStruct(act[0].shape, BF),
+            jax.ShapeDtypeStruct(weights.shape, BF),
+        ),
+        grid=(places,),
+        in_specs=[
+            pl.BlockSpec((batches, 2, rows, head_width), lambda n: (0, 0, n, 0)),
+            pl.BlockSpec((batches, rows, head_width), lambda n: (0, n, 0)),
+            pl.BlockSpec((batches, 1, rows, total), lambda n: (0, n, 0, 0)),
+            small, small, own, other,
+            pl.BlockSpec(weights.shape, lambda n: (0, 0), **fixed),
+        ],
+        out_specs=(own, other, pl.BlockSpec(weights.shape, lambda n: (0, 0))),
+        scratch_shapes=[
+            pltpu.VMEM(weights.shape, F32), pltpu.VMEM((batches * rows, total), BF)
+        ],
+        compiler_params=pltpu.CompilerParams(vmem_limit_bytes=60 << 20),
+        name="project_back",
+    )(d_norm, d_value, pre, sums, inners, *act, weights)
+
+
+def scatter_all(pairs, partners, name, number, extra=()):
     if pairs[0][0].shape[0] == 4:
-        return scatter_rows(pairs, partner, name, number, extra)
-    total = pairs[0][0].shape[1]
-    count = total // 2 if partner else total
-    sums = [
-        jnp.concatenate(
-            [
-                scatter_rows([(own[:, m::count], other[:, m::count])], partner, name, number)[0]
-                for m in range(count)
-            ]
-        )
-        for own, other in pairs
-    ]
-    if not extra:
-        return sums
-    blocks, down = extra
-    lanes, lane = lax.axis_size("lane"), lax.axis_index("lane")
-    down = down.reshape(down.shape[0], lanes, -1, down.shape[2]).swapaxes(0, 1)
-    moved = [
-        lax.ppermute(
-            lax.dynamic_index_in_dim(down, lane ^ d, 0, keepdims=False),
-            "lane", [(i, i ^ d) for i in range(lanes)],
-        )
-        for d in range(1, lanes)
-    ]
-    return sums + [exchange(blocks, DP), jnp.stack(moved)]
+        return scatter_rows(pairs, partners, name, number, extra)
+    sums = []
+    for i, ((own, other), partner) in enumerate(zip(pairs, partners)):
+        count = own.shape[1] // 2 if partner else own.shape[1]
+        parts = [
+            scatter_rows(
+                [(own[:, m::count], other[:, m::count])], (partner,), name, number + 8 * i
+            )[0]
+            for m in range(count)
+        ]
+        sums.append(jnp.concatenate(parts))
+    return sums + [exchange(blocks, DP) for blocks in extra]
 
 
 def on_device(
@@ -961,14 +1229,12 @@
     slot_len = rows * ctx_size
     block_rows = rows // 2
     head_width = width // ctx_size
-    heads = head_width // HEAD
     shard = w_query.shape[0]
     expert_count = w_router.shape[1]
     local_experts = w_gate.shape[0]
     hidden_units = w_gate.shape[2]
     hidden_half = hidden_units // 2
     depth_part = w_gate.shape[1]
-    factor = 1.0 / math.sqrt(HEAD)
     pair = lax.axis_index("pair")
 
     qkv = jnp.stack([w_query, w_key, w_value], axis=1).reshape(shard, 3, ctx_size, head_width)
@@ -980,9 +1246,9 @@
     tok_own, tok_other, qkv_w, small, out_w = start_gather(
         tokens[:, 0], qkv, small.reshape(1, -1), w_out
     )
+    out_w = lax.all_gather(out_w, CTX, axis=1, tiled=False).reshape(width, width)
     token_rows = (tok_own, tok_other)
     qkv_w = qkv_w.reshape(width, 3 * head_width)
-    out_w = out_w.reshape(width, width)
     small = small.reshape(dp_size * ctx_size, -1)
     gain_attn = small[:, :shard].reshape(width).astype(F32)
     gain_mlp = small[:, shard : 2 * shard].reshape(width).astype(F32)
@@ -1008,10 +1274,7 @@
     halves = [jnp.repeat(part, lanes, axis=0) for part in halves]
     next_w = exchange(halves[0], DP)
     down_parts = lane_parts(w_down)
-    g_rows = [
-        lax.all_gather(part, CTX, axis=0, tiled=False)
-        for part in (crossing, swap(crossing, "half"))
-    ]
+    g_own = lax.all_gather(crossing, CTX, axis=0, tiled=False)
 
     def places_of(device):
         stored = device * rows + jnp.arange(rows, dtype=jnp.int32)
@@ -1033,57 +1296,16 @@
 
     inputs = tokens[:, 0].astype(F32)
     attn_root = inv_rms(inputs)
-    act = []
-    for part in token_rows:
-        values = part.astype(F32)
-        act.append((values * inv_rms(values) * gain_attn).astype(BF))
-    pre = [
-        dot("td,de->te", part.reshape(-1, width), qkv_w).reshape(quads, batches, rows, -1)
-        for part in act
-    ]
-    pre = jnp.stack(pre)
-
-    squares = jnp.stack(
-        [
-            jnp.sum(part * part, axis=-1)
-            for part in (pre[..., :head_width], pre[..., head_width : 2 * head_width])
-        ],
-        axis=2,
-    )
-    squares = sum_ctx(squares.reshape(2 * quads, 2 * batches, rows), "sum_squares", 6)
-    roots = lax.rsqrt(squares.reshape(2 * quads, 2, batches, rows) / width + EPSILON)
-
-    saved = []
-    attended_all = []
-    for m in range(batches):
-        pre_m = pre[:, :, m].reshape(slot_len, 3 * head_width)
-        query_pre = pre_m[:, :head_width]
-        key_pre = pre_m[:, head_width : 2 * head_width]
-        value = pre_m[:, 2 * head_width :].astype(BF).reshape(slot_len, heads, HEAD)
-        query_root = roots[:, 0, m].reshape(slot_len, 1)
-        key_root = roots[:, 1, m].reshape(slot_len, 1)
-        query = rotate(
-            (query_pre * query_root * gain_query).reshape(slot_len, heads, HEAD), cosine, sine
-        ).astype(BF)
-        key = rotate(
-            (key_pre * key_root * gain_key).reshape(slot_len, heads, HEAD), cosine, sine
-        ).astype(BF)
-        allowed = (places[None, :] <= places[:, None]) & (places[None, :] < lengths[m, 0])
-        scores = dot("qhd,khd->hqk", query, key) * factor
-        scores = jnp.where(allowed[None], scores, MASKED)
-        expo = jnp.exp(scores - jnp.max(scores, axis=-1, keepdims=True))
-        probs = expo / jnp.sum(expo, axis=-1, keepdims=True)
-        probs_low = probs.astype(BF)
-        attended = dot("hqk,khd->qhd", probs_low, value).astype(BF)
-        attended_all.append(attended.reshape(2 * quads, rows, head_width))
-        saved.append(
-            dict(
-                query_pre=query_pre, key_pre=key_pre, query_root=query_root, key_root=key_root,
-                query=query, key=key, value=value, probs=probs, probs_low=probs_low,
-            )
-        )
-    attended = jnp.stack(attended_all, axis=1)[None]
-    attended = exchange_rows(attended, "inward", "attended_to_rows", 7)[0]
+    act_own, act_other, pre, squares = project(token_rows, gain_attn, qkv_w)
+    squares = sum_ctx(squares, "sum_squares", 6)
+    squares = squares.reshape(2 * quads, 2, batches, rows).transpose(2, 1, 0, 3)
+    qk_gains = jnp.stack([gain_query, gain_key])[:, None]
+    signed = jnp.where(jnp.arange(HEAD) < HEAD // 2, -sine[:, 0], sine[:, 0])
+    context = (pre, squares, qk_gains, cosine[:, 0], signed, places[:, None], places[None, :])
+    context = context + (lengths[:, 0],)
+    *saved, attended = attend(*context)
+    attended = exchange_rows(attended[None], "inward", "attended_to_rows", 7)[0]
+    attended, next_w = lax.optimization_barrier((attended, next_w))
     attended = attended.transpose(1, 2, 0, 3).reshape(batches, rows, width)
     x_mid = inputs + dot("mtd,de->mte", attended, out_w)
     mlp_root = inv_rms(x_mid)
@@ -1091,10 +1313,11 @@
     router = jax.nn.softmax(dot("mtd,de->mte", mixed_in, router_w), axis=-1)
     routed = jnp.any(routes[:, 0, :, :, None] == expert_range, axis=2).astype(F32)
     gates = (router * routed).transpose(2, 0, 1).reshape(ctx_size, local_experts, batches, rows)
+    x_rows, cross_rows = gather_rows([mixed_in, grad_low], ("both", "partner"), "gather_mixed", 2)
+    gates, x_rows = lax.optimization_barrier((gates, x_rows))
     gates = exchange_rows(gates, "outward", "gates_to_experts", 8, 2)
+    g_rows = (g_own,) + cross_rows
     gates = gates.transpose(1, 0, 3, 4, 2).reshape(4 * quads, batches * rows, local_experts)
-    gates, mixed_rows = lax.optimization_barrier((gates, mixed_in))
-    x_rows = gather_rows([mixed_rows], (True,), "gather_mixed", 2)[0]
     number = jnp.arange(2 * quads, dtype=jnp.int32)
     place = (lax.axis_index("quad") ^ (number % quads)) * 2 + (pair ^ (number // quads))
     x_rows, next_w, down_parts, halves, gates = lax.optimization_barrier(
@@ -1121,18 +1344,28 @@
         grads_both.append(exchange(grad_both, DP) if e < local_experts - 1 else grad_both)
         grads_down.append(grad_down)
     moe_own, moe_other, d_own, d_other = sums
-    d_own, grads_both, grads_down = lax.optimization_barrier((d_own, grads_both, grads_down))
+    done, grads_down, d_own = lax.optimization_barrier((grads_both[:-1], grads_down, d_own))
+    grads_both[:-1] = done
     grads_down = jnp.stack(grads_down)
-    d_mixed, moe_sum, last_both, down_others = scatter_all(
-        [(d_own, d_other), (moe_own, moe_other)], True, "scatter_experts", 3,
-        (grads_both[-1], grads_down),
+    grads_down = grads_down.reshape(local_experts, lanes, -1, width).swapaxes(0, 1)
+    lane = lax.axis_index("lane")
+    down_others = [
+        lax.ppermute(
+            lax.dynamic_index_in_dim(grads_down, lane ^ d, 0, keepdims=False),
+            "lane", [(i, i ^ d) for i in range(lanes)],
+        )
+        for d in range(1, lanes)
+    ]
+    d_mixed, moe_sum = scatter_all(
+        [(d_own, d_other), (moe_own, moe_other)], (True, True), "scatter_experts", 24
     )
-    grads_both[-1] = last_both
     d_gates = jnp.concatenate(d_gates, axis=-1)
     d_gates = d_gates.reshape(2 * quads, 2, batches, rows, local_experts)
     d_gates = d_gates.transpose(1, 0, 4, 2, 3)
-    d_gates, d_mixed = lax.optimization_barrier((d_gates, d_mixed))
+    d_gates, d_mixed, down_others = lax.optimization_barrier((d_gates, d_mixed, down_others))
     d_router = exchange_rows(d_gates, "inward", "gate_gradients", 9, 2)
+    d_router, last_both = lax.optimization_barrier((d_router, grads_both[-1]))
+    grads_both[-1] = exchange(last_both, DP)
     d_router = jnp.sum(d_router, axis=0).reshape(expert_count, batches, rows)
     d_router = d_router.transpose(1, 2, 0) * routed
     d_logits = (
@@ -1153,66 +1386,25 @@
     grad_out = lax.psum_scatter(grad_out, ALL, scatter_dimension=0, tiled=True).astype(F32)
     d_attended = d_attended.reshape(batches, rows, ctx_size, head_width).transpose(2, 0, 1, 3)
     d_attended = exchange_rows(d_attended, "outward", "attended_gradients", 10)[0]
-    part_query_gain = part_key_gain = 0.0
-    parts = []
-    inners = []
-    for m in range(batches):
-        s = saved[m]
-        d_att = d_attended[:, m].reshape(slot_len, heads, HEAD)
-        probs, query, key = s["probs"], s["query"], s["key"]
-        d_probs = dot("qhd,khd->hqk", d_att, s["value"])
-        inner = jnp.sum(probs * d_probs, axis=-1, keepdims=True)
-        d_scores = (probs * (d_probs - inner)).astype(BF)
-        d_query = dot("hqk,khd->qhd", d_scores, key) * factor
-        d_key = dot("hqk,qhd->khd", d_scores, query) * factor
-        d_value = dot("hqk,qhd->khd", s["probs_low"], d_att)
-        d_query = rotate_back(d_query, cosine, sine).reshape(slot_len, head_width)
-        d_key = rotate_back(d_key, cosine, sine).reshape(slot_len, head_width)
-        parts.append((d_query, d_key, d_value))
-        inners += [
-            jnp.sum(d_query * gain_query * s["query_pre"], axis=1).reshape(-1, rows),
-            jnp.sum(d_key * gain_key * s["key_pre"], axis=1).reshape(-1, rows),
-        ]
-    inners = sum_ctx(jnp.stack(inners, axis=1), "sum_inner", 11) / width
-    d_pre_all = []
-    for m in range(batches):
-        s = saved[m]
-        d_query, d_key, d_value = parts[m]
-        query_pre, key_pre = s["query_pre"], s["key_pre"]
-        query_root, key_root = s["query_root"], s["key_root"]
-        query_inner = inners[:, 2 * m].reshape(slot_len, 1)
-        key_inner = inners[:, 2 * m + 1].reshape(slot_len, 1)
-        d_query_pre = query_root * (d_query * gain_query) - query_pre * query_root**3 * query_inner
-        d_key_pre = key_root * (d_key * gain_key) - key_pre * key_root**3 * key_inner
-        part_query_gain = part_query_gain + jnp.sum(d_query * query_pre * query_root, axis=0)
-        part_key_gain = part_key_gain + jnp.sum(d_key * key_pre * key_root, axis=0)
-        d_pre = jnp.concatenate(
-            [
-                d_query_pre.astype(BF),
-                d_key_pre.astype(BF),
-                d_value.reshape(slot_len, head_width).astype(BF),
-            ],
-            axis=1,
-        )
-        d_pre_all.append(d_pre.reshape(2, quads, rows, 3 * head_width))
-    d_pre = jnp.stack(d_pre_all, axis=2).reshape(2, -1, 3 * head_width)
-    d_act = [
-        dot("te,de->td", d_pre[i], qkv_w).astype(BF).reshape(quads, batches, rows, width)
-        for i in range(2)
-    ]
-    d_act = scatter_all([(d_act[0], d_act[1])], False, "scatter_act", 4)[0]
+    d_norm, d_value, inners, d_gains = attend_back(saved, d_attended, *context)
+    inners = inners.transpose(2, 0, 1, 3).reshape(2 * quads, 2 * batches, rows)
+    inners = sum_ctx(inners, "sum_inner", 11).reshape(2 * quads, batches, 2, rows)
+    d_act_own, d_act_other, grad_qkv = project_back(
+        d_norm, d_value, pre, squares, inners, (act_own, act_other), qkv_w
+    )
+    grad_qkv = grad_qkv.reshape(dp_size, -1, 3 * head_width)
+    d_act, grad_qkv = scatter_all(
+        [(d_act_own, d_act_other)], (False,), "scatter_act", 25, (grad_qkv,)
+    )
     d_inputs, part_attn_gain = norm_back_all(inputs, attn_root, gain_attn, d_act)
     mixed = (x_mid + moe_sum).astype(BF)
 
     grad_gate, grad_up = finish_grads(grads_both)
-    grads_down = grads_down.reshape(local_experts, lanes, -1, width)
-    grad_down = lax.dynamic_index_in_dim(grads_down, lax.axis_index("lane"), 1, keepdims=False)
-    grad_down = grad_down.astype(F32) + jnp.sum(down_others.astype(F32), axis=0)
-
-    acts = [part.reshape(-1, width) for part in act]
-    grad_qkv = sum(dot("td,te->de", x, y) for x, y in zip(acts, d_pre)).astype(BF)
-    grad_qkv, grad_out = lax.optimization_barrier((grad_qkv, grad_out))
-    grad_qkv = lax.psum_scatter(grad_qkv, DP, scatter_dimension=0, tiled=True)
+    grad_down = lax.dynamic_index_in_dim(grads_down, lane, 0, keepdims=False).astype(F32)
+    for part in down_others:
+        grad_down = grad_down + part.astype(F32)
+
+    grad_qkv = jnp.sum(grad_qkv.astype(F32), axis=0).astype(BF)
     grad_qkv = grad_qkv.reshape(ctx_size, shard, 3 * head_width)
     grad_qkv = exchange_rows(grad_qkv, "ctx", "qkv_gradients", 14).astype(F32)
     grad_qkv = grad_qkv.reshape(ctx_size, shard, 3, head_width).transpose(2, 1, 0, 3)
@@ -1225,7 +1417,7 @@
         return jnp.where(columns, part[None, :], 0.0).reshape(width)
 
     gains = jnp.stack(
-        [part_attn_gain, part_mlp_gain, placed(part_query_gain), placed(part_key_gain)]
+        [part_attn_gain, part_mlp_gain, placed(d_gains[0, 0]), placed(d_gains[1, 0])]
     )
     gains = gains.reshape(4, dp_size, ctx_size, shard).transpose(1, 2, 0, 3)
     packed = jnp.concatenate(

time: 1140 us -> 1090 us (0.956)
  Pallas kernels: 792 us -> 914 us
  matrix products: 89.3 us -> 19.2 us
  other arithmetic: 87.5 us -> 36.8 us
  waiting for transfers between devices: 42 us -> 11 us
  local copies, waits for them, and re-layouts: 88 us -> 63 us
    pallas_call x2 -> x6, Pallas kernels: 252 us -> 326 us  [the longest x2 229 us: scatter_rows(): pl.pallas_call(functools.partial(scatter_body, quads, lanes, partners, co...]
    dot_general x21 -> x5, matrix products: 74.8 us -> 17.5 us  [dot(): return jnp.einsum(spec, left, right, preferred_element_type=F32)]
    pallas_call x1, Pallas kernels: 89.3 us -> 145 us  [gather_rows(): pl.pallas_call(functools.partial(gather_body, quads, partners), out_shape...]
    reduce_scatter x1, waiting for transfers between devices: 41.9 us -> 0.01 us  [on_device(): lax.psum_scatter(grad_out, ALL, scatter_dimension=0, tiled=True).astype(F32)]
    pallas_call x1, Pallas kernels: 110 us -> 82.5 us  [start_gather(): pl.pallas_call(functools.partial(start_body, quads, lanes), out_shape=[li...]
    convert_element_type x6 -> x0, other arithmetic: 18.8 us -> none  [the longest x2 7.62 us: on_device(): d_scores = (probs * (d_probs - inner)).astype(BF)]
    pallas_call x6, Pallas kernels: 98.4 us -> 114 us  [exchange_rows(): pl.pallas_call(functools.partial(exchange_body, mode, lanes, quads, halve...]
    sub x2 -> x0, matrix products: 12.6 us -> none  [on_device(): expo = jnp.exp(scores - jnp.max(scores, axis=-1, keepdims=True))]
  transfers between devices with their start and end apart: 9 -> 9, of which waited for: 1 -> 1; matrix products, arithmetic and copies ran while one was open for 19% -> 8% of each run, Pallas kernels for 39% -> 76%
where the time goes in v5:
time: 1090 us; the launch traced here: 1080 us
  Pallas kernels  914 us (84%)
  local copies, waits for them, and re-layouts  63 us (6%)
  other arithmetic  36.8 us (3%)
  starting transfers between devices  25.6 us (2%)
  matrix products  19.2 us (2%)
  between operations  14.6 us (1%)
  waiting for transfers between devices  11 us (1%)
    pallas_call x2, Pallas kernels, scatter_rows(): pl.pallas_call(functools.partial(scatter_body, quads, lanes, partners, co...  229 us
    pallas_call x1, Pallas kernels, gather_rows(): pl.pallas_call(functools.partial(gather_body, quads, partners), out_shape...  145 us
    pallas_call x2, Pallas kernels, expert(): pl.pallas_call(functools.partial(expert_body, quads, bool(before)), out_s...  143 us
    pallas_call x6, Pallas kernels, exchange_rows(): pl.pallas_call(functools.partial(exchange_body, mode, lanes, quads, halve...  114 us
    pallas_call x1, Pallas kernels, start_gather(): pl.pallas_call(functools.partial(start_body, quads, lanes), out_shape=[li...  82.5 us
    pallas_call x2, Pallas kernels, expert_grads(): pl.pallas_call(functools.partial(grads_body, quads), out_shape=(jax.Shape...  74.9 us
    pallas_call x1, Pallas kernels, project_back(): pl.pallas_call(functools.partial(back_body, quads), out_shape=(jax.ShapeD...  30.4 us
    pallas_call x1, Pallas kernels, attend_back(): pl.pallas_call(functools.partial(attend_back_body, 256), out_shape=(jax.S...  29.1 us
  transfers between devices with their start and end apart: 9, of which 1 were waited for; matrix products, arithmetic and copies ran while one was open for 8% of the time, Pallas kernels for 76%

profile of v5, /device:TPU:0, one launch (start us, length us, event | category | flops | bytes accessed | tf_op | source)
XLA Modules:
  0.0 1084.8 jit_solution(5265484650715354545)
XLA Ops:
  18.3 82.5 %start_gather.1 = (bf16[4,2,128,2048]{3,2,1,0:T(8,128)(2,1)}, bf16[4,2,128,2048]{3,2,1,0:T(8,128)(2,1)}, bf16[4,8,64,768]{3,2,1,0:T(8,128)(2,1)}, bf16[32,1,1280]{2,1,0:T(2,128)(2,1)}, bf16[4,64,2048]{2,1,0:T(8,128)(2,1)}) custom-call(bf16[2,128,2048]{2,1,0:T(8,128)(2,1)} %bitcast.148, bf16[8,64,768]{2,1,0:T(8,128)(2,1)} %reshape.486.qkv_ref, ...), custom_call_target="tpu_custom_call" | custom-call | tf_op jit(solution)/shard_map/start_gather/pallas_call | solution.py:347
  123.3 17.8 %project.1 = (bf16[4,2,128,2048]{3,2,1,0:T(8,128)(2,1)S(1)}, bf16[4,2,128,2048]{3,2,1,0:T(8,128)(2,1)S(1)}, f32[2,8,128,768]{3,2,1,0:T(8,128)}, f32[8,4,128]{2,1,0:T(4,128)S(1)}) custom-call(bf16[4,2,128,2048]{3,2,1,0:T(8,128)(2,1)} %get-tuple-element.96.xo_ref, bf16[4,2,128,2048]{3,2,1,0:T(8,128)(2,1)} %get-tuple-element.97.xt_ref, ...), custom_call_target="tpu_custom_call" | custom-call | tf_op jit(solution)/shard_map/project/pallas_call | solution.py:927
  145.7 8.0 sum_squares.1
  155.0 19.6 %attend.1 = (bf16[2,1024,256]{2,1,0:T(8,128)(2,1)}, bf16[2,1024,256]{2,1,0:T(8,128)(2,1)}, bf16[2,1024,256]{2,1,0:T(8,128)(2,1)}, bf16[8,2,128,256]{3,2,1,0:T(8,128)(2,1)}) custom-call(f32[2,8,128,768]{3,2,1,0:T(8,128)} %get-tuple-element.101.pre_ref, f32[2,2,8,128]{3,2,1,0:T(8,128)} %bitcast.188, f32[2,1,256]{2,1,0:T(1,128)} %reshape.512.gain_ref, ...), custom_call_target="tpu_custom_call" | custom-call | tf_op jit(solution)/shard_map/attend/pallas_call | solution.py:1002
  174.6 19.8 %attended_to_rows.1 = bf16[1,8,2,128,256]{4,3,2,1,0:T(8,128)(2,1)} custom-call(bf16[1,8,2,128,256]{4,3,2,1,0:T(8,128)(2,1)} %bitcast.179), custom_call_target="tpu_custom_call" | custom-call | tf_op jit(solution)/shard_map/attended_to_rows/pallas_call | solution.py:598
  196.0 10.2 all-to-all-done.both_ref
  207.5 6.3 multiply_reduce_fusion.2
  215.0 145.5 %gather_mixed.1 = (bf16[4,4,128,2048]{3,2,1,0:T(8,128)(2,1)}, bf16[4,4,128,2048]{3,2,1,0:T(8,128)(2,1)}, bf16[4,2,128,2048]{3,2,1,0:T(8,128)(2,1)}, bf16[4,2,128,2048]{3,2,1,0:T(8,128)(2,1)}) custom-call(bf16[2,128,2048]{2,1,0:T(8,128)(2,1)} %multiply_convert_fusion.refs_0_, bf16[2,128,2048]{2,1,0:T(8,128)(2,1)} %bitcast.159), custom_call_target="tpu_custom_call" | custom-call | tf_op jit(solution)/shard_map/gather_mixed/pallas_call | solution.py:259
  363.0 8.1 gates_to_experts.1
  377.8 5.4 all-to-all-start.1
  392.9 71.0 %expert_0.1 = (bf16[4,4,128,2048]{3,2,1,0:T(8,128)(2,1)}, bf16[4,4,128,2048]{3,2,1,0:T(8,128)(2,1)}, bf16[4,4,128,2048]{3,2,1,0:T(8,128)(2,1)}, bf16[4,4,128,204...) custom-call(s32[8]{0:T(128)} %fusion.34._, ...), custom_call_target="tpu_custom_call" | custom-call | tf_op jit(solution)/shard_map/expert_0/pallas_call | solution.py:744
  463.8 37.5 %expert_grads_0.1 = (bf16[4,2,512,512]{3,2,1,0:T(8,128)(2,1)}, bf16[512,2048]{1,0:T(8,128)(2,1)}) custom-call(s32[8]{0:T(128)} %fusion.34._, bf16[4,4,128,2048]{3,2,1,0:T(8,128)(2,1)} %get-tuple-element.116.xo_ref, bf16[4,4,128,2048]{3,2,1,0:T(8,128)(2,1)} %get-tuple-element.117.xt_ref, bf16[8,2,128,2048]{3,2,1,0:T(8,128)(2,1)} %bitcast.145, ...), custom_call_target="tpu_custom_call" | custom-call | tf_op jit(solution)/shard_map/expert_grads_0/pallas_call | solution.py:816
  506.6 72.4 %expert_1.1 = (bf16[4,4,128,2048]{3,2,1,0:T(8,128)(2,1)}, bf16[4,4,128,2048]{3,2,1,0:T(8,128)(2,1)}, bf16[4,4,128,2048]{3,2,1,0:T(8,128)(2,1)}, bf16[4,4,128,204...) custom-call(s32[8]{0:T(128)} %fusion.34._, ...), custom_call_target="tpu_custom_call", output_to_operand_aliasing={{0}: (9, {}), {1}: (10, {}), {2}: (11, {}), {3}: (12, {})} | custom-call | tf_op jit(solution)/shard_map/expert_1/pallas_call | solution.py:744
  579.0 37.5 %expert_grads_1.1 = (bf16[4,2,512,512]{3,2,1,0:T(8,128)(2,1)}, bf16[512,2048]{1,0:T(8,128)(2,1)}) custom-call(s32[8]{0:T(128)} %fusion.34._, bf16[4,4,128,2048]{3,2,1,0:T(8,128)(2,1)} %get-tuple-element.116.xo_ref, bf16[4,4,128,2048]{3,2,1,0:T(8,128)(2,1)} %get-tuple-element.117.xt_ref, bf16[8,2,128,2048]{3,2,1,0:T(8,128)(2,1)} %bitcast.147, ...), custom_call_target="tpu_custom_call" | custom-call | tf_op jit(solution)/shard_map/expert_grads_1/pallas_call | solution.py:816
  626.6 153.9 %scatter_experts.1 = (f32[2,128,2048]{2,1,0:T(8,128)}, f32[2,128,2048]{2,1,0:T(8,128)}) custom-call(bf16[4,4,128,2048]{3,2,1,0:T(8,128)(2,1)} %get-tuple-element.141.refs_0_, bf16[4,4,128,2048]{3,2,1,0:T(8,128)(2,1)} %get-tuple-element.142.refs_1_, bf16[4,4,128,2048]{3,2,1,0:T(8,128)(2,1)} %get-tuple-element.145.refs_2_, ...), custom_call_target="tpu_custom_call" | custom-call | tf_op jit(solution)/shard_map/scatter_experts/pallas_call | solution.py:513
  780.5 8.0 gate_gradients.1
  814.9 21.9 %attended_gradients.1 = bf16[1,8,2,128,256]{4,3,2,1,0:T(8,128)(2,1)} custom-call(bf16[8,2,128,256]{3,2,1,0:T(8,128)(2,1)} %bitcast.170), custom_call_target="tpu_custom_call" | custom-call | tf_op jit(solution)/shard_map/attended_gradients/pallas_call | solution.py:598
  836.8 29.1 %attend_back.1 = (f32[2,2,1024,256]{3,2,1,0:T(8,128)}, bf16[2,1024,256]{2,1,0:T(8,128)(2,1)}, f32[2,2,8,128]{3,2,1,0:T(8,128)}, f32[2,1,256]{2,1,0:T(1,128)}) custom-call(bf16[2,1024,256]{2,1,0:T(8,128)(2,1)} %get-tuple-element.148.query_ref, bf16[2,1024,256]{2,1,0:T(8,128)(2,1)} %get-tuple-element.149.key_ref, ...), custom_call_target="tpu_custom_call" | custom-call | tf_op jit(solution)/shard_map/attend_back/pallas_call | solution.py:1078
  868.1 13.7 %sum_inner.1 = f32[8,4,128]{2,1,0:T(4,128)} custom-call(f32[8,4,128]{2,1,0:T(4,128)} %bitcast.200), custom_call_target="tpu_custom_call" | custom-call | tf_op jit(solution)/shard_map/sum_inner/pallas_call | solution.py:638
  881.9 30.4 %project_back.1 = (bf16[4,2,128,2048]{3,2,1,0:T(8,128)(2,1)}, bf16[4,2,128,2048]{3,2,1,0:T(8,128)(2,1)}, bf16[2048,768]{1,0:T(8,128)(2,1)}) custom-call(f32[2,2,1024,256]{3,2,1,0:T(8,128)} %get-tuple-element.161.dn_ref, bf16[2,1024,256]{2,1,0:T(8,128)(2,1)} %get-tuple-element.162.dv_ref, f32[2,8,128,768]{3,2,1,0:T(8,128)} %get-tuple-element.101.pre_ref, ...), custom_call_target="tpu_custom_call" | custom-call | tf_op jit(solution)/shard_map/project_back/pallas_call | solution.py:1166
  912.3 75.1 %scatter_act.1 = (f32[2,128,2048]{2,1,0:T(8,128)}, bf16[4,512,768]{2,1,0:T(8,128)(2,1)}) custom-call(bf16[4,2,128,2048]{3,2,1,0:T(8,128)(2,1)} %get-tuple-element.166.refs_0_, bf16[4,2,128,2048]{3,2,1,0:T(8,128)(2,1)} %get-tuple-element.167.refs_1_, bf16[4,512,768]{2,1,0:T(8,128)(2,1)} %bitcast.172), custom_call_target="tpu_custom_call" | custom-call | tf_op jit(solution)/shard_map/scatter_act/pallas_call | solution.py:513
  991.0 28.6 %qkv_gradients.1 = bf16[8,64,768]{2,1,0:T(8,128)(2,1)} custom-call(bf16[8,64,768]{2,1,0:T(8,128)(2,1)} %bitcast.171), custom_call_target="tpu_custom_call" | custom-call | tf_op jit(solution)/shard_map/qkv_gradients/pallas_call | solution.py:598
  1021.5 27.1 %small_gradients.1 = f32[32,1,1280]{2,1,0:T(1,128)} custom-call(f32[32,1,1280]{2,1,0:T(1,128)} %pad_maximum_fusion.3.x_ref), custom_call_target="tpu_custom_call" | custom-call | tf_op jit(solution)/shard_map/small_gradients/pallas_call | solution.py:598
  1069.2 7.1 finish_gradients.1
  (192 shorter events, 133.7 us)
Async XLA Ops:
  7.2 7.2 copy-start.17
  7.2 200.3 %all-gather.5.cloned.1.call-start = ((), (), s32[]{:S(2)}) async-start(), calls=%async_computation.6 | async-start | bytes 9437184 | tf_op jit(solution)/shard_map/all_gather | solution.py:1249
  100.8 292.1 %all-gather.7.cloned.1.call-start = ((), (), s32[]{:S(2)}) async-start(), calls=%async_computation.7 | async-start | bytes 9437184 | tf_op jit(solution)/shard_map/all_gather | solution.py:1277
  107.0 7.5 copy-start.21
  107.0 7.8 copy-start.18
  107.0 8.1 copy-start.20
  107.0 99.2 %all-to-all-start = ((bf16[4,2,512,512]{3,2,1,0:T(8,128)(2,1)}), bf16[4,2,512,512]{3,2,1,0:T(8,128)(2,1)}, u32[]{:S(2)}, u32[]{:S(2)}) async-start(bf16[4,2,512,512]{3,2,1,0:T(8,128)(2,1)} %bitcast.150), calls=%async_computation | async-start | bytes 8388608 | tf_op jit(solution)/shard_map/all_to_all | solution.py:52
  112.3 261.5 %collective-permute-start = (bf16[2,256,2048]{2,1,0:T(8,128)(2,1)}, bf16[2,256,2048]{2,1,0:T(8,128)(2,1)}, u32[]{:S(2)}, u32[]{:S(2)}) collective-permute-start(bf16[2,256,2048]{2,1,0:T(8,128)(2,1)} %param.29), channel_id=1, source_target_pairs={{0,8},{8,0},{1,9},{9,1},{2,10},{10,2},{3,11},{11,3},{4,12},{12,4},... | collective-permute-start | bytes 6291464 | tf_op jit(solution)/shard_map/ppermute | solution.py:48
  114.7 5.7 copy-start.19
  117.2 6.1 copy-start
  174.6 19.8 %copy-start.15 = (bf16[1,2,512,512]{3,2,1,0:T(8,128)(2,1)S(1)}, bf16[1,2,512,512]{3,2,1,0:T(8,128)(2,1)}, u32[]{:S(2)}) copy-start(bf16[1,2,512,512]{3,2,1,0:T(8,128)(2,1)} %maximum_bitcast_fusion.4) | copy-start | bytes 3145732
  174.6 19.8 %copy-start.16 = (bf16[1,2,512,512]{3,2,1,0:T(8,128)(2,1)S(1)}, bf16[1,2,512,512]{3,2,1,0:T(8,128)(2,1)}, u32[]{:S(2)}) copy-start(bf16[1,2,512,512]{3,2,1,0:T(8,128)(2,1)} %maximum_bitcast_fusion.5) | copy-start | bytes 3145732
  194.4 11.7 %copy-start.14 = (bf16[1,8,2,128,256]{4,3,2,1,0:T(8,128)(2,1)S(1)}, bf16[1,8,2,128,256]{4,3,2,1,0:T(8,128)(2,1)}, u32[]{:S(2)}) copy-start(bf16[1,8,2,128,256]{4,3,2,1,0:T(8,128)(2,1)} %attended_to_rows.1) | copy-start | bytes 3145732
  195.9 11.6 %copy-start.4 = (bf16[2,1,128,2048]{3,2,1,0:T(8,128)(2,1)S(1)}, bf16[2,1,128,2048]{3,2,1,0:T(8,128)(2,1)}, u32[]{:S(2)}) copy-start(bf16[2,1,128,2048]{3,2,1,0:T(8,128)(2,1)} %param.17) | copy-start | bytes 3145732
  377.8 123.5 %all-to-all-start.1 = ((bf16[4,2,512,512]{3,2,1,0:T(8,128)(2,1)}), bf16[4,2,512,512]{3,2,1,0:T(8,128)(2,1)}, u32[]{:S(2)}, u32[]{:S(2)}) async-start(bf16[4,2,512,512]{3,2,1,0:T(8,128)(2,1)} %bitcast.151), calls=%async_computation.1 | async-start | bytes 8388608 | tf_op jit(solution)/shard_map/all_to_all | solution.py:52
  501.3 115.1 %all-to-all-start.2 = ((bf16[4,2,512,512]{3,2,1,0:T(8,128)(2,1)}), bf16[4,2,512,512]{3,2,1,0:T(8,128)(2,1)}, u32[]{:S(2)}, u32[]{:S(2)}) async-start(bf16[4,2,512,512]{3,2,1,0:T(8,128)(2,1)} %get-tuple-element.129), calls=%async_computation.2 | async-start | bytes 8388608 | tf_op jit(solution)/shard_map/all_to_all | solution.py:52
  506.4 569.9 %reduce-scatter.2.cloned.1.call-start = ((), (), s32[]{:S(2)}) async-start(), calls=%async_computation.5 | async-start | bytes 8650752 | tf_op jit(solution)/shard_map/reduce_scatter | solution.py:1386
  619.5 161.0 %collective-permute-start.1 = (bf16[2,256,2048]{2,1,0:T(8,128)(2,1)}, bf16[2,256,2048]{2,1,0:T(8,128)(2,1)}, u32[]{:S(2)}, u32[]{:S(2)}) collective-permute-start(bf16[2,256,2048]{2,1,0:T(8,128)(2,1)} %fusion.12), channel_id=1, source_target_pairs={{0,8},{8,0},{1,9},{9,1},{2,10},{10,2},{3,11},{11,3},{4,12},{12,4},... | collective-permute-start | bytes 6291464 | tf_op jit(solution)/shard_map/ppermute | solution.py:1353
  789.4 7.0 slice-start
  792.2 4.3 slice-start.1
  804.5 6.5 copy-start.8
  804.5 264.7 %all-to-all-start.3 = ((bf16[4,2,512,512]{3,2,1,0:T(8,128)(2,1)}), bf16[4,2,512,512]{3,2,1,0:T(8,128)(2,1)}, u32[]{:S(2)}, u32[]{:S(2)}) async-start(bf16[4,2,512,512]{3,2,1,0:T(8,128)(2,1)} %get-tuple-element.174), calls=%async_computation.4 | async-start | bytes 8388608 | tf_op jit(solution)/shard_map/all_to_all | solution.py:52
  987.4 32.2 %copy-start.11 = (f32[2,128,2048]{2,1,0:T(8,128)S(1)}, f32[2,128,2048]{2,1,0:T(8,128)}, u32[]{:S(2)}) copy-start(f32[2,128,2048]{2,1,0:T(8,128)} %get-tuple-element.169) | copy-start | bytes 6291460
  1062.8 4.5 copy-start.6
  (9 other events, 21.9 us)
Sparse Core Ops, SparseCore 0:
  100.9 53.6 all-gather.4
  156.5 58.5 all-gather.6
  804.6 188.0 reduce-scatter.1

commit v6 on v5

--- a/solution.py
+++ b/solution.py
@@ -63,10 +63,6 @@
         first = lax.axis_index("lane") == 0
         return jnp.stack([jnp.where(first, values, parts), jnp.where(first, parts, values)])
     return parts
-
-
-def reduce_small(values):
-    return jnp.sum(exchange_rows(values, "all", "small_gradients", 15), axis=(0, 1))
 
 
 def toggled(index, bits):
@@ -176,8 +172,8 @@
                 c.wait_recv()
 
 
-def relative_slots(own_ref, other_ref, s):
-    return lambda core, kr, km: (other_ref if core else own_ref).at[kr, s]
+def relative_slots(ref, s):
+    return lambda core, kr, km: ref.at[core, kr, s]
 
 
 def ctx_peers(quads):
@@ -196,8 +192,8 @@
 def gather_body(quads, partners, *refs):
     inputs = refs[: len(partners)]
     refs = refs[len(partners) :]
-    outputs = [(refs[2 * i], refs[2 * i + 1]) for i in range(len(partners))]
-    refs = refs[2 * len(partners) :]
+    outputs = refs[: len(partners)]
+    refs = refs[len(partners) :]
     keeps = {}
     for i, partner in enumerate(partners):
         if partner != "own":
@@ -213,10 +209,10 @@
     def add(sources, i, offset):
         plans = []
         for s, src in enumerate(sources):
-            p = Spread(mover, quads, src, relative_slots(*outputs[i], offset + s))
+            p = Spread(mover, quads, src, relative_slots(outputs[i], offset + s))
             p.begin()
             plans.append(p)
-            mover.keep(src, outputs[i][0].at[0, offset + s])
+            mover.keep(src, outputs[i].at[0, 0, offset + s])
         return plans
 
     crossing = {}
@@ -237,9 +233,10 @@
         for c in crossing[i]:
             c.wait_recv()
         offset = keep.shape[0] if partners[i] == "both" else 0
-        late += add([keep.at[s] for s in range(keep.shape[0])], i, offset)
-    for p in late:
-        p.forward()
+        added = add([keep.at[s] for s in range(keep.shape[0])], i, offset)
+        for p in added:
+            p.forward()
+        late += added
     for p in plans + late:
         p.arrive()
     mover.finish()
@@ -253,10 +250,10 @@
         count = x.shape[0] * (2 if partner == "both" else 1)
         total += count
         sems += count * Spread.count(quads) + (x.shape[0] if partner != "own" else 0)
-        shapes += [jax.ShapeDtypeStruct((quads, count) + x.shape[1:], x.dtype)] * 2
+        shapes.append(jax.ShapeDtypeStruct((2, quads, count) + x.shape[1:], x.dtype))
         if partner != "own":
             keeps.append(pltpu.VMEM(x.shape, x.dtype))
-    out = pl.pallas_call(
+    return pl.pallas_call(
         functools.partial(gather_body, quads, partners),
         out_shape=shapes,
         in_specs=[pl.BlockSpec(memory_space=pltpu.VMEM)] * len(sources),
@@ -270,12 +267,11 @@
         compiler_params=pltpu.CompilerParams(collective_id=number, has_side_effects=True),
         name=name,
     )(*sources)
-    return [(out[2 * i], out[2 * i + 1]) for i in range(len(sources))]
 
 
 def start_body(
     quads, lanes, tok_ref, qkv_ref, small_ref, wout_ref,
-    tok_own, tok_other, qkv_out, small_out, wout_out, local, send, recv,
+    tok_out, qkv_out, small_out, wout_out, local, send, recv,
 ):
     mover = Mover(send, recv, local)
     half, lane = lax.axis_index("half"), lax.axis_index("lane")
@@ -311,10 +307,10 @@
     mover.go(*columns)
     tokens = []
     for s in range(tok_ref.shape[0]):
-        p = Spread(mover, quads, tok_ref.at[s], relative_slots(tok_own, tok_other, s))
+        p = Spread(mover, quads, tok_ref.at[s], relative_slots(tok_out, s))
         p.begin()
         tokens.append(p)
-        mover.keep(tok_ref.at[s], tok_own.at[0, s])
+        mover.keep(tok_ref.at[s], tok_out.at[0, 0, s])
     for c in columns:
         c.wait_recv()
     kept.wait()
@@ -346,10 +342,10 @@
     sems += Spread.count(quads) * count
     return pl.pallas_call(
         functools.partial(start_body, quads, lanes),
-        out_shape=[like((quads,), tokens)] * 2
+        out_shape=[like((2, quads), tokens)]
         + [like((planes,), qkv), like((devices,), small), like((planes,), w_out)],
         in_specs=[pl.BlockSpec(memory_space=pltpu.VMEM)] * 4,
-        out_specs=[pl.BlockSpec(memory_space=pl.ANY)] * 5,
+        out_specs=[pl.BlockSpec(memory_space=pl.ANY)] * 4,
         scratch_shapes=[
             pltpu.SemaphoreType.DMA((3 + count,)),
             pltpu.SemaphoreType.DMA((sems,)),
@@ -375,8 +371,7 @@
 
 def scatter_body(quads, lanes, partners, count, extra, *refs):
     kinds = len(partners)
-    inputs = [(refs[2 * i], refs[2 * i + 1]) for i in range(kinds)]
-    refs = refs[2 * kinds :]
+    inputs, refs = refs[:kinds], refs[kinds:]
     if extra:
         blocks_ref, *refs = refs
     outputs, refs = refs[:kinds], refs[kinds:]
@@ -388,7 +383,7 @@
     local, send, recv = rest
     mover = Mover(send, recv, local)
     mover.local_number = local.shape[0] - 2
-    rows = inputs[0][0].shape[2]
+    rows = inputs[0].shape[3]
     first, second = pl.ds(0, rows // 2), pl.ds(rows // 2, rows // 2)
     quad = lax.axis_index("quad")
     to_quad = [{"quad": toggled(quad, k)} for k in range(quads)]
@@ -411,19 +406,39 @@
     order += [(i, s) for i in range(kinds) for s in range(count)]
     ks = [3, 1, 2, 0] if quads == 4 else list(range(quads - 1, -1, -1))
     sib, loc = {}, {}
+
+    def pieces(i, core, k, s):
+        if len(inputs[i].shape) == 5:
+            return [(inputs[i].at[core, k, s], pl.ds(0, rows))]
+        shard = inputs[i].shape[2]
+        place = ctx_at(quads, core * quads + k)[1]
+        each = rows // shard
+        return [
+            (inputs[i].at[s * each + j, place], pl.ds(j * shard, shard)) for j in range(each)
+        ]
+
+    def load(src, dst, number):
+        c = pltpu.make_async_copy(src, dst, local.at[number])
+        c.start()
+        return c
+
     for n, (i, s) in enumerate(order):
         for k in ks:
-            sib[n, k] = go(inputs[i][1].at[k, s], theirs.at[n, k], sibling)
-            loc[n, k] = pltpu.make_async_copy(
-                inputs[i][0].at[k, s], mine.at[n, k], local.at[n * quads + k]
-            )
-            loc[n, k].start()
+            sib[n, k] = [
+                go(src, theirs.at[n, k, part], sibling) for src, part in pieces(i, 1, k, s)
+            ]
+            loc[n, k] = [
+                load(src, mine.at[n, k, part], (n * quads + k) * 2 + j)
+                for j, (src, part) in enumerate(pieces(i, 0, k, s))
+            ]
     sends = {}
 
     def merge(n):
         for k in ks:
-            sib[n, k].wait_recv()
-            loc[n, k].wait()
+            for c in sib[n, k]:
+                c.wait_recv()
+            for c in loc[n, k]:
+                c.wait()
             add_rows(mine.at[n, k], mine.at[n, k], theirs.at[n, k])
             if quads == 4:
                 if k == 3:
@@ -485,14 +500,17 @@
     mover.finish()
 
 
-def scatter_rows(pairs, partners, name, number, extra=()):
+def scatter_rows(parts, partners, name, number, extra=()):
     lanes = lax.axis_size("lane")
-    quads, _, rows, width = pairs[0][0].shape
-    shards = sum(own.shape[1] for own, _ in pairs)
-    kinds = len(pairs)
+    _, quads, _, rows, width = parts[0].shape
+    shards = sum(
+        part.shape[2] if len(part.shape) == 5 else part.shape[0] * part.shape[2] // rows
+        for part in parts
+    )
+    kinds = len(parts)
     count = shards // sum(2 if partner else 1 for partner in partners)
     incoming = 2 if quads == 4 else quads - 1
-    sems = shards * (quads + (6 if quads == 4 else quads - 1)) + count * sum(partners)
+    sems = shards * (2 * quads + (6 if quads == 4 else quads - 1)) + count * sum(partners)
 
     def buf(*lead):
         return pltpu.VMEM(lead + (rows, width), BF)
@@ -513,11 +531,11 @@
     return pl.pallas_call(
         functools.partial(scatter_body, quads, lanes, partners, count, bool(extra)),
         out_shape=shapes,
-        in_specs=[anywhere] * (2 * kinds + len(extra)),
+        in_specs=[anywhere] * (kinds + len(extra)),
         out_specs=specs,
         scratch_shapes=scratch
         + [
-            pltpu.SemaphoreType.DMA((shards * quads + 2,)),
+            pltpu.SemaphoreType.DMA((2 * shards * quads + 2,)),
             pltpu.SemaphoreType.DMA((sems,)),
             pltpu.SemaphoreType.DMA((sems,)),
         ],
@@ -525,7 +543,7 @@
             collective_id=number, has_side_effects=True, vmem_limit_bytes=60 << 20
         ),
         name=name,
-    )(*[ref for pair in pairs for ref in pair], *extra)
+    )(*parts, *extra)
 
 
 def ctx_place():
@@ -610,6 +628,52 @@
     )(x)
 
 
+def final_body(quads, lanes, count, *refs):
+    inputs, outputs = refs[:count], refs[count : 2 * count]
+    local, send, recv = refs[2 * count :]
+    mover = Mover(send, recv, local)
+    plane, planes = planes_of(lanes)
+    here = ctx_place()
+    devices = [all_at(lanes, quads, n) for n in range(4 * lanes * quads)]
+    greet([device for device, _ in devices[1:]])
+    me = plane * 2 * quads + here
+    qkv, small = inputs[:2]
+    copies = [(qkv.at[place], outputs[0].at[here], device) for device, place in
+              [ctx_at(quads, n) for n in range(1, 2 * quads)]]
+    for ref, out in zip(inputs[2:], outputs[2:]):
+        copies += [(ref.at[place], out.at[plane], device) for device, place in planes]
+    copies += [(small.at[place], outputs[1].at[me], device) for device, place in devices[1:]]
+    started = [mover.copy(*c) for c in copies]
+    mover.go(*started)
+    mover.keep(qkv.at[here], outputs[0].at[here])
+    mover.keep(small.at[me], outputs[1].at[me])
+    for ref, out in zip(inputs[2:], outputs[2:]):
+        mover.keep(ref.at[plane], out.at[plane])
+    for c in started:
+        c.wait_recv()
+    mover.finish()
+
+
+def final_exchange(qkv, small, planes):
+    quads, lanes = lax.axis_size("quad"), lax.axis_size("lane")
+    arrays = [qkv, small, *planes]
+    sems = 2 * quads - 1 + 4 * lanes * quads - 1 + len(planes) * (2 * lanes - 1)
+    vmem = pl.BlockSpec(memory_space=pltpu.VMEM)
+    return pl.pallas_call(
+        functools.partial(final_body, quads, lanes, len(arrays)),
+        out_shape=[jax.ShapeDtypeStruct(x.shape, x.dtype) for x in arrays],
+        in_specs=[vmem] * len(arrays),
+        out_specs=[vmem] * len(arrays),
+        scratch_shapes=[
+            pltpu.SemaphoreType.DMA((len(arrays),)),
+            pltpu.SemaphoreType.DMA((sems,)),
+            pltpu.SemaphoreType.DMA((sems,)),
+        ],
+        compiler_params=pltpu.CompilerParams(collective_id=14, has_side_effects=True),
+        name="final_exchange",
+    )(*arrays)
+
+
 def sum_body(quads, x_ref, out_ref, landed, send, recv):
     count = 2 * quads
     greet([ctx_at(quads, n)[0] for n in range(1, count)])
@@ -662,21 +726,18 @@
     return lax.dot_general(left, right, (((0,), (0,)), ((), ())), preferred_element_type=F32)
 
 
-def expert_body(quads, before, _, gate_ref, xo_ref, xt_ref, go_ref, gpo_ref, gpt_ref, both_ref,
-                down_ref, *refs):
-    sums = refs[:4] if before else None
-    mo_ref, mt_ref, do_ref, dt_ref, dgate_ref, hid_ref, dg_ref, du_ref = refs[-8:]
+def expert_body(quads, before, _, gate_ref, x_ref, go_ref, gp_ref, both_ref, down_ref, *refs):
+    sums = refs[:2] if before else None
+    moe_ref, d_ref, dgate_ref, hid_ref, dg_ref, du_ref = refs[-6:]
     t = pl.program_id(0)
-    core_other = t >= 2 * quads
-    partner = t % 2 == 1
     hidden, width = down_ref.shape
-    x = jnp.where(core_other, xt_ref[0], xo_ref[0]).reshape(-1, width)
-    g_partner = jnp.where(core_other, gpt_ref[0], gpo_ref[0])
-    g = jnp.where(partner, g_partner, go_ref[0]).reshape(-1, width)
+    x = x_ref[0, 0].reshape(-1, width)
     gate = gate_ref[0]
     wg = both_ref[:, 0].reshape(width, hidden)
     wu = both_ref[:, 1].reshape(width, hidden)
     wd = down_ref[...]
+
+    g = jnp.where(t % 2 == 1, gp_ref[0, 0], go_ref[0]).reshape(-1, width)
     gate_pre = nn(x, wg)
     up_pre = nn(x, wu)
     d_hidden = nt(g, wd)
@@ -691,85 +752,61 @@
     hid_ref[0] = scaled
     dg_ref[0] = d_gate_pre
     du_ref[0] = d_up_pre
-    moe = nn(scaled, wd).reshape(mo_ref.shape[1:])
-    d_rows = (nt(d_gate_pre, wg) + nt(d_up_pre, wu)).reshape(mo_ref.shape[1:])
+    shape = moe_ref.shape[2:]
+    moe = nn(scaled, wd).reshape(shape)
+    d_rows = (nt(d_gate_pre, wg) + nt(d_up_pre, wu)).reshape(shape)
     if before:
-        moe = moe + jnp.where(core_other, sums[1][0], sums[0][0]).astype(F32)
-        d_rows = d_rows + jnp.where(core_other, sums[3][0], sums[2][0]).astype(F32)
-    moe, d_rows = moe.astype(BF), d_rows.astype(BF)
-
-    @pl.when(jnp.logical_not(core_other))
-    def _():
-        mo_ref[0] = moe
-        do_ref[0] = d_rows
-
-    @pl.when(core_other)
-    def _():
-        mt_ref[0] = moe
-        dt_ref[0] = d_rows
+        moe = moe + sums[0][0, 0].astype(F32)
+        d_rows = d_rows + sums[1][0, 0].astype(F32)
+    moe_ref[0, 0] = moe.astype(BF)
+    d_ref[0, 0] = d_rows.astype(BF)
 
 
 def expert(place, gates, x_rows, g_rows, both, down, before, name):
-    quads, shards, rows, width = x_rows[0].shape
+    _, quads, shards, rows, width = x_rows.shape
     batches = shards // 2
     hidden = down.shape[0]
     tiles = 4 * quads
     tile = batches * rows
 
-    def own(t, p):
-        return (jnp.minimum(t, 2 * quads - 1) // 2, jnp.minimum(t, 2 * quads - 1) % 2, 0, 0)
-
-    def other(t, p):
-        u = jnp.maximum(t - 2 * quads, 0)
-        return (u // 2, u % 2, 0, 0)
-
-    def cot(t, p):
-        return (p[t // 2], 0, 0, 0)
-
-    def own_g(t, p):
-        return (jnp.minimum(t // 2, quads - 1), 0, 0, 0)
-
-    def other_g(t, p):
-        return (jnp.maximum(t // 2 - quads, 0), 0, 0, 0)
-
-    shard_block = (1, batches, rows, width)
+    def row_block(t, p):
+        return (t // (2 * quads), t // 2 % quads, t % 2, 0, 0)
+
+    block = pl.BlockSpec((1, 1, batches, rows, width), row_block)
     saved_spec = pl.BlockSpec((1, tile, hidden), lambda t, p: (t, 0, 0))
     saved = jax.ShapeDtypeStruct((tiles, tile, hidden), BF)
-    rows_shape = jax.ShapeDtypeStruct(x_rows[0].shape, BF)
+    rows_shape = jax.ShapeDtypeStruct(x_rows.shape, BF)
     fixed = dict(pipeline_mode=pl.Buffered(1))
-    sums_specs = [
-        pl.BlockSpec(shard_block, own), pl.BlockSpec(shard_block, other),
-        pl.BlockSpec(shard_block, own), pl.BlockSpec(shard_block, other),
-    ]
+    column = pl.BlockSpec((1, tile, 1), lambda t, p: (t, 0, 0))
     return pl.pallas_call(
         functools.partial(expert_body, quads, bool(before)),
-        out_shape=(rows_shape,) * 4
+        out_shape=(rows_shape,) * 2
         + (jax.ShapeDtypeStruct((tiles, tile, 1), F32), saved, saved, saved),
         grid_spec=pltpu.PrefetchScalarGridSpec(
             num_scalar_prefetch=1,
             grid=(tiles,),
             in_specs=[
-                pl.BlockSpec((1, tile, 1), lambda t, p: (t, 0, 0)),
-                pl.BlockSpec(shard_block, own),
-                pl.BlockSpec(shard_block, other),
-                pl.BlockSpec(shard_block, cot),
-                pl.BlockSpec(shard_block, own_g), pl.BlockSpec(shard_block, other_g),
+                column, block,
+                pl.BlockSpec((1, batches, rows, width), lambda t, p: (p[t // 2], 0, 0, 0)),
+                pl.BlockSpec(
+                    (1, 1, batches, rows, width),
+                    lambda t, p: (t // (2 * quads), t // 2 % quads, 0, 0, 0),
+                ),
                 pl.BlockSpec(both.shape, lambda t, p: (0, 0, 0, 0), **fixed),
                 pl.BlockSpec(down.shape, lambda t, p: (0, 0), **fixed),
             ]
-            + (sums_specs if before else []),
-            out_specs=sums_specs
-            + [pl.BlockSpec((1, tile, 1), lambda t, p: (t, 0, 0)), saved_spec, saved_spec, saved_spec],
+            + ([block] * 2 if before else []),
+            out_specs=[block, block, column, saved_spec, saved_spec, saved_spec],
         ),
-        input_output_aliases={9 + i: i for i in range(4)} if before else {},
+        input_output_aliases={7 + i: i for i in range(2)} if before else {},
         compiler_params=pltpu.CompilerParams(
             dimension_semantics=("arbitrary",), vmem_limit_bytes=60 << 20
         ),
         name=name,
-    )(place, gates, *x_rows, *g_rows, both, down, *before)
-
-
-def grads_body(quads, _, xo_ref, xt_ref, go_ref, gpo_ref, gpt_ref, hid_ref, dg_ref, du_ref, both_ref, down_ref,
+    )(place, gates, x_rows, *g_rows, both, down, *before)
+
+
+def grads_body(_, x_ref, go_ref, gp_ref, hid_ref, dg_ref, du_ref, both_ref, down_ref,
                gate_acc, up_acc, down_acc):
     t = pl.program_id(0)
     width = down_acc.shape[1]
@@ -781,9 +818,8 @@
         up_acc[...] = jnp.zeros_like(up_acc)
         down_acc[...] = jnp.zeros_like(down_acc)
 
-    x = jnp.where(t >= quads, xt_ref[0], xo_ref[0]).reshape(-1, width)
-    g_partner = jnp.where(t >= quads, gpt_ref[0], gpo_ref[0]).reshape(-1, width)
-    g = jnp.concatenate([go_ref[0].reshape(-1, width), g_partner], axis=0)
+    x = x_ref[0, 0].reshape(-1, width)
+    g = jnp.concatenate([go_ref[0].reshape(-1, width), gp_ref[0, 0].reshape(-1, width)], axis=0)
     gate_acc[...] += tn(x, dg_ref[...].reshape(-1, hidden))
     up_acc[...] += tn(x, du_ref[...].reshape(-1, hidden))
     down_acc[...] += tn(hid_ref[...].reshape(-1, hidden), g)
@@ -797,24 +833,17 @@
 
 
 def expert_grads(place, x_rows, g_rows, hid, dg, du, dp, name):
-    quads, shards, rows, width = x_rows[0].shape
+    _, quads, shards, rows, width = x_rows.shape
     batches = shards // 2
     tiles, tile, hidden = hid.shape
 
     saved = pl.BlockSpec((2, tile, hidden), lambda t, p: (t, 0, 0))
 
-    def own(t, p):
-        return (jnp.minimum(t, quads - 1), 0, 0, 0)
-
-    def other(t, p):
-        return (jnp.maximum(t - quads, 0), 0, 0, 0)
-
-    def cot(t, p):
-        return (p[t], 0, 0, 0)
-
-    g_block = (1, batches, rows, width)
+    def row_block(t, p):
+        return (t // quads, t % quads, 0, 0, 0)
+
     return pl.pallas_call(
-        functools.partial(grads_body, quads),
+        grads_body,
         out_shape=(
             jax.ShapeDtypeStruct((dp, 2, width // dp, hidden), BF),
             jax.ShapeDtypeStruct((hidden, width), BF),
@@ -823,9 +852,9 @@
             num_scalar_prefetch=1,
             grid=(tiles // 2,),
             in_specs=[
-                pl.BlockSpec((1, shards, rows, width), own),
-                pl.BlockSpec((1, shards, rows, width), other),
-                pl.BlockSpec(g_block, cot), pl.BlockSpec(g_block, own), pl.BlockSpec(g_block, other),
+                pl.BlockSpec((1, 1, shards, rows, width), row_block),
+                pl.BlockSpec((1, batches, rows, width), lambda t, p: (p[t], 0, 0, 0)),
+                pl.BlockSpec((1, 1, batches, rows, width), row_block),
                 saved, saved, saved,
             ],
             out_specs=[
@@ -839,7 +868,7 @@
             dimension_semantics=("arbitrary",), vmem_limit_bytes=60 << 20
         ),
         name=name,
-    )(place, *x_rows, *g_rows, hid, dg, du)
+    )(place, x_rows, *g_rows, hid, dg, du)
 
 
 def finish_body(lanes, *refs):
@@ -883,12 +912,10 @@
     return jnp.concatenate([turned[:, i : i + 1] for i in range(values.shape[0])], axis=0)
 
 
-def qkv_body(quads, xo_ref, xt_ref, gain_ref, w_ref, ao_ref, at_ref, pre_ref, square_ref):
-    n = pl.program_id(0)
-    other = n >= quads
-    batches, rows, width = xo_ref.shape[1:]
+def qkv_body(x_ref, gain_ref, w_ref, act_ref, pre_ref, square_ref):
+    batches, rows, width = x_ref.shape[2:]
     head_width = w_ref.shape[1] // 3
-    x = jnp.where(other, xt_ref[0], xo_ref[0]).astype(F32).reshape(-1, width)
+    x = x_ref[0, 0].astype(F32).reshape(-1, width)
     root = lax.rsqrt(jnp.mean(x * x, axis=1, keepdims=True) + EPSILON)
     act = (x * root * gain_ref[...]).astype(BF)
     pre = nn(act, w_ref[...])
@@ -899,53 +926,39 @@
         for m in range(batches):
             i = kind * batches + m
             square_ref[0, i : i + 1] = sums[:, m * rows : (m + 1) * rows]
-    act = act.reshape(batches, rows, width)
-
-    @pl.when(jnp.logical_not(other))
-    def _():
-        ao_ref[0] = act
-
-    @pl.when(other)
-    def _():
-        at_ref[0] = act
-
-
-def own_block(quads):
-    return lambda n: (jnp.minimum(n, quads - 1), 0, 0, 0)
-
-
-def other_block(quads):
-    return lambda n: (jnp.maximum(n - quads, 0), 0, 0, 0)
+    act_ref[0, 0] = act.reshape(batches, rows, width)
+
+
+def row_spec(quads, shape):
+    return pl.BlockSpec((1, 1) + shape, lambda n: (n // quads, n % quads, 0, 0, 0))
 
 
 def project(token_rows, gain, weights):
-    quads, batches, rows, width = token_rows[0].shape
+    _, quads, batches, rows, width = token_rows.shape
     total = weights.shape[1]
-    block = (1, batches, rows, width)
     fixed = dict(pipeline_mode=pl.Buffered(1))
-    own, other = pl.BlockSpec(block, own_block(quads)), pl.BlockSpec(block, other_block(quads))
+    block = row_spec(quads, (batches, rows, width))
     return pl.pallas_call(
-        functools.partial(qkv_body, quads),
+        qkv_body,
         out_shape=(
-            jax.ShapeDtypeStruct(token_rows[0].shape, BF),
-            jax.ShapeDtypeStruct(token_rows[0].shape, BF),
+            jax.ShapeDtypeStruct(token_rows.shape, BF),
             jax.ShapeDtypeStruct((batches, 2 * quads, rows, total), F32),
             jax.ShapeDtypeStruct((2 * quads, 2 * batches, rows), F32),
         ),
         grid=(2 * quads,),
         in_specs=[
-            own, other,
+            block,
             pl.BlockSpec((1, width), lambda n: (0, 0)),
             pl.BlockSpec((width, total), lambda n: (0, 0), **fixed),
         ],
         out_specs=(
-            own, other,
+            block,
             pl.BlockSpec((batches, 1, rows, total), lambda n: (0, n, 0, 0)),
             pl.BlockSpec((1, 2 * batches, rows), lambda n: (n, 0, 0)),
         ),
         compiler_params=pltpu.CompilerParams(vmem_limit_bytes=40 << 20),
         name="project",
-    )(*token_rows, gain.reshape(1, width), weights)
+    )(token_rows, gain.reshape(1, width), weights)
 
 
 def turned(values, cosine, sine):
@@ -1110,11 +1123,9 @@
 
 
 def back_body(
-    quads, dn_ref, dv_ref, pre_ref, sum_ref, inner_ref, ao_ref, at_ref, w_ref,
-    do_ref, dt_ref, dw_ref, dw, cols,
+    quads, dn_ref, dv_ref, pre_ref, sum_ref, inner_ref, act_ref, w_ref, d_ref, dw_ref, dw, cols,
 ):
     n = pl.program_id(0)
-    other = n >= quads
     batches, _, rows, head_width = dn_ref.shape
     width = w_ref.shape[0]
     total = head_width * 2 * quads
@@ -1129,8 +1140,8 @@
             cols[here, part] = grad.astype(BF)
         cols[here, 2 * head_width :] = dv_ref[m]
     d_pre = cols[...]
-    act = jnp.where(other, at_ref[0], ao_ref[0]).reshape(-1, width)
-    d_act = nt(d_pre, w_ref[...]).astype(BF).reshape(batches, rows, width)
+    act = act_ref[0, 0].reshape(-1, width)
+    d_ref[0, 0] = nt(d_pre, w_ref[...]).astype(BF).reshape(batches, rows, width)
     part = tn(act, d_pre)
 
     @pl.when(n == 0)
@@ -1145,57 +1156,45 @@
     def _():
         dw_ref[...] = dw[...].astype(BF)
 
-    @pl.when(jnp.logical_not(other))
-    def _():
-        do_ref[0] = d_act
-
-    @pl.when(other)
-    def _():
-        dt_ref[0] = d_act
-
 
 def project_back(d_norm, d_value, pre, sums, inners, act, weights):
     batches, places, rows, total = pre.shape
     quads, width, head_width = places // 2, weights.shape[0], total // 3
-    block = (1, batches, rows, width)
     fixed = dict(pipeline_mode=pl.Buffered(1))
-    own, other = pl.BlockSpec(block, own_block(quads)), pl.BlockSpec(block, other_block(quads))
+    block = row_spec(quads, (batches, act.shape[3], width))
     sums = sums.transpose(2, 0, 1, 3)[:, :, :, None]
     inners = inners[:, :, :, None]
     small = pl.BlockSpec((1, batches, 2, 1, rows), lambda n: (n, 0, 0, 0, 0))
     return pl.pallas_call(
         functools.partial(back_body, quads),
         out_shape=(
-            jax.ShapeDtypeStruct(act[0].shape, BF), jax.ShapeDtypeStruct(act[0].shape, BF),
-            jax.ShapeDtypeStruct(weights.shape, BF),
+            jax.ShapeDtypeStruct(act.shape, BF), jax.ShapeDtypeStruct(weights.shape, BF),
         ),
         grid=(places,),
         in_specs=[
             pl.BlockSpec((batches, 2, rows, head_width), lambda n: (0, 0, n, 0)),
             pl.BlockSpec((batches, rows, head_width), lambda n: (0, n, 0)),
             pl.BlockSpec((batches, 1, rows, total), lambda n: (0, n, 0, 0)),
-            small, small, own, other,
+            small, small, block,
             pl.BlockSpec(weights.shape, lambda n: (0, 0), **fixed),
         ],
-        out_specs=(own, other, pl.BlockSpec(weights.shape, lambda n: (0, 0))),
+        out_specs=(block, pl.BlockSpec(weights.shape, lambda n: (0, 0))),
         scratch_shapes=[
             pltpu.VMEM(weights.shape, F32), pltpu.VMEM((batches * rows, total), BF)
         ],
         compiler_params=pltpu.CompilerParams(vmem_limit_bytes=60 << 20),
         name="project_back",
-    )(d_norm, d_value, pre, sums, inners, *act, weights)
-
-
-def scatter_all(pairs, partners, name, number, extra=()):
-    if pairs[0][0].shape[0] == 4:
-        return scatter_rows(pairs, partners, name, number, extra)
+    )(d_norm, d_value, pre, sums, inners, act, weights)
+
+
+def scatter_all(kinds, partners, name, number, extra=()):
+    if kinds[0].shape[1] == 4:
+        return scatter_rows(kinds, partners, name, number, extra)
     sums = []
-    for i, ((own, other), partner) in enumerate(zip(pairs, partners)):
-        count = own.shape[1] // 2 if partner else own.shape[1]
+    for i, (kind, partner) in enumerate(zip(kinds, partners)):
+        count = kind.shape[2] // 2 if partner else kind.shape[2]
         parts = [
-            scatter_rows(
-                [(own[:, m::count], other[:, m::count])], (partner,), name, number + 8 * i
-            )[0]
+            scatter_rows([kind[:, :, m::count]], (partner,), name, number + 8 * i)[0]
             for m in range(count)
         ]
         sums.append(jnp.concatenate(parts))
@@ -1243,11 +1242,10 @@
         [attn_gain, mlp_gain, query_gain, key_gain, w_router.reshape(shard * expert_count)]
     )
     grad_low = cotangent[:, 0]
-    tok_own, tok_other, qkv_w, small, out_w = start_gather(
+    token_rows, qkv_w, small, out_w = start_gather(
         tokens[:, 0], qkv, small.reshape(1, -1), w_out
     )
     out_w = lax.all_gather(out_w, CTX, axis=1, tiled=False).reshape(width, width)
-    token_rows = (tok_own, tok_other)
     qkv_w = qkv_w.reshape(width, 3 * head_width)
     small = small.reshape(dp_size * ctx_size, -1)
     gain_attn = small[:, :shard].reshape(width).astype(F32)
@@ -1296,8 +1294,10 @@
 
     inputs = tokens[:, 0].astype(F32)
     attn_root = inv_rms(inputs)
-    act_own, act_other, pre, squares = project(token_rows, gain_attn, qkv_w)
+    act, pre, squares = project(token_rows, gain_attn, qkv_w)
     squares = sum_ctx(squares, "sum_squares", 6)
+    squares, crossing = lax.optimization_barrier((squares, crossing))
+    crossing = swap(crossing, "half")
     squares = squares.reshape(2 * quads, 2, batches, rows).transpose(2, 1, 0, 3)
     qk_gains = jnp.stack([gain_query, gain_key])[:, None]
     signed = jnp.where(jnp.arange(HEAD) < HEAD // 2, -sine[:, 0], sine[:, 0])
@@ -1313,10 +1313,10 @@
     router = jax.nn.softmax(dot("mtd,de->mte", mixed_in, router_w), axis=-1)
     routed = jnp.any(routes[:, 0, :, :, None] == expert_range, axis=2).astype(F32)
     gates = (router * routed).transpose(2, 0, 1).reshape(ctx_size, local_experts, batches, rows)
-    x_rows, cross_rows = gather_rows([mixed_in, grad_low], ("both", "partner"), "gather_mixed", 2)
+    x_rows, cross_rows = gather_rows([mixed_in, crossing], ("both", "own"), "gather_mixed", 2)
     gates, x_rows = lax.optimization_barrier((gates, x_rows))
     gates = exchange_rows(gates, "outward", "gates_to_experts", 8, 2)
-    g_rows = (g_own,) + cross_rows
+    g_rows = (g_own, cross_rows)
     gates = gates.transpose(1, 0, 3, 4, 2).reshape(4 * quads, batches * rows, local_experts)
     number = jnp.arange(2 * quads, dtype=jnp.int32)
     place = (lax.axis_index("quad") ^ (number % quads)) * 2 + (pair ^ (number // quads))
@@ -1343,8 +1343,8 @@
         sums[0], grad_both, next_w = lax.optimization_barrier((sums[0], grad_both, next_w))
         grads_both.append(exchange(grad_both, DP) if e < local_experts - 1 else grad_both)
         grads_down.append(grad_down)
-    moe_own, moe_other, d_own, d_other = sums
-    done, grads_down, d_own = lax.optimization_barrier((grads_both[:-1], grads_down, d_own))
+    moe_rows, d_rows = sums
+    done, grads_down, d_rows = lax.optimization_barrier((grads_both[:-1], grads_down, d_rows))
     grads_both[:-1] = done
     grads_down = jnp.stack(grads_down)
     grads_down = grads_down.reshape(local_experts, lanes, -1, width).swapaxes(0, 1)
@@ -1357,7 +1357,7 @@
         for d in range(1, lanes)
     ]
     d_mixed, moe_sum = scatter_all(
-        [(d_own, d_other), (moe_own, moe_other)], (True, True), "scatter_experts", 24
+        [d_rows, moe_rows], (True, True), "scatter_experts", 24
     )
     d_gates = jnp.concatenate(d_gates, axis=-1)
     d_gates = d_gates.reshape(2 * quads, 2, batches, rows, local_experts)
@@ -1382,19 +1382,21 @@
     d_att_out = d_mid.astype(BF)
     grad_out = dot("mtd,mte->de", attended, d_att_out).astype(BF)
     d_attended = dot("mte,de->mtd", d_att_out, out_w).astype(BF)
-    d_attended, grad_out = lax.optimization_barrier((d_attended, grad_out))
-    grad_out = lax.psum_scatter(grad_out, ALL, scatter_dimension=0, tiled=True).astype(F32)
+    beside = quads == 4 and dp_size * shard == batches * rows
+    if not beside:
+        grad_out = lax.psum_scatter(grad_out, ALL, scatter_dimension=0, tiled=True).astype(F32)
     d_attended = d_attended.reshape(batches, rows, ctx_size, head_width).transpose(2, 0, 1, 3)
     d_attended = exchange_rows(d_attended, "outward", "attended_gradients", 10)[0]
     d_norm, d_value, inners, d_gains = attend_back(saved, d_attended, *context)
     inners = inners.transpose(2, 0, 1, 3).reshape(2 * quads, 2 * batches, rows)
     inners = sum_ctx(inners, "sum_inner", 11).reshape(2 * quads, batches, 2, rows)
-    d_act_own, d_act_other, grad_qkv = project_back(
-        d_norm, d_value, pre, squares, inners, (act_own, act_other), qkv_w
-    )
+    d_act, grad_qkv = project_back(d_norm, d_value, pre, squares, inners, act, qkv_w)
     grad_qkv = grad_qkv.reshape(dp_size, -1, 3 * head_width)
-    d_act, grad_qkv = scatter_all(
-        [(d_act_own, d_act_other)], (False,), "scatter_act", 25, (grad_qkv,)
+    kinds = [d_act]
+    if beside:
+        kinds.append(grad_out.reshape(dp_size, ctx_size, shard, width))
+    d_act, *grad_planes, grad_qkv = scatter_all(
+        kinds, (False,) * len(kinds), "scatter_act", 25, (grad_qkv,)
     )
     d_inputs, part_attn_gain = norm_back_all(inputs, attn_root, gain_attn, d_act)
     mixed = (x_mid + moe_sum).astype(BF)
@@ -1406,10 +1408,7 @@
 
     grad_qkv = jnp.sum(grad_qkv.astype(F32), axis=0).astype(BF)
     grad_qkv = grad_qkv.reshape(ctx_size, shard, 3 * head_width)
-    grad_qkv = exchange_rows(grad_qkv, "ctx", "qkv_gradients", 14).astype(F32)
-    grad_qkv = grad_qkv.reshape(ctx_size, shard, 3, head_width).transpose(2, 1, 0, 3)
-    grad_qkv = grad_qkv.reshape(3, shard, width)
-
+    grad_planes = [part.reshape(dp_size, shard, width).astype(BF) for part in grad_planes]
     grad_router = dot("mtd,mte->de", mixed_in, d_logits)
     columns = jnp.arange(ctx_size, dtype=jnp.int32)[:, None] == here
 
@@ -1427,7 +1426,14 @@
         ],
         axis=2,
     )
-    packed = reduce_small(packed)
+    grad_qkv, packed, *grad_planes = final_exchange(grad_qkv, packed, grad_planes)
+    packed = jnp.sum(packed, axis=(0, 1))
+    grad_qkv = grad_qkv.astype(F32)
+    if beside:
+        grad_out = jnp.sum(grad_planes[0].astype(F32), axis=0)
+    grad_qkv = grad_qkv.reshape(ctx_size, shard, 3, head_width).transpose(2, 1, 0, 3)
+    grad_qkv = grad_qkv.reshape(3, shard, width)
+
     return (
         mixed[:, None],
         (d_inputs + d_mid)[:, None],

time: 1090 us -> 1050 us (0.963)
  Pallas kernels: 914 us -> 832 us
  waiting for transfers between devices: 11 us -> 44.9 us
    pallas_call x6 -> x4, Pallas kernels: 114 us -> 53.4 us  [exchange_rows(): pl.pallas_call(functools.partial(exchange_body, mode, lanes, quads, halve...]
    pallas_call x1, Pallas kernels: 145 us -> 113 us  [gather_rows(): pl.pallas_call(functools.partial(gather_body, quads, partners), out_shape...]
    ppermute x1 -> x2, waiting for transfers between devices: 0.01 us -> 29.9 us  [swap(): return lax.ppermute(values, axis, [(0, 1), (1, 0)])]
    pallas_call x3 -> x4, Pallas kernels: 92.7 us -> 121 us  [the longest x2 71.3 us: expert_grads(): pl.pallas_call(grads_body, out_shape=(jax.ShapeDtypeStruct((dp, 2, width...]
    pallas_call x2, Pallas kernels: 143 us -> 130 us  [expert(): pl.pallas_call(functools.partial(expert_body, quads, bool(before)), out_s...]
  transfers between devices with their start and end apart: 9 -> 9, of which waited for: 1 -> 2; matrix products, arithmetic and copies ran while one was open for 8% -> 10% of each run, Pallas kernels for 76% -> 70%
where the time goes in v6:
time: 1050 us; the launch traced here: 1040 us
  Pallas kernels  832 us (79%)
  local copies, waits for them, and re-layouts  63.2 us (6%)
  waiting for transfers between devices  44.9 us (4%)
  other arithmetic  38.3 us (4%)
  starting transfers between devices  29.5 us (3%)
  matrix products  21.5 us (2%)
  between operations  14.9 us (1%)
    pallas_call x2, Pallas kernels, scatter_rows(): pl.pallas_call(functools.partial(scatter_body, quads, lanes, partners, co...  233 us
    pallas_call x2, Pallas kernels, expert(): pl.pallas_call(functools.partial(expert_body, quads, bool(before)), out_s...  130 us
    pallas_call x1, Pallas kernels, gather_rows(): pl.pallas_call(functools.partial(gather_body, quads, partners), out_shape...  113 us
    pallas_call x1, Pallas kernels, start_gather(): pl.pallas_call(functools.partial(start_body, quads, lanes), out_shape=[li...  82.6 us
    pallas_call x2, Pallas kernels, expert_grads(): pl.pallas_call(grads_body, out_shape=(jax.ShapeDtypeStruct((dp, 2, width...  71.3 us
    pallas_call x4, Pallas kernels, exchange_rows(): pl.pallas_call(functools.partial(exchange_body, mode, lanes, quads, halve...  53.4 us
    pallas_call x1, Pallas kernels, final_exchange(): pl.pallas_call(functools.partial(final_body, quads, lanes, len(arrays)),...  34.6 us
    ppermute x2, waiting for transfers between devices, swap(): return lax.ppermute(values, axis, [(0, 1), (1, 0)])  29.9 us
  transfers between devices with their start and end apart: 9, of which 2 were waited for; matrix products, arithmetic and copies ran while one was open for 10% of the time, Pallas kernels for 70%

profile of v6, /device:TPU:0, one launch (start us, length us, event | category | flops | bytes accessed | tf_op | source)
XLA Modules:
  0.0 1043.9 jit_solution(6960279609738724240)
XLA Ops:
  18.3 82.6 %start_gather.1 = (bf16[2,4,2,128,2048]{4,3,2,1,0:T(8,128)(2,1)}, bf16[4,8,64,768]{3,2,1,0:T(8,128)(2,1)}, bf16[32,1,1280]{2,1,0:T(2,128)(2,1)}, bf16[4,64,2048]{2,1,0:T(8,128)(2,1)}) custom-call(bf16[2,128,2048]{2,1,0:T(8,128)(2,1)} %bitcast.151, bf16[8,64,768]{2,1,0:T(8,128)(2,1)} %reshape.491.qkv_ref, bf16[1,1280]{1,0:T(2,128)(2,1)} %reshape.493.small_ref, ...), custom_call_target="tpu_custom_call" | custom-call | tf_op jit(solution)/shard_map/start_gather/pallas_call | solution.py:343
  115.3 15.4 %project.1 = (bf16[2,4,2,128,2048]{4,3,2,1,0:T(8,128)(2,1)}, f32[2,8,128,768]{3,2,1,0:T(8,128)S(1)}, f32[8,4,128]{2,1,0:T(4,128)S(1)}) custom-call(bf16[2,4,2,128,2048]{4,3,2,1,0:T(8,128)(2,1)} %get-tuple-element.89.x_ref, f32[1,2048]{1,0:T(1,128)S(1)} %reshape.517.gain_ref, bf16[2048,768]{1,0:T(8,128)(2,1)S(1)} %bitcast.145), custom_call_target="tpu_custom_call" | custom-call | tf_op jit(solution)/shard_map/project/pallas_call | solution.py:941
  134.0 8.1 sum_squares.1
  153.2 19.7 %attend.1 = (bf16[2,1024,256]{2,1,0:T(8,128)(2,1)}, bf16[2,1024,256]{2,1,0:T(8,128)(2,1)}, bf16[2,1024,256]{2,1,0:T(8,128)(2,1)}, bf16[8,2,128,256]{3,2,1,0:T(8,128)(2,1)}) custom-call(f32[2,8,128,768]{3,2,1,0:T(8,128)} %copy-done, f32[2,2,8,128]{3,2,1,0:T(8,128)} %bitcast.192, f32[2,1,256]{2,1,0:T(1,128)} %reshape.518.gain_ref, ...), custom_call_target="tpu_custom_call" | custom-call | tf_op jit(solution)/shard_map/attend/pallas_call | solution.py:1015
  172.9 19.0 %attended_to_rows.1 = bf16[1,8,2,128,256]{4,3,2,1,0:T(8,128)(2,1)} custom-call(bf16[1,8,2,128,256]{4,3,2,1,0:T(8,128)(2,1)} %bitcast.183), custom_call_target="tpu_custom_call" | custom-call | tf_op jit(solution)/shard_map/attended_to_rows/pallas_call | solution.py:616
  193.4 14.3 %all-to-all-done.both_ref = bf16[4,2,512,512]{3,2,1,0:T(8,128)(2,1)} async-done(((bf16[4,2,512,512]{3,2,1,0:T(8,128)(2,1)}), bf16[4,2,512,512]{3,2,1,0:T(8,128)(2,1)}, u32[]{:S(2)}, u32[]{:S(2)}) %all-to-all-start) | async-done | bytes 4194336 | tf_op jit(solution)/shard_map/all_to_all | solution.py:52
  209.0 6.2 multiply_reduce_fusion.2
  218.9 29.9 %collective-permute-done.refs_1_ = bf16[2,128,2048]{2,1,0:T(8,128)(2,1)} collective-permute-done((bf16[2,128,2048]{2,1,0:T(8,128)(2,1)}, bf16[2,128,2048]{2,1,0:T(8,128)(2,1)}, u32[]{:S(2)}, u32[]{:S(2)}) %collective-permute-start) | collective-permute-done | bytes 1048608 | tf_op jit(solution)/shard_map/ppermute | solution.py:48
  248.7 113.0 %gather_mixed.1 = (bf16[2,4,4,128,2048]{4,3,2,1,0:T(8,128)(2,1)}, bf16[2,4,2,128,2048]{4,3,2,1,0:T(8,128)(2,1)}) custom-call(bf16[2,128,2048]{2,1,0:T(8,128)(2,1)} %multiply_convert_fusion.refs_0_, bf16[2,128,2048]{2,1,0:T(8,128)(2,1)} %collective-permute-done.refs_1_), custom_call_target="tpu_custom_call" | custom-call | tf_op jit(solution)/shard_map/gather_mixed/pallas_call | solution.py:256
  361.8 9.2 gates_to_experts.1
  377.6 5.8 all-to-all-start.1
  393.1 64.7 %expert_0.1 = (bf16[2,4,4,128,2048]{4,3,2,1,0:T(8,128)(2,1)}, bf16[2,4,4,128,2048]{4,3,2,1,0:T(8,128)(2,1)}, f32[16,256,1]{2,1,0:T(8,128)}, bf16[16,256,512]{2,1...) custom-call(s32[8]{0:T(128)} %fusion.34._, f32[16,256,1]{2,1,0:T(8,128)} %get-tuple-element.258.gate_ref, ...), custom_call_target="tpu_custom_call" | custom-call | tf_op jit(solution)/shard_map/expert_0/pallas_call | solution.py:781
  457.8 35.7 %expert_grads_0.1 = (bf16[4,2,512,512]{3,2,1,0:T(8,128)(2,1)}, bf16[512,2048]{1,0:T(8,128)(2,1)}) custom-call(s32[8]{0:T(128)} %fusion.34._, bf16[2,4,4,128,2048]{4,3,2,1,0:T(8,128)(2,1)} %get-tuple-element.109.x_ref, bf16[8,2,128,2048]{3,2,1,0:T(8,128)(2,1)} %bitcast.147, bf16[2,4,2,128,2048]{4,3,2,1,0:T(8,128)(2,1)} %get-tuple-element.110.gp_ref, ...), custom_call_target="tpu_custom_call" | custom-call | tf_op jit(solution)/shard_map/expert_grads_0/pallas_call | solution.py:845
  498.7 65.4 %expert_1.1 = (bf16[2,4,4,128,2048]{4,3,2,1,0:T(8,128)(2,1)}, bf16[2,4,4,128,2048]{4,3,2,1,0:T(8,128)(2,1)}, f32[16,256,1]{2,1,0:T(8,128)}, bf16[16,256,512]{2,1...) custom-call(s32[8]{0:T(128)} %fusion.34._, ...), custom_call_target="tpu_custom_call", output_to_operand_aliasing={{0}: (7, {}), {1}: (8, {})} | custom-call | tf_op jit(solution)/shard_map/expert_1/pallas_call | solution.py:781
  564.2 35.7 %expert_grads_1.1 = (bf16[4,2,512,512]{3,2,1,0:T(8,128)(2,1)}, bf16[512,2048]{1,0:T(8,128)(2,1)}) custom-call(s32[8]{0:T(128)} %fusion.34._, bf16[2,4,4,128,2048]{4,3,2,1,0:T(8,128)(2,1)} %get-tuple-element.109.x_ref, bf16[8,2,128,2048]{3,2,1,0:T(8,128)(2,1)} %bitcast.149, bf16[2,4,2,128,2048]{4,3,2,1,0:T(8,128)(2,1)} %get-tuple-element.110.gp_ref, ...), custom_call_target="tpu_custom_call" | custom-call | tf_op jit(solution)/shard_map/expert_grads_1/pallas_call | solution.py:845
  611.6 153.9 %scatter_experts.1 = (f32[2,128,2048]{2,1,0:T(8,128)}, f32[2,128,2048]{2,1,0:T(8,128)}) custom-call(bf16[2,4,4,128,2048]{4,3,2,1,0:T(8,128)(2,1)} %get-tuple-element.129.refs_0_, bf16[2,4,4,128,2048]{4,3,2,1,0:T(8,128)(2,1)} %get-tuple-element.132.refs_1_), custom_call_target="tpu_custom_call" | custom-call | tf_op jit(solution)/shard_map/scatter_experts/pallas_call | solution.py:531
  765.6 8.0 gate_gradients.1
  796.3 17.2 %attended_gradients.1 = bf16[1,8,2,128,256]{4,3,2,1,0:T(8,128)(2,1)} custom-call(bf16[8,2,128,256]{3,2,1,0:T(8,128)(2,1)} %bitcast.174), custom_call_target="tpu_custom_call" | custom-call | tf_op jit(solution)/shard_map/attended_gradients/pallas_call | solution.py:616
  813.5 29.0 %attend_back.1 = (f32[2,2,1024,256]{3,2,1,0:T(8,128)}, bf16[2,1024,256]{2,1,0:T(8,128)(2,1)}, f32[2,2,8,128]{3,2,1,0:T(8,128)}, f32[2,1,256]{2,1,0:T(1,128)}) custom-call(bf16[2,1024,256]{2,1,0:T(8,128)(2,1)} %get-tuple-element.134.query_ref, bf16[2,1024,256]{2,1,0:T(8,128)(2,1)} %get-tuple-element.135.key_ref, ...), custom_call_target="tpu_custom_call" | custom-call | tf_op jit(solution)/shard_map/attend_back/pallas_call | solution.py:1091
  844.9 6.5 sum_inner.1
  851.3 27.9 %project_back.1 = (bf16[2,4,2,128,2048]{4,3,2,1,0:T(8,128)(2,1)}, bf16[2048,768]{1,0:T(8,128)(2,1)}) custom-call(f32[2,2,1024,256]{3,2,1,0:T(8,128)} %get-tuple-element.146.dn_ref, bf16[2,1024,256]{2,1,0:T(8,128)(2,1)} %get-tuple-element.147.dv_ref, f32[2,8,128,768]{3,2,1,0:T(8,128)} %copy-done, f32[8,2,2,1,128]{4,3,2,1,0:T(1,128)} %bitcast.205, ...), custom_call_target="tpu_custom_call" | custom-call | tf_op jit(solution)/shard_map/project_back/pallas_call | solution.py:1168
  885.0 78.8 %scatter_act.1 = (f32[2,128,2048]{2,1,0:T(8,128)}, f32[2,128,2048]{2,1,0:T(8,128)}, bf16[4,512,768]{2,1,0:T(8,128)(2,1)}) custom-call(bf16[2,4,2,128,2048]{4,3,2,1,0:T(8,128)(2,1)} %get-tuple-element.150.refs_0_, bf16[4,8,64,2048]{3,2,1,0:T(8,128)(2,1)} %bitcast.150, bf16[4,512,768]{2,1,0:T(8,128)(2,1)} %bitcast.175), custom_call_target="tpu_custom_call" | custom-call | tf_op jit(solution)/shard_map/scatter_act/pallas_call | solution.py:531
  973.3 34.6 %final_exchange.1 = (bf16[8,64,768]{2,1,0:T(8,128)(2,1)}, f32[32,1,1280]{2,1,0:T(1,128)}, bf16[4,64,2048]{2,1,0:T(8,128)(2,1)}) custom-call(bf16[8,64,768]{2,1,0:T(8,128)(2,1)} %bitcast.176, f32[32,1,1280]{2,1,0:T(1,128)} %pad_maximum_fusion.3.refs_1_, bf16[4,64,2048]{2,1,0:T(8,128)(2,1)} %bitcast.171), custom_call_target="tpu_custom_call" | custom-call | tf_op jit(solution)/shard_map/final_exchange/pallas_call | solution.py:662
  1029.7 7.1 finish_gradients.1
  (193 shorter events, 141.2 us)
Async XLA Ops:
  7.2 7.2 copy-start.16
  7.2 201.8 %all-gather.5.cloned.1.call-start = ((), (), s32[]{:S(2)}) async-start(), calls=%async_computation.4 | async-start | bytes 9437184 | tf_op jit(solution)/shard_map/all_gather | solution.py:1248
  18.3 83.4 %copy-start.14 = (bf16[2,512,1024]{2,1,0:T(8,128)(2,1)S(1)}, bf16[2,512,1024]{2,1,0:T(8,128)(2,1)}, u32[]{:S(2)}) copy-start(bf16[2,512,1024]{2,1,0:T(8,128)(2,1)} %param.27) | copy-start | bytes 6291460
  101.0 292.1 %all-gather.7.cloned.1.call-start = ((), (), s32[]{:S(2)}) async-start(), calls=%async_computation.5 | async-start | bytes 9437184 | tf_op jit(solution)/shard_map/all_gather | solution.py:1275
  107.6 7.5 copy-start.17
  107.6 7.6 copy-start.1
  107.6 100.1 %all-to-all-start = ((bf16[4,2,512,512]{3,2,1,0:T(8,128)(2,1)}), bf16[4,2,512,512]{3,2,1,0:T(8,128)(2,1)}, u32[]{:S(2)}, u32[]{:S(2)}) async-start(bf16[4,2,512,512]{3,2,1,0:T(8,128)(2,1)} %bitcast.153), calls=%async_computation | async-start | bytes 8388608 | tf_op jit(solution)/shard_map/all_to_all | solution.py:52
  113.0 260.6 %collective-permute-start.1 = (bf16[2,256,2048]{2,1,0:T(8,128)(2,1)}, bf16[2,256,2048]{2,1,0:T(8,128)(2,1)}, u32[]{:S(2)}, u32[]{:S(2)}) collective-permute-start(bf16[2,256,2048]{2,1,0:T(8,128)(2,1)} %param.29), channel_id=1, source_target_pairs={{0,8},{8,0},{1,9},{9,1},{2,10},{10,2},{3,11},{11,3},{4,12},{12,4},... | collective-permute-start | bytes 6291464 | tf_op jit(solution)/shard_map/ppermute | solution.py:48
  115.3 29.3 %copy-start.22 = (s32[16]{0:T(128)S(1)}, s32[16]{0:T(128)}, u32[]{:S(2)}) copy-start(s32[16]{0:T(128)} %param.21) | copy-start | bytes 196
  115.3 29.8 %copy-start.21 = (s32[2,1,128,8]{2,3,1,0:T(8,128)S(1)}, s32[2,1,128,8]{2,3,1,0:T(8,128)}, u32[]{:S(2)}) copy-start(s32[2,1,128,8]{2,3,1,0:T(8,128)} %param.19) | copy-start | bytes 24580
  134.0 12.5 %copy-start.12 = (bf16[1,512,512]{2,1,0:T(8,128)(2,1)S(1)}, bf16[1,512,512]{2,1,0:T(8,128)(2,1)}, u32[]{:S(2)}) copy-start(bf16[1,512,512]{2,1,0:T(8,128)(2,1)} %get-tuple-element.260) | copy-start | bytes 1572868
  134.0 12.5 %copy-start.13 = (bf16[1,512,512]{2,1,0:T(8,128)(2,1)S(1)}, bf16[1,512,512]{2,1,0:T(8,128)(2,1)}, u32[]{:S(2)}) copy-start(bf16[1,512,512]{2,1,0:T(8,128)(2,1)} %get-tuple-element.290) | copy-start | bytes 1572868
  142.1 106.7 %collective-permute-start = (bf16[2,128,2048]{2,1,0:T(8,128)(2,1)}, bf16[2,128,2048]{2,1,0:T(8,128)(2,1)}, u32[]{:S(2)}, u32[]{:S(2)}) collective-permute-start(bf16[2,128,2048]{2,1,0:T(8,128)(2,1)} %bitcast.169), channel_id=1, source_target_pairs={{0,16},{16,0},{1,17},{17,1},{2,18},{18,2},{3,19},{19,3},{4,20},{20... | collective-permute-start | bytes 3145736 | tf_op jit(solution)/shard_map/ppermute | solution.py:48
  146.6 6.0 copy-start.20
  191.9 15.8 %copy-start.11 = (bf16[1,8,2,128,256]{4,3,2,1,0:T(8,128)(2,1)S(1)}, bf16[1,8,2,128,256]{4,3,2,1,0:T(8,128)(2,1)}, u32[]{:S(2)}) copy-start(bf16[1,8,2,128,256]{4,3,2,1,0:T(8,128)(2,1)} %attended_to_rows.1) | copy-start | bytes 3145732
  193.4 15.6 %copy-start.3 = (bf16[2,1,128,2048]{3,2,1,0:T(8,128)(2,1)S(1)}, bf16[2,1,128,2048]{3,2,1,0:T(8,128)(2,1)}, u32[]{:S(2)}) copy-start(bf16[2,1,128,2048]{3,2,1,0:T(8,128)(2,1)} %param.17) | copy-start | bytes 3145732
  377.6 115.8 %all-to-all-start.1 = ((bf16[4,2,512,512]{3,2,1,0:T(8,128)(2,1)}), bf16[4,2,512,512]{3,2,1,0:T(8,128)(2,1)}, u32[]{:S(2)}, u32[]{:S(2)}) async-start(bf16[4,2,512,512]{3,2,1,0:T(8,128)(2,1)} %bitcast.154), calls=%async_computation.1 | async-start | bytes 8388608 | tf_op jit(solution)/shard_map/all_to_all | solution.py:52
  493.4 106.4 %all-to-all-start.2 = ((bf16[4,2,512,512]{3,2,1,0:T(8,128)(2,1)}), bf16[4,2,512,512]{3,2,1,0:T(8,128)(2,1)}, u32[]{:S(2)}, u32[]{:S(2)}) async-start(bf16[4,2,512,512]{3,2,1,0:T(8,128)(2,1)} %get-tuple-element.119), calls=%async_computation.2 | async-start | bytes 8388608 | tf_op jit(solution)/shard_map/all_to_all | solution.py:52
  602.9 162.7 %collective-permute-start.2 = (bf16[2,256,2048]{2,1,0:T(8,128)(2,1)}, bf16[2,256,2048]{2,1,0:T(8,128)(2,1)}, u32[]{:S(2)}, u32[]{:S(2)}) collective-permute-start(bf16[2,256,2048]{2,1,0:T(8,128)(2,1)} %fusion.12), channel_id=1, source_target_pairs={{0,8},{8,0},{1,9},{9,1},{2,10},{10,2},{3,11},{11,3},{4,12},{12,4},... | collective-permute-start | bytes 6291464 | tf_op jit(solution)/shard_map/ppermute | solution.py:1353
  773.6 5.9 copy-start.18
  773.6 256.1 %all-to-all-start.3 = ((bf16[4,2,512,512]{3,2,1,0:T(8,128)(2,1)}), bf16[4,2,512,512]{3,2,1,0:T(8,128)(2,1)}, u32[]{:S(2)}, u32[]{:S(2)}) async-start(bf16[4,2,512,512]{3,2,1,0:T(8,128)(2,1)} %get-tuple-element.160), calls=%async_computation.3 | async-start | bytes 8388608 | tf_op jit(solution)/shard_map/all_to_all | solution.py:52
  783.9 8.0 slice-start
  786.7 5.3 slice-start.1
  851.3 27.9 %copy-start.5 = (f32[2,128,2048]{2,1,0:T(8,128)S(1)}, f32[2,128,2048]{2,1,0:T(8,128)}, u32[]{:S(2)}) copy-start(f32[2,128,2048]{2,1,0:T(8,128)} %copy-done.4) | copy-start | bytes 6291460
  (10 other events, 27.6 us)
Sparse Core Ops, SparseCore 0:
  101.1 53.9 all-gather.4
  156.9 62.4 all-gather.6

commit v7 on v6

--- a/solution.py
+++ b/solution.py
@@ -638,14 +638,21 @@
     greet([device for device, _ in devices[1:]])
     me = plane * 2 * quads + here
     qkv, small = inputs[:2]
-    copies = [(qkv.at[place], outputs[0].at[here], device) for device, place in
-              [ctx_at(quads, n) for n in range(1, 2 * quads)]]
+    part = qkv.shape[2] // 3
+    columns = pl.ds(pl.multiple_of(here * part, 128), part)
+    split = [(slice(kind * part, (kind + 1) * part), kind) for kind in range(3)]
+    copies = [
+        (qkv.at[place, :, src], outputs[0].at[kind, :, columns], device)
+        for device, place in [ctx_at(quads, n) for n in range(1, 2 * quads)]
+        for src, kind in split
+    ]
     for ref, out in zip(inputs[2:], outputs[2:]):
         copies += [(ref.at[place], out.at[plane], device) for device, place in planes]
     copies += [(small.at[place], outputs[1].at[me], device) for device, place in devices[1:]]
     started = [mover.copy(*c) for c in copies]
     mover.go(*started)
-    mover.keep(qkv.at[here], outputs[0].at[here])
+    for src, kind in split:
+        mover.keep(qkv.at[here, :, src], outputs[0].at[kind, :, columns])
     mover.keep(small.at[me], outputs[1].at[me])
     for ref, out in zip(inputs[2:], outputs[2:]):
         mover.keep(ref.at[plane], out.at[plane])
@@ -657,15 +664,17 @@
 def final_exchange(qkv, small, planes):
     quads, lanes = lax.axis_size("quad"), lax.axis_size("lane")
     arrays = [qkv, small, *planes]
-    sems = 2 * quads - 1 + 4 * lanes * quads - 1 + len(planes) * (2 * lanes - 1)
+    sems = 3 * (2 * quads - 1) + 4 * lanes * quads - 1 + len(planes) * (2 * lanes - 1)
+    shapes = [x.shape for x in arrays]
+    shapes[0] = (3, qkv.shape[1], qkv.shape[0] * qkv.shape[2] // 3)
     vmem = pl.BlockSpec(memory_space=pltpu.VMEM)
     return pl.pallas_call(
         functools.partial(final_body, quads, lanes, len(arrays)),
-        out_shape=[jax.ShapeDtypeStruct(x.shape, x.dtype) for x in arrays],
+        out_shape=[jax.ShapeDtypeStruct(shape, x.dtype) for shape, x in zip(shapes, arrays)],
         in_specs=[vmem] * len(arrays),
         out_specs=[vmem] * len(arrays),
         scratch_shapes=[
-            pltpu.SemaphoreType.DMA((len(arrays),)),
+            pltpu.SemaphoreType.DMA((len(arrays) + 2,)),
             pltpu.SemaphoreType.DMA((sems,)),
             pltpu.SemaphoreType.DMA((sems,)),
         ],
@@ -1305,7 +1314,7 @@
     context = context + (lengths[:, 0],)
     *saved, attended = attend(*context)
     attended = exchange_rows(attended[None], "inward", "attended_to_rows", 7)[0]
-    attended, next_w = lax.optimization_barrier((attended, next_w))
+    attended, next_w, halves = lax.optimization_barrier((attended, next_w, halves))
     attended = attended.transpose(1, 2, 0, 3).reshape(batches, rows, width)
     x_mid = inputs + dot("mtd,de->mte", attended, out_w)
     mlp_root = inv_rms(x_mid)
@@ -1431,8 +1440,6 @@
     grad_qkv = grad_qkv.astype(F32)
     if beside:
         grad_out = jnp.sum(grad_planes[0].astype(F32), axis=0)
-    grad_qkv = grad_qkv.reshape(ctx_size, shard, 3, head_width).transpose(2, 1, 0, 3)
-    grad_qkv = grad_qkv.reshape(3, shard, width)
 
     return (
         mixed[:, None],

time: 1050 us -> 1040 us (level)
  local copies, waits for them, and re-layouts: 63.2 us -> 52 us
  transfers between devices with their start and end apart: 9 -> 9, of which waited for: 2 -> 2; matrix products, arithmetic and copies ran while one was open for 10% -> 9% of each run, Pallas kernels for 70% -> 71%
where the time goes in v7:
time: 1040 us; the launch traced here: 1030 us
  Pallas kernels  831 us (80%)
  local copies, waits for them, and re-layouts  52 us (5%)
  other arithmetic  41.6 us (4%)
  waiting for transfers between devices  41.1 us (4%)
  starting transfers between devices  29.3 us (3%)
  matrix products  21.6 us (2%)
  between operations  15.1 us (1%)
    pallas_call x2, Pallas kernels, scatter_rows(): pl.pallas_call(functools.partial(scatter_body, quads, lanes, partners, co...  233 us
    pallas_call x2, Pallas kernels, expert(): pl.pallas_call(functools.partial(expert_body, quads, bool(before)), out_s...  130 us
    pallas_call x1, Pallas kernels, gather_rows(): pl.pallas_call(functools.partial(gather_body, quads, partners), out_shape...  113 us
    pallas_call x1, Pallas kernels, start_gather(): pl.pallas_call(functools.partial(start_body, quads, lanes), out_shape=[li...  82.6 us
    pallas_call x2, Pallas kernels, expert_grads(): pl.pallas_call(grads_body, out_shape=(jax.ShapeDtypeStruct((dp, 2, width...  71.4 us
    pallas_call x4, Pallas kernels, exchange_rows(): pl.pallas_call(functools.partial(exchange_body, mode, lanes, quads, halve...  52.8 us
    pallas_call x1, Pallas kernels, final_exchange(): pl.pallas_call(functools.partial(final_body, quads, lanes, len(arrays)),...  34.9 us
    pallas_call x1, Pallas kernels, attend_back(): pl.pallas_call(functools.partial(attend_back_body, 256), out_shape=(jax.S...  29.1 us
  transfers between devices with their start and end apart: 9, of which 2 were waited for; matrix products, arithmetic and copies ran while one was open for 9% of the time, Pallas kernels for 71%

profile of v7, /device:TPU:0, one launch (start us, length us, event | category | flops | bytes accessed | tf_op | source)
XLA Modules:
  0.0 1031.8 jit_solution(14350576791506667400)
XLA Ops:
  18.3 82.6 %start_gather.1 = (bf16[2,4,2,128,2048]{4,3,2,1,0:T(8,128)(2,1)}, bf16[4,8,64,768]{3,2,1,0:T(8,128)(2,1)}, bf16[32,1,1280]{2,1,0:T(2,128)(2,1)}, bf16[4,64,2048]{2,1,0:T(8,128)(2,1)}) custom-call(bf16[2,128,2048]{2,1,0:T(8,128)(2,1)} %bitcast.147, bf16[8,64,768]{2,1,0:T(8,128)(2,1)} %reshape.480.qkv_ref, bf16[1,1280]{1,0:T(2,128)(2,1)} %reshape.482.small_ref, ...), custom_call_target="tpu_custom_call" | custom-call | tf_op jit(solution)/shard_map/start_gather/pallas_call | solution.py:343
  115.2 15.4 %project.1 = (bf16[2,4,2,128,2048]{4,3,2,1,0:T(8,128)(2,1)}, f32[2,8,128,768]{3,2,1,0:T(8,128)S(1)}, f32[8,4,128]{2,1,0:T(4,128)S(1)}) custom-call(bf16[2,4,2,128,2048]{4,3,2,1,0:T(8,128)(2,1)} %get-tuple-element.90.x_ref, f32[1,2048]{1,0:T(1,128)S(1)} %reshape.505.gain_ref, bf16[2048,768]{1,0:T(8,128)(2,1)S(1)} %bitcast.141), custom_call_target="tpu_custom_call" | custom-call | tf_op jit(solution)/shard_map/project/pallas_call | solution.py:950
  133.9 8.1 sum_squares.1
  154.0 19.6 %attend.1 = (bf16[2,1024,256]{2,1,0:T(8,128)(2,1)}, bf16[2,1024,256]{2,1,0:T(8,128)(2,1)}, bf16[2,1024,256]{2,1,0:T(8,128)(2,1)}, bf16[8,2,128,256]{3,2,1,0:T(8,128)(2,1)}) custom-call(f32[2,8,128,768]{3,2,1,0:T(8,128)} %copy-done, f32[2,2,8,128]{3,2,1,0:T(8,128)} %bitcast.181, f32[2,1,256]{2,1,0:T(1,128)} %reshape.506.gain_ref, ...), custom_call_target="tpu_custom_call" | custom-call | tf_op jit(solution)/shard_map/attend/pallas_call | solution.py:1024
  173.6 18.3 %attended_to_rows.1 = bf16[1,8,2,128,256]{4,3,2,1,0:T(8,128)(2,1)} custom-call(bf16[1,8,2,128,256]{4,3,2,1,0:T(8,128)(2,1)} %bitcast.175), custom_call_target="tpu_custom_call" | custom-call | tf_op jit(solution)/shard_map/attended_to_rows/pallas_call | solution.py:616
  193.7 14.0 %all-to-all-done.both_ref = bf16[4,2,512,512]{3,2,1,0:T(8,128)(2,1)} async-done(((bf16[4,2,512,512]{3,2,1,0:T(8,128)(2,1)}), bf16[4,2,512,512]{3,2,1,0:T(8,128)(2,1)}, u32[]{:S(2)}, u32[]{:S(2)}) %all-to-all-start) | async-done | bytes 4194336 | tf_op jit(solution)/shard_map/all_to_all | solution.py:52
  212.4 6.2 multiply_reduce_fusion.2
  222.3 26.4 %collective-permute-done.refs_1_ = bf16[2,128,2048]{2,1,0:T(8,128)(2,1)} collective-permute-done((bf16[2,128,2048]{2,1,0:T(8,128)(2,1)}, bf16[2,128,2048]{2,1,0:T(8,128)(2,1)}, u32[]{:S(2)}, u32[]{:S(2)}) %collective-permute-start) | collective-permute-done | bytes 1048608 | tf_op jit(solution)/shard_map/ppermute | solution.py:48
  248.7 113.0 %gather_mixed.1 = (bf16[2,4,4,128,2048]{4,3,2,1,0:T(8,128)(2,1)}, bf16[2,4,2,128,2048]{4,3,2,1,0:T(8,128)(2,1)}) custom-call(bf16[2,128,2048]{2,1,0:T(8,128)(2,1)} %multiply_convert_fusion.refs_0_, bf16[2,128,2048]{2,1,0:T(8,128)(2,1)} %collective-permute-done.refs_1_), custom_call_target="tpu_custom_call" | custom-call | tf_op jit(solution)/shard_map/gather_mixed/pallas_call | solution.py:256
  361.7 9.2 gates_to_experts.1
  389.0 64.6 %expert_0.1 = (bf16[2,4,4,128,2048]{4,3,2,1,0:T(8,128)(2,1)}, bf16[2,4,4,128,2048]{4,3,2,1,0:T(8,128)(2,1)}, f32[16,256,1]{2,1,0:T(8,128)}, bf16[16,256,512]{2,1...) custom-call(s32[8]{0:T(128)} %fusion.34._, f32[16,256,1]{2,1,0:T(8,128)} %get-tuple-element.243.gate_ref, ...), custom_call_target="tpu_custom_call" | custom-call | tf_op jit(solution)/shard_map/expert_0/pallas_call | solution.py:790
  453.6 35.7 %expert_grads_0.1 = (bf16[4,2,512,512]{3,2,1,0:T(8,128)(2,1)}, bf16[512,2048]{1,0:T(8,128)(2,1)}) custom-call(s32[8]{0:T(128)} %fusion.34._, bf16[2,4,4,128,2048]{4,3,2,1,0:T(8,128)(2,1)} %get-tuple-element.111.x_ref, bf16[8,2,128,2048]{3,2,1,0:T(8,128)(2,1)} %bitcast.143, bf16[2,4,2,128,2048]{4,3,2,1,0:T(8,128)(2,1)} %get-tuple-element.112.gp_ref, ...), custom_call_target="tpu_custom_call" | custom-call | tf_op jit(solution)/shard_map/expert_grads_0/pallas_call | solution.py:854
  494.6 65.4 %expert_1.1 = (bf16[2,4,4,128,2048]{4,3,2,1,0:T(8,128)(2,1)}, bf16[2,4,4,128,2048]{4,3,2,1,0:T(8,128)(2,1)}, f32[16,256,1]{2,1,0:T(8,128)}, bf16[16,256,512]{2,1...) custom-call(s32[8]{0:T(128)} %fusion.34._, ...), custom_call_target="tpu_custom_call", output_to_operand_aliasing={{0}: (7, {}), {1}: (8, {})} | custom-call | tf_op jit(solution)/shard_map/expert_1/pallas_call | solution.py:790
  560.0 35.7 %expert_grads_1.1 = (bf16[4,2,512,512]{3,2,1,0:T(8,128)(2,1)}, bf16[512,2048]{1,0:T(8,128)(2,1)}) custom-call(s32[8]{0:T(128)} %fusion.34._, bf16[2,4,4,128,2048]{4,3,2,1,0:T(8,128)(2,1)} %get-tuple-element.111.x_ref, bf16[8,2,128,2048]{3,2,1,0:T(8,128)(2,1)} %bitcast.145, bf16[2,4,2,128,2048]{4,3,2,1,0:T(8,128)(2,1)} %get-tuple-element.112.gp_ref, ...), custom_call_target="tpu_custom_call" | custom-call | tf_op jit(solution)/shard_map/expert_grads_1/pallas_call | solution.py:854
  608.3 153.9 %scatter_experts.1 = (f32[2,128,2048]{2,1,0:T(8,128)}, f32[2,128,2048]{2,1,0:T(8,128)}) custom-call(bf16[2,4,4,128,2048]{4,3,2,1,0:T(8,128)(2,1)} %get-tuple-element.131.refs_0_, bf16[2,4,4,128,2048]{4,3,2,1,0:T(8,128)(2,1)} %get-tuple-element.134.refs_1_), custom_call_target="tpu_custom_call" | custom-call | tf_op jit(solution)/shard_map/scatter_experts/pallas_call | solution.py:531
  762.2 8.0 gate_gradients.1
  792.9 17.3 %attended_gradients.1 = bf16[1,8,2,128,256]{4,3,2,1,0:T(8,128)(2,1)} custom-call(bf16[8,2,128,256]{3,2,1,0:T(8,128)(2,1)} %bitcast.169), custom_call_target="tpu_custom_call" | custom-call | tf_op jit(solution)/shard_map/attended_gradients/pallas_call | solution.py:616
  810.2 29.1 %attend_back.1 = (f32[2,2,1024,256]{3,2,1,0:T(8,128)}, bf16[2,1024,256]{2,1,0:T(8,128)(2,1)}, f32[2,2,8,128]{3,2,1,0:T(8,128)}, f32[2,1,256]{2,1,0:T(1,128)}) custom-call(bf16[2,1024,256]{2,1,0:T(8,128)(2,1)} %get-tuple-element.136.query_ref, bf16[2,1024,256]{2,1,0:T(8,128)(2,1)} %get-tuple-element.137.key_ref, ...), custom_call_target="tpu_custom_call" | custom-call | tf_op jit(solution)/shard_map/attend_back/pallas_call | solution.py:1100
  841.5 6.4 sum_inner.1
  848.0 27.7 %project_back.1 = (bf16[2,4,2,128,2048]{4,3,2,1,0:T(8,128)(2,1)}, bf16[2048,768]{1,0:T(8,128)(2,1)}) custom-call(f32[2,2,1024,256]{3,2,1,0:T(8,128)} %get-tuple-element.148.dn_ref, bf16[2,1024,256]{2,1,0:T(8,128)(2,1)} %get-tuple-element.149.dv_ref, f32[2,8,128,768]{3,2,1,0:T(8,128)} %copy-done, f32[8,2,2,1,128]{4,3,2,1,0:T(1,128)} %bitcast.194, ...), custom_call_target="tpu_custom_call" | custom-call | tf_op jit(solution)/shard_map/project_back/pallas_call | solution.py:1177
  875.7 5.9 bitcast_convert_fusion
  881.6 78.9 %scatter_act.1 = (f32[2,128,2048]{2,1,0:T(8,128)}, f32[2,128,2048]{2,1,0:T(8,128)}, bf16[4,512,768]{2,1,0:T(8,128)(2,1)}) custom-call(bf16[2,4,2,128,2048]{4,3,2,1,0:T(8,128)(2,1)} %get-tuple-element.152.refs_0_, bf16[4,8,64,2048]{3,2,1,0:T(8,128)(2,1)} %bitcast.146, bf16[4,512,768]{2,1,0:T(8,128)(2,1)} %bitcast.170), custom_call_target="tpu_custom_call" | custom-call | tf_op jit(solution)/shard_map/scatter_act/pallas_call | solution.py:531
  970.0 34.9 %final_exchange.1 = (bf16[3,64,2048]{2,1,0:T(8,128)(2,1)}, f32[32,1,1280]{2,1,0:T(1,128)}, bf16[4,64,2048]{2,1,0:T(8,128)(2,1)}) custom-call(bf16[8,64,768]{2,1,0:T(8,128)(2,1)} %bitcast.171, f32[32,1,1280]{2,1,0:T(1,128)} %pad_maximum_fusion.3.refs_1_, bf16[4,64,2048]{2,1,0:T(8,128)(2,1)} %bitcast.166), custom_call_target="tpu_custom_call" | custom-call | tf_op jit(solution)/shard_map/final_exchange/pallas_call | solution.py:671
  1017.3 7.1 finish_gradients.1
  (183 shorter events, 133.1 us)
Async XLA Ops:
  7.2 7.2 copy-start.15
  7.2 205.2 %all-gather.5.cloned.1.call-start = ((), (), s32[]{:S(2)}) async-start(), calls=%async_computation.4 | async-start | bytes 9437184 | tf_op jit(solution)/shard_map/all_gather | solution.py:1257
  18.3 83.4 %copy-start.13 = (bf16[2,512,1024]{2,1,0:T(8,128)(2,1)S(1)}, bf16[2,512,1024]{2,1,0:T(8,128)(2,1)}, u32[]{:S(2)}) copy-start(bf16[2,512,1024]{2,1,0:T(8,128)(2,1)} %param.27) | copy-start | bytes 6291460
  101.0 288.1 %all-gather.7.cloned.1.call-start = ((), (), s32[]{:S(2)}) async-start(), calls=%async_computation.5 | async-start | bytes 9437184 | tf_op jit(solution)/shard_map/all_gather | solution.py:1284
  107.6 7.4 copy-start.16
  107.6 7.6 copy-start.1
  107.6 100.0 %all-to-all-start = ((bf16[4,2,512,512]{3,2,1,0:T(8,128)(2,1)}), bf16[4,2,512,512]{3,2,1,0:T(8,128)(2,1)}, u32[]{:S(2)}, u32[]{:S(2)}) async-start(bf16[4,2,512,512]{3,2,1,0:T(8,128)(2,1)} %bitcast.149), calls=%async_computation | async-start | bytes 8388608 | tf_op jit(solution)/shard_map/all_to_all | solution.py:52
  113.0 260.6 %collective-permute-start.1 = (bf16[2,256,2048]{2,1,0:T(8,128)(2,1)}, bf16[2,256,2048]{2,1,0:T(8,128)(2,1)}, u32[]{:S(2)}, u32[]{:S(2)}) collective-permute-start(bf16[2,256,2048]{2,1,0:T(8,128)(2,1)} %param.29), channel_id=1, source_target_pairs={{0,8},{8,0},{1,9},{9,1},{2,10},{10,2},{3,11},{11,3},{4,12},{12,4},... | collective-permute-start | bytes 6291464 | tf_op jit(solution)/shard_map/ppermute | solution.py:48
  115.2 29.3 %copy-start.20 = (s32[16]{0:T(128)S(1)}, s32[16]{0:T(128)}, u32[]{:S(2)}) copy-start(s32[16]{0:T(128)} %param.21) | copy-start | bytes 196
  115.2 29.8 %copy-start.19 = (s32[2,1,128,8]{2,3,1,0:T(8,128)S(1)}, s32[2,1,128,8]{2,3,1,0:T(8,128)}, u32[]{:S(2)}) copy-start(s32[2,1,128,8]{2,3,1,0:T(8,128)} %param.19) | copy-start | bytes 24580
  133.9 12.5 %copy-start.11 = (bf16[1,512,512]{2,1,0:T(8,128)(2,1)S(1)}, bf16[1,512,512]{2,1,0:T(8,128)(2,1)}, u32[]{:S(2)}) copy-start(bf16[1,512,512]{2,1,0:T(8,128)(2,1)} %get-tuple-element.245) | copy-start | bytes 1572868
  133.9 12.5 %copy-start.12 = (bf16[1,512,512]{2,1,0:T(8,128)(2,1)S(1)}, bf16[1,512,512]{2,1,0:T(8,128)(2,1)}, u32[]{:S(2)}) copy-start(bf16[1,512,512]{2,1,0:T(8,128)(2,1)} %get-tuple-element.278) | copy-start | bytes 1572868
  141.9 106.7 %collective-permute-start = (bf16[2,128,2048]{2,1,0:T(8,128)(2,1)}, bf16[2,128,2048]{2,1,0:T(8,128)(2,1)}, u32[]{:S(2)}, u32[]{:S(2)}) collective-permute-start(bf16[2,128,2048]{2,1,0:T(8,128)(2,1)} %bitcast.164), channel_id=1, source_target_pairs={{0,16},{16,0},{1,17},{17,1},{2,18},{18,2},{3,19},{19,3},{4,20},{20... | collective-permute-start | bytes 3145736 | tf_op jit(solution)/shard_map/ppermute | solution.py:48
  144.7 5.8 copy-start.17
  147.4 6.0 copy-start.18
  373.6 115.7 %all-to-all-start.1 = ((bf16[4,2,512,512]{3,2,1,0:T(8,128)(2,1)}), bf16[4,2,512,512]{3,2,1,0:T(8,128)(2,1)}, u32[]{:S(2)}, u32[]{:S(2)}) async-start(bf16[4,2,512,512]{3,2,1,0:T(8,128)(2,1)} %bitcast.150), calls=%async_computation.1 | async-start | bytes 8388608 | tf_op jit(solution)/shard_map/all_to_all | solution.py:52
  489.3 106.4 %all-to-all-start.2 = ((bf16[4,2,512,512]{3,2,1,0:T(8,128)(2,1)}), bf16[4,2,512,512]{3,2,1,0:T(8,128)(2,1)}, u32[]{:S(2)}, u32[]{:S(2)}) async-start(bf16[4,2,512,512]{3,2,1,0:T(8,128)(2,1)} %get-tuple-element.121), calls=%async_computation.2 | async-start | bytes 8388608 | tf_op jit(solution)/shard_map/all_to_all | solution.py:52
  598.8 163.4 %collective-permute-start.2 = (bf16[2,256,2048]{2,1,0:T(8,128)(2,1)}, bf16[2,256,2048]{2,1,0:T(8,128)(2,1)}, u32[]{:S(2)}, u32[]{:S(2)}) collective-permute-start(bf16[2,256,2048]{2,1,0:T(8,128)(2,1)} %fusion.12), channel_id=1, source_target_pairs={{0,8},{8,0},{1,9},{9,1},{2,10},{10,2},{3,11},{11,3},{4,12},{12,4},... | collective-permute-start | bytes 6291464 | tf_op jit(solution)/shard_map/ppermute | solution.py:1362
  771.1 246.2 %all-to-all-start.3 = ((bf16[4,2,512,512]{3,2,1,0:T(8,128)(2,1)}), bf16[4,2,512,512]{3,2,1,0:T(8,128)(2,1)}, u32[]{:S(2)}, u32[]{:S(2)}) async-start(bf16[4,2,512,512]{3,2,1,0:T(8,128)(2,1)} %get-tuple-element.162), calls=%async_computation.3 | async-start | bytes 8388608 | tf_op jit(solution)/shard_map/all_to_all | solution.py:52
  780.5 2.8 copy-start.7
  780.5 8.0 slice-start
  783.3 5.3 slice-start.1
  848.0 27.8 %copy-start.5 = (f32[2,128,2048]{2,1,0:T(8,128)S(1)}, f32[2,128,2048]{2,1,0:T(8,128)}, u32[]{:S(2)}) copy-start(f32[2,128,2048]{2,1,0:T(8,128)} %copy-done.4) | copy-start | bytes 6291460
  1010.9 4.5 copy-start.8
  (8 other events, 15.4 us)
Sparse Core Ops, SparseCore 0:
  101.1 53.9 all-gather.4
  156.9 61.5 all-gather.6
